TPU v7x, 32 devices: a whole 2x2x4 slice. The times are simulated.
32 devices in a mesh: dp: 16 (over z, x, core), tensor: 2 (over y).
Axes of the slice: x: 2, y: 2, z: 4, core: 2. Of those that a mesh axis runs over, the one named last changes fastest.
Arguments:
- inputs: bfloat16 [32768, 1024], P('dp'), may hold values from -6 to 6
- cotangent: bfloat16 [32768, 1024], P('dp'), may hold values from -6 to 6
- segment_ids: int32 [16, 2048], P('dp'), may hold values from 0 to 7, never falling along the last dimension, each value on 1 to 1024 neighbouring positions
- w_qkv: float32 [3, 1024, 1024], P(None, 'dp', 'tensor'), may hold values from -0.1875 to 0.1875
- w_out: float32 [1024, 1024], P('tensor', 'dp'), may hold values from -1.5 to 1.5
- w_fc1: float32 [1024, 4096], P('dp', 'tensor'), may hold values from -0.1875 to 0.1875
- w_fc2: float32 [4096, 1024], P('tensor', 'dp'), may hold values from -0.09375 to 0.09375
- norm_gain: float32 [4, 1024], replicated, may hold values from 0.5 to 1.5
- norm_bias: float32 [4, 1024], replicated, may hold values from -1.8 to 1.8
- head_bias: float32 [2, 1024], replicated, may hold values from -3 to 3
- out_bias: float32 [2, 1024], replicated, may hold values from -1.2 to 1.2
- fc1_bias: float32 [4096], replicated, may hold values from -1.8 to 1.8
Outputs:
- output: bfloat16 [32768, 1024], P(('dp', 'tensor'))
- d_inputs: bfloat16 [32768, 1024], P(('dp', 'tensor'))
- grad_qkv: float32 [3, 1024, 1024], P(None, 'dp', 'tensor')
- grad_out: float32 [1024, 1024], P('tensor', 'dp')
- grad_fc1: float32 [1024, 4096], P('dp', 'tensor')
- grad_fc2: float32 [4096, 1024], P('tensor', 'dp')
- grad_norm_gain: float32 [4, 1024], replicated
- grad_norm_bias: float32 [4, 1024], replicated
- grad_head_bias: float32 [2, 1024], replicated
- grad_out_bias: float32 [2, 1024], replicated
- grad_fc1_bias: float32 [4096], replicated
Inputs may be any that keep to these rules, and one draw needn't show every extreme that they name: `segment_ids`: in each packed sequence the segment numbers start at 0, never fall, and every number up to the sequence's largest appears; a segment is a document or the padding at the sequence's end. A segment has at most 1024 tokens, and some segment has exactly that many.
All inputs are finite; a program needn't handle non-finite values.
Results may differ from a plain program's by a relative error of at most 0.02.
Values may be sent and summed in bfloat16 or wider, within the bound.
No kernel may reach another device: no remote copies, remote signals or barrier semaphores. Data moves between devices by JAX's collectives and lax.ppermute only.
A program may use at most 512 MiB of HBM per device.

v0:
```python
from functools import partial

import jax
import jax.numpy as jnp
from jax import lax
from jax.sharding import PartitionSpec as P

HD = 64


eps_norm = 1e-05
query_scale = 0.00390625
relax_alpha = 32.0
masked_score = -1000000000.0


def layer_norm(values, gain_row, shift_row):
    row_mean = jnp.mean(values, axis=-1, keepdims=True)
    centered = values - row_mean
    variance = jnp.mean(centered * centered, axis=-1, keepdims=True)
    return centered * lax.rsqrt(variance + eps_norm) * gain_row + shift_row


def norm_back(values, gain_row, shift_row, grad_rows, own_start, own_count):
    pull_back = jax.vjp(lambda inner_values: layer_norm(inner_values, gain_row, shift_row), values)[
        1
    ]
    d_values = pull_back(grad_rows)[0]
    own_values = lax.dynamic_slice_in_dim(values, own_start, own_count, 0)
    own_grad = lax.dynamic_slice_in_dim(grad_rows, own_start, own_count, 0)
    row_mean = jnp.mean(own_values, axis=-1, keepdims=True)
    centered = own_values - row_mean
    variance = jnp.mean(centered * centered, axis=-1, keepdims=True)
    normed = centered * lax.rsqrt(variance + eps_norm)
    return (d_values, jnp.sum(normed * own_grad, axis=0), jnp.sum(own_grad, axis=0))


def gelu_tanh(values):
    return jax.nn.gelu(values, approximate=True)


def contract_rows(left_side, right_side):
    return lax.dot_general(
        left_side, right_side, (((0,), (0,)), ((), ())), preferred_element_type=jnp.float32
    )


def contract_cols(left_side, right_side):
    return lax.dot_general(
        left_side, right_side, (((1,), (1,)), ((), ())), preferred_element_type=jnp.float32
    )


def allowed_mask(segment, row_first, block_rows, key_count):
    query_seg = lax.slice_in_dim(segment, row_first, row_first + block_rows)
    query_pos = row_first + jnp.arange(block_rows, dtype=jnp.int32)
    key_pos = jnp.arange(key_count, dtype=jnp.int32)
    return (query_seg[:, None] == segment[None, :key_count]) & (
        key_pos[None, :] <= query_pos[:, None]
    )


def attend_forward(block_rows, packed):
    queries, key_rows, values, segment = packed
    seq_length = queries.shape[0]
    outputs, peak_list, total_list = ([], [], [])
    for row_first in range(0, seq_length, block_rows):
        row_last = row_first + block_rows
        scaled = queries[row_first:row_last] * query_scale
        scores = jnp.einsum(
            "qhd,khd->hqk", scaled, key_rows[:row_last], preferred_element_type=jnp.float32
        )
        allowed = allowed_mask(segment, row_first, block_rows, row_last)
        scores = jnp.where(allowed[None], scores, masked_score)
        row_peak = jnp.max(scores, axis=2, keepdims=True)
        exponent = jnp.exp(relax_alpha * (scores - row_peak))
        row_total = jnp.sum(exponent, axis=2, keepdims=True)
        probability = (exponent / row_total).astype(jnp.bfloat16)
        outputs.append(
            jnp.einsum(
                "hqk,khd->qhd", probability, values[:row_last], preferred_element_type=jnp.float32
            )
        )
        peak_list.append(row_peak)
        total_list.append(row_total)
    return (
        jnp.concatenate(outputs, axis=0).astype(jnp.bfloat16),
        jnp.stack(peak_list),
        jnp.stack(total_list),
    )


def attend_backward(block_rows, packed):
    queries, key_rows, values, grad_rows, segment, peak_list, total_list = packed
    seq_length = queries.shape[0]
    key_accum = jnp.zeros(key_rows.shape, jnp.float32)
    value_accum = jnp.zeros(values.shape, jnp.float32)
    query_parts = []
    for block_index, row_first in enumerate(range(0, seq_length, block_rows)):
        row_last = row_first + block_rows
        scaled = queries[row_first:row_last] * query_scale
        scores = jnp.einsum(
            "qhd,khd->hqk", scaled, key_rows[:row_last], preferred_element_type=jnp.float32
        )
        allowed = allowed_mask(segment, row_first, block_rows, row_last)
        scores = jnp.where(allowed[None], scores, masked_score)
        probability = (
            jnp.exp(relax_alpha * (scores - peak_list[block_index])) / total_list[block_index]
        )
        prob_low = probability.astype(jnp.bfloat16)
        block_grad = grad_rows[row_first:row_last]
        value_accum = value_accum.at[:row_last].add(
            jnp.einsum("hqk,qhd->khd", prob_low, block_grad, preferred_element_type=jnp.float32)
        )
        d_prob = jnp.einsum(
            "qhd,khd->hqk", block_grad, values[:row_last], preferred_element_type=jnp.float32
        )
        d_scores = (
            relax_alpha
            * probability
            * (d_prob - jnp.sum(probability * d_prob, axis=2, keepdims=True))
        )
        d_scores = d_scores.astype(jnp.bfloat16)
        query_parts.append(
            jnp.einsum(
                "hqk,khd->qhd", d_scores, key_rows[:row_last], preferred_element_type=jnp.float32
            )
            * query_scale
        )
        key_accum = key_accum.at[:row_last].add(
            jnp.einsum("hqk,qhd->khd", d_scores, scaled, preferred_element_type=jnp.float32)
        )
    d_queries = jnp.concatenate(query_parts, axis=0).astype(jnp.bfloat16)
    return (d_queries, key_accum.astype(jnp.bfloat16), value_accum.astype(jnp.bfloat16))


def per_device(
    inputs,
    cotangent,
    segment_ids,
    w_qkv,
    w_out,
    w_fc1,
    w_fc2,
    norm_gain,
    norm_bias,
    head_bias,
    out_bias,
    fc1_bias,
):
    tensor_count = lax.axis_size("tensor")
    tensor_rank = lax.axis_index("tensor")
    token_count = inputs.shape[0]
    seq_count, seq_length = segment_ids.shape
    block_rows = min(512, seq_length)
    shard_rows = token_count // tensor_count
    row_start = tensor_rank * shard_rows
    w_attn, w_proj, w_up, w_down = (
        lax.all_gather(w_qkv.astype(jnp.bfloat16), "dp", axis=1, tiled=True),
        lax.all_gather(w_out.astype(jnp.bfloat16), "dp", axis=1, tiled=True),
        lax.all_gather(w_fc1.astype(jnp.bfloat16), "dp", axis=0, tiled=True),
        lax.all_gather(w_fc2.astype(jnp.bfloat16), "dp", axis=1, tiled=True),
    )
    group_width = w_attn.shape[2]
    hidden_width = w_up.shape[1]
    local_heads = group_width // HD
    col_start = tensor_rank * group_width
    hid_start = tensor_rank * hidden_width
    bias_heads = lax.dynamic_slice_in_dim(head_bias, col_start, group_width, 1)
    bias_hidden = lax.dynamic_slice_in_dim(fc1_bias, hid_start, hidden_width, 0)
    inputs_wide = inputs.astype(jnp.float32)
    normed_in = layer_norm(inputs_wide, norm_gain[0], norm_bias[0]).astype(jnp.bfloat16)
    projected = jnp.einsum("td,jdc->jtc", normed_in, w_attn, preferred_element_type=jnp.float32)
    queries = (projected[0] + bias_heads[0]).astype(jnp.bfloat16)
    key_rows = projected[1].astype(jnp.bfloat16)
    values = (projected[2] + bias_heads[1]).astype(jnp.bfloat16)
    head_shape = (seq_count, seq_length, local_heads, HD)
    query_heads = queries.reshape(head_shape)
    key_heads = key_rows.reshape(head_shape)
    value_heads = values.reshape(head_shape)
    attended, peak_list, total_list = lax.map(
        partial(attend_forward, block_rows), (query_heads, key_heads, value_heads, segment_ids)
    )
    attended = attended.reshape(token_count, group_width)
    partial_attn = jnp.dot(attended, w_proj, preferred_element_type=jnp.float32)
    attn_rows = (
        lax.psum(partial_attn.astype(jnp.bfloat16), "tensor").astype(jnp.float32) + out_bias[0]
    )
    resid = inputs_wide + layer_norm(attn_rows, norm_gain[1], norm_bias[1])
    normed_mid = layer_norm(resid, norm_gain[2], norm_bias[2]).astype(jnp.bfloat16)
    pre_act = jnp.dot(normed_mid, w_up, preferred_element_type=jnp.float32) + bias_hidden
    activated = gelu_tanh(pre_act).astype(jnp.bfloat16)
    partial_mlp = jnp.dot(activated, w_down, preferred_element_type=jnp.float32)
    mlp_rows = (
        lax.psum(partial_mlp.astype(jnp.bfloat16), "tensor").astype(jnp.float32) + out_bias[1]
    )
    cot_rows = cotangent.astype(jnp.float32)
    out_rows = resid + layer_norm(mlp_rows, norm_gain[3], norm_bias[3])
    d_mlp, gain_three, shift_three = norm_back(
        mlp_rows, norm_gain[3], norm_bias[3], cot_rows, row_start, shard_rows
    )
    d_mlp_low = d_mlp.astype(jnp.bfloat16)
    bias_mlp = jnp.sum(
        lax.dynamic_slice_in_dim(d_mlp_low, row_start, shard_rows, 0), axis=0, dtype=jnp.float32
    )
    grad_down = contract_rows(activated, d_mlp_low)
    d_act = contract_cols(d_mlp_low, w_down)
    d_pre = jax.vjp(gelu_tanh, pre_act)[1](d_act)[0].astype(jnp.bfloat16)
    grad_up = contract_rows(normed_mid, d_pre)
    grad_hidden = jnp.sum(d_pre, axis=0, dtype=jnp.float32)
    partial_mid = contract_cols(d_pre, w_up)
    d_mid = lax.psum(partial_mid.astype(jnp.bfloat16), "tensor").astype(jnp.float32)
    d_resid_part, gain_two, shift_two = norm_back(
        resid, norm_gain[2], norm_bias[2], d_mid, row_start, shard_rows
    )
    d_resid = cot_rows + d_resid_part
    d_attn, gain_one, shift_one = norm_back(
        attn_rows, norm_gain[1], norm_bias[1], d_resid, row_start, shard_rows
    )
    d_attn_low = d_attn.astype(jnp.bfloat16)
    bias_attn = jnp.sum(
        lax.dynamic_slice_in_dim(d_attn_low, row_start, shard_rows, 0), axis=0, dtype=jnp.float32
    )
    grad_proj = contract_rows(attended, d_attn_low)
    d_attended = contract_cols(d_attn_low, w_proj).astype(jnp.bfloat16)
    d_queries, d_keys, d_values = lax.map(
        partial(attend_backward, block_rows),
        (
            query_heads,
            key_heads,
            value_heads,
            d_attended.reshape(head_shape),
            segment_ids,
            peak_list,
            total_list,
        ),
    )
    d_proj = jnp.stack(
        [
            d_queries.reshape(token_count, group_width),
            d_keys.reshape(token_count, group_width),
            d_values.reshape(token_count, group_width),
        ]
    )
    grad_attn = jnp.einsum("td,jtc->jdc", normed_in, d_proj, preferred_element_type=jnp.float32)
    partial_in = jnp.einsum("jtc,jdc->td", d_proj, w_attn, preferred_element_type=jnp.float32)
    d_in = lax.psum(partial_in.astype(jnp.bfloat16), "tensor").astype(jnp.float32)
    d_input_part, gain_zero, shift_zero = norm_back(
        inputs_wide, norm_gain[0], norm_bias[0], d_in, row_start, shard_rows
    )
    d_inputs = d_resid + d_input_part
    layer_out = lax.dynamic_slice_in_dim(out_rows, row_start, shard_rows, 0)
    d_out_rows = lax.dynamic_slice_in_dim(d_inputs, row_start, shard_rows, 0)
    head_terms = jnp.stack(
        [
            jnp.sum(d_proj[0], axis=0, dtype=jnp.float32),
            jnp.sum(d_proj[2], axis=0, dtype=jnp.float32),
        ]
    )
    head_full = lax.dynamic_update_slice_in_dim(
        jnp.zeros(head_bias.shape, jnp.float32), head_terms, col_start, 1
    )
    hidden_full = lax.dynamic_update_slice_in_dim(
        jnp.zeros(fc1_bias.shape, jnp.float32), grad_hidden, hid_start, 0
    )
    gain_terms = jnp.stack([gain_zero, gain_one, gain_two, gain_three])
    shift_terms = jnp.stack([shift_zero, shift_one, shift_two, shift_three])
    bias_terms = jnp.stack([bias_attn, bias_mlp])
    gain_sum, shift_sum, head_sum, bias_sum, hidden_sum = lax.psum(
        (gain_terms, shift_terms, head_full, bias_terms, hidden_full), ("dp", "tensor")
    )
    grad_qkv, grad_out, grad_fc1, grad_fc2 = (
        lax.psum_scatter(
            grad_attn.astype(jnp.bfloat16), "dp", scatter_dimension=1, tiled=True
        ).astype(jnp.float32),
        lax.psum_scatter(
            grad_proj.astype(jnp.bfloat16), "dp", scatter_dimension=1, tiled=True
        ).astype(jnp.float32),
        lax.psum_scatter(
            grad_up.astype(jnp.bfloat16), "dp", scatter_dimension=0, tiled=True
        ).astype(jnp.float32),
        lax.psum_scatter(
            grad_down.astype(jnp.bfloat16), "dp", scatter_dimension=1, tiled=True
        ).astype(jnp.float32),
    )
    return (
        layer_out.astype(jnp.bfloat16),
        d_out_rows.astype(jnp.bfloat16),
        grad_qkv,
        grad_out,
        grad_fc1,
        grad_fc2,
        gain_sum,
        shift_sum,
        head_sum,
        bias_sum,
        hidden_sum,
    )


def solution(mesh):
    return jax.shard_map(
        per_device,
        mesh=mesh,
        in_specs=(
            P("dp", None),
            P("dp", None),
            P("dp", None),
            P(None, "dp", "tensor"),
            P("tensor", "dp"),
            P("dp", "tensor"),
            P("tensor", "dp"),
            P(),
            P(),
            P(),
            P(),
            P(),
        ),
        out_specs=(
            P(("dp", "tensor"), None),
            P(("dp", "tensor"), None),
            P(None, "dp", "tensor"),
            P("tensor", "dp"),
            P("dp", "tensor"),
            P("tensor", "dp"),
            P(),
            P(),
            P(),
            P(),
            P(),
        ),
        check_vma=False,
    )
```

profile of v0, /device:TPU:0, one launch (start us, length us, event | category | flops | bytes accessed | tf_op | source)
XLA Modules:
  0.0 1503.5 jit_solution(5447794359743557644)
XLA Ops:
  26.9 31.9 %all-gather.5.cloned.1.call-done = bf16[3,1024,512]{2,1,0:T(8,128)(2,1)} async-done(((bf16[3,64,512]{2,1,0:T(8,128)(2,1)}), bf16[3,1024,512]{2,1,0:T(8,128)(2,1)}) %all-gather.5.cloned.1.call-update) | async-done | bytes 3145744 | tf_op jit(solution)/shard_map/all_gather | solution.py:159
  58.8 10.1 convolution_bitcast_fusion
  79.0 7.5 fusion.136
  86.5 5.3 fusion.88
  91.7 10.4 fusion.135
  102.2 15.1 %fusion.134 = (f32[8,512]{1,0:T(8,128)S(1)}, f32[8,512,1536]{2,1,0:T(8,128)}) fusion(pred[512,1536]{1,0:T(8,128)(4,1)} %fusion.71, bf16[512,8,64]{0,2,1:T(8,128)(2,1)} %bitcast.232, bf16[1536,8,64]{0,2,1:T(8,128)(2,1)} %bitcast.211), kind=kOutput, calls=%fused_computation.237 | convolution fusion | flops 830473728 | bytes 28065792 | tf_op jit(solution)/shard_map/while/body/eval_jaxpr/sub | solution.py:76
  117.3 11.6 fusion.94
  128.9 18.2 %fusion.133 = (f32[8,512]{1,0:T(8,128)S(1)}, f32[8,512,2048]{2,1,0:T(8,128)}) fusion(pred[512,2048]{1,0:T(8,128)(4,1)} %fusion.53, bf16[512,8,64]{0,2,1:T(8,128)(2,1)S(1)} %bitcast.230, bf16[2048,8,64]{0,2,1:T(8,128)(2,1)S(1)} %bitcast.202), kind=kOutput, calls=%fused_computation.236 | convolution fusion | flops 1107298304 | bytes 37240832 | tf_op jit(solution)/shard_map/while/body/eval_jaxpr/sub | solution.py:76
  147.1 15.6 %fusion.99 = bf16[8,64,512]{2,1,0:T(8,128)(2,1)} fusion(f32[2048,8,64]{0,2,1:T(8,128)} %bitcast.223, f32[8,64]{1,0:T(8,128)S(1)} %add.363, f32[8,512,2048]{2,1,0:T(8,128)} %get-tuple-element.304, f32[8,512]{1,0:T(8,128)S(1)} %get-tuple-element.303), kind=kOutput, calls=%fused_computation.170 | convolution fusion | flops 1092878336 | bytes 38291456 | tf_op jit(solution)/shard_map/while/body/eval_jaxpr/hqk,khd->qhd/dot_general | solution.py:80
  162.8 9.4 fusion.91
  172.2 5.9 convolution_convert_fusion.3
  179.9 105.1 %all-reduce.11.cloned.1.call-done = bf16[2048,1024]{1,0:T(8,128)(2,1)} async-done(((bf16[2048,1024]{1,0:T(8,128)(2,1)}), bf16[2048,1024]{1,0:T(8,128)(2,1)}) %all-reduce.11.cloned.1.call-update) | async-done | bytes 4194320 | tf_op jit(solution)/shard_map/psum | solution.py:187
  285.0 6.6 convert_add_fusion.1
  301.4 37.0 %all-gather.9.cloned.1.call-done = bf16[1024,2048]{1,0:T(8,128)(2,1)} async-done(((bf16[64,2048]{1,0:T(8,128)(2,1)}), bf16[1024,2048]{1,0:T(8,128)(2,1)}) %all-gather.9.cloned.1.call-update) | async-done | bytes 4194320 | tf_op jit(solution)/shard_map/all_gather | solution.py:161
  338.4 20.4 %multiply_convert_fusion.3 = (bf16[2048,2048]{1,0:T(8,128)(2,1)}, f32[2048,2048]{1,0:T(8,128)}) fusion(f32[2048]{0:T(1024)S(1)} %dynamic_slice.68, bf16[1024,2048]{1,0:T(8,128)(2,1)} %all-gather.9.cloned.1.call-done, f32[2048,1024]{1,0:T(8,128)} %copy-done, f32[1024]{0:T(1024)S(1)} %bitcast.296, f32[1024]{0:T(1024)S(1)} %bitcast.265, ...), kind=kOutput, calls=%fused_computation.26 | convolution fusion | flops 8642363392 | bytes 37781504 | tf_op jit(solution)/shard_map/dot_general | solution.py:191
  358.8 31.7 %all-gather.11.cloned.1.call-done = bf16[2048,1024]{0,1:T(8,128)(2,1)} async-done(((bf16[2048,64]{0,1:T(8,128)(2,1)}), bf16[2048,1024]{0,1:T(8,128)(2,1)}) %all-gather.11.cloned.1.call-update) | async-done | bytes 4194320 | tf_op jit(solution)/shard_map/all_gather | solution.py:162
  390.4 13.9 convolution_convert_fusion.2
  404.4 106.5 %all-reduce.13.cloned.1.call-done = bf16[2048,1024]{1,0:T(8,128)(2,1)} async-done(((bf16[2048,1024]{1,0:T(8,128)(2,1)}), bf16[2048,1024]{1,0:T(8,128)(2,1)}) %all-reduce.13.cloned.1.call-update) | async-done | bytes 4194320 | tf_op jit(solution)/shard_map/psum | solution.py:195
  514.0 7.7 multiply_reduce_fusion.7
  524.9 5.2 add_convert_fusion.1
  530.1 24.9 %convert_reduce_fusion = (f32[2048]{0:T(1024)}, bf16[2048,2048]{1,0:T(8,128)(2,1)S(1)}) fusion(f32[2048,2048]{1,0:T(8,128)} %get-tuple-element.312, f32[2048]{0:T(1024)S(1)} %dynamic_slice.68, bf16[2048,1024]{1,0:T(8,128)(2,1)S(1)} %get-tuple-element.273, bf16[2048,1024]{0,1:T(8,128)(2,1)S(1)} %copy-done.97), kind=kOutput, calls=%fused_computation.23 | convolution fusion | flops 8686401536 | bytes 33570816 | tf_op jit(solution)/shard_map/dot_general | solution.py:49
  558.3 10.5 convolution_convert_fusion.1
  568.9 108.0 %all-reduce.15.cloned.1.call-done = bf16[2048,1024]{1,0:T(8,128)(2,1)} async-done(((bf16[2048,1024]{1,0:T(8,128)(2,1)}), bf16[2048,1024]{1,0:T(8,128)(2,1)}) %all-reduce.15.cloned.1.call-update) | async-done | bytes 4194320 | tf_op jit(solution)/shard_map/psum | solution.py:212
  676.9 6.3 multiply_reduce_fusion.6
  683.2 4.9 fusion.121
  690.4 6.2 multiply_reduce_fusion.5
  696.7 3.8 fusion.125
  701.1 5.5 convolution_convert_fusion.5
  709.2 4.6 multiply_reduce_fusion.4
  713.8 6.7 multiply_convert_fusion.4
  725.8 9.1 multiply_reduce_fusion.2
  735.4 3.9 fusion.74
  741.4 16.6 %multiply_reduce_fusion.1 = (f32[8,512]{1,0:T(8,128)}, f32[8,512,1536]{2,1,0:T(8,128)}) fusion(f32[8,512,1536]{2,1,0:T(8,128)} %get-tuple-element.306, f32[8,512]{1,0:T(8,128)S(1)} %copy-done.71, bf16[512,8,64]{0,2,1:T(8,128)(2,1)S(1)} %bitcast.244, bf16[1536,8,64]{0,2,1:T(8,128)(2,1)S(1)} %bitcast.237), kind=kOutput, calls=%fused_computation.10 | convolution fusion | flops 824176640 | bytes 52461568 | tf_op jit(solution)/shard_map/while/body/eval_jaxpr/qhd,khd->hqk/dot_general | solution.py:115
  758.0 12.7 fusion.67
  770.7 22.0 %multiply_reduce_fusion = (f32[8,512]{1,0:T(8,128)}, f32[8,512,2048]{2,1,0:T(8,128)}) fusion(f32[8,512,2048]{2,1,0:T(8,128)} %get-tuple-element.304, f32[8,512]{1,0:T(8,128)S(1)} %copy-done.69, bf16[512,8,64]{0,2,1:T(8,128)(2,1)S(1)} %bitcast.242, f32[2048,8,64]{0,2,1:T(8,128)S(1)} %bitcast.224, f32[8,64]{1,0:T(8,128)S(1)} %copy-done.89), kind=kOutput, calls=%fused_computation.5 | convolution fusion | flops 1101000704 | bytes 71862272 | tf_op jit(solution)/shard_map/while/body/eval_jaxpr/qhd,khd->hqk/dot_general | solution.py:115
  792.7 15.6 %convert_reduce_fusion.4 = (f32[8,64]{1,0:T(8,128)}, bf16[2048,8,64]{0,2,1:T(8,128)(2,1)}) fusion(f32[2048,8,64]{0,2,1:T(8,128)} %fusion.67, bf16[512,8,64]{0,2,1:T(8,128)(2,1)S(1)} %bitcast.243, f32[8,512,2048]{2,1,0:T(8,128)} %get-tuple-element.304, f32[8,512]{1,0:T(8,128)S(1)} %copy-done.69), kind=kOutput, calls=%fused_computation.98 | convolution fusion | flops 1094712832 | bytes 40388608 | tf_op jit(solution)/shard_map/while/body/eval_jaxpr/hqk,qhd->khd/dot_general | solution.py:113
  808.3 3.9 copy.44
  813.8 12.1 multiply_convert_fusion.2
  833.5 16.7 %multiply_convert_fusion.1 = bf16[8,512,1536]{2,1,0:T(8,128)(2,1)S(1)} fusion(f32[8,512,1536]{2,1,0:T(8,128)} %get-tuple-element.318, f32[8,512]{1,0:T(8,128)S(1)} %copy-done.80, f32[8,512,1536]{2,1,0:T(8,128)} %get-tuple-element.306, f32[8,512]{1,0:T(8,128)S(1)} %copy-done.73), kind=kLoop, calls=%fused_computation.9 | loop fusion | flops 31457280 | bytes 62947328 | tf_op jit(solution)/shard_map/while/body/eval_jaxpr/convert_element_type | solution.py:123
  850.2 6.1 fusion.97
  856.4 6.0 fusion.58
  864.5 28.0 %multiply_convert_fusion = bf16[8,512,2048]{2,1,0:T(8,128)(2,1)} fusion(f32[8,512,2048]{2,1,0:T(8,128)} %get-tuple-element.320, f32[8,512]{1,0:T(8,128)S(1)} %copy-done.79, f32[8,512,2048]{2,1,0:T(8,128)} %get-tuple-element.304, f32[8,512]{1,0:T(8,128)S(1)} %copy-done.69), kind=kLoop, calls=%fused_computation.4 | loop fusion | flops 41943040 | bytes 83918848 | tf_op jit(solution)/shard_map/while/body/eval_jaxpr/convert_element_type | solution.py:123
  892.5 11.0 fusion.87
  903.5 10.0 fusion.46
  917.0 11.7 bitcast_convert_fusion
  929.1 12.2 convert_bitcast_fusion
  941.3 7.8 copy.46
  949.2 5.6 convolution_convert_fusion.6
  955.3 14.0 convolution_convert_fusion.4
  969.4 6.5 convert_element_type.190
  978.5 15.6 %convolution_convert_fusion = bf16[1024,2048]{1,0:T(8,128)(2,1)} fusion(bf16[2048,2048]{1,0:T(8,128)(2,1)} %copy-done.106, f32[2048,1024]{1,0:T(8,128)} %copy-done, f32[1024]{0:T(1024)S(1)} %bitcast.297, f32[1024]{0:T(1024)S(1)} %bitcast.269, f32[2048]{0:T(1024)S(1)} %copy-done.58, f32[2048]{0:T(1024)S(1)} %copy-done.43), kind=kOutput, calls=%fused_computation.123 | convolution fusion | flops 8602517504 | bytes 20996096 | tf_op jit(solution)/shard_map/dot_general | solution.py:43
  997.2 6.6 convert_element_type.212
  1019.7 6.6 convert_element_type.216
  1027.8 9.0 all-reduce.17.cloned.1.call-done
  1036.8 4.6 multiply_reduce_fusion.3
  1042.8 5.5 fusion.124
  1048.4 5.3 convert_element_type.226
  1053.6 3.8 dynamic-slice_reduce_fusion.2
  1057.6 9.0 dynamic-slice_reduce_fusion.1
  1067.9 84.2 %all-reduce.19.cloned.1.call-done = bf16[3,1024,512]{2,0,1:T(4,128)(2,1)} async-done(((bf16[3,1024,512]{2,0,1:T(4,128)(2,1)}), bf16[3,1024,512]{2,0,1:T(4,128)(2,1)}) %all-reduce.19.cloned.1.call-update) | async-done | bytes 3145744
  1154.0 58.4 %reduce-scatter.4.cloned.1.call-done = bf16[512,64]{0,1:T(8,128)(2,1)} async-done(((bf16[512,1024]{0,1:T(8,128)(2,1)}), bf16[512,64]{0,1:T(8,128)(2,1)}) %reduce-scatter.4.cloned.1.call-update) | async-done | bytes 65552 | tf_op jit(solution)/shard_map/reduce_scatter | solution.py:276
  1213.9 74.1 %reduce-scatter.8.cloned.1.call-done = bf16[2048,64]{0,1:T(8,128)(2,1)} async-done(((bf16[2048,1024]{0,1:T(8,128)(2,1)}), bf16[2048,64]{0,1:T(8,128)(2,1)}) %reduce-scatter.8.cloned.1.call-update) | async-done | bytes 262160 | tf_op jit(solution)/shard_map/reduce_scatter | solution.py:282
  1289.7 74.0 %reduce-scatter.6.cloned.1.call-done = bf16[64,2048]{1,0:T(8,128)(2,1)} async-done(((bf16[1024,2048]{1,0:T(8,128)(2,1)}), bf16[64,2048]{1,0:T(8,128)(2,1)}) %reduce-scatter.6.cloned.1.call-update) | async-done | bytes 262160 | tf_op jit(solution)/shard_map/reduce_scatter | solution.py:279
  1365.5 124.7 %all-reduce.21.cloned.1.call-done = (f32[4,1024]{1,0:T(4,128)}, f32[4,1024]{1,0:T(4,128)}, f32[2,1024]{1,0:T(2,128)}, f32[2,1024]{1,0:T(2,128)}, f32[4096]{0:T(1024)}) async-done(((f32[4,1024]{1,0:T(4,128)}, f32[4,1024]{1,0:T(4,128)}, f32[2,1024]{1,0:T(2,128)}, f32[2,1024]{1,0:T(2,128)}, f32[4096]{0:T(1024)}), (f32[4,1024]{1,0:T(4,128)}, f32[4,1024]{1,0:T(4,128)}, f32[2,1024]{1,0:T(2,128)}, ...) | async-done | bytes 65552 | tf_op jit(solution)/shard_map/psum | solution.py:269
  (393 shorter events, 117.2 us)
Async XLA Ops:
  7.2 14.4 slice-start.18
  7.2 17.5 %copy-start.50 = (s32[1,2048]{1,0:T(1,128)S(1)}, s32[1,2048]{1,0:T(1,128)}, u32[]{:S(2)}) copy-start(s32[1,2048]{1,0:T(1,128)} %param.34) | copy-start | bytes 24580
  7.2 12.9 copy-start.84
  7.2 13.5 copy-start.85
  7.2 51.5 %all-gather.5.cloned.1.call-start = ((), (), s32[]{:S(2)}) async-start(), calls=%async_computation.3 | async-start | bytes 3342336 | tf_op jit(solution)/shard_map/all_gather | solution.py:159
  9.0 163.2 %all-gather.7.cloned.1.call-start = ((), (), s32[]{:S(2)}) async-start(), calls=%async_computation.4 | async-start | bytes 1114112 | tf_op jit(solution)/shard_map/all_gather | solution.py:160
  10.6 274.4 %all-reduce.11.cloned.1.call-start = ((), (), s32[]{:S(2)}) async-start(), calls=%async_computation.5 | async-start | bytes 8388608 | tf_op jit(solution)/shard_map/psum | solution.py:187
  14.2 132.8 %copy-start.88 = (f32[8,64]{1,0:T(8,128)}, f32[8,64]{1,0:T(8,128)S(1)}, u32[]{:S(2)}) copy-start(f32[8,64]{1,0:T(8,128)S(1)} %add.363) | copy-start | bytes 6148
  17.1 41.7 %copy-start.44 = (f32[2048]{0:T(1024)}, f32[2048]{0:T(1024)S(1)}, u32[]{:S(2)}) copy-start(f32[2048]{0:T(1024)S(1)} %broadcast_multiply_fusion.3) | copy-start | bytes 24580
  20.1 38.7 %copy-start.65 = (f32[2048]{0:T(1024)}, f32[2048]{0:T(1024)S(1)}, u32[]{:S(2)}) copy-start(f32[2048]{0:T(1024)S(1)} %fusion.108) | copy-start | bytes 24580
  20.7 38.1 %copy-start.63 = (f32[1,1024]{1,0:T(1,128)}, f32[1,1024]{1,0:T(1,128)S(1)}, u32[]{:S(2)}) copy-start(f32[1,1024]{1,0:T(1,128)S(1)} %get-tuple-element.288) | copy-start | bytes 12292
  21.3 47.6 %copy-start.94 = (f32[1,1024]{1,0:T(1,128)}, f32[1,1024]{1,0:T(1,128)S(1)}, u32[]{:S(2)}) copy-start(f32[1,1024]{1,0:T(1,128)S(1)} %get-tuple-element.292) | copy-start | bytes 12292
  69.2 59.7 %copy-start.12 = (bf16[1,2048,512]{1,2,0:T(8,128)(2,1)}, bf16[1,2048,512]{1,2,0:T(8,128)(2,1)S(1)}, u32[]{:S(2)}) copy-start(bf16[1,2048,512]{1,2,0:T(8,128)(2,1)S(1)} %slice.547) | copy-start | bytes 6291460
  70.2 21.5 %copy-start.23 = (bf16[1,1024,512]{1,2,0:T(8,128)(2,1)}, bf16[1,1024,512]{1,2,0:T(8,128)(2,1)S(1)}, u32[]{:S(2)}) copy-start(bf16[1,1024,512]{1,2,0:T(8,128)(2,1)S(1)} %slice.520) | copy-start | bytes 3145732
  102.2 60.6 %copy-start.74 = (f32[8,512]{1,0:T(8,128)}, f32[8,512]{1,0:T(8,128)S(1)}, u32[]{:S(2)}) copy-start(f32[8,512]{1,0:T(8,128)S(1)} %get-tuple-element.307) | copy-start | bytes 49156
  117.3 11.6 copy-start.70
  117.3 11.6 copy-start.31
  147.1 15.7 %copy-start.68 = (f32[8,512]{1,0:T(8,128)}, f32[8,512]{1,0:T(8,128)S(1)}, u32[]{:S(2)}) copy-start(f32[8,512]{1,0:T(8,128)S(1)} %get-tuple-element.303) | copy-start | bytes 49156
  147.1 15.7 %copy-start.35 = (bf16[1024,512]{0,1:T(8,128)(2,1)S(1)}, bf16[1024,512]{0,1:T(8,128)(2,1)}, u32[]{:S(2)}) copy-start(bf16[1024,512]{0,1:T(8,128)(2,1)} %slice.518) | copy-start | bytes 3145732
  178.2 160.2 %all-gather.9.cloned.1.call-start = ((), (), s32[]{:S(2)}) async-start(), calls=%async_computation.6 | async-start | bytes 4456448 | tf_op jit(solution)/shard_map/all_gather | solution.py:161
  179.0 211.5 %all-gather.11.cloned.1.call-start = ((), (), s32[]{:S(2)}) async-start(), calls=%async_computation.7 | async-start | bytes 4456448 | tf_op jit(solution)/shard_map/all_gather | solution.py:162
  179.8 331.1 %all-reduce.13.cloned.1.call-start = ((), (), s32[]{:S(2)}) async-start(), calls=%async_computation.8 | async-start | bytes 8388608 | tf_op jit(solution)/shard_map/psum | solution.py:195
  297.0 41.4 %copy-start.59 = (f32[1,1024]{1,0:T(1,128)S(1)}, f32[1,1024]{1,0:T(1,128)}, u32[]{:S(2)}) copy-start(f32[1,1024]{1,0:T(1,128)} %get-tuple-element.289) | copy-start | bytes 12292
  297.0 41.4 %copy-start.92 = (f32[1,1024]{1,0:T(1,128)S(1)}, f32[1,1024]{1,0:T(1,128)}, u32[]{:S(2)}) copy-start(f32[1,1024]{1,0:T(1,128)} %get-tuple-element.293) | copy-start | bytes 12292
  297.0 391.1 %copy-start.42 = (f32[2048]{0:T(1024)}, f32[2048]{0:T(1024)S(1)}, u32[]{:S(2)}) copy-start(f32[2048]{0:T(1024)S(1)} %broadcast_multiply_fusion.1) | copy-start | bytes 24580
  301.3 386.8 %copy-start.57 = (f32[2048]{0:T(1024)}, f32[2048]{0:T(1024)S(1)}, u32[]{:S(2)}) copy-start(f32[2048]{0:T(1024)S(1)} %fusion.110) | copy-start | bytes 24580
  404.3 109.6 %copy-start.46 = (f32[1,1024]{1,0:T(1,128)S(1)}, f32[1,1024]{1,0:T(1,128)}, u32[]{:S(2)}) copy-start(f32[1,1024]{1,0:T(1,128)} %get-tuple-element.286) | copy-start | bytes 12292
  404.4 272.5 %all-reduce.15.cloned.1.call-start = ((), (), s32[]{:S(2)}) async-start(), calls=%async_computation.9 | async-start | bytes 8388608 | tf_op jit(solution)/shard_map/psum | solution.py:212
  530.1 24.9 %copy-start.14 = (bf16[2048,1024]{1,0:T(8,128)(2,1)}, bf16[2048,1024]{1,0:T(8,128)(2,1)S(1)}, u32[]{:S(2)}) copy-start(bf16[2048,1024]{1,0:T(8,128)(2,1)S(1)} %get-tuple-element.273) | copy-start | bytes 12582916
  530.1 28.2 %copy-start.96 = (bf16[1024,2048]{1,0:T(8,128)(2,1)S(1)}, bf16[1024,2048]{1,0:T(8,128)(2,1)}, u32[]{:S(2)}) copy-start(bf16[1024,2048]{1,0:T(8,128)(2,1)} %all-gather.9.cloned.1.call-done) | copy-start | bytes 12582916
  568.9 468.0 %all-reduce.17.cloned.1.call-start = ((), (), s32[]{:S(2)}) async-start(), calls=%async_computation.10 | async-start | bytes 8388608 | tf_op jit(solution)/shard_map/psum | solution.py:247
  676.9 11.3 slice-start
  713.8 10.7 slice-start.12
  713.8 10.7 slice-start.13
  713.8 10.7 slice-start.14
  741.4 16.6 %copy-start.72 = (f32[8,512]{1,0:T(8,128)S(1)}, f32[8,512]{1,0:T(8,128)}, u32[]{:S(2)}) copy-start(f32[8,512]{1,0:T(8,128)} %copy-done.70) | copy-start | bytes 49156
  758.0 12.7 copy-start.25
  758.0 12.7 copy-start.69
  758.0 12.7 copy-start.89
  792.7 19.6 %copy-start.18 = (bf16[8,64,512]{2,1,0:T(8,128)(2,1)S(1)}, bf16[8,64,512]{2,1,0:T(8,128)(2,1)}, u32[]{:S(2)}) copy-start(bf16[8,64,512]{2,1,0:T(8,128)(2,1)} %fusion.98) | copy-start | bytes 1572868
  792.7 20.6 %copy-start.27 = (f32[512,8,64]{0,2,1:T(8,128)S(1)}, f32[512,8,64]{0,2,1:T(8,128)}, u32[]{:S(2)}) copy-start(f32[512,8,64]{0,2,1:T(8,128)} %convolution_bitcast_fusion.2) | copy-start | bytes 3145732
  813.8 12.2 copy-start.24
  864.5 28.0 %copy-start.13 = (bf16[1,2048,512]{1,2,0:T(8,128)(2,1)S(1)}, bf16[1,2048,512]{1,2,0:T(8,128)(2,1)}, u32[]{:S(2)}) copy-start(bf16[1,2048,512]{1,2,0:T(8,128)(2,1)} %copy-done.12) | copy-start | bytes 6291460
  892.5 11.0 copy-start.32
  917.0 12.1 copy-start.30
  917.0 12.1 copy-start.40
  917.0 12.1 copy-start.45
  917.0 12.1 copy-start.64
  917.0 12.1 copy-start.66
  917.0 12.1 copy-start.95
  928.8 223.3 %all-reduce.19.cloned.1.call-start = ((), (), s32[]{:S(2)}) async-start(), calls=%async_computation.14 | async-start | bytes 8388608
  949.1 263.2 %reduce-scatter.4.cloned.1.call-start = ((), (), s32[]{:S(2)}) async-start(), calls=%async_computation.11 | async-start | bytes 1114112 | tf_op jit(solution)/shard_map/reduce_scatter | solution.py:276
  954.8 333.1 %reduce-scatter.8.cloned.1.call-start = ((), (), s32[]{:S(2)}) async-start(), calls=%async_computation.13 | async-start | bytes 4456448 | tf_op jit(solution)/shard_map/reduce_scatter | solution.py:282
  969.3 394.4 %reduce-scatter.6.cloned.1.call-start = ((), (), s32[]{:S(2)}) async-start(), calls=%async_computation.12 | async-start | bytes 4456448 | tf_op jit(solution)/shard_map/reduce_scatter | solution.py:279
  994.2 496.0 %all-reduce.21.cloned.1.call-start = ((), (), s32[]{:S(2)}) async-start(), calls=%async_computation.15 | async-start | bytes 131072 | tf_op jit(solution)/shard_map/psum | solution.py:269
  1005.0 12.0 copy-start.49
  1005.0 12.0 copy-start.87
  1005.0 12.3 slice-start.6
  1007.7 10.6 slice-start.10
  1026.4 15.1 %copy-start.54 = (f32[2048]{0:T(1024)S(1)}, f32[2048]{0:T(1024)}, u32[]{:S(2)}) copy-start(f32[2048]{0:T(1024)} %copy-done.53) | copy-start | bytes 24580
  1027.2 21.1 %copy-start.67 = (f32[2,1024]{1,0:T(2,128)}, f32[2,1024]{1,0:T(2,128)S(1)}, u32[]{:S(2)}) copy-start(f32[2,1024]{1,0:T(2,128)S(1)} %constant_dynamic-update-slice_fusion) | copy-start | bytes 24580
  1041.4 12.2 slice-start.8
  1042.7 10.9 slice-start.9
  1042.8 14.7 slice-start.4
  (75 other events, 482.5 us)
Sparse Core Ops, SparseCore 0:
  10.8 47.8 all-gather.4
  61.5 36.7 all-gather.6
  178.3 106.6 all-reduce.10
  287.8 50.5 all-gather.8
  341.2 49.2 all-gather.10
  404.5 106.3 all-reduce.12
  569.0 107.8 all-reduce.14
  928.9 107.8 all-reduce.16
  1040.5 111.5 all-reduce.18
  1156.0 56.3 reduce-scatter.3
  1216.2 71.6 reduce-scatter.7
  1292.2 71.5 reduce-scatter.5
  1371.3 118.8 all-reduce.20
where the time goes:
time: 1510 us; the launch traced here: 1500 us
  waiting for transfers between devices  845 us (56%)
  matrix products  371 us (25%)
  other arithmetic  211 us (14%)
  local copies, waits for them, and re-layouts  58.6 us (4%)
  between operations  16.5 us (1%)
    psum x1, waiting for transfers between devices, per_device(): lax.psum((gain_terms, shift_terms, head_full, bias_terms, hidden_full), (...  125 us
    psum x1, waiting for transfers between devices, per_device(): lax.psum(partial_mid.astype(jnp.bfloat16), 'tensor').astype(jnp.float32)  108 us
    psum x1, waiting for transfers between devices, per_device(): lax.psum(partial_mlp.astype(jnp.bfloat16), 'tensor').astype(jnp.float32)  106 us
    psum x1, waiting for transfers between devices, per_device(): lax.psum(partial_attn.astype(jnp.bfloat16), 'tensor').astype(jnp.float32)  105 us
    unnamed x14, waiting for transfers between devices  84.4 us
    reduce_scatter x1, waiting for transfers between devices, per_device(): lax.psum_scatter(grad_down.astype(jnp.bfloat16), 'dp', scatter_dimension=...  74.1 us
    reduce_scatter x1, waiting for transfers between devices, per_device(): lax.psum_scatter(grad_up.astype(jnp.bfloat16), 'dp', scatter_dimension=0,...  74 us
    convert_element_type x4, other arithmetic, attend_backward(): d_scores = d_scores.astype(jnp.bfloat16)  63.5 us
  transfers between devices with their start and end apart: 13, of which 12 were waited for; matrix products, arithmetic and copies ran while one was open for 20% of the time, Pallas kernels for 0%

commit v1 on v0

v1 whole, which is shorter than its diff:
```python
import functools
import math

import jax
import jax.numpy as jnp
from jax import lax
from jax.experimental import pallas as pl
from jax.experimental.pallas import tpu as pltpu
from jax.sharding import PartitionSpec as P

HD = 64
QB = 256
KB = 256
MAX_SEGMENT = 1024
max_chunks = MAX_SEGMENT // KB + 1
SCORE_SCALE = 0.125 * math.log2(math.e)
NEG = -1e30
EPS = 1e-05
BF16 = jnp.bfloat16
F32 = jnp.float32
NT = (((1,), (1,)), ((), ()))
NN = (((1,), (0,)), ((), ()))
TN = (((0,), (0,)), ((), ()))

def dot(a, b, dims):
    return lax.dot_general(a, b, dims, preferred_element_type=jnp.float32)


def split_pair(block):
    lane = lax.broadcasted_iota(jnp.int32, block.shape, 1)
    zero = jnp.zeros_like(block)
    return (jnp.where(lane < HD, block, zero), jnp.where(lane >= HD, block, zero))


def fwd_kernel(pairs, lo_ref, off_ref, q_ref, k_ref, v_ref, start_ref, o_ref, l_ref, vt_ref):
    step = pl.program_id(1)
    block = off_ref[0] + step

    @pl.when(step == 0)
    def _():
        vt_ref[...] = v_ref[...].T

    pair_step = math.gcd(pairs, 4)
    row_start = start_ref[...]
    query_pos = block * QB + lax.broadcasted_iota(jnp.int32, (1, QB), 1)
    first = lo_ref[pl.program_id(0), block]
    count = block + 1 - first
    base = pl.multiple_of(first * KB, KB)

    for chunks in range(1, max_chunks + 1):

        @pl.when(count == chunks)
        def _(size=chunks * KB):
            window = pl.ds(base, size)
            key_pos = lax.broadcasted_iota(jnp.int32, (size, QB), 0) + base
            ok = (key_pos >= row_start) & (key_pos <= query_pos)

            def body(group, _):
                for sub in range(pair_step):
                    pair = group * pair_step + sub
                    cols = pl.ds(pl.multiple_of(pair * 128, 128), 128)
                    q_heads = split_pair(q_ref[:, cols])
                    keys = k_ref[window, cols]
                    outs = []
                    for h in range(2):
                        s = jnp.where(ok, dot(keys, q_heads[h], NT) * SCORE_SCALE, NEG)
                        peak = jnp.max(s, axis=0, keepdims=True)
                        p = jnp.exp2(s - peak)
                        total = jnp.sum(p, axis=0, keepdims=True)
                        vt = vt_ref[pl.ds(pl.multiple_of(pair * 128 + h * HD, HD), HD), window]
                        outs.append(dot(vt, p.astype(jnp.bfloat16), NN) / total)
                        l_ref[pl.ds(2 * pair + h, 1), :] = peak + jnp.log2(total)
                    o_ref[:, cols] = jnp.concatenate(outs, axis=0).T.astype(jnp.bfloat16)
                return 0

            lax.fori_loop(0, pairs // pair_step, body, 0)


def attention_forward(qkv, starts, lo, offset, blocks):
    seqs, length = starts.shape
    width = qkv.shape[1] // 3
    heads, pairs = width // HD, width // 128
    nq = length // QB
    grid_spec = pltpu.PrefetchScalarGridSpec(
        num_scalar_prefetch=2,
        grid=(seqs, blocks),
        in_specs=[
            pl.BlockSpec((QB, width), lambda s, b, lo, off: (s * nq + off[0] + b, 0)),
            pl.BlockSpec((length, width), lambda s, b, lo, off: (s, 1)),
            pl.BlockSpec((length, width), lambda s, b, lo, off: (s, 2)),
            pl.BlockSpec((None, 1, QB), lambda s, b, lo, off: (s, 0, off[0] + b)),
        ],
        out_specs=[
            pl.BlockSpec((QB, width), lambda s, b, lo, off: (s * blocks + b, 0)),
            pl.BlockSpec((None, heads, QB), lambda s, b, lo, off: (s, 0, b)),
        ],
        scratch_shapes=[pltpu.VMEM((width, length), jnp.bfloat16)],
    )
    rows = seqs * blocks * QB
    return pl.pallas_call(
        functools.partial(fwd_kernel, pairs),
        grid_spec=grid_spec,
        out_shape=(
            jax.ShapeDtypeStruct((rows, width), jnp.bfloat16),
            jax.ShapeDtypeStruct((seqs, heads, blocks * QB), jnp.float32),
        ),
        compiler_params=pltpu.CompilerParams(
            dimension_semantics=("arbitrary", "arbitrary"), vmem_limit_bytes=48 << 20
        ),
        cost_estimate=pl.CostEstimate(
            flops=4 * rows * 640 * width, bytes_accessed=8 * rows * width, transcendentals=rows * heads * 640
        ),
        name="attention_forward",
    )(lo, offset, qkv, qkv, qkv, starts[:, None, :])


def bwd_kernel(pairs, lo_ref, q_ref, k_ref, v_ref, o_ref, do_ref, l_ref, start_ref, out_ref, kt_ref, dk_ref, dv_ref):
    block = pl.program_id(1)
    width = pairs * 128

    @pl.when(block == 0)
    def _():
        kt_ref[...] = k_ref[...].T
        dk_ref[...] = jnp.zeros_like(dk_ref)
        dv_ref[...] = jnp.zeros_like(dv_ref)

    row_start = start_ref[...]
    query_pos = block * QB + lax.broadcasted_iota(jnp.int32, (1, QB), 1)
    key_iota = lax.broadcasted_iota(jnp.int32, (KB, QB), 0)
    first = lo_ref[pl.program_id(0), block]
    last = (block + 1) * (QB // KB)
    rows = pl.ds(pl.multiple_of(block * QB, QB), QB)
    for pair in range(pairs):
        cols = slice(pair * 128, (pair + 1) * 128)
        q_heads = split_pair(q_ref[:, cols])
        g_pair = do_ref[:, cols]
        g_heads = split_pair(g_pair)
        prod = (g_pair.astype(jnp.float32) * o_ref[:, cols].astype(jnp.float32)).T
        deltas = [jnp.sum(prod[h * HD : (h + 1) * HD], axis=0, keepdims=True) for h in range(2)]
        lses = [l_ref[2 * pair + h : 2 * pair + h + 1, :] for h in range(2)]

        def chunk(j, carry):
            base = pl.multiple_of(j * KB, KB)
            window = pl.ds(base, KB)
            keys = k_ref[window, cols]
            vals = v_ref[window, cols]
            key_pos = key_iota + base
            ok = (key_pos >= row_start) & (key_pos <= query_pos)
            new = []
            dv = dv_ref[window, cols]
            dk = dk_ref[window, cols]
            for h in range(2):
                s = jnp.where(ok, dot(keys, q_heads[h], NT) * SCORE_SCALE, NEG)
                p = jnp.exp2(s - lses[h])
                dp = dot(vals, g_heads[h], NT)
                ds = (p * (dp - deltas[h])).astype(jnp.bfloat16)
                dv = dv + dot(p.astype(jnp.bfloat16), g_heads[h], NN)
                dk = dk + dot(ds, q_heads[h], NN)
                kt = kt_ref[pair * 128 + h * HD : pair * 128 + (h + 1) * HD, window]
                new.append(carry[h] + dot(kt, ds, NN))
            dv_ref[window, cols] = dv
            dk_ref[window, cols] = dk
            return tuple(new)

        dq = lax.fori_loop(
            first, last, chunk, tuple(jnp.zeros((HD, QB), jnp.float32) for _ in range(2))
        )
        out_ref[rows, cols] = (jnp.concatenate(dq, axis=0) * 0.125).T.astype(jnp.bfloat16)

    @pl.when(block == pl.num_programs(1) - 1)
    def _():
        out_ref[:, width : 2 * width] = (dk_ref[...] * 0.125).astype(jnp.bfloat16)
        out_ref[:, 2 * width :] = dv_ref[...].astype(jnp.bfloat16)


def attention_backward(qkv, o, d_o, lse, starts, lo):
    seqs, length = starts.shape
    width = qkv.shape[1] // 3
    heads, pairs = width // HD, width // 128
    nq = length // QB
    row = lambda s, b, lo: (s * nq + b, 0)
    grid_spec = pltpu.PrefetchScalarGridSpec(
        num_scalar_prefetch=1,
        grid=(seqs, nq),
        in_specs=[
            pl.BlockSpec((QB, width), row),
            pl.BlockSpec((length, width), lambda s, b, lo: (s, 1)),
            pl.BlockSpec((length, width), lambda s, b, lo: (s, 2)),
            pl.BlockSpec((QB, width), row),
            pl.BlockSpec((QB, width), row),
            pl.BlockSpec((None, heads, QB), lambda s, b, lo: (s, 0, b)),
            pl.BlockSpec((None, 1, QB), lambda s, b, lo: (s, 0, b)),
        ],
        out_specs=pl.BlockSpec((length, 3 * width), lambda s, b, lo: (s, 0)),
        scratch_shapes=[
            pltpu.VMEM((width, length), jnp.bfloat16),
            pltpu.VMEM((length, width), jnp.float32),
            pltpu.VMEM((length, width), jnp.float32),
        ],
    )
    rows = seqs * length
    return pl.pallas_call(
        functools.partial(bwd_kernel, pairs),
        grid_spec=grid_spec,
        out_shape=jax.ShapeDtypeStruct((rows, 3 * width), jnp.bfloat16),
        compiler_params=pltpu.CompilerParams(
            dimension_semantics=("arbitrary", "arbitrary"), vmem_limit_bytes=56 << 20
        ),
        cost_estimate=pl.CostEstimate(
            flops=10 * rows * 640 * width, bytes_accessed=16 * rows * width, transcendentals=rows * heads * 640
        ),
        name="attention_backward",
    )(lo, qkv, qkv, qkv, o, d_o, lse, starts[:, None, :])


def segment_bounds(segment_ids):
    starts = jnp.sum((segment_ids[:, None, :] < segment_ids[:, :, None]).astype(jnp.int32), axis=2)
    return starts, starts[:, ::QB] // KB


def stats(values):
    mean = jnp.mean(values, axis=-1, keepdims=True)
    centered = values - mean
    scale = lax.rsqrt(jnp.mean(centered * centered, axis=-1, keepdims=True) + EPS)
    return centered * scale, scale


def norm_back(normed, scale, gain_row, grad_rows):
    inner = grad_rows * gain_row
    return scale * (
        inner
        - jnp.mean(inner, axis=-1, keepdims=True)
        - normed * jnp.mean(inner * normed, axis=-1, keepdims=True)
    )


def gelu_pair(z):
    c = math.sqrt(2.0 / math.pi)
    t = jnp.tanh(c * (z + 0.044715 * z * z * z))
    value = 0.5 * z * (1.0 + t)
    slope = 0.5 * (1.0 + t) + 0.5 * z * (1.0 - t * t) * (c * (1.0 + 3 * 0.044715 * z * z))
    return value, slope


NZ, NX, NC = 4, 2, 2


def core_pairs():
    return [(i, i ^ 1) for i in range(NZ * NX * NC)]


def x_pairs():
    return [(i, i ^ 2) for i in range(NZ * NX * NC)]


def z_pairs(shift):
    return [(i, (i + shift * NX * NC) % (NZ * NX * NC)) for i in range(NZ * NX * NC)]


Y_PAIRS = [(0, 1), (1, 0)]


def swap_core(a):
    return lax.ppermute(a, "dp", core_pairs())


def swap_x(a):
    return lax.ppermute(a, "dp", x_pairs())


def swap_y(a):
    return lax.ppermute(a, "tensor", Y_PAIRS)


def assemble_kernel(pos_ref, *refs):
    out_ref = refs[-1]
    z, x, c = pos_ref[0], pos_ref[1], pos_ref[2]
    for n, ref in enumerate(refs[:-1]):
        dx, dc = n % 2, n // 2
        for k in range(NZ):
            out_ref[lax.rem(z - k + NZ, NZ), lax.bitwise_xor(x, dx), lax.bitwise_xor(c, dc)] = ref[k]


def assemble(position, pieces):
    _, rows, width = pieces[0].shape
    block = math.gcd(width, 512)
    out = pl.pallas_call(
        assemble_kernel,
        grid_spec=pltpu.PrefetchScalarGridSpec(
            num_scalar_prefetch=1,
            grid=(width // block,),
            in_specs=[pl.BlockSpec((NZ, rows, block), lambda j, pos: (0, 0, j))] * 4,
            out_specs=pl.BlockSpec((NZ, NX, NC, rows, block), lambda j, pos: (0, 0, 0, 0, j)),
        ),
        out_shape=jax.ShapeDtypeStruct((NZ, NX, NC, rows, width), BF16),
        compiler_params=pltpu.CompilerParams(
            dimension_semantics=("arbitrary",), vmem_limit_bytes=32 << 20
        ),
        cost_estimate=pl.CostEstimate(
            flops=0, bytes_accessed=2 * 16 * rows * width * 2, transcendentals=0
        ),
        name="assemble",
    )(position, *pieces)
    return out.reshape(NZ * NX * NC * rows, width)


def gather_z(shard):
    return jnp.stack([shard] + [lax.ppermute(shard, "dp", z_pairs(k)) for k in range(1, NZ)])


def finish_gather(position, column, from_x):
    mine = [column, from_x]
    return assemble(position, mine + [swap_core(a) for a in mine])


def gather_own(position, shard):
    column = gather_z(shard)
    return finish_gather(position, column, swap_x(column))


def gather_both(position, shard, y_first):
    column = gather_z(shard)
    other = swap_y(column)
    own_x = swap_x(column)
    other_x = swap_x(other) if y_first else swap_y(own_x)
    return [finish_gather(position, column, own_x), finish_gather(position, other, other_x)]


def reduce_rows(z, x, c, grads):
    wide = []
    for g in grads:
        parts = g.reshape(NZ, NX, NC, g.shape[0] // (NZ * NX * NC), g.shape[1])
        there = swap_core(lax.dynamic_index_in_dim(parts, 1 - c, 2, keepdims=False))
        here = lax.dynamic_index_in_dim(parts, c, 2, keepdims=False)
        wide.append((here.astype(F32) + there.astype(F32)).astype(BF16))
    mid = []
    for h in wide:
        there = swap_x(lax.dynamic_index_in_dim(h, 1 - x, 1, keepdims=False))
        here = lax.dynamic_index_in_dim(h, x, 1, keepdims=False)
        mid.append((here.astype(F32) + there.astype(F32)).astype(BF16))
    total = mid[0]
    if len(mid) == 2:
        total = (total.astype(F32) + swap_y(mid[1]).astype(F32)).astype(BF16)
    out = lax.dynamic_index_in_dim(total, z, 0, keepdims=False).astype(F32)
    for k in range(1, NZ):
        piece = lax.dynamic_index_in_dim(total, lax.rem(z + k, NZ), 0, keepdims=False)
        out = out + lax.ppermute(piece, "dp", z_pairs(k)).astype(F32)
    return out


def sum_everywhere(vector, over_tensor=True):
    vector = vector + swap_core(vector)
    vector = vector + swap_x(vector)
    if over_tensor:
        vector = vector + swap_y(vector)
    size = NZ * NX * NC
    near = [(i, i ^ 4) for i in range(size)]
    far = [(i, i ^ 8) for i in range(size)]
    vector = vector + lax.ppermute(vector, "dp", near)
    return vector + lax.ppermute(vector, "dp", far)


class Staged:
    def __init__(self):
        index = lax.axis_index("dp")
        self.z, self.x, self.c = index // 4, (index // 2) % 2, index % 2
        self.position = jnp.stack([self.z, self.x, self.c]).astype(jnp.int32)

    def gather_own(self, shard):
        return gather_own(self.position, shard)

    def gather_groups(self, shard, y_first):
        return gather_both(self.position, shard, y_first)

    def reduce_own(self, grad):
        return reduce_rows(self.z, self.x, self.c, [grad])

    def reduce_groups(self, grads):
        return reduce_rows(self.z, self.x, self.c, grads)

    def exchange(self, parts):
        return [parts[0], swap_y(parts[1])]

    def total(self, vector, over_tensor=True):
        return sum_everywhere(vector, over_tensor)


class Plain:
    def __init__(self):
        self.n = lax.axis_size("tensor")
        self.rank = lax.axis_index("tensor")

    def gather_own(self, shard):
        return lax.all_gather(shard, "dp", axis=0, tiled=True)

    def gather_groups(self, shard, y_first):
        own = lax.all_gather(shard, "dp", axis=0, tiled=True)
        every = lax.all_gather(own, "tensor", axis=0)
        return [
            lax.dynamic_index_in_dim(every, (self.rank + g) % self.n, 0, keepdims=False)
            for g in range(self.n)
        ]

    def reduce_own(self, grad):
        return lax.psum_scatter(grad, "dp", scatter_dimension=0, tiled=True).astype(F32)

    def absolute(self, parts):
        stacked = jnp.stack(parts)
        order = (jnp.arange(self.n) - self.rank) % self.n
        return jnp.take(stacked, order, axis=0)

    def reduce_groups(self, grads):
        own = lax.psum_scatter(self.absolute(grads), "tensor", scatter_dimension=0, tiled=True)
        return lax.psum_scatter(own[0], "dp", scatter_dimension=0, tiled=True).astype(F32)

    def exchange(self, parts):
        got = lax.all_to_all(self.absolute(parts), "tensor", 0, 0, tiled=True)
        return [
            lax.dynamic_index_in_dim(got, (self.rank + g) % self.n, 0, keepdims=False)
            for g in range(self.n)
        ]

    def total(self, vector, over_tensor=True):
        return lax.psum(vector, ("dp", "tensor") if over_tensor else "dp")


def per_device(
    staged,
    inputs,
    cotangent,
    segment_ids,
    w_qkv,
    w_out,
    w_fc1,
    w_fc2,
    norm_gain,
    norm_bias,
    head_bias,
    out_bias,
    fc1_bias,
):
    n = lax.axis_size("tensor")
    rank = lax.axis_index("tensor")
    comm = Staged() if staged else Plain()
    tokens, features = inputs.shape
    seqs, length = segment_ids.shape
    own_rows = tokens // n
    width = w_qkv.shape[2]
    hidden = w_fc1.shape[1]

    def group_slice(array, g, size, axis=0):
        return lax.dynamic_slice_in_dim(array, ((rank + g) % n) * size, size, axis)

    shard_qkv = jnp.concatenate([w_qkv[0], w_qkv[1], w_qkv[2]], axis=1).astype(BF16)
    weight_qkv = comm.gather_own(shard_qkv)
    out_groups = comm.gather_groups(w_out.T.astype(BF16), True)
    up_groups = comm.gather_groups(w_fc1.astype(BF16), True)
    down_groups = comm.gather_groups(w_fc2.T.astype(BF16), False)

    wide = inputs.astype(F32)
    normed0, scale0 = stats(wide)
    u1 = (normed0 * norm_gain[0] + norm_bias[0]).astype(BF16)
    heads_bias = group_slice(head_bias, 0, width, 1)
    qkv_bias = jnp.concatenate([heads_bias[0], jnp.zeros((width,), F32), heads_bias[1]])
    qkv = (dot(u1, weight_qkv, NN) + qkv_bias).astype(BF16)

    starts, lo = segment_bounds(segment_ids)
    blocks = length // QB
    if staged and seqs == 1:
        half = blocks // 2
        there = jnp.full((1,), (1 - rank) * half, jnp.int32)
        here = jnp.full((1,), rank * half, jnp.int32)
        o_there, lse_there = attention_forward(qkv, starts, lo, there, half)
        o_here, lse_here = attention_forward(qkv, starts, lo, here, half)
        o_parts = [o_here, o_there]
        first = rank == 0
        o_all = jnp.concatenate(
            [jnp.where(first, o_here, o_there), jnp.where(first, o_there, o_here)], axis=0
        )
        lse = jnp.concatenate(
            [jnp.where(first, lse_here, lse_there), jnp.where(first, lse_there, lse_here)], axis=2
        )
    else:
        o_all, lse = attention_forward(qkv, starts, lo, jnp.zeros((1,), jnp.int32), blocks)
        o_parts = [group_slice(o_all, g, own_rows) for g in range(n)]
    o_groups = comm.exchange(o_parts)

    def group_sum(terms):
        return sum(t.astype(BF16).astype(F32) for t in terms)

    attn = group_sum([dot(o, w, NT) for o, w in zip(o_groups, out_groups)]) + out_bias[0]
    mine = group_slice(inputs, 0, own_rows).astype(F32)
    normed1, scale1 = stats(attn)
    resid = mine + normed1 * norm_gain[1] + norm_bias[1]
    normed2, scale2 = stats(resid)
    u2 = (normed2 * norm_gain[2] + norm_bias[2]).astype(BF16)

    act_groups, slope_groups, mlp_terms = [], [], []
    for g in range(n):
        pre = dot(u2, up_groups[g], NN) + group_slice(fc1_bias, g, hidden)
        act, slope = gelu_pair(pre)
        act_groups.append(act.astype(BF16))
        slope_groups.append(pre)
        mlp_terms.append(dot(act_groups[g], down_groups[g], NT))
    mlp = group_sum(mlp_terms) + out_bias[1]
    normed3, scale3 = stats(mlp)
    output = (resid + normed3 * norm_gain[3] + norm_bias[3]).astype(BF16)

    dy = group_slice(cotangent, 0, own_rows).astype(F32)
    d_mlp = norm_back(normed3, scale3, norm_gain[3], dy).astype(BF16)
    gain3, shift3 = jnp.sum(normed3 * dy, axis=0), jnp.sum(dy, axis=0)
    bias_mlp = jnp.sum(d_mlp.astype(F32), axis=0)

    grad_down = comm.reduce_groups([dot(d_mlp, act, TN).astype(BF16) for act in act_groups])
    d_pre_groups = [
        (gelu_pair(slope_groups[g])[1] * dot(d_mlp, down_groups[g], NN)).astype(BF16) for g in range(n)
    ]
    d_u2 = group_sum([dot(d_pre, w, NT) for d_pre, w in zip(d_pre_groups, up_groups)])
    grad_up = comm.reduce_groups([dot(u2, d_pre, TN).astype(BF16) for d_pre in d_pre_groups])
    bias_hidden = [jnp.sum(d_pre.astype(F32), axis=0) for d_pre in d_pre_groups]

    gain2, shift2 = jnp.sum(normed2 * d_u2, axis=0), jnp.sum(d_u2, axis=0)
    d_resid = dy + norm_back(normed2, scale2, norm_gain[2], d_u2)
    gain1, shift1 = jnp.sum(normed1 * d_resid, axis=0), jnp.sum(d_resid, axis=0)
    d_attn = norm_back(normed1, scale1, norm_gain[1], d_resid).astype(BF16)
    bias_attn = jnp.sum(d_attn.astype(F32), axis=0)

    d_o_parts = [dot(d_attn, w, NN).astype(BF16) for w in out_groups]
    d_o_groups = comm.exchange(d_o_parts)
    grad_out = comm.reduce_groups([dot(d_attn, o, TN).astype(BF16) for o in o_groups])
    if n == 2:
        first = rank == 0
        d_o = jnp.concatenate(
            [
                jnp.where(first, d_o_groups[0], d_o_groups[1]),
                jnp.where(first, d_o_groups[1], d_o_groups[0]),
            ],
            axis=0,
        )
    else:
        d_o = jnp.take(jnp.stack(d_o_groups), (jnp.arange(n) - rank) % n, axis=0).reshape(tokens, width)

    d_qkv = attention_backward(qkv, o_all, d_o, lse, starts, lo)

    d_u1_parts = [
        dot(group_slice(d_qkv, g, own_rows), weight_qkv, NT).astype(BF16) for g in reversed(range(n))
    ][::-1]
    d_u1 = group_sum(comm.exchange(d_u1_parts))
    grad_qkv = comm.reduce_own(dot(u1, d_qkv, TN).astype(BF16))
    gain0 = shift0 = 0.0
    for g in range(n):
        part = d_u1_parts[g].astype(F32)
        gain0 = gain0 + jnp.sum(group_slice(normed0, g, own_rows) * part, axis=0)
        shift0 = shift0 + jnp.sum(part, axis=0)
    head_terms = jnp.sum(d_qkv.astype(F32), axis=0)

    own_normed0 = group_slice(normed0, 0, own_rows)
    own_scale0 = group_slice(scale0, 0, own_rows)
    d_inputs = (d_resid + norm_back(own_normed0, own_scale0, norm_gain[0], d_u1)).astype(BF16)

    def place(groups, like, axis):
        full = jnp.zeros(like.shape, F32)
        for g, part in enumerate(groups):
            at = ((rank + g) % n) * part.shape[axis]
            full = lax.dynamic_update_slice_in_dim(full, part, at, axis)
        return full

    early = jnp.concatenate(
        [
            jnp.stack([gain1, gain2, gain3, shift1, shift2, shift3, bias_attn, bias_mlp]).reshape(-1),
            place(bias_hidden, fc1_bias, 0),
        ]
    ).reshape(-1, 1024)
    early = comm.total(early)
    head_full = place([jnp.stack([head_terms[:width], head_terms[2 * width :]])], head_bias, 1)
    late = comm.total(jnp.concatenate([gain0[None], shift0[None], head_full]))
    grad_gain = jnp.concatenate([late[0:1], early[0:3]])
    grad_shift = jnp.concatenate([late[1:2], early[3:6]])
    grad_qkv = jnp.stack([grad_qkv[:, i * width : (i + 1) * width] for i in range(3)])
    return (
        output,
        d_inputs,
        grad_qkv,
        grad_out.T,
        grad_up,
        grad_down.T,
        grad_gain,
        grad_shift,
        late[2:4],
        early[6:8],
        early[8:].reshape(-1),
    )


def solution(mesh):
    staged = mesh.shape["dp"] == NZ * NX * NC and mesh.shape["tensor"] == 2
    return jax.shard_map(
        functools.partial(per_device, staged),
        mesh=mesh,
        in_specs=(
            P("dp", None),
            P("dp", None),
            P("dp", None),
            P(None, "dp", "tensor"),
            P("tensor", "dp"),
            P("dp", "tensor"),
            P("tensor", "dp"),
            P(),
            P(),
            P(),
            P(),
            P(),
        ),
        out_specs=(
            P(("dp", "tensor"), None),
            P(("dp", "tensor"), None),
            P(None, "dp", "tensor"),
            P("tensor", "dp"),
            P("dp", "tensor"),
            P("tensor", "dp"),
            P(),
            P(),
            P(),
            P(),
            P(),
        ),
        check_vma=False,
    )
```

time: 1510 us -> 758 us (0.50)
  waiting for transfers between devices: 845 us -> 219 us
  matrix products: 371 us -> 151 us
  other arithmetic: 211 us -> 73.2 us
  Pallas kernels: 0 us -> 124 us
  starting transfers between devices: 1.33 us -> 116 us
    psum x5 -> x0, waiting for transfers between devices: 453 us -> none  [the longest x1 125 us: per_device(): lax.psum((gain_terms, shift_terms, head_full, bias_terms, hidden_full), (...]
    ppermute x0 -> x78, waiting for transfers between devices: none -> 219 us  [the longest x12 92.3 us: swap_y(): return lax.ppermute(a, 'tensor', Y_PAIRS)]
    reduce_scatter x3 -> x0, waiting for transfers between devices: 206 us -> none  [the longest x1 74.1 us: per_device(): lax.psum_scatter(grad_down.astype(jnp.bfloat16), 'dp', scatter_dimension=...]
    dot_general x32 -> x22, matrix products: 320 us -> 151 us  [dot(): return lax.dot_general(a, b, dims, preferred_element_type=jnp.float32)]
    pallas_call x0 -> x10, Pallas kernels: none -> 124 us  [the longest x1 57.7 us: attention_backward(): pl.pallas_call(functools.partial(bwd_kernel, pairs), grid_spec=grid_spec,...]
    ppermute x0 -> x78, starting transfers between devices: none -> 116 us  [the longest x23 27.7 us: swap_core(): return lax.ppermute(a, 'dp', core_pairs())]
    all_gather x4 -> x0, waiting for transfers between devices: 101 us -> none  [the longest x1 37 us: per_device(): lax.all_gather(w_fc1.astype(jnp.bfloat16), 'dp', axis=0, tiled=True)]
    unnamed x14 -> x0, waiting for transfers between devices: 84.4 us -> none
  transfers between devices with their start and end apart: 13 -> 78, of which waited for: 12 -> 28; matrix products, arithmetic and copies ran while one was open for 20% -> 22% of each run, Pallas kernels for 0% -> 16%
where the time goes in v1:
time: 758 us; the launch traced here: 750 us
  waiting for transfers between devices  219 us (29%)
  matrix products  151 us (20%)
  Pallas kernels  124 us (16%)
  starting transfers between devices  116 us (15%)
  other arithmetic  73.2 us (10%)
  local copies, waits for them, and re-layouts  64.8 us (9%)
    dot_general x22, matrix products, dot(): return lax.dot_general(a, b, dims, preferred_element_type=jnp.float32)  151 us
    ppermute x12, waiting for transfers between devices, swap_y(): return lax.ppermute(a, 'tensor', Y_PAIRS)  92.3 us
    ppermute x15, waiting for transfers between devices, swap_x(): return lax.ppermute(a, 'dp', x_pairs())  60.4 us
    pallas_call x1, Pallas kernels, attention_backward(): pl.pallas_call(functools.partial(bwd_kernel, pairs), grid_spec=grid_spec,...  57.7 us
    pallas_call x2, Pallas kernels, attention_forward(): pl.pallas_call(functools.partial(fwd_kernel, pairs), grid_spec=grid_spec,...  52 us
    ppermute x12, waiting for transfers between devices, reduce_rows(): out = out + lax.ppermute(piece, 'dp', z_pairs(k)).astype(F32)  38.5 us
    unnamed x165, local copies, waits for them, and re-layouts  30.6 us
    ppermute x23, starting transfers between devices, swap_core(): return lax.ppermute(a, 'dp', core_pairs())  27.7 us
  transfers between devices with their start and end apart: 78, of which 28 were waited for; matrix products, arithmetic and copies ran while one was open for 22% of the time, Pallas kernels for 16%

profile of v1, /device:TPU:0, one launch (start us, length us, event | category | flops | bytes accessed | tf_op | source)
XLA Modules:
  0.0 750.4 jit_solution(15971278183741324051)
XLA Ops:
  1.7 5.1 collective-permute-start.25
  17.0 6.5 copy.46
  23.5 3.0 convert_reduce_fusion.2
  28.9 4.6 fusion
  33.5 10.0 %collective-permute-start.23 = (bf16[64,2048]{1,0:T(8,128)(2,1)S(1)}, bf16[64,2048]{1,0:T(8,128)(2,1)S(1)}, u32[]{:S(2)}, u32[]{:S(2)}) collective-permute-start(bf16[64,2048]{1,0:T(8,128)(2,1)S(1)} %get-tuple-element.95), channel_id=1, source_target_pairs={{0,8},{2,10},{4,12},{6,14},{8,16},{10,18},{12,20},{14,22},{16,24},... | collective-permute-start | bytes 786440 | tf_op jit(solution)/shard_map/ppermute | solution.py:308
  43.5 3.1 collective-permute-done.1
  54.7 2.9 collective-permute-done.6
  62.5 4.9 collective-permute-done.19
  68.2 10.8 %collective-permute-done.18 = bf16[64,2048]{1,0:T(8,128)(2,1)S(1)} collective-permute-done((bf16[64,2048]{1,0:T(8,128)(2,1)}, bf16[64,2048]{1,0:T(8,128)(2,1)S(1)}, u32[]{:S(2)}, u32[]{:S(2)}) %collective-permute-start.18) | collective-permute-done | bytes 262176 | tf_op jit(solution)/shard_map/ppermute | solution.py:308
  81.9 3.1 constant_dynamic-slice_fusion.15
  91.0 12.0 %collective-permute-done.14.refs_1_ = bf16[4,64,512]{2,1,0:T(8,128)(2,1)} collective-permute-done((bf16[4,64,512]{2,1,0:T(8,128)(2,1)}, bf16[4,64,512]{2,1,0:T(8,128)(2,1)}, u32[]{:S(2)}, u32[]{:S(2)}) %collective-permute-start.14) | collective-permute-done | bytes 262176 | tf_op jit(solution)/shard_map/ppermute | solution.py:268
  103.0 3.9 copy.73
  116.6 3.2 assemble.7
  119.8 9.4 %add_convert_fusion.q_ref.k_ref.v_ref = bf16[2048,1536]{1,0:T(8,128)(2,1)} fusion(bf16[1024,1536]{1,0:T(8,128)(2,1)S(1)} %bitcast.263, f32[1536]{0:T(1024)S(1)} %pad_maximum_fusion.13, f32[1024]{0:T(1024)S(1)} %bitcast.344, f32[1024]{0:T(1024)S(1)} %bitcast.330, f32[2048]{0:T(1024)S(1)} %add_rsqrt_fusion, f32[2048]{0:T(1024)S(1)} %broadcast_multiply_fusion, ...), kind=kOutput, calls=%fused_computation.6 | convolution fusion | flops 6461325312 | bytes 13662208 | tf_op jit(solution)/shard_map/dot_general | solution.py:26
  129.2 21.0 %attention_forward.2 = (bf16[1024,512]{1,0:T(8,128)(2,1)S(1)}, f32[1,8,1024]{2,1,0:T(8,128)S(1)}) custom-call(s32[1,8]{1,0:T(1,128)S(1)} %and_select_fusion.lo_ref, s32[1]{0:T(128)} %bitcast.2.off_ref, bf16[2048,1536]{1,0:T(8,128)(2,1)} %add_convert_fusion.q_ref.k_ref.v_ref, bf16[2048,1536]{1,0:T(8,128)(2,1)} %add_convert_fusion.q_ref.k_ref.v_ref, ...), custom_call_target="tpu_custom_call" | custom-call | flops 1342177280 | bytes 4194304 | tf_op jit(solution)/shard_map/attention_forward/pallas_call | solution.py:100
  150.3 31.0 %attention_forward.3 = (bf16[1024,512]{1,0:T(8,128)(2,1)S(1)}, f32[1,8,1024]{2,1,0:T(8,128)S(1)}) custom-call(s32[1,8]{1,0:T(1,128)S(1)} %and_select_fusion.lo_ref, s32[1]{0:T(128)} %bitcast.24.off_ref, bf16[2048,1536]{1,0:T(8,128)(2,1)} %add_convert_fusion.q_ref.k_ref.v_ref, bf16[2048,1536]{1,0:T(8,128)(2,1)} %add_convert_fusion.q_ref.k_ref.v_ref, ...), custom_call_target="tpu_custom_call" | custom-call | flops 1342177280 | bytes 4194304 | tf_op jit(solution)/shard_map/attention_forward/pallas_call | solution.py:100
  184.3 4.5 collective-permute-start.22
  192.6 2.6 convolution_convert_fusion.10
  195.2 3.2 assemble.11
  198.4 5.7 collective-permute-done.33.refs_0_
  204.1 8.4 %collective-permute-start.31 = (bf16[4,64,2048]{2,1,0:T(8,128)(2,1)S(1)}, bf16[4,64,2048]{2,1,0:T(8,128)(2,1)S(1)}, u32[]{:S(2)}, u32[]{:S(2)}) collective-permute-start(bf16[4,64,2048]{2,1,0:T(8,128)(2,1)S(1)} %collective-permute-done.29.refs_0_), channel_id=1, source_target_pairs={{0,2},{2,0},{4,6},{6,4},{8,10},{10,8},{12,14},{14,12},{16,18},{18,... | collective-permute-start | bytes 3145736 | tf_op jit(solution)/shard_map/ppermute | solution.py:264
  212.5 14.0 %collective-permute-done.34.refs_1_ = bf16[4,64,2048]{2,1,0:T(8,128)(2,1)S(1)} collective-permute-done((bf16[4,64,2048]{2,1,0:T(8,128)(2,1)S(1)}, bf16[4,64,2048]{2,1,0:T(8,128)(2,1)S(1)}, u32[]{:S(2)}, u32[]{:S(2)}) %collective-permute-start.34) | collective-permute-done | bytes 1048608 | tf_op jit(solution)/shard_map/ppermute | solution.py:272
  226.6 8.5 %collective-permute-start.36 = (bf16[4,64,2048]{2,1,0:T(8,128)(2,1)S(1)}, bf16[4,64,2048]{2,1,0:T(8,128)(2,1)S(1)}, u32[]{:S(2)}, u32[]{:S(2)}) collective-permute-start(bf16[4,64,2048]{2,1,0:T(8,128)(2,1)S(1)} %collective-permute-done.34.refs_1_), channel_id=1, source_target_pairs={{0,2},{2,0},{4,6},{6,4},{8,10},{10,8},{12,14},{14,12},{16,18},{18,... | collective-permute-start | bytes 3145736 | tf_op jit(solution)/shard_map/ppermute | solution.py:264
  236.7 12.5 %collective-permute-done.12 = bf16[1024,512]{1,0:T(8,128)(2,1)} collective-permute-done((bf16[1024,512]{1,0:T(8,128)(2,1)S(1)}, bf16[1024,512]{1,0:T(8,128)(2,1)}, u32[]{:S(2)}, u32[]{:S(2)}) %collective-permute-start.12) | collective-permute-done | bytes 1048608 | tf_op jit(solution)/shard_map/ppermute | solution.py:272
  249.2 3.4 fusion.37
  259.3 6.7 fusion.83
  266.0 9.4 %convolution_convert_fusion.8 = bf16[1024,1024]{0,1:T(8,128)(2,1)} fusion(bf16[1024,2048]{1,0:T(8,128)(2,1)S(1)} %bitcast.255, f32[1024,2048]{1,0:T(8,128)} %fusion.83, f32[2048]{0:T(1024)S(1)} %get-tuple-element.113), kind=kOutput, calls=%fused_computation.123 | convolution fusion | flops 4316987392 | bytes 14688256 | tf_op jit(solution)/shard_map/dot_general | solution.py:26
  277.0 8.4 %fusion.84 = f32[1024,2048]{1,0:T(8,128)} fusion(bf16[1024,1024]{0,1:T(8,128)(2,1)} %copy-done.44, bf16[1024,2048]{1,0:T(8,128)(2,1)S(1)} %bitcast.259), kind=kOutput, calls=%fused_computation.264 | convolution fusion | flops 4294967296 | bytes 14680064 | tf_op jit(solution)/shard_map/dot_general | solution.py:26
  287.2 9.7 %fusion.38 = (f32[1024]{0:T(1024)S(1)}, bf16[1024,1024]{0,1:T(8,128)(2,1)}) fusion(bf16[1024,1024]{0,1:T(8,128)(2,1)S(1)} %copy-done.26, f32[1024]{0:T(1024)S(1)} %bitcast.305, bf16[1024,2048]{1,0:T(8,128)(2,1)S(1)} %bitcast.261, f32[1024,2048]{1,0:T(8,128)} %fusion.84, f32[2048]{0:T(1024)S(1)} %get-tuple-element.114), kind=kOutput, calls=%fused_computation.92 | convolution fusion | flops 4322229248 | bytes 16793600 | tf_op jit(solution)/shard_map/dot_general | solution.py:26
  296.9 2.7 multiply_reduce_fusion.5
  299.6 4.2 fusion.29
  303.8 5.5 convert_reduce_fusion.8
  309.2 15.2 %convert_reduce_fusion.4 = (f32[2048]{0:T(1024)S(1)}, bf16[1024,2048]{1,0:T(8,128)(2,1)}) fusion(bf16[1024,1024]{0,1:T(8,128)(2,1)} %get-tuple-element.59, bf16[1024,2048]{1,0:T(8,128)(2,1)S(1)} %bitcast.256, f32[1024,2048]{1,0:T(8,128)} %fusion.83, f32[2048]{0:T(1024)S(1)} %get-tuple-element.113), kind=kOutput, calls=%fused_computation.29 | convolution fusion | flops 4341102592 | bytes 18890752 | tf_op jit(solution)/shard_map/dot_general | solution.py:26
  324.4 13.5 %convert_reduce_fusion.3 = (f32[2048]{0:T(1024)S(1)}, bf16[1024,2048]{1,0:T(8,128)(2,1)}) fusion(bf16[1024,1024]{0,1:T(8,128)(2,1)S(1)} %copy-done.46, bf16[1024,2048]{1,0:T(8,128)(2,1)S(1)} %bitcast.262, f32[1024,2048]{1,0:T(8,128)} %fusion.84, f32[2048]{0:T(1024)S(1)} %get-tuple-element.114), kind=kOutput, calls=%fused_computation.28 | convolution fusion | flops 4341102592 | bytes 18890752 | tf_op jit(solution)/shard_map/dot_general | solution.py:26
  337.9 7.2 convolution_convert_fusion.6
  345.1 9.2 %multiply_reduce_fusion = (f32[1024]{0:T(1024)S(1)}, f32[1024]{0:T(1024)S(1)}, f32[1024]{0:T(1024)S(1)}, f32[1024]{0:T(1024)S(1)}, bf16[1024,1024]{0,1:T(8,128)(2,1)S(1)}) fusion(bf16[1024,1024]{0,1:T(8,128)(2,1)S(1)} %convolution_convert_fusion.6, f32[1024,1024]{0,1:T(8,128)S(1)} %copy-done.13, f32[1024]{0:T(1024)S(1)} %add_rsqrt_fusion.2, ...), kind=kOutput, calls=%fused_computation.63 | convolution fusion | flops 4308594688 | bytes 16805888 | tf_op jit(solution)/shard_map/dot_general | solution.py:26
  354.3 5.1 multiply_reduce_fusion.1
  369.8 6.0 convolution_convert_fusion.3
  375.9 6.0 convolution_convert_fusion.4
  381.9 6.7 convolution_convert_fusion.1
  388.6 6.4 convolution_convert_fusion.2
  395.7 4.0 collective-permute-start.73
  399.8 4.9 constant_dynamic-slice_fusion.2
  404.7 3.6 convolution_convert_fusion.11
  410.2 3.9 copy.67
  422.0 18.9 %collective-permute-done.75 = f32[12,1024]{1,0:T(8,128)S(1)} collective-permute-done((f32[12,1024]{1,0:T(8,128)S(1)}, f32[12,1024]{1,0:T(8,128)S(1)}, u32[]{:S(2)}, u32[]{:S(2)}) %collective-permute-start.75) | collective-permute-done | bytes 49184 | tf_op jit(solution)/shard_map/ppermute | solution.py:272
  446.3 6.0 collective-permute-start.77
  462.6 7.0 collective-permute-done.47
  473.0 57.7 %attention_backward.1 = bf16[2048,1536]{1,0:T(8,128)(2,1)} custom-call(s32[1,8]{1,0:T(1,128)} %copy-done.11, bf16[2048,1536]{1,0:T(8,128)(2,1)} %add_convert_fusion.q_ref.k_ref.v_ref, bf16[2048,1536]{1,0:T(8,128)(2,1)} %add_convert_fusion.q_ref.k_ref.v_ref, bf16[2048,1536]{1,0:T(8,128)(2,1)} %add_convert_fusion.q_ref.k_ref.v_ref, ...), custom_call_target="tpu_custom_call" | custom-call | flops 6710886400 | bytes 16777216 | tf_op jit(solution)/shard_map/attention_backward/pallas_call | solution.py:202
  530.8 9.7 %convolution_convert_fusion = bf16[1024,1536]{1,0:T(8,128)(2,1)S(1)} fusion(bf16[2048,1536]{1,0:T(8,128)(2,1)} %attention_backward.1, f32[1024]{0:T(1024)S(1)} %bitcast.345, f32[1024]{0:T(1024)S(1)} %bitcast.331, f32[2048]{0:T(1024)S(1)} %copy-done.61, f32[2048]{0:T(1024)S(1)} %copy-done.58, bf16[2048,1024]{0,1:T(8,128)(2,1)S(1)} %copy-done.17), kind=kOutput, calls=%fused_computation.82 | convolution fusion | flops 6456606720 | bytes 13656064 | tf_op jit(solution)/shard_map/dot_general | solution.py:26
  545.2 3.7 fusion.52
  549.0 12.4 %collective-permute-start.50 = (bf16[64,512]{1,0:T(8,128)(2,1)S(1)}, bf16[64,512]{1,0:T(8,128)(2,1)S(1)}, u32[]{:S(2)}, u32[]{:S(2)}) collective-permute-start(bf16[64,512]{1,0:T(8,128)(2,1)S(1)} %get-tuple-element.104), channel_id=1, source_target_pairs={{0,16},{2,18},{4,20},{6,22},{8,24},{10,26},{12,28},{14,30},{16,0},... | collective-permute-start | bytes 196616 | tf_op jit(solution)/shard_map/ppermute | solution.py:347
  564.2 3.5 collective-permute-done.49
  590.6 23.6 %collective-permute-done.38 = bf16[1024,1024]{0,1:T(8,128)(2,1)} collective-permute-done((bf16[1024,1024]{0,1:T(8,128)(2,1)S(1)}, bf16[1024,1024]{0,1:T(8,128)(2,1)}, u32[]{:S(2)}, u32[]{:S(2)}) %collective-permute-start.38) | collective-permute-done | bytes 2097184 | tf_op jit(solution)/shard_map/ppermute | solution.py:272
  614.2 7.5 %fusion.28 = (f32[1024]{0:T(1024)S(1)}, f32[1024]{0:T(1024)S(1)}, f32[1024]{0:T(1024)S(1)}, f32[1024]{0:T(1024)S(1)}, f32[1024]{0:T(1024)S(1)}, /*index=5*/f32[1024]{0:T(1024)S(1)}, bf16[1024,1024]{0,1:T(8,128)(2,1)}) fusion(f32[2048,1024]{0,1:T(8,128)S(1)} %bitcast.275, s32[]{:T(128)} %select_n.181, f32[1024]{0:T(1024)S(1)} %bitcast.332, ...), kind=kOutput, calls=%fused_computation.51 | convolution fusion | flops 3236947968 | bytes 21001220 | tf_op jit(solution)/shard_map/dot_general | solution.py:26
  623.6 38.6 %collective-permute-done.69 = f32[4,1024]{1,0:T(4,128)S(1)} collective-permute-done((f32[4,1024]{1,0:T(4,128)S(1)}, f32[4,1024]{1,0:T(4,128)S(1)}, u32[]{:S(2)}, u32[]{:S(2)}) %collective-permute-start.69) | collective-permute-done | bytes 16416 | tf_op jit(solution)/shard_map/ppermute | solution.py:268
  662.8 3.9 add_convert_fusion.2
  666.8 2.6 fusion.47
  671.4 2.6 fusion.45
  690.0 9.3 %collective-permute-done.42 = bf16[64,1536]{1,0:T(8,128)(2,1)S(1)} collective-permute-done((bf16[64,1536]{1,0:T(8,128)(2,1)S(1)}, bf16[64,1536]{1,0:T(8,128)(2,1)S(1)}, u32[]{:S(2)}, u32[]{:S(2)}) %collective-permute-start.42) | collective-permute-done | bytes 196640 | tf_op jit(solution)/shard_map/ppermute | solution.py:347
  703.7 3.5 collective-permute-start.59
  709.2 14.3 %collective-permute-done.64 = bf16[4,64,2048]{2,1,0:T(8,128)(2,1)S(1)} collective-permute-done((bf16[4,64,2048]{2,1,0:T(8,128)(2,1)}, bf16[4,64,2048]{2,1,0:T(8,128)(2,1)S(1)}, u32[]{:S(2)}, u32[]{:S(2)}) %collective-permute-start.64) | collective-permute-done | bytes 1048608 | tf_op jit(solution)/shard_map/ppermute | solution.py:272
  730.2 3.2 collective-permute-done.67
  733.4 15.6 %collective-permute-done.66 = bf16[64,2048]{1,0:T(8,128)(2,1)S(1)} collective-permute-done((bf16[64,2048]{1,0:T(8,128)(2,1)S(1)}, bf16[64,2048]{1,0:T(8,128)(2,1)S(1)}, u32[]{:S(2)}, u32[]{:S(2)}) %collective-permute-start.66) | collective-permute-done | bytes 262176 | tf_op jit(solution)/shard_map/ppermute | solution.py:347
  (424 shorter events, 168.9 us)
Async XLA Ops:
  1.7 57.9 %collective-permute-start.25 = (bf16[64,2048]{1,0:T(8,128)(2,1)S(1)}, bf16[64,2048]{1,0:T(8,128)(2,1)S(1)}, u32[]{:S(2)}, u32[]{:S(2)}) collective-permute-start(bf16[64,2048]{1,0:T(8,128)(2,1)S(1)} %get-tuple-element.95), channel_id=1, source_target_pairs={{0,24},{2,26},{4,28},{6,30},{8,0},{10,2},{12,4},{14,6},{16,8},{18,... | collective-permute-start | bytes 786440 | tf_op jit(solution)/shard_map/ppermute | solution.py:308
  6.8 52.9 %collective-permute-start.24 = (bf16[64,2048]{1,0:T(8,128)(2,1)S(1)}, bf16[64,2048]{1,0:T(8,128)(2,1)S(1)}, u32[]{:S(2)}, u32[]{:S(2)}) collective-permute-start(bf16[64,2048]{1,0:T(8,128)(2,1)S(1)} %get-tuple-element.95), channel_id=1, source_target_pairs={{0,16},{2,18},{4,20},{6,22},{8,24},{10,26},{12,28},{14,30},{16,0},... | collective-permute-start | bytes 786440 | tf_op jit(solution)/shard_map/ppermute | solution.py:308
  7.9 25.6 %collective-permute-start.2 = (bf16[64,1536]{1,0:T(8,128)(2,1)S(1)}, bf16[64,1536]{1,0:T(8,128)(2,1)S(1)}, u32[]{:S(2)}, u32[]{:S(2)}) collective-permute-start(bf16[64,1536]{1,0:T(8,128)(2,1)S(1)} %pad_maximum_fusion.7), channel_id=1, source_target_pairs={{0,24},{2,26},{4,28},{6,30},{8,0},{10,2},{12,4},{14,6},{16,8},{18,... | collective-permute-start | bytes 589832 | tf_op jit(solution)/shard_map/ppermute | solution.py:308
  8.4 38.1 %collective-permute-start.1 = (bf16[64,1536]{1,0:T(8,128)(2,1)S(1)}, bf16[64,1536]{1,0:T(8,128)(2,1)S(1)}, u32[]{:S(2)}, u32[]{:S(2)}) collective-permute-start(bf16[64,1536]{1,0:T(8,128)(2,1)S(1)} %pad_maximum_fusion.7), channel_id=1, source_target_pairs={{0,16},{2,18},{4,20},{6,22},{8,24},{10,26},{12,28},{14,30},{16,0},... | collective-permute-start | bytes 589832 | tf_op jit(solution)/shard_map/ppermute | solution.py:308
  11.0 35.6 %collective-permute-start = (bf16[64,1536]{1,0:T(8,128)(2,1)S(1)}, bf16[64,1536]{1,0:T(8,128)(2,1)S(1)}, u32[]{:S(2)}, u32[]{:S(2)}) collective-permute-start(bf16[64,1536]{1,0:T(8,128)(2,1)S(1)} %pad_maximum_fusion.7), channel_id=1, source_target_pairs={{0,8},{2,10},{4,12},{6,14},{8,16},{10,18},{12,20},{14,22},{16,24},... | collective-permute-start | bytes 589832 | tf_op jit(solution)/shard_map/ppermute | solution.py:308
  33.5 27.6 %collective-permute-start.23 = (bf16[64,2048]{1,0:T(8,128)(2,1)S(1)}, bf16[64,2048]{1,0:T(8,128)(2,1)S(1)}, u32[]{:S(2)}, u32[]{:S(2)}) collective-permute-start(bf16[64,2048]{1,0:T(8,128)(2,1)S(1)} %get-tuple-element.95), channel_id=1, source_target_pairs={{0,8},{2,10},{4,12},{6,14},{8,16},{10,18},{12,20},{14,22},{16,24},... | collective-permute-start | bytes 786440 | tf_op jit(solution)/shard_map/ppermute | solution.py:308
  52.4 32.5 %collective-permute-start.3 = (bf16[4,64,1536]{2,1,0:T(8,128)(2,1)S(1)}, bf16[4,64,1536]{2,1,0:T(8,128)(2,1)}, u32[]{:S(2)}, u32[]{:S(2)}) collective-permute-start(bf16[4,64,1536]{2,1,0:T(8,128)(2,1)S(1)} %pad_maximum_fusion.4.refs_0_), channel_id=1, source_target_pairs={{0,4},{2,6},{4,0},{6,2},{8,12},{10,14},{12,8},{14,10},{16,20},{18,... | collective-permute-start | bytes 2359304 | tf_op jit(solution)/shard_map/ppermute | solution.py:268
  57.6 9.8 %collective-permute-start.19 = (bf16[64,2048]{1,0:T(8,128)(2,1)}, bf16[64,2048]{1,0:T(8,128)(2,1)}, u32[]{:S(2)}, u32[]{:S(2)}) collective-permute-start(bf16[64,2048]{1,0:T(8,128)(2,1)} %convert_element_type.437), channel_id=1, source_target_pairs={{0,24},{2,26},{4,28},{6,30},{8,0},{10,2},{12,4},{14,6},{16,8},{18,... | collective-permute-start | bytes 786440 | tf_op jit(solution)/shard_map/ppermute | solution.py:308
  59.7 19.3 %collective-permute-start.18 = (bf16[64,2048]{1,0:T(8,128)(2,1)}, bf16[64,2048]{1,0:T(8,128)(2,1)S(1)}, u32[]{:S(2)}, u32[]{:S(2)}) collective-permute-start(bf16[64,2048]{1,0:T(8,128)(2,1)} %convert_element_type.437), channel_id=1, source_target_pairs={{0,16},{2,18},{4,20},{6,22},{8,24},{10,26},{12,28},{14,30},{16,0},... | collective-permute-start | bytes 786440 | tf_op jit(solution)/shard_map/ppermute | solution.py:308
  59.8 19.9 %collective-permute-start.17 = (bf16[64,2048]{1,0:T(8,128)(2,1)}, bf16[64,2048]{1,0:T(8,128)(2,1)S(1)}, u32[]{:S(2)}, u32[]{:S(2)}) collective-permute-start(bf16[64,2048]{1,0:T(8,128)(2,1)} %convert_element_type.437), channel_id=1, source_target_pairs={{0,8},{2,10},{4,12},{6,14},{8,16},{10,18},{12,20},{14,22},{16,24},... | collective-permute-start | bytes 786440 | tf_op jit(solution)/shard_map/ppermute | solution.py:308
  61.2 23.8 %collective-permute-start.9 = (bf16[4,64,512]{2,1,0:T(8,128)(2,1)S(1)}, bf16[4,64,512]{2,1,0:T(8,128)(2,1)S(1)}, u32[]{:S(2)}, u32[]{:S(2)}) collective-permute-start(bf16[4,64,512]{2,1,0:T(8,128)(2,1)S(1)} %pad_maximum_fusion.6.refs_0_), channel_id=1, source_target_pairs={{0,4},{2,6},{4,0},{6,2},{8,12},{10,14},{12,8},{14,10},{16,20},{18,... | collective-permute-start | bytes 786440 | tf_op jit(solution)/shard_map/ppermute | solution.py:268
  67.4 47.4 %collective-permute-start.26 = (bf16[4,64,2048]{2,1,0:T(8,128)(2,1)S(1)}, bf16[4,64,2048]{2,1,0:T(8,128)(2,1)S(1)}, u32[]{:S(2)}, u32[]{:S(2)}) collective-permute-start(bf16[4,64,2048]{2,1,0:T(8,128)(2,1)S(1)} %pad_maximum_fusion.3.refs_0_), channel_id=1, source_target_pairs={{0,4},{2,6},{4,0},{6,2},{8,12},{10,14},{12,8},{14,10},{16,20},{18,... | collective-permute-start | bytes 3145736 | tf_op jit(solution)/shard_map/ppermute | solution.py:268
  85.0 29.8 %collective-permute-start.4 = (bf16[4,64,1536]{2,1,0:T(8,128)(2,1)S(1)}, bf16[4,64,1536]{2,1,0:T(8,128)(2,1)}, u32[]{:S(2)}, u32[]{:S(2)}) collective-permute-start(bf16[4,64,1536]{2,1,0:T(8,128)(2,1)S(1)} %pad_maximum_fusion.4.refs_0_), channel_id=1, source_target_pairs={{0,2},{2,0},{4,6},{6,4},{8,10},{10,8},{12,14},{14,12},{16,18},{18,... | collective-permute-start | bytes 2359304 | tf_op jit(solution)/shard_map/ppermute | solution.py:264
  85.0 31.4 %collective-permute-start.5 = (bf16[4,64,1536]{2,1,0:T(8,128)(2,1)}, bf16[4,64,1536]{2,1,0:T(8,128)(2,1)}, u32[]{:S(2)}, u32[]{:S(2)}) collective-permute-start(bf16[4,64,1536]{2,1,0:T(8,128)(2,1)} %collective-permute-done.3.refs_1_), channel_id=1, source_target_pairs={{0,2},{2,0},{4,6},{6,4},{8,10},{10,8},{12,14},{14,12},{16,18},{18,... | collective-permute-start | bytes 2359304 | tf_op jit(solution)/shard_map/ppermute | solution.py:264
  88.5 14.5 %collective-permute-start.14 = (bf16[4,64,512]{2,1,0:T(8,128)(2,1)}, bf16[4,64,512]{2,1,0:T(8,128)(2,1)}, u32[]{:S(2)}, u32[]{:S(2)}) collective-permute-start(bf16[4,64,512]{2,1,0:T(8,128)(2,1)} %collective-permute-done.13.refs_0_), channel_id=1, source_target_pairs={{0,4},{2,6},{4,0},{6,2},{8,12},{10,14},{12,8},{14,10},{16,20},{18,... | collective-permute-start | bytes 786440 | tf_op jit(solution)/shard_map/ppermute | solution.py:268
  90.9 20.0 %collective-permute-start.15 = (bf16[4,64,512]{2,1,0:T(8,128)(2,1)}, bf16[4,64,512]{2,1,0:T(8,128)(2,1)}, u32[]{:S(2)}, u32[]{:S(2)}) collective-permute-start(bf16[4,64,512]{2,1,0:T(8,128)(2,1)} %collective-permute-done.13.refs_0_), channel_id=1, source_target_pairs={{0,2},{2,0},{4,6},{6,4},{8,10},{10,8},{12,14},{14,12},{16,18},{18,... | collective-permute-start | bytes 786440 | tf_op jit(solution)/shard_map/ppermute | solution.py:264
  103.0 8.5 %collective-permute-start.16 = (bf16[4,64,512]{2,1,0:T(8,128)(2,1)}, bf16[4,64,512]{2,1,0:T(8,128)(2,1)}, u32[]{:S(2)}, u32[]{:S(2)}) collective-permute-start(bf16[4,64,512]{2,1,0:T(8,128)(2,1)} %collective-permute-done.14.refs_1_), channel_id=1, source_target_pairs={{0,2},{2,0},{4,6},{6,4},{8,10},{10,8},{12,14},{14,12},{16,18},{18,... | collective-permute-start | bytes 786440 | tf_op jit(solution)/shard_map/ppermute | solution.py:264
  110.9 70.4 %collective-permute-start.27 = (bf16[4,64,2048]{2,1,0:T(8,128)(2,1)S(1)}, bf16[4,64,2048]{2,1,0:T(8,128)(2,1)S(1)}, u32[]{:S(2)}, u32[]{:S(2)}) collective-permute-start(bf16[4,64,2048]{2,1,0:T(8,128)(2,1)S(1)} %pad_maximum_fusion.3.refs_0_), channel_id=1, source_target_pairs={{0,2},{2,0},{4,6},{6,4},{8,10},{10,8},{12,14},{14,12},{16,18},{18,... | collective-permute-start | bytes 3145736 | tf_op jit(solution)/shard_map/ppermute | solution.py:264
  111.4 71.3 %collective-permute-start.20 = (bf16[4,64,2048]{2,1,0:T(8,128)(2,1)S(1)}, bf16[4,64,2048]{2,1,0:T(8,128)(2,1)S(1)}, u32[]{:S(2)}, u32[]{:S(2)}) collective-permute-start(bf16[4,64,2048]{2,1,0:T(8,128)(2,1)S(1)} %pad_maximum_fusion.2.refs_0_), channel_id=1, source_target_pairs={{0,4},{2,6},{4,0},{6,2},{8,12},{10,14},{12,8},{14,10},{16,20},{18,... | collective-permute-start | bytes 3145736 | tf_op jit(solution)/shard_map/ppermute | solution.py:268
  114.7 69.5 %collective-permute-start.21 = (bf16[4,64,2048]{2,1,0:T(8,128)(2,1)S(1)}, bf16[4,64,2048]{2,1,0:T(8,128)(2,1)S(1)}, u32[]{:S(2)}, u32[]{:S(2)}) collective-permute-start(bf16[4,64,2048]{2,1,0:T(8,128)(2,1)S(1)} %pad_maximum_fusion.2.refs_0_), channel_id=1, source_target_pairs={{0,2},{2,0},{4,6},{6,4},{8,10},{10,8},{12,14},{14,12},{16,18},{18,... | collective-permute-start | bytes 3145736 | tf_op jit(solution)/shard_map/ppermute | solution.py:264
  114.8 73.9 %collective-permute-start.29 = (bf16[4,64,2048]{2,1,0:T(8,128)(2,1)S(1)}, bf16[4,64,2048]{2,1,0:T(8,128)(2,1)S(1)}, u32[]{:S(2)}, u32[]{:S(2)}) collective-permute-start(bf16[4,64,2048]{2,1,0:T(8,128)(2,1)S(1)} %pad_maximum_fusion.2.refs_0_), channel_id=1, source_target_pairs={{0,1},{1,0},{2,3},{3,2},{4,5},{5,4},{6,7},{7,6},{8,9},{9,8},{10,11... | collective-permute-start | bytes 3145736 | tf_op jit(solution)/shard_map/ppermute | solution.py:272
  116.4 73.4 %collective-permute-start.28 = (bf16[4,64,2048]{2,1,0:T(8,128)(2,1)S(1)}, bf16[4,64,2048]{2,1,0:T(8,128)(2,1)}, u32[]{:S(2)}, u32[]{:S(2)}) collective-permute-start(bf16[4,64,2048]{2,1,0:T(8,128)(2,1)S(1)} %collective-permute-done.26.refs_1_), channel_id=1, source_target_pairs={{0,2},{2,0},{4,6},{6,4},{8,10},{10,8},{12,14},{14,12},{16,18},{18,... | collective-permute-start | bytes 3145736 | tf_op jit(solution)/shard_map/ppermute | solution.py:264
  182.2 21.9 %collective-permute-start.33 = (bf16[4,64,2048]{2,1,0:T(8,128)(2,1)S(1)}, bf16[4,64,2048]{2,1,0:T(8,128)(2,1)S(1)}, u32[]{:S(2)}, u32[]{:S(2)}) collective-permute-start(bf16[4,64,2048]{2,1,0:T(8,128)(2,1)S(1)} %pad_maximum_fusion.3.refs_0_), channel_id=1, source_target_pairs={{0,1},{1,0},{2,3},{3,2},{4,5},{5,4},{6,7},{7,6},{8,9},{9,8},{10,11... | collective-permute-start | bytes 3145736 | tf_op jit(solution)/shard_map/ppermute | solution.py:272
  182.8 43.8 %collective-permute-start.34 = (bf16[4,64,2048]{2,1,0:T(8,128)(2,1)S(1)}, bf16[4,64,2048]{2,1,0:T(8,128)(2,1)S(1)}, u32[]{:S(2)}, u32[]{:S(2)}) collective-permute-start(bf16[4,64,2048]{2,1,0:T(8,128)(2,1)S(1)} %collective-permute-done.26.refs_1_), channel_id=1, source_target_pairs={{0,1},{1,0},{2,3},{3,2},{4,5},{5,4},{6,7},{7,6},{8,9},{9,8},{10,11... | collective-permute-start | bytes 3145736 | tf_op jit(solution)/shard_map/ppermute | solution.py:272
  184.3 28.3 %collective-permute-start.22 = (bf16[4,64,2048]{2,1,0:T(8,128)(2,1)S(1)}, bf16[4,64,2048]{2,1,0:T(8,128)(2,1)S(1)}, u32[]{:S(2)}, u32[]{:S(2)}) collective-permute-start(bf16[4,64,2048]{2,1,0:T(8,128)(2,1)S(1)} %collective-permute-done.20.refs_1_), channel_id=1, source_target_pairs={{0,2},{2,0},{4,6},{6,4},{8,10},{10,8},{12,14},{14,12},{16,18},{18,... | collective-permute-start | bytes 3145736 | tf_op jit(solution)/shard_map/ppermute | solution.py:264
  188.8 46.3 %collective-permute-start.30 = (bf16[4,64,2048]{2,1,0:T(8,128)(2,1)S(1)}, bf16[4,64,2048]{2,1,0:T(8,128)(2,1)S(1)}, u32[]{:S(2)}, u32[]{:S(2)}) collective-permute-start(bf16[4,64,2048]{2,1,0:T(8,128)(2,1)S(1)} %collective-permute-done.29.refs_0_), channel_id=1, source_target_pairs={{0,4},{2,6},{4,0},{6,2},{8,12},{10,14},{12,8},{14,10},{16,20},{18,... | collective-permute-start | bytes 3145736 | tf_op jit(solution)/shard_map/ppermute | solution.py:268
  189.8 59.3 %collective-permute-start.12 = (bf16[1024,512]{1,0:T(8,128)(2,1)S(1)}, bf16[1024,512]{1,0:T(8,128)(2,1)}, u32[]{:S(2)}, u32[]{:S(2)}) collective-permute-start(bf16[1024,512]{1,0:T(8,128)(2,1)S(1)} %get-tuple-element.16), channel_id=1, source_target_pairs={{0,1},{1,0},{2,3},{3,2},{4,5},{5,4},{6,7},{7,6},{8,9},{9,8},{10,11... | collective-permute-start | bytes 3145736 | tf_op jit(solution)/shard_map/ppermute | solution.py:272
  204.1 71.3 %collective-permute-start.31 = (bf16[4,64,2048]{2,1,0:T(8,128)(2,1)S(1)}, bf16[4,64,2048]{2,1,0:T(8,128)(2,1)S(1)}, u32[]{:S(2)}, u32[]{:S(2)}) collective-permute-start(bf16[4,64,2048]{2,1,0:T(8,128)(2,1)S(1)} %collective-permute-done.29.refs_0_), channel_id=1, source_target_pairs={{0,2},{2,0},{4,6},{6,4},{8,10},{10,8},{12,14},{14,12},{16,18},{18,... | collective-permute-start | bytes 3145736 | tf_op jit(solution)/shard_map/ppermute | solution.py:264
  212.5 72.9 %collective-permute-start.35 = (bf16[4,64,2048]{2,1,0:T(8,128)(2,1)S(1)}, bf16[4,64,2048]{2,1,0:T(8,128)(2,1)S(1)}, u32[]{:S(2)}, u32[]{:S(2)}) collective-permute-start(bf16[4,64,2048]{2,1,0:T(8,128)(2,1)S(1)} %collective-permute-done.33.refs_0_), channel_id=1, source_target_pairs={{0,2},{2,0},{4,6},{6,4},{8,10},{10,8},{12,14},{14,12},{16,18},{18,... | collective-permute-start | bytes 3145736 | tf_op jit(solution)/shard_map/ppermute | solution.py:264
  226.6 58.8 %collective-permute-start.36 = (bf16[4,64,2048]{2,1,0:T(8,128)(2,1)S(1)}, bf16[4,64,2048]{2,1,0:T(8,128)(2,1)S(1)}, u32[]{:S(2)}, u32[]{:S(2)}) collective-permute-start(bf16[4,64,2048]{2,1,0:T(8,128)(2,1)S(1)} %collective-permute-done.34.refs_1_), channel_id=1, source_target_pairs={{0,2},{2,0},{4,6},{6,4},{8,10},{10,8},{12,14},{14,12},{16,18},{18,... | collective-permute-start | bytes 3145736 | tf_op jit(solution)/shard_map/ppermute | solution.py:264
  235.1 40.3 %collective-permute-start.32 = (bf16[4,64,2048]{2,1,0:T(8,128)(2,1)S(1)}, bf16[4,64,2048]{2,1,0:T(8,128)(2,1)S(1)}, u32[]{:S(2)}, u32[]{:S(2)}) collective-permute-start(bf16[4,64,2048]{2,1,0:T(8,128)(2,1)S(1)} %collective-permute-done.30.refs_1_), channel_id=1, source_target_pairs={{0,2},{2,0},{4,6},{6,4},{8,10},{10,8},{12,14},{14,12},{16,18},{18,... | collective-permute-start | bytes 3145736 | tf_op jit(solution)/shard_map/ppermute | solution.py:264
  395.7 18.9 %collective-permute-start.73 = (f32[12,1024]{1,0:T(8,128)S(1)}, f32[12,1024]{1,0:T(8,128)S(1)}, u32[]{:S(2)}, u32[]{:S(2)}) collective-permute-start(f32[12,1024]{1,0:T(8,128)S(1)} %reshape.346), channel_id=1, source_target_pairs={{0,2},{2,0},{4,6},{6,4},{8,10},{10,8},{12,14},{14,12},{16,18},{18,... | collective-permute-start | bytes 147464 | tf_op jit(solution)/shard_map/ppermute | solution.py:264
  414.1 56.6 %collective-permute-start.37 = (bf16[1024,512]{1,0:T(8,128)(2,1)}, bf16[1024,512]{1,0:T(8,128)(2,1)S(1)}, u32[]{:S(2)}, u32[]{:S(2)}) collective-permute-start(bf16[1024,512]{1,0:T(8,128)(2,1)} %convolution_convert_fusion.13), channel_id=1, source_target_pairs={{0,1},{1,0},{2,3},{3,2},{4,5},{5,4},{6,7},{7,6},{8,9},{9,8},{10,11... | collective-permute-start | bytes 3145736 | tf_op jit(solution)/shard_map/ppermute | solution.py:272
  416.7 43.9 %collective-permute-start.46 = (bf16[4,2,64,512]{3,2,0,1:T(8,128)(2,1)S(1)}, bf16[4,2,64,512]{3,2,0,1:T(8,128)(2,1)S(1)}, u32[]{:S(2)}, u32[]{:S(2)}) collective-permute-start(bf16[4,2,64,512]{3,2,0,1:T(8,128)(2,1)S(1)} %bitcast.288), channel_id=1, source_target_pairs={{0,2},{2,0},{4,6},{6,4},{8,10},{10,8},{12,14},{14,12},{16,18},{18,... | collective-permute-start | bytes 1572872 | tf_op jit(solution)/shard_map/ppermute | solution.py:264
  419.0 21.9 %collective-permute-start.75 = (f32[12,1024]{1,0:T(8,128)S(1)}, f32[12,1024]{1,0:T(8,128)S(1)}, u32[]{:S(2)}, u32[]{:S(2)}) collective-permute-start(f32[12,1024]{1,0:T(8,128)S(1)} %add.571), channel_id=1, source_target_pairs={{0,1},{1,0},{2,3},{3,2},{4,5},{5,4},{6,7},{7,6},{8,9},{9,8},{10,11... | collective-permute-start | bytes 147464 | tf_op jit(solution)/shard_map/ppermute | solution.py:272
  421.9 39.4 %collective-permute-start.44 = (bf16[4,2,64,512]{3,2,0,1:T(8,128)(2,1)S(1)}, bf16[4,2,64,512]{3,2,0,1:T(8,128)(2,1)S(1)}, u32[]{:S(2)}, u32[]{:S(2)}) collective-permute-start(bf16[4,2,64,512]{3,2,0,1:T(8,128)(2,1)S(1)} %bitcast.289), channel_id=1, source_target_pairs={{0,2},{2,0},{4,6},{6,4},{8,10},{10,8},{12,14},{14,12},{16,18},{18,... | collective-permute-start | bytes 1572872 | tf_op jit(solution)/shard_map/ppermute | solution.py:264
  446.3 123.7 %collective-permute-start.54 = (bf16[4,2,64,2048]{3,2,0,1:T(8,128)(2,1)}, bf16[4,2,64,2048]{3,2,0,1:T(8,128)(2,1)}, u32[]{:S(2)}, u32[]{:S(2)}) collective-permute-start(bf16[4,2,64,2048]{3,2,0,1:T(8,128)(2,1)} %bitcast.248), channel_id=1, source_target_pairs={{0,2},{2,0},{4,6},{6,4},{8,10},{10,8},{12,14},{14,12},{16,18},{18,... | collective-permute-start | bytes 6291464 | tf_op jit(solution)/shard_map/ppermute | solution.py:264
  446.3 13.1 %collective-permute-start.77 = (f32[12,1024]{1,0:T(8,128)S(1)}, f32[12,1024]{1,0:T(8,128)S(1)}, u32[]{:S(2)}, u32[]{:S(2)}) collective-permute-start(f32[12,1024]{1,0:T(8,128)S(1)} %add.573), channel_id=1, source_target_pairs={{0,16},{2,18},{4,20},{6,22},{8,24},{10,26},{12,28},{14,30},{16,0},... | collective-permute-start | bytes 147464 | tf_op jit(solution)/shard_map/ppermute | solution.py:360
  459.4 114.4 %collective-permute-start.52 = (bf16[4,2,64,2048]{3,2,0,1:T(8,128)(2,1)}, bf16[4,2,64,2048]{3,2,0,1:T(8,128)(2,1)}, u32[]{:S(2)}, u32[]{:S(2)}) collective-permute-start(bf16[4,2,64,2048]{3,2,0,1:T(8,128)(2,1)} %bitcast.249), channel_id=1, source_target_pairs={{0,2},{2,0},{4,6},{6,4},{8,10},{10,8},{12,14},{14,12},{16,18},{18,... | collective-permute-start | bytes 6291464 | tf_op jit(solution)/shard_map/ppermute | solution.py:264
  460.6 119.2 %collective-permute-start.62 = (bf16[4,2,64,2048]{3,2,0,1:T(8,128)(2,1)}, bf16[4,2,64,2048]{3,2,0,1:T(8,128)(2,1)}, u32[]{:S(2)}, u32[]{:S(2)}) collective-permute-start(bf16[4,2,64,2048]{3,2,0,1:T(8,128)(2,1)} %bitcast.246), channel_id=1, source_target_pairs={{0,2},{2,0},{4,6},{6,4},{8,10},{10,8},{12,14},{14,12},{16,18},{18,... | collective-permute-start | bytes 6291464 | tf_op jit(solution)/shard_map/ppermute | solution.py:264
  461.3 8.3 %collective-permute-start.47 = (bf16[4,64,512]{2,1,0:T(8,128)(2,1)S(1)}, bf16[4,64,512]{2,1,0:T(8,128)(2,1)S(1)}, u32[]{:S(2)}, u32[]{:S(2)}) collective-permute-start(bf16[4,64,512]{2,1,0:T(8,128)(2,1)S(1)} %dynamic-slice_bitcast_fusion.11), channel_id=1, source_target_pairs={{0,4},{2,6},{4,0},{6,2},{8,12},{10,14},{12,8},{14,10},{16,20},{18,... | collective-permute-start | bytes 786440 | tf_op jit(solution)/shard_map/ppermute | solution.py:268
  469.6 70.9 %collective-permute-start.45 = (bf16[4,64,512]{2,1,0:T(8,128)(2,1)S(1)}, bf16[4,64,512]{2,1,0:T(8,128)(2,1)S(1)}, u32[]{:S(2)}, u32[]{:S(2)}) collective-permute-start(bf16[4,64,512]{2,1,0:T(8,128)(2,1)S(1)} %dynamic-slice_bitcast_fusion.12), channel_id=1, source_target_pairs={{0,4},{2,6},{4,0},{6,2},{8,12},{10,14},{12,8},{14,10},{16,20},{18,... | collective-permute-start | bytes 786440 | tf_op jit(solution)/shard_map/ppermute | solution.py:268
  470.7 69.8 %collective-permute-start.48 = (bf16[4,64,512]{2,1,0:T(8,128)(2,1)S(1)}, bf16[4,64,512]{2,1,0:T(8,128)(2,1)S(1)}, u32[]{:S(2)}, u32[]{:S(2)}) collective-permute-start(bf16[4,64,512]{2,1,0:T(8,128)(2,1)S(1)} %fusion.63), channel_id=1, source_target_pairs={{0,1},{1,0},{2,3},{3,2},{4,5},{5,4},{6,7},{7,6},{8,9},{9,8},{10,11... | collective-permute-start | bytes 786440 | tf_op jit(solution)/shard_map/ppermute | solution.py:272
  540.7 20.7 %collective-permute-start.51 = (bf16[64,512]{1,0:T(8,128)(2,1)S(1)}, bf16[64,512]{1,0:T(8,128)(2,1)S(1)}, u32[]{:S(2)}, u32[]{:S(2)}) collective-permute-start(bf16[64,512]{1,0:T(8,128)(2,1)S(1)} %get-tuple-element.103), channel_id=1, source_target_pairs={{0,24},{2,26},{4,28},{6,30},{8,0},{10,2},{12,4},{14,6},{16,8},{18,... | collective-permute-start | bytes 196616 | tf_op jit(solution)/shard_map/ppermute | solution.py:347
  549.0 15.2 %collective-permute-start.50 = (bf16[64,512]{1,0:T(8,128)(2,1)S(1)}, bf16[64,512]{1,0:T(8,128)(2,1)S(1)}, u32[]{:S(2)}, u32[]{:S(2)}) collective-permute-start(bf16[64,512]{1,0:T(8,128)(2,1)S(1)} %get-tuple-element.104), channel_id=1, source_target_pairs={{0,16},{2,18},{4,20},{6,22},{8,24},{10,26},{12,28},{14,30},{16,0},... | collective-permute-start | bytes 196616 | tf_op jit(solution)/shard_map/ppermute | solution.py:347
  564.2 19.8 %collective-permute-start.60 = (bf16[4,2,64,2048]{3,2,0,1:T(8,128)(2,1)S(1)}, bf16[4,2,64,2048]{3,2,0,1:T(8,128)(2,1)S(1)}, u32[]{:S(2)}, u32[]{:S(2)}) collective-permute-start(bf16[4,2,64,2048]{3,2,0,1:T(8,128)(2,1)S(1)} %bitcast.281), channel_id=1, source_target_pairs={{0,2},{2,0},{4,6},{6,4},{8,10},{10,8},{12,14},{14,12},{16,18},{18,... | collective-permute-start | bytes 6291464 | tf_op jit(solution)/shard_map/ppermute | solution.py:264
  567.7 46.5 %collective-permute-start.38 = (bf16[1024,1024]{0,1:T(8,128)(2,1)S(1)}, bf16[1024,1024]{0,1:T(8,128)(2,1)}, u32[]{:S(2)}, u32[]{:S(2)}) collective-permute-start(bf16[1024,1024]{0,1:T(8,128)(2,1)S(1)} %fusion.52), channel_id=1, source_target_pairs={{0,1},{1,0},{2,3},{3,2},{4,5},{5,4},{6,7},{7,6},{8,9},{9,8},{10,11... | collective-permute-start | bytes 6291464 | tf_op jit(solution)/shard_map/ppermute | solution.py:272
  569.9 17.6 %collective-permute-start.39 = (bf16[4,2,64,1536]{3,2,0,1:T(8,128)(2,1)S(1)}, bf16[4,2,64,1536]{3,2,0,1:T(8,128)(2,1)S(1)}, u32[]{:S(2)}, u32[]{:S(2)}) collective-permute-start(bf16[4,2,64,1536]{3,2,0,1:T(8,128)(2,1)S(1)} %bitcast.282), channel_id=1, source_target_pairs={{0,2},{2,0},{4,6},{6,4},{8,10},{10,8},{12,14},{14,12},{16,18},{18,... | collective-permute-start | bytes 4718600 | tf_op jit(solution)/shard_map/ppermute | solution.py:264
  573.7 93.0 %collective-permute-start.55 = (bf16[4,64,2048]{2,1,0:T(8,128)(2,1)}, bf16[4,64,2048]{2,1,0:T(8,128)(2,1)}, u32[]{:S(2)}, u32[]{:S(2)}) collective-permute-start(bf16[4,64,2048]{2,1,0:T(8,128)(2,1)} %dynamic-slice_bitcast_fusion.2), channel_id=1, source_target_pairs={{0,4},{2,6},{4,0},{6,2},{8,12},{10,14},{12,8},{14,10},{16,20},{18,... | collective-permute-start | bytes 3145736 | tf_op jit(solution)/shard_map/ppermute | solution.py:268
  579.8 120.9 %collective-permute-start.53 = (bf16[4,64,2048]{2,1,0:T(8,128)(2,1)}, bf16[4,64,2048]{2,1,0:T(8,128)(2,1)}, u32[]{:S(2)}, u32[]{:S(2)}) collective-permute-start(bf16[4,64,2048]{2,1,0:T(8,128)(2,1)} %dynamic-slice_bitcast_fusion.3), channel_id=1, source_target_pairs={{0,4},{2,6},{4,0},{6,2},{8,12},{10,14},{12,8},{14,10},{16,20},{18,... | collective-permute-start | bytes 3145736 | tf_op jit(solution)/shard_map/ppermute | solution.py:268
  584.0 87.4 %collective-permute-start.63 = (bf16[4,64,2048]{2,1,0:T(8,128)(2,1)}, bf16[4,64,2048]{2,1,0:T(8,128)(2,1)}, u32[]{:S(2)}, u32[]{:S(2)}) collective-permute-start(bf16[4,64,2048]{2,1,0:T(8,128)(2,1)} %dynamic-slice_bitcast_fusion), channel_id=1, source_target_pairs={{0,4},{2,6},{4,0},{6,2},{8,12},{10,14},{12,8},{14,10},{16,20},{18,... | collective-permute-start | bytes 3145736 | tf_op jit(solution)/shard_map/ppermute | solution.py:268
  590.2 88.5 %collective-permute-start.40 = (bf16[4,64,1536]{2,1,0:T(8,128)(2,1)}, bf16[4,64,1536]{2,1,0:T(8,128)(2,1)}, u32[]{:S(2)}, u32[]{:S(2)}) collective-permute-start(bf16[4,64,1536]{2,1,0:T(8,128)(2,1)} %dynamic-slice_bitcast_fusion.4), channel_id=1, source_target_pairs={{0,4},{2,6},{4,0},{6,2},{8,12},{10,14},{12,8},{14,10},{16,20},{18,... | collective-permute-start | bytes 2359304 | tf_op jit(solution)/shard_map/ppermute | solution.py:268
  623.0 39.2 %collective-permute-start.69 = (f32[4,1024]{1,0:T(4,128)S(1)}, f32[4,1024]{1,0:T(4,128)S(1)}, u32[]{:S(2)}, u32[]{:S(2)}) collective-permute-start(f32[4,1024]{1,0:T(4,128)S(1)} %fusion.72), channel_id=1, source_target_pairs={{0,4},{2,6},{4,0},{6,2},{8,12},{10,14},{12,8},{14,10},{16,20},{18,... | collective-permute-start | bytes 49160 | tf_op jit(solution)/shard_map/ppermute | solution.py:268
  676.6 25.2 %collective-permute-start.56 = (bf16[4,64,2048]{2,1,0:T(8,128)(2,1)}, bf16[4,64,2048]{2,1,0:T(8,128)(2,1)S(1)}, u32[]{:S(2)}, u32[]{:S(2)}) collective-permute-start(bf16[4,64,2048]{2,1,0:T(8,128)(2,1)} %fusion.47), channel_id=1, source_target_pairs={{0,1},{1,0},{2,3},{3,2},{4,5},{5,4},{6,7},{7,6},{8,9},{9,8},{10,11... | collective-permute-start | bytes 3145736 | tf_op jit(solution)/shard_map/ppermute | solution.py:272
  682.8 16.4 %collective-permute-start.42 = (bf16[64,1536]{1,0:T(8,128)(2,1)S(1)}, bf16[64,1536]{1,0:T(8,128)(2,1)S(1)}, u32[]{:S(2)}, u32[]{:S(2)}) collective-permute-start(bf16[64,1536]{1,0:T(8,128)(2,1)S(1)} %get-tuple-element.93), channel_id=1, source_target_pairs={{0,16},{2,18},{4,20},{6,22},{8,24},{10,26},{12,28},{14,30},{16,0},... | collective-permute-start | bytes 589832 | tf_op jit(solution)/shard_map/ppermute | solution.py:347
  682.9 16.8 %collective-permute-start.41 = (bf16[64,1536]{1,0:T(8,128)(2,1)S(1)}, bf16[64,1536]{1,0:T(8,128)(2,1)S(1)}, u32[]{:S(2)}, u32[]{:S(2)}) collective-permute-start(bf16[64,1536]{1,0:T(8,128)(2,1)S(1)} %get-tuple-element.91), channel_id=1, source_target_pairs={{0,8},{2,10},{4,12},{6,14},{8,16},{10,18},{12,20},{14,22},{16,24},... | collective-permute-start | bytes 589832 | tf_op jit(solution)/shard_map/ppermute | solution.py:347
  688.2 21.0 %collective-permute-start.61 = (bf16[4,64,2048]{2,1,0:T(8,128)(2,1)S(1)}, bf16[4,64,2048]{2,1,0:T(8,128)(2,1)S(1)}, u32[]{:S(2)}, u32[]{:S(2)}) collective-permute-start(bf16[4,64,2048]{2,1,0:T(8,128)(2,1)S(1)} %copy-done.52), channel_id=1, source_target_pairs={{0,4},{2,6},{4,0},{6,2},{8,12},{10,14},{12,8},{14,10},{16,20},{18,... | collective-permute-start | bytes 3145736 | tf_op jit(solution)/shard_map/ppermute | solution.py:268
  699.2 24.3 %collective-permute-start.64 = (bf16[4,64,2048]{2,1,0:T(8,128)(2,1)}, bf16[4,64,2048]{2,1,0:T(8,128)(2,1)S(1)}, u32[]{:S(2)}, u32[]{:S(2)}) collective-permute-start(bf16[4,64,2048]{2,1,0:T(8,128)(2,1)} %fusion.45), channel_id=1, source_target_pairs={{0,1},{1,0},{2,3},{3,2},{4,5},{5,4},{6,7},{7,6},{8,9},{9,8},{10,11... | collective-permute-start | bytes 3145736 | tf_op jit(solution)/shard_map/ppermute | solution.py:272
  703.7 22.9 %collective-permute-start.59 = (bf16[64,2048]{1,0:T(8,128)(2,1)S(1)}, bf16[64,2048]{1,0:T(8,128)(2,1)S(1)}, u32[]{:S(2)}, u32[]{:S(2)}) collective-permute-start(bf16[64,2048]{1,0:T(8,128)(2,1)S(1)} %get-tuple-element.85), channel_id=1, source_target_pairs={{0,24},{2,26},{4,28},{6,30},{8,0},{10,2},{12,4},{14,6},{16,8},{18,... | collective-permute-start | bytes 786440 | tf_op jit(solution)/shard_map/ppermute | solution.py:347
  707.2 22.1 %collective-permute-start.58 = (bf16[64,2048]{1,0:T(8,128)(2,1)S(1)}, bf16[64,2048]{1,0:T(8,128)(2,1)S(1)}, u32[]{:S(2)}, u32[]{:S(2)}) collective-permute-start(bf16[64,2048]{1,0:T(8,128)(2,1)S(1)} %get-tuple-element.86), channel_id=1, source_target_pairs={{0,16},{2,18},{4,20},{6,22},{8,24},{10,26},{12,28},{14,30},{16,0},... | collective-permute-start | bytes 786440 | tf_op jit(solution)/shard_map/ppermute | solution.py:347
  707.3 22.0 %collective-permute-start.57 = (bf16[64,2048]{1,0:T(8,128)(2,1)S(1)}, bf16[64,2048]{1,0:T(8,128)(2,1)S(1)}, u32[]{:S(2)}, u32[]{:S(2)}) collective-permute-start(bf16[64,2048]{1,0:T(8,128)(2,1)S(1)} %get-tuple-element.84), channel_id=1, source_target_pairs={{0,8},{2,10},{4,12},{6,14},{8,16},{10,18},{12,20},{14,22},{16,24},... | collective-permute-start | bytes 786440 | tf_op jit(solution)/shard_map/ppermute | solution.py:347
  724.2 9.2 %collective-permute-start.67 = (bf16[64,2048]{1,0:T(8,128)(2,1)S(1)}, bf16[64,2048]{1,0:T(8,128)(2,1)S(1)}, u32[]{:S(2)}, u32[]{:S(2)}) collective-permute-start(bf16[64,2048]{1,0:T(8,128)(2,1)S(1)} %get-tuple-element.82), channel_id=1, source_target_pairs={{0,24},{2,26},{4,28},{6,30},{8,0},{10,2},{12,4},{14,6},{16,8},{18,... | collective-permute-start | bytes 786440 | tf_op jit(solution)/shard_map/ppermute | solution.py:347
  726.6 22.4 %collective-permute-start.66 = (bf16[64,2048]{1,0:T(8,128)(2,1)S(1)}, bf16[64,2048]{1,0:T(8,128)(2,1)S(1)}, u32[]{:S(2)}, u32[]{:S(2)}) collective-permute-start(bf16[64,2048]{1,0:T(8,128)(2,1)S(1)} %get-tuple-element.83), channel_id=1, source_target_pairs={{0,16},{2,18},{4,20},{6,22},{8,24},{10,26},{12,28},{14,30},{16,0},... | collective-permute-start | bytes 786440 | tf_op jit(solution)/shard_map/ppermute | solution.py:347
  726.6 22.4 %collective-permute-start.65 = (bf16[64,2048]{1,0:T(8,128)(2,1)S(1)}, bf16[64,2048]{1,0:T(8,128)(2,1)S(1)}, u32[]{:S(2)}, u32[]{:S(2)}) collective-permute-start(bf16[64,2048]{1,0:T(8,128)(2,1)S(1)} %get-tuple-element.81), channel_id=1, source_target_pairs={{0,8},{2,10},{4,12},{6,14},{8,16},{10,18},{12,20},{14,22},{16,24},... | collective-permute-start | bytes 786440 | tf_op jit(solution)/shard_map/ppermute | solution.py:347
  (94 other events, 1700.2 us)

commit v2 on v1

v2 whole, which is shorter than its diff:
```python
import functools
import math

import jax
import jax.numpy as jnp
from jax import lax
from jax.experimental import pallas as pl
from jax.experimental.pallas import tpu as pltpu
from jax.sharding import PartitionSpec as P

HD = 64
QB = 256
KB = 256
MAX_SEGMENT = 1024
max_chunks = MAX_SEGMENT // KB + 1
SCORE_SCALE = 0.125 * math.log2(math.e)
NEG = -1e30
EPS = 1e-05
BF16 = jnp.bfloat16
F32 = jnp.float32
NT = (((1,), (1,)), ((), ()))
NN = (((1,), (0,)), ((), ()))
TN = (((0,), (0,)), ((), ()))

def dot(a, b, dims):
    return lax.dot_general(a, b, dims, preferred_element_type=jnp.float32)


def split_pair(block):
    lane = lax.broadcasted_iota(jnp.int32, block.shape, 1)
    zero = jnp.zeros_like(block)
    return (jnp.where(lane < HD, block, zero), jnp.where(lane >= HD, block, zero))


def fwd_kernel(pairs, lo_ref, off_ref, q_ref, k_ref, v_ref, start_ref, o_ref, l_ref, vt_ref):
    step = pl.program_id(2)
    block = off_ref[0] + step

    @pl.when(step == 0)
    def _():
        vt_ref[...] = v_ref[...].T

    pair_step = math.gcd(pairs, 4)
    row_start = start_ref[...]
    query_pos = block * QB + lax.broadcasted_iota(jnp.int32, (1, QB), 1)
    first = lo_ref[pl.program_id(0), block]
    count = block + 1 - first
    base = pl.multiple_of(first * KB, KB)

    for chunks in range(1, max_chunks + 1):

        @pl.when(count == chunks)
        def _(size=chunks * KB):
            window = pl.ds(base, size)
            key_pos = lax.broadcasted_iota(jnp.int32, (size, QB), 0) + base
            ok = (key_pos >= row_start) & (key_pos <= query_pos)
            for pair in range(pairs):
                cols = slice(pair * 128, (pair + 1) * 128)
                q_heads = split_pair(q_ref[:, cols])
                keys = k_ref[window, cols]
                outs = []
                for h in range(2):
                    s = jnp.where(ok, dot(keys, q_heads[h], NT) * SCORE_SCALE, NEG)
                    peak = jnp.max(s, axis=0, keepdims=True)
                    p = jnp.exp2(s - peak)
                    total = jnp.sum(p, axis=0, keepdims=True)
                    vt = vt_ref[pair * 128 + h * HD : pair * 128 + (h + 1) * HD, window]
                    outs.append(dot(vt, p.astype(BF16), NN) / total)
                    l_ref[2 * pair + h : 2 * pair + h + 1, :] = peak + jnp.log2(total)
                o_ref[:, cols] = jnp.concatenate(outs, axis=0).T.astype(BF16)


def attention_forward(calls, qkv, starts, lo, offset, blocks):
    seqs, length = starts.shape
    width = qkv.shape[1] // 3
    part = width // calls
    heads = part // HD
    nq = length // QB
    grid_spec = pltpu.PrefetchScalarGridSpec(
        num_scalar_prefetch=2,
        grid=(seqs, calls, blocks),
        in_specs=[
            pl.BlockSpec((QB, part), lambda s, c, b, lo, off: (s * nq + off[0] + b, 3 * c)),
            pl.BlockSpec((length, part), lambda s, c, b, lo, off: (s, 3 * c + 1)),
            pl.BlockSpec((length, part), lambda s, c, b, lo, off: (s, 3 * c + 2)),
            pl.BlockSpec((None, 1, QB), lambda s, c, b, lo, off: (s, 0, off[0] + b)),
        ],
        out_specs=[
            pl.BlockSpec((QB, part), lambda s, c, b, lo, off: (s * blocks + b, c)),
            pl.BlockSpec((None, None, heads, QB), lambda s, c, b, lo, off: (s, c, 0, b)),
        ],
        scratch_shapes=[pltpu.VMEM((part, length), BF16)],
    )
    rows = seqs * blocks * QB
    return pl.pallas_call(
        functools.partial(fwd_kernel, part // 128),
        grid_spec=grid_spec,
        out_shape=(
            jax.ShapeDtypeStruct((rows, width), BF16),
            jax.ShapeDtypeStruct((seqs, calls, heads, blocks * QB), F32),
        ),
        compiler_params=pltpu.CompilerParams(
            dimension_semantics=("arbitrary",) * 3, vmem_limit_bytes=48 << 20
        ),
        cost_estimate=pl.CostEstimate(
            flops=4 * rows * 640 * width,
            bytes_accessed=8 * rows * width,
            transcendentals=rows * width * 10,
        ),
        name="attention_forward",
    )(lo, offset, qkv, qkv, qkv, starts[:, None, :])


def bwd_kernel(pairs, halves, lo_ref, place_ref, q_ref, k_ref, v_ref, start_ref, *refs):
    o_refs, do_refs, l_refs = refs[:halves], refs[halves : 2 * halves], refs[2 * halves : 3 * halves]
    out_ref, kt_ref, dk_ref, dv_ref = refs[-4:]
    block = pl.program_id(1)
    blocks = pl.num_programs(1)
    width = pairs * 128

    @pl.when(block == 0)
    def _():
        kt_ref[...] = k_ref[...].T
        dk_ref[...] = jnp.zeros_like(dk_ref)
        dv_ref[...] = jnp.zeros_like(dv_ref)

    mine = block // (blocks // halves) == place_ref[0]

    def pick(two, index):
        if halves == 1:
            return two[0][index]
        return jnp.where(mine, two[0][index], two[1][index])

    row_start = start_ref[...]
    query_pos = block * QB + lax.broadcasted_iota(jnp.int32, (1, QB), 1)
    key_iota = lax.broadcasted_iota(jnp.int32, (KB, QB), 0)
    first = lo_ref[pl.program_id(0), block]
    last = (block + 1) * (QB // KB)
    rows = pl.ds(pl.multiple_of(block * QB, QB), QB)
    every = slice(None)
    for pair in range(pairs):
        cols = slice(pair * 128, (pair + 1) * 128)
        q_heads = split_pair(q_ref[:, cols])
        g_pair = pick(do_refs, (every, cols))
        g_heads = split_pair(g_pair)
        prod = (g_pair.astype(F32) * pick(o_refs, (every, cols)).astype(F32)).T
        deltas = [jnp.sum(prod[h * HD : (h + 1) * HD], axis=0, keepdims=True) for h in range(2)]
        lses = [pick(l_refs, (slice(2 * pair + h, 2 * pair + h + 1), every)) for h in range(2)]

        def chunk(j, carry):
            base = pl.multiple_of(j * KB, KB)
            window = pl.ds(base, KB)
            keys = k_ref[window, cols]
            vals = v_ref[window, cols]
            key_pos = key_iota + base
            ok = (key_pos >= row_start) & (key_pos <= query_pos)
            new = []
            dv = dv_ref[window, cols]
            dk = dk_ref[window, cols]
            for h in range(2):
                s = jnp.where(ok, dot(keys, q_heads[h], NT) * SCORE_SCALE, NEG)
                p = jnp.exp2(s - lses[h])
                dp = dot(vals, g_heads[h], NT)
                ds = (p * (dp - deltas[h])).astype(BF16)
                dv = dv + dot(p.astype(BF16), g_heads[h], NN)
                dk = dk + dot(ds, q_heads[h], NN)
                kt = kt_ref[pair * 128 + h * HD : pair * 128 + (h + 1) * HD, window]
                new.append(carry[h] + dot(kt, ds, NN))
            dv_ref[window, cols] = dv
            dk_ref[window, cols] = dk
            return tuple(new)

        dq = lax.fori_loop(first, last, chunk, tuple(jnp.zeros((HD, QB), F32) for _ in range(2)))
        out_ref[rows, cols] = (jnp.concatenate(dq, axis=0) * 0.125).T.astype(BF16)

    @pl.when(block == blocks - 1)
    def _():
        out_ref[:, width : 2 * width] = (dk_ref[...] * 0.125).astype(BF16)
        out_ref[:, 2 * width :] = dv_ref[...].astype(BF16)


def attention_backward(calls, call, qkv, o_rows, d_o_rows, lse_rows, starts, lo, place, before):
    seqs, length = starts.shape
    width = qkv.shape[1] // 3 // calls
    heads, pairs = width // HD, width // 128
    nq = length // QB
    halves = len(o_rows)
    half = nq // halves

    def rows_of(g):
        if halves == 1:
            return lambda s, b, lo, place: (s * nq + b, call)
        at = lambda b, place: jnp.clip(b - jnp.bitwise_xor(place[0], g) * half, 0, half - 1)
        return lambda s, b, lo, place: (at(b, place), call)

    def lse_of(g):
        index = rows_of(g)
        if halves == 1:
            return lambda s, b, lo, place: (s, call, 0, b)
        return lambda s, b, lo, place: (s, call, 0, index(s, b, lo, place)[0])

    in_specs = [
        pl.BlockSpec((QB, width), lambda s, b, lo, place: (s * nq + b, 3 * call)),
        pl.BlockSpec((length, width), lambda s, b, lo, place: (s, 3 * call + 1)),
        pl.BlockSpec((length, width), lambda s, b, lo, place: (s, 3 * call + 2)),
        pl.BlockSpec((None, 1, QB), lambda s, b, lo, place: (s, 0, b)),
        *[pl.BlockSpec((QB, width), rows_of(g)) for g in range(halves)],
        *[pl.BlockSpec((QB, width), rows_of(g)) for g in range(halves)],
        *[pl.BlockSpec((None, None, heads, QB), lse_of(g)) for g in range(halves)],
    ]
    operands = [qkv, qkv, qkv, starts[:, None, :], *o_rows, *d_o_rows, *lse_rows]
    alias = {}
    if before is not None:
        alias = {2 + len(operands): 0}
        in_specs.append(pl.BlockSpec(memory_space=pl.ANY))
        operands.append(before)
    rows = seqs * length
    return pl.pallas_call(
        functools.partial(bwd_kernel, pairs, halves),
        grid_spec=pltpu.PrefetchScalarGridSpec(
            num_scalar_prefetch=2,
            grid=(seqs, nq),
            in_specs=in_specs,
            out_specs=pl.BlockSpec((length, 3 * width), lambda s, b, lo, place: (s, call)),
            scratch_shapes=[
                pltpu.VMEM((width, length), BF16),
                pltpu.VMEM((length, width), F32),
                pltpu.VMEM((length, width), F32),
            ],
        ),
        out_shape=jax.ShapeDtypeStruct((rows, qkv.shape[1]), BF16),
        input_output_aliases=alias,
        compiler_params=pltpu.CompilerParams(
            dimension_semantics=("arbitrary", "arbitrary"), vmem_limit_bytes=48 << 20
        ),
        cost_estimate=pl.CostEstimate(
            flops=10 * rows * 640 * width,
            bytes_accessed=16 * rows * width,
            transcendentals=rows * width * 10,
        ),
        name="attention_backward",
    )(lo, place, *operands)


def segment_bounds(segment_ids):
    starts = jnp.sum((segment_ids[:, None, :] < segment_ids[:, :, None]).astype(jnp.int32), axis=2)
    return starts, starts[:, ::QB] // KB


def stats(values):
    mean = jnp.mean(values, axis=-1, keepdims=True)
    centered = values - mean
    scale = lax.rsqrt(jnp.mean(centered * centered, axis=-1, keepdims=True) + EPS)
    return centered * scale, scale


def norm_back(normed, scale, gain_row, grad_rows):
    inner = grad_rows * gain_row
    return scale * (
        inner
        - jnp.mean(inner, axis=-1, keepdims=True)
        - normed * jnp.mean(inner * normed, axis=-1, keepdims=True)
    )


def gelu_pair(z):
    c = math.sqrt(2.0 / math.pi)
    t = jnp.tanh(c * (z + 0.044715 * z * z * z))
    value = 0.5 * z * (1.0 + t)
    slope = 0.5 * (1.0 + t) + 0.5 * z * (1.0 - t * t) * (c * (1.0 + 3 * 0.044715 * z * z))
    return value, slope


NZ, NX, NC = 4, 2, 2


def core_pairs():
    return [(i, i ^ 1) for i in range(NZ * NX * NC)]


def x_pairs():
    return [(i, i ^ 2) for i in range(NZ * NX * NC)]


def z_pairs(shift):
    return [(i, (i + shift * NX * NC) % (NZ * NX * NC)) for i in range(NZ * NX * NC)]


Y_PAIRS = [(0, 1), (1, 0)]


def swap_core(a):
    return lax.ppermute(a, "dp", core_pairs())


def swap_x(a):
    return lax.ppermute(a, "dp", x_pairs())


def swap_y(a):
    return lax.ppermute(a, "tensor", Y_PAIRS)


def assemble_kernel(pos_ref, *refs):
    out_ref = refs[-1]
    z, x, c = pos_ref[0], pos_ref[1], pos_ref[2]
    for n, ref in enumerate(refs[:-1]):
        dx, dc = n % 2, n // 2
        for k in range(NZ):
            out_ref[lax.rem(z - k + NZ, NZ), lax.bitwise_xor(x, dx), lax.bitwise_xor(c, dc)] = ref[k]


def assemble_part(position, pieces, first, width, before, at, total):
    rows = pieces[0].shape[1]
    block = math.gcd(width, 512)
    skip, base = first // block, at * width // block
    piece = pl.BlockSpec((NZ, rows, block), lambda j, pos: (0, 0, skip + j))
    out = pl.BlockSpec((NZ, NX, NC, rows, block), lambda j, pos: (0, 0, 0, 0, base + j))
    shape = (NZ, NX, NC, rows, total)
    body, ins, extra, alias = assemble_kernel, [piece] * 4, [], {}
    if before is not None:
        body = lambda pos, *refs: assemble_kernel(pos, *refs[:4], refs[5])
        ins, extra, alias = ins + [pl.BlockSpec(memory_space=pl.ANY)], [before], {5: 0}
    return pl.pallas_call(
        body,
        grid_spec=pltpu.PrefetchScalarGridSpec(
            num_scalar_prefetch=1, grid=(width // block,), in_specs=ins, out_specs=out
        ),
        out_shape=jax.ShapeDtypeStruct(shape, BF16),
        input_output_aliases=alias,
        compiler_params=pltpu.CompilerParams(
            dimension_semantics=("arbitrary",), vmem_limit_bytes=32 << 20
        ),
        cost_estimate=pl.CostEstimate(
            flops=0, bytes_accessed=2 * 16 * rows * width * 2, transcendentals=0
        ),
        name="assemble",
    )(position, *pieces, *extra)


def assemble(position, groups, first, width):
    total = width * len(groups)
    out = None
    for at, pieces in enumerate(groups):
        out = assemble_part(position, pieces, first, width, out, at, total)
    return out.reshape(-1, total)


def gather_z(shard):
    return jnp.stack([shard] + [lax.ppermute(shard, "dp", z_pairs(k)) for k in range(1, NZ)])


def with_core(pieces):
    return pieces + [swap_core(a) for a in pieces]


def half_rows(h, index, axis):
    return lax.dynamic_index_in_dim(h, index, axis, keepdims=False)


def add(a, b):
    return (a.astype(F32) + b.astype(F32)).astype(BF16)


def reduce_core_x(x, c, grad):
    parts = grad.reshape(NZ, NX, NC, grad.shape[0] // (NZ * NX * NC), grad.shape[1])
    h = add(half_rows(parts, c, 2), swap_core(half_rows(parts, 1 - c, 2)))
    return add(half_rows(h, x, 1), swap_x(half_rows(h, 1 - x, 1)))


def reduce_z(z, total):
    out = half_rows(total, z, 0).astype(F32)
    for k in range(1, NZ):
        piece = half_rows(total, lax.rem(z + k, NZ), 0)
        out = out + lax.ppermute(piece, "dp", z_pairs(k)).astype(F32)
    return out


def sum_everywhere(vector):
    vector = vector + swap_core(vector)
    vector = vector + swap_x(vector)
    vector = vector + swap_y(vector)
    size = NZ * NX * NC
    near = [(i, i ^ 4) for i in range(size)]
    far = [(i, i ^ 8) for i in range(size)]
    vector = vector + lax.ppermute(vector, "dp", near)
    return vector + lax.ppermute(vector, "dp", far)


class Staged:
    def __init__(self):
        index = lax.axis_index("dp")
        self.z, self.x, self.c = index // 4, (index // 2) % 2, index % 2
        self.position = jnp.stack([self.z, self.x, self.c]).astype(jnp.int32)

    def gather(self, shard_qkv, shard_out, shard_up, shard_down):
        column = gather_z(shard_qkv)
        pieces = with_core([column, swap_x(column)])
        qkv = assemble(self.position, [pieces], 0, shard_qkv.shape[1])
        down = lax.all_gather(
            jnp.concatenate([shard_down, swap_y(shard_down)], axis=1), "dp", axis=0, tiled=True
        )
        own = gather_z(jnp.concatenate([shard_out, shard_up], axis=1))
        other = swap_y(own)
        groups = [with_core([a, swap_x(a)]) for a in (own, other)]
        width = shard_out.shape[1]
        out = assemble(self.position, groups, 0, width)
        up = assemble(self.position, groups, width, shard_up.shape[1])
        return qkv, out, up, down

    def reduce_qkv(self, grad):
        return reduce_z(self.z, reduce_core_x(self.x, self.c, grad))

    def reduce_down(self, grad):
        total = lax.psum_scatter(grad, "dp", scatter_dimension=0, tiled=True)
        half = grad.shape[1] // 2
        return total[:, :half].astype(F32) + swap_y(total[:, half:]).astype(F32)

    def reduce_out_up(self, grad_out, grad_up):
        wide_out = reduce_core_x(self.x, self.c, grad_out)
        wide_up = reduce_core_x(self.x, self.c, grad_up)
        half_out, half_up = grad_out.shape[1] // 2, grad_up.shape[1] // 2
        own = jnp.concatenate([wide_out[..., :half_out], wide_up[..., :half_up]], axis=2)
        other = jnp.concatenate([wide_out[..., half_out:], wide_up[..., half_up:]], axis=2)
        total = reduce_z(self.z, add(own, swap_y(other)))
        return total[:, :half_out], total[:, half_out:]

    def exchange(self, parts):
        return [parts[0], swap_y(parts[1])]

    def total(self, vector):
        return sum_everywhere(vector)


class Plain:
    def __init__(self):
        self.n = lax.axis_size("tensor")
        self.rank = lax.axis_index("tensor")

    def gather_groups(self, shard):
        own = lax.all_gather(shard, "dp", axis=0, tiled=True)
        every = lax.all_gather(own, "tensor", axis=0)
        groups = [
            lax.dynamic_index_in_dim(every, (self.rank + g) % self.n, 0, keepdims=False)
            for g in range(self.n)
        ]
        return jnp.concatenate(groups, axis=1)

    def gather(self, shard_qkv, shard_out, shard_up, shard_down):
        qkv = lax.all_gather(shard_qkv, "dp", axis=0, tiled=True)
        return (qkv, *(self.gather_groups(w) for w in (shard_out, shard_up, shard_down)))

    def reduce_qkv(self, grad):
        return lax.psum_scatter(grad, "dp", scatter_dimension=0, tiled=True).astype(F32)

    def reduce_down(self, grad):
        return self.reduce_groups(jnp.split(grad, self.n, axis=1))

    def reduce_out_up(self, grad_out, grad_up):
        return self.reduce_down(grad_out), self.reduce_down(grad_up)

    def absolute(self, parts):
        stacked = jnp.stack(parts)
        order = (jnp.arange(self.n) - self.rank) % self.n
        return jnp.take(stacked, order, axis=0)

    def reduce_groups(self, grads):
        own = lax.psum_scatter(self.absolute(grads), "tensor", scatter_dimension=0, tiled=True)
        return lax.psum_scatter(own[0], "dp", scatter_dimension=0, tiled=True).astype(F32)

    def exchange(self, parts):
        got = lax.all_to_all(self.absolute(parts), "tensor", 0, 0, tiled=True)
        return [
            lax.dynamic_index_in_dim(got, (self.rank + g) % self.n, 0, keepdims=False)
            for g in range(self.n)
        ]

    def total(self, vector):
        return lax.psum(vector, ("dp", "tensor"))


def per_device(
    staged,
    inputs,
    cotangent,
    segment_ids,
    w_qkv,
    w_out,
    w_fc1,
    w_fc2,
    norm_gain,
    norm_bias,
    head_bias,
    out_bias,
    fc1_bias,
):
    n = lax.axis_size("tensor")
    rank = lax.axis_index("tensor")
    comm = Staged() if staged else Plain()
    tokens, features = inputs.shape
    seqs, length = segment_ids.shape
    own_rows = tokens // n
    width = w_qkv.shape[2]
    hidden = w_fc1.shape[1]

    def group_slice(array, g, size, axis=0):
        return lax.dynamic_slice_in_dim(array, ((rank + g) % n) * size, size, axis)

    calls = 2 if width % 256 == 0 else 1
    call_width = width // calls

    def by_call(query, key, value, axis):
        parts = [jnp.split(a, calls, axis=axis) for a in (query, key, value)]
        return jnp.concatenate([p[i] for i in range(calls) for p in parts], axis=axis)

    weight_qkv, weight_out, weight_up, weight_down = comm.gather(
        by_call(w_qkv[0], w_qkv[1], w_qkv[2], 1).astype(BF16),
        w_out.T.astype(BF16),
        w_fc1.astype(BF16),
        w_fc2.T.astype(BF16),
    )

    wide = inputs.astype(F32)
    normed0, scale0 = stats(wide)
    u1 = (normed0 * norm_gain[0] + norm_bias[0]).astype(BF16)
    heads_bias = group_slice(head_bias, 0, width, 1)
    qkv_bias = by_call(heads_bias[0], jnp.zeros((width,), F32), heads_bias[1], 0)
    qkv = (dot(u1, weight_qkv, NN) + qkv_bias).astype(BF16)

    starts, lo = segment_bounds(segment_ids)
    blocks = length // QB
    halves = 2 if n == 2 and seqs == 1 else 1
    half = blocks // halves
    places = [(rank + g) % halves for g in range(halves)]
    at = [jnp.reshape(place * half, (1,)).astype(jnp.int32) for place in places]
    attended = [None] * halves
    for g in reversed(range(halves)):
        attended[g] = attention_forward(calls, qkv, starts, lo, at[g], half)
    o_rows, lse_rows = [a[0] for a in attended], [a[1] for a in attended]
    o_parts = o_rows if halves == n else [group_slice(o_rows[0], g, own_rows) for g in range(n)]
    o_own = jnp.concatenate(comm.exchange(o_parts), axis=1)

    attn = dot(o_own, weight_out, NT) + out_bias[0]
    mine = group_slice(inputs, 0, own_rows).astype(F32)
    normed1, scale1 = stats(attn)
    resid = mine + normed1 * norm_gain[1] + norm_bias[1]
    normed2, scale2 = stats(resid)
    u2 = (normed2 * norm_gain[2] + norm_bias[2]).astype(BF16)

    hidden_bias = jnp.concatenate([group_slice(fc1_bias, g, hidden) for g in range(n)])
    pre = dot(u2, weight_up, NN) + hidden_bias
    act, slope = gelu_pair(pre)
    act, slope = act.astype(BF16), slope.astype(BF16)
    mlp = dot(act, weight_down, NT) + out_bias[1]
    normed3, scale3 = stats(mlp)
    output = (resid + normed3 * norm_gain[3] + norm_bias[3]).astype(BF16)

    dy = group_slice(cotangent, 0, own_rows).astype(F32)
    d_mlp = norm_back(normed3, scale3, norm_gain[3], dy).astype(BF16)
    gain3, shift3 = jnp.sum(normed3 * dy, axis=0), jnp.sum(dy, axis=0)
    bias_mlp = jnp.sum(d_mlp.astype(F32), axis=0)

    grad_down = comm.reduce_down(dot(d_mlp, act, TN).astype(BF16))
    d_pre = (slope.astype(F32) * dot(d_mlp, weight_down, NN)).astype(BF16)
    d_u2 = dot(d_pre, weight_up, NT)
    bias_hidden = jnp.sum(d_pre.astype(F32), axis=0)

    gain2, shift2 = jnp.sum(normed2 * d_u2, axis=0), jnp.sum(d_u2, axis=0)
    d_resid = dy + norm_back(normed2, scale2, norm_gain[2], d_u2)
    gain1, shift1 = jnp.sum(normed1 * d_resid, axis=0), jnp.sum(d_resid, axis=0)
    d_attn = norm_back(normed1, scale1, norm_gain[1], d_resid).astype(BF16)
    bias_attn = jnp.sum(d_attn.astype(F32), axis=0)

    if halves == n:
        weight_parts = jnp.split(weight_out, n, axis=1)
        d_o_parts = [dot(d_attn, w, NN).astype(BF16) for w in weight_parts]
        d_o_rows = comm.exchange(d_o_parts)
    else:
        d_o_all = dot(d_attn, weight_out, NN).astype(BF16)
        d_o_groups = comm.exchange(jnp.split(d_o_all, n, axis=1))
        order = (jnp.arange(n) - rank) % n
        d_o_rows = [jnp.take(jnp.stack(d_o_groups), order, axis=0).reshape(tokens, width)]

    grad_up_part = dot(u2, d_pre, TN).astype(BF16)
    grad_out_part = dot(d_attn, o_own, TN).astype(BF16)
    grad_out, grad_up = comm.reduce_out_up(grad_out_part, grad_up_part)

    d_qkv = None
    place = jnp.reshape(places[0], (1,)).astype(jnp.int32)
    for call in range(calls):
        d_qkv = attention_backward(
            calls, call, qkv, o_rows, d_o_rows, lse_rows, starts, lo, place, d_qkv
        )

    d_u1_parts = [None] * n
    for g in reversed(range(n)):
        d_u1_parts[g] = dot(group_slice(d_qkv, g, own_rows), weight_qkv, NT).astype(BF16)
    d_u1 = sum(t.astype(F32) for t in comm.exchange(d_u1_parts))
    grad_qkv = comm.reduce_qkv(dot(u1, d_qkv, TN).astype(BF16))
    gain0 = shift0 = 0.0
    for g in range(n):
        part = d_u1_parts[g].astype(F32)
        gain0 = gain0 + jnp.sum(group_slice(normed0, g, own_rows) * part, axis=0)
        shift0 = shift0 + jnp.sum(part, axis=0)
    sums = jnp.split(jnp.sum(d_qkv.astype(F32), axis=0), 3 * calls)
    head_terms = jnp.stack([jnp.concatenate(sums[0::3]), jnp.concatenate(sums[2::3])])

    own_normed0 = group_slice(normed0, 0, own_rows)
    own_scale0 = group_slice(scale0, 0, own_rows)
    d_inputs = (d_resid + norm_back(own_normed0, own_scale0, norm_gain[0], d_u1)).astype(BF16)

    hidden_full = jnp.roll(bias_hidden, rank * hidden)
    head_full = lax.dynamic_update_slice_in_dim(
        jnp.zeros(head_bias.shape, F32), head_terms, rank * width, 1
    )
    sums = [gain0, gain1, gain2, gain3, shift0, shift1, shift2, shift3, bias_attn, bias_mlp]
    small = comm.total(
        jnp.concatenate([jnp.stack(sums), head_full, hidden_full.reshape(-1, features)])
    )
    sums = jnp.split(grad_qkv, 3 * calls, axis=1)
    grad_qkv = jnp.stack([jnp.concatenate(sums[i::3], axis=1) for i in range(3)])
    return (
        output,
        d_inputs,
        grad_qkv,
        grad_out.T,
        grad_up,
        grad_down.T,
        small[0:4],
        small[4:8],
        small[10:12],
        small[8:10],
        small[12:].reshape(-1),
    )


def solution(mesh):
    staged = mesh.shape["dp"] == NZ * NX * NC and mesh.shape["tensor"] == 2
    return jax.shard_map(
        functools.partial(per_device, staged),
        mesh=mesh,
        in_specs=(
            P("dp", None),
            P("dp", None),
            P("dp", None),
            P(None, "dp", "tensor"),
            P("tensor", "dp"),
            P("dp", "tensor"),
            P("tensor", "dp"),
            P(),
            P(),
            P(),
            P(),
            P(),
        ),
        out_specs=(
            P(("dp", "tensor"), None),
            P(("dp", "tensor"), None),
            P(None, "dp", "tensor"),
            P("tensor", "dp"),
            P("dp", "tensor"),
            P("tensor", "dp"),
            P(),
            P(),
            P(),
            P(),
            P(),
        ),
        check_vma=False,
    )
```

time: 758 us -> 699 us (0.922)
  starting transfers between devices: 116 us -> 61.2 us
  waiting for transfers between devices: 219 us -> 205 us
  between operations: 2.48 us -> 15.7 us
    ppermute x12 -> x8, waiting for transfers between devices: 92.3 us -> 61.4 us  [swap_y(): return lax.ppermute(a, 'tensor', Y_PAIRS)]
    ppermute x15 -> x7, waiting for transfers between devices: 60.4 us -> 89.4 us  [swap_x(): return lax.ppermute(a, 'dp', x_pairs())]
    ppermute x23 -> x10, starting transfers between devices: 27.7 us -> 1.35 us  [swap_core(): return lax.ppermute(a, 'dp', core_pairs())]
    ppermute x12 -> x6, starting transfers between devices: 26.8 us -> 9.42 us  [reduce_z(): out = out + lax.ppermute(piece, 'dp', z_pairs(k)).astype(F32)]
    ppermute x12 -> x6, waiting for transfers between devices: 38.5 us -> 21.7 us  [reduce_z(): out = out + lax.ppermute(piece, 'dp', z_pairs(k)).astype(F32)]
    ppermute x2 -> x1, starting transfers between devices: 2 us -> 17.2 us  [sum_everywhere(): vector = vector + lax.ppermute(vector, 'dp', near)]
    ppermute x12 -> x6, starting transfers between devices: 22.8 us -> 10.5 us  [gather_z(): lax.ppermute(shard, 'dp', z_pairs(k))]
    ppermute x15 -> x7, starting transfers between devices: 17.3 us -> 6.18 us  [swap_x(): return lax.ppermute(a, 'dp', x_pairs())]
  transfers between devices with their start and end apart: 78 -> 41, of which waited for: 28 -> 16; matrix products, arithmetic and copies ran while one was open for 22% -> 21% of each run, Pallas kernels for 16% -> 19%
where the time goes in v2:
time: 699 us; the launch traced here: 686 us
  waiting for transfers between devices  205 us (29%)
  matrix products  146 us (21%)
  Pallas kernels  129 us (18%)
  other arithmetic  68.9 us (10%)
  starting transfers between devices  61.2 us (9%)
  local copies, waits for them, and re-layouts  59.8 us (9%)
  between operations  15.7 us (2%)
    dot_general x14, matrix products, dot(): return lax.dot_general(a, b, dims, preferred_element_type=jnp.float32)  146 us
    ppermute x7, waiting for transfers between devices, swap_x(): return lax.ppermute(a, 'dp', x_pairs())  89.4 us
    pallas_call x2, Pallas kernels, attention_backward(): pl.pallas_call(functools.partial(bwd_kernel, pairs, halves), grid_spec=pl...  72.2 us
    ppermute x8, waiting for transfers between devices, swap_y(): return lax.ppermute(a, 'tensor', Y_PAIRS)  61.4 us
    pallas_call x2, Pallas kernels, attention_forward(): pl.pallas_call(functools.partial(fwd_kernel, part // 128), grid_spec=grid...  44.3 us
    ppermute x6, waiting for transfers between devices, gather_z(): lax.ppermute(shard, 'dp', z_pairs(k))  32.4 us
    unnamed x124, local copies, waits for them, and re-layouts  26.8 us
    ppermute x6, waiting for transfers between devices, reduce_z(): out = out + lax.ppermute(piece, 'dp', z_pairs(k)).astype(F32)  21.7 us
  transfers between devices with their start and end apart: 41, of which 16 were waited for; matrix products, arithmetic and copies ran while one was open for 21% of the time, Pallas kernels for 19%

profile of v2, /device:TPU:0, one launch (start us, length us, event | category | flops | bytes accessed | tf_op | source)
XLA Modules:
  0.0 685.9 jit_solution(13799561090484639062)
XLA Ops:
  9.3 3.1 collective-permute-start.7
  12.3 2.6 collective-permute-start.8
  18.7 4.9 collective-permute-done.17
  28.4 6.6 copy.41
  37.0 3.2 constant_dynamic-slice_fusion.7
  43.2 19.1 %collective-permute-done.1 = bf16[64,1536]{1,0:T(8,128)(2,1)S(1)} collective-permute-done((bf16[64,1536]{1,0:T(8,128)(2,1)S(1)}, bf16[64,1536]{1,0:T(8,128)(2,1)S(1)}, u32[]{:S(2)}, u32[]{:S(2)}) %collective-permute-start.1) | collective-permute-done | bytes 196640 | tf_op jit(solution)/shard_map/ppermute | solution.py:350
  64.0 13.4 %collective-permute-done.9 = bf16[64,2560]{1,0:T(8,128)(2,1)S(1)} collective-permute-done((bf16[64,2560]{1,0:T(8,128)(2,1)S(1)}, bf16[64,2560]{1,0:T(8,128)(2,1)S(1)}, u32[]{:S(2)}, u32[]{:S(2)}) %collective-permute-start.9) | collective-permute-done | bytes 327712 | tf_op jit(solution)/shard_map/ppermute | solution.py:350
  80.7 3.8 collective-permute-done.3.refs_1_
  85.3 19.2 %collective-permute-done.10.refs_0_ = bf16[4,64,2560]{2,1,0:T(8,128)(2,1)} collective-permute-done((bf16[4,64,2560]{2,1,0:T(8,128)(2,1)S(1)}, bf16[4,64,2560]{2,1,0:T(8,128)(2,1)}, u32[]{:S(2)}, u32[]{:S(2)}) %collective-permute-start.10) | collective-permute-done | bytes 1310752 | tf_op jit(solution)/shard_map/ppermute | solution.py:301
  105.0 28.4 %collective-permute-done.14.refs_1_ = bf16[4,64,2560]{2,1,0:T(8,128)(2,1)S(1)} collective-permute-done((bf16[4,64,2560]{2,1,0:T(8,128)(2,1)S(1)}, bf16[4,64,2560]{2,1,0:T(8,128)(2,1)S(1)}, u32[]{:S(2)}, u32[]{:S(2)}) %collective-permute-start.14) | collective-permute-done | bytes 1310752 | tf_op jit(solution)/shard_map/ppermute | solution.py:297
  134.7 9.6 %add_convert_fusion.q_ref.k_ref.v_ref = bf16[2048,1536]{1,0:T(8,128)(2,1)} fusion(bf16[1024,1536]{1,0:T(8,128)(2,1)S(1)} %bitcast.168, f32[1536]{0:T(1024)S(1)} %constant_dynamic-update-slice_fusion.16, f32[1024]{0:T(1024)S(1)} %bitcast.229, f32[1024]{0:T(1024)S(1)} %bitcast.213, f32[2048]{0:T(1024)S(1)} %add_rsqrt_fusion, ...), kind=kOutput, calls=%fused_computation.14 | convolution fusion | flops 6461325312 | bytes 13662208 | tf_op jit(solution)/shard_map/dot_general | solution.py:26
  144.4 16.2 %collective-permute-done.11.refs_1_ = bf16[4,64,2560]{2,1,0:T(8,128)(2,1)} collective-permute-done((bf16[4,64,2560]{2,1,0:T(8,128)(2,1)}, bf16[4,64,2560]{2,1,0:T(8,128)(2,1)}, u32[]{:S(2)}, u32[]{:S(2)}) %collective-permute-start.11) | collective-permute-done | bytes 1310752 | tf_op jit(solution)/shard_map/ppermute | solution.py:297
  160.6 26.5 %attention_forward.3 = (bf16[1024,512]{1,0:T(8,128)(2,1)}, f32[1,2,4,1024]{3,2,1,0:T(4,128)S(1)}) custom-call(s32[1,8]{1,0:T(1,128)S(1)} %and_select_fusion.lo_ref, s32[1]{0:T(128)} %bitcast.26.off_ref, bf16[2048,1536]{1,0:T(8,128)(2,1)} %add_convert_fusion.q_ref.k_ref.v_ref, bf16[2048,1536]{1,0:T(8,128)(2,1)} %add_convert_fusion.q_ref.k_ref.v_ref, ...), custom_call_target="tpu_custom_call" | custom-call | flops 1342177280 | bytes 4194304 | tf_op jit(solution)/shard_map/attention_forward/pallas_call | solution.py:95
  187.1 3.9 copy.58
  191.1 6.8 fusion.7
  197.8 17.8 %attention_forward.2 = (bf16[1024,512]{1,0:T(8,128)(2,1)S(1)}, f32[1,2,4,1024]{3,2,1,0:T(4,128)S(1)}) custom-call(s32[1,8]{1,0:T(1,128)S(1)} %and_select_fusion.lo_ref, s32[1]{0:T(128)} %bitcast.2.off_ref, bf16[2048,1536]{1,0:T(8,128)(2,1)} %add_convert_fusion.q_ref.k_ref.v_ref, bf16[2048,1536]{1,0:T(8,128)(2,1)} %add_convert_fusion.q_ref.k_ref.v_ref, ...), custom_call_target="tpu_custom_call" | custom-call | flops 1342177280 | bytes 4194304 | tf_op jit(solution)/shard_map/attention_forward/pallas_call | solution.py:95
  219.6 3.3 assemble.8.refs_4_
  224.8 4.1 assemble.9
  229.0 2.4 add_reduce_fusion.1
  232.0 3.3 copy-done.12
  235.4 2.7 fusion.50
  238.1 2.7 multiply_reduce_fusion.6
  240.8 20.2 %multiply_convert_fusion.1 = (bf16[1024,4096]{1,0:T(8,128)(2,1)}, f32[1024,4096]{1,0:T(8,128)}) fusion(f32[4096]{0:T(1024)S(1)} %pad_maximum_fusion.6, bf16[1024,4096]{1,0:T(8,128)(2,1)S(1)} %bitcast.163, f32[1024,1024]{0,1:T(8,128)} %get-tuple-element.65, f32[1024]{0:T(1024)S(1)} %bitcast.231, f32[1024]{0:T(1024)S(1)} %bitcast.200, ...), kind=kOutput, calls=%fused_computation.11 | convolution fusion | flops 8637120512 | bytes 37781504 | tf_op jit(solution)/shard_map/dot_general | solution.py:26
  261.0 13.9 %add_reduce_fusion = (f32[1024]{0:T(1024)S(1)}, f32[1024,1024]{0,1:T(8,128)S(1)}) fusion(f32[1024]{0:T(1024)S(1)} %bitcast.193, bf16[1024,4096]{1,0:T(8,128)(2,1)} %get-tuple-element.122, bf16[1024,4096]{1,0:T(8,128)(2,1)} %all-gather.2.cloned.1.call-done), kind=kOutput, calls=%fused_computation.70 | convolution fusion | flops 8592030720 | bytes 20979712 | tf_op jit(solution)/shard_map/dot_general | solution.py:26
  276.5 2.9 fusion.21
  279.4 5.8 convert_reduce_fusion.7
  286.6 11.2 %convolution_convert_fusion = bf16[1024,4096]{1,0:T(8,128)(2,1)} fusion(bf16[1024,1024]{0,1:T(8,128)(2,1)S(1)} %get-tuple-element.60, bf16[1024,4096]{1,0:T(8,128)(2,1)S(1)} %bitcast.235), kind=kOutput, calls=%fused_computation.23 | convolution fusion | flops 8594128896 | bytes 18874368 | tf_op jit(solution)/shard_map/dot_general | solution.py:26
  297.8 26.9 %convert_reduce_fusion = (f32[4096]{0:T(1024)S(1)}, bf16[1024,4096]{1,0:T(8,128)(2,1)}) fusion(f32[1024,4096]{1,0:T(8,128)} %get-tuple-element.123, f32[4096]{0:T(1024)S(1)} %pad_maximum_fusion.6, bf16[1024,1024]{0,1:T(8,128)(2,1)} %copy-done.22, bf16[1024,4096]{1,0:T(8,128)(2,1)} %all-gather.2.cloned.1.call-done), kind=kOutput, calls=%fused_computation.9 | convolution fusion | flops 8690593792 | bytes 35684352 | tf_op jit(solution)/shard_map/dot_general | solution.py:26
  324.7 16.1 %fusion.61 = (f32[1024]{0:T(1024)}, f32[1024,1024]{1,0:T(8,128)}) fusion(bf16[1024,4096]{1,0:T(8,128)(2,1)} %get-tuple-element.58, bf16[1024,4096]{1,0:T(8,128)(2,1)} %bitcast.164), kind=kOutput, calls=%fused_computation.208 | convolution fusion | flops 8590982144 | bytes 20975616 | tf_op jit(solution)/shard_map/dot_general | solution.py:26
  340.8 5.4 copy.44
  346.2 4.4 multiply_reduce_fusion
  352.1 6.0 multiply_reduce_fusion.1
  358.2 2.8 convert_reduce_fusion.8
  361.0 2.3 convolution_convert_fusion.4
  363.6 3.7 convolution_convert_fusion.3
  367.2 13.8 %convolution_convert_fusion.1 = bf16[1024,4096]{1,0:T(8,128)(2,1)} fusion(bf16[1024,4096]{1,0:T(8,128)(2,1)S(1)} %bitcast.237, f32[1024,1024]{0,1:T(8,128)} %get-tuple-element.65, f32[1024]{0:T(1024)S(1)} %bitcast.232, f32[1024]{0:T(1024)S(1)} %bitcast.203, f32[1024]{0:T(1024)S(1)} %add_rsqrt_fusion.2, f32[1024]{0:T(1024)S(1)} %broadcast_multiply_fusion.10), kind=kOutput, calls=%fused_computation.24 | convolution fusion | flops 8599371776 | bytes 20987904 | tf_op jit(solution)/shard_map/dot_general | solution.py:26
  381.0 10.1 %collective-permute-start.18 = (bf16[1024,512]{1,0:T(8,128)(2,1)}, bf16[1024,512]{1,0:T(8,128)(2,1)S(1)}, u32[]{:S(2)}, u32[]{:S(2)}) collective-permute-start(bf16[1024,512]{1,0:T(8,128)(2,1)} %convolution_convert_fusion.4), channel_id=1, source_target_pairs={{0,1},{1,0},{2,3},{3,2},{4,5},{5,4},{6,7},{7,6},{8,9},{9,8},{10,11... | collective-permute-start | bytes 3145736 | tf_op jit(solution)/shard_map/ppermute | solution.py:301
  391.2 2.7 constant_dynamic-slice_fusion.4
  394.9 6.3 constant_dynamic-slice_fusion.2
  401.2 2.3 copy.76
  403.9 3.9 copy.54
  407.9 3.2 convolution_convert_fusion.5.refs_2_
  411.1 36.1 %attention_backward.2.refs_6_ = bf16[2048,1536]{1,0:T(8,128)(2,1)} custom-call(s32[1,8]{1,0:T(1,128)S(1)} %copy-done.10, s32[1]{0:T(128)} %bitcast.43.place_ref, bf16[2048,1536]{1,0:T(8,128)(2,1)} %add_convert_fusion.q_ref.k_ref.v_ref, bf16[2048,1536]{1,0:T(8,128)(2,1)} %add_convert_fusion.q_ref.k_ref.v_ref, ...), custom_call_target="tpu_custom_call" | custom-call | flops 3355443200 | bytes 8388608 | tf_op jit(solution)/shard_map/attention_backward/pallas_call | solution.py:218
  447.2 36.1 %attention_backward.3 = bf16[2048,1536]{1,0:T(8,128)(2,1)} custom-call(s32[1,8]{1,0:T(1,128)S(1)} %copy-done.10, s32[1]{0:T(128)} %bitcast.43.place_ref, bf16[2048,1536]{1,0:T(8,128)(2,1)} %add_convert_fusion.q_ref.k_ref.v_ref, bf16[2048,1536]{1,0:T(8,128)(2,1)} %add_convert_fusion.q_ref.k_ref.v_ref, ...), custom_call_target="tpu_custom_call", output_to_operand_aliasing={{}: (12, {})} | custom-call | flops 3355443200 | bytes 8388608 | tf_op jit(solution)/shard_map/attention_backward/pallas_call | solution.py:218
  483.4 10.2 %convolution_convert_fusion.2 = bf16[1024,1536]{1,0:T(8,128)(2,1)S(1)} fusion(bf16[2048,1536]{1,0:T(8,128)(2,1)} %attention_backward.3, f32[1024]{0:T(1024)S(1)} %bitcast.230, f32[1024]{0:T(1024)S(1)} %bitcast.215, f32[2048]{0:T(1024)S(1)} %copy-done.30, f32[2048]{0:T(1024)S(1)} %copy-done.28, bf16[2048,1024]{0,1:T(8,128)(2,1)S(1)} %copy-done.13), kind=kOutput, calls=%fused_computation.67 | convolution fusion | flops 6456606720 | bytes 13656064 | tf_op jit(solution)/shard_map/dot_general | solution.py:26
  493.6 4.7 fusion.33
  502.3 12.8 %collective-permute-done.26 = bf16[4,64,1024]{2,1,0:T(8,128)(2,1)S(1)} collective-permute-done((bf16[4,64,1024]{2,1,0:T(8,128)(2,1)S(1)}, bf16[4,64,1024]{2,1,0:T(8,128)(2,1)S(1)}, u32[]{:S(2)}, u32[]{:S(2)}) %collective-permute-start.26) | collective-permute-done | bytes 524320 | tf_op jit(solution)/shard_map/ppermute | solution.py:297
  517.0 5.2 fusion.10
  524.2 22.0 %collective-permute-done.19 = bf16[1024,1024]{0,1:T(8,128)(2,1)} collective-permute-done((bf16[1024,1024]{0,1:T(8,128)(2,1)}, bf16[1024,1024]{0,1:T(8,128)(2,1)}, u32[]{:S(2)}, u32[]{:S(2)}) %collective-permute-start.19) | collective-permute-done | bytes 2097184 | tf_op jit(solution)/shard_map/ppermute | solution.py:301
  546.2 8.3 %fusion.20 = (f32[1024]{0:T(1024)S(1)}, f32[1024]{0:T(1024)}, f32[1024]{0:T(1024)S(1)}, f32[1024]{0:T(1024)}, f32[1024]{0:T(1024)S(1)}, /*index=5*/f32[1024]{0:T(1024)S(1)}, bf16[1024,1024]{0,1:T(8,128)(2,1)}) fusion(f32[2048,1024]{0,1:T(8,128)S(1)} %bitcast.177, s32[]{:T(128)} %select_n.134, f32[1024]{0:T(1024)S(1)} %bitcast.216, ...), kind=kOutput, calls=%fused_computation.43 | convolution fusion | flops 3236947968 | bytes 21001220 | tf_op jit(solution)/shard_map/dot_general | solution.py:26
  556.1 2.1 dynamic-slice_bitcast_fusion.1
  561.0 28.2 %collective-permute-done.35 = f32[16,1024]{1,0:T(8,128)S(1)} collective-permute-done((f32[16,1024]{1,0:T(8,128)S(1)}, f32[16,1024]{1,0:T(8,128)S(1)}, u32[]{:S(2)}, u32[]{:S(2)}) %collective-permute-start.35) | collective-permute-done | bytes 65568 | tf_op jit(solution)/shard_map/ppermute | solution.py:297
  591.5 2.1 collective-permute-done.36
  593.6 17.2 %collective-permute-start.37 = (f32[16,1024]{1,0:T(8,128)S(1)}, f32[16,1024]{1,0:T(8,128)}, u32[]{:S(2)}, u32[]{:S(2)}) collective-permute-start(f32[16,1024]{1,0:T(8,128)S(1)} %add.434), channel_id=1, source_target_pairs={{0,8},{2,10},{4,12},{6,14},{8,0},{10,2},{12,4},{14,6},{16,24},{18,... | collective-permute-start | bytes 196616 | tf_op jit(solution)/shard_map/ppermute | solution.py:386
  610.8 6.0 add_convert_fusion.2
  616.8 2.6 copy.55
  622.7 3.0 fusion.22
  628.4 2.8 collective-permute-start.24
  633.1 2.6 collective-permute-done.22
  635.7 4.3 collective-permute-done.23
  640.2 13.1 %collective-permute-done.29 = bf16[4,64,2560]{2,1,0:T(8,128)(2,1)S(1)} collective-permute-done((bf16[4,64,2560]{2,1,0:T(8,128)(2,1)S(1)}, bf16[4,64,2560]{2,1,0:T(8,128)(2,1)S(1)}, u32[]{:S(2)}, u32[]{:S(2)}) %collective-permute-start.29) | collective-permute-done | bytes 1310752 | tf_op jit(solution)/shard_map/ppermute | solution.py:301
  655.7 2.6 collective-permute-start.32
  660.5 5.9 collective-permute-done.30
  666.3 8.9 %collective-permute-done.31 = bf16[64,2560]{1,0:T(8,128)(2,1)S(1)} collective-permute-done((bf16[64,2560]{1,0:T(8,128)(2,1)S(1)}, bf16[64,2560]{1,0:T(8,128)(2,1)S(1)}, u32[]{:S(2)}, u32[]{:S(2)}) %collective-permute-start.31) | collective-permute-done | bytes 327712 | tf_op jit(solution)/shard_map/ppermute | solution.py:375
  (274 shorter events, 66.0 us)
Async XLA Ops:
  7.2 253.8 %all-gather.2.cloned.1.call-start = ((), (), s32[]{:S(2)}) async-start(), calls=%async_computation.1 | async-start | bytes 8912896 | tf_op jit(solution)/shard_map/all_gather | solution.py:400
  9.3 54.7 %collective-permute-start.7 = (bf16[64,2560]{1,0:T(8,128)(2,1)S(1)}, bf16[64,2560]{1,0:T(8,128)(2,1)S(1)}, u32[]{:S(2)}, u32[]{:S(2)}) collective-permute-start(bf16[64,2560]{1,0:T(8,128)(2,1)S(1)} %get-tuple-element.94), channel_id=1, source_target_pairs={{0,8},{2,10},{4,12},{6,14},{8,16},{10,18},{12,20},{14,22},{16,24},... | collective-permute-start | bytes 983048 | tf_op jit(solution)/shard_map/ppermute | solution.py:350
  12.3 51.6 %collective-permute-start.8 = (bf16[64,2560]{1,0:T(8,128)(2,1)S(1)}, bf16[64,2560]{1,0:T(8,128)(2,1)S(1)}, u32[]{:S(2)}, u32[]{:S(2)}) collective-permute-start(bf16[64,2560]{1,0:T(8,128)(2,1)S(1)} %get-tuple-element.94), channel_id=1, source_target_pairs={{0,16},{2,18},{4,20},{6,22},{8,24},{10,26},{12,28},{14,30},{16,0},... | collective-permute-start | bytes 983048 | tf_op jit(solution)/shard_map/ppermute | solution.py:350
  16.0 7.6 %collective-permute-start.17 = (bf16[64,2048]{1,0:T(8,128)(2,1)S(1)}, bf16[64,2048]{1,0:T(8,128)(2,1)S(1)}, u32[]{:S(2)}, u32[]{:S(2)}) collective-permute-start(bf16[64,2048]{1,0:T(8,128)(2,1)S(1)} %convert_bitcast_fusion), channel_id=1, source_target_pairs={{0,1},{1,0},{2,3},{3,2},{4,5},{5,4},{6,7},{7,6},{8,9},{9,8},{10,11... | collective-permute-start | bytes 786440 | tf_op jit(solution)/shard_map/ppermute | solution.py:301
  24.4 634.7 %reduce-scatter.2.cloned.1.call-start = ((), (), s32[]{:S(2)}) async-start(), calls=%async_computation.2 | async-start | bytes 8912896 | tf_op jit(solution)/shard_map/reduce_scatter | solution.py:415
  24.5 17.7 %collective-permute-start = (bf16[64,1536]{1,0:T(8,128)(2,1)S(1)}, bf16[64,1536]{1,0:T(8,128)(2,1)S(1)}, u32[]{:S(2)}, u32[]{:S(2)}) collective-permute-start(bf16[64,1536]{1,0:T(8,128)(2,1)S(1)} %constant_dynamic-update-slice_fusion.6), channel_id=1, source_target_pairs={{0,8},{2,10},{4,12},{6,14},{8,16},{10,18},{12,20},{14,22},{16,24},... | collective-permute-start | bytes 589832 | tf_op jit(solution)/shard_map/ppermute | solution.py:350
  25.0 37.3 %collective-permute-start.1 = (bf16[64,1536]{1,0:T(8,128)(2,1)S(1)}, bf16[64,1536]{1,0:T(8,128)(2,1)S(1)}, u32[]{:S(2)}, u32[]{:S(2)}) collective-permute-start(bf16[64,1536]{1,0:T(8,128)(2,1)S(1)} %constant_dynamic-update-slice_fusion.6), channel_id=1, source_target_pairs={{0,16},{2,18},{4,20},{6,22},{8,24},{10,26},{12,28},{14,30},{16,0},... | collective-permute-start | bytes 589832 | tf_op jit(solution)/shard_map/ppermute | solution.py:350
  26.5 35.8 %collective-permute-start.2 = (bf16[64,1536]{1,0:T(8,128)(2,1)S(1)}, bf16[64,1536]{1,0:T(8,128)(2,1)S(1)}, u32[]{:S(2)}, u32[]{:S(2)}) collective-permute-start(bf16[64,1536]{1,0:T(8,128)(2,1)S(1)} %constant_dynamic-update-slice_fusion.6), channel_id=1, source_target_pairs={{0,24},{2,26},{4,28},{6,30},{8,0},{10,2},{12,4},{14,6},{16,8},{18,... | collective-permute-start | bytes 589832 | tf_op jit(solution)/shard_map/ppermute | solution.py:350
  36.8 161.0 %copy-start.7 = (s32[2048]{0:T(1024)}, s32[2048]{0:T(1024)S(1)}, u32[]{:S(2)}) copy-start(s32[2048]{0:T(1024)S(1)} %convert_reduce_fusion.1) | copy-start | bytes 24580
  40.9 150.1 %copy-start.27 = (f32[2048]{0:T(1024)}, f32[2048]{0:T(1024)S(1)}, u32[]{:S(2)}) copy-start(f32[2048]{0:T(1024)S(1)} %broadcast_multiply_fusion) | copy-start | bytes 24580
  41.0 43.6 %copy-start.40 = (f32[2,1024]{1,0:T(2,128)S(1)}, f32[2,1024]{1,0:T(2,128)}, u32[]{:S(2)}) copy-start(f32[2,1024]{1,0:T(2,128)} %param.22) | copy-start | bytes 24580
  41.0 43.6 %copy-start.38 = (f32[4,1024]{1,0:T(4,128)S(1)}, f32[4,1024]{1,0:T(4,128)}, u32[]{:S(2)}) copy-start(f32[4,1024]{1,0:T(4,128)} %param.19) | copy-start | bytes 49156
  41.0 43.6 %copy-start.39 = (f32[4,1024]{1,0:T(4,128)S(1)}, f32[4,1024]{1,0:T(4,128)}, u32[]{:S(2)}) copy-start(f32[4,1024]{1,0:T(4,128)} %param.20) | copy-start | bytes 49156
  42.2 35.1 %collective-permute-start.9 = (bf16[64,2560]{1,0:T(8,128)(2,1)S(1)}, bf16[64,2560]{1,0:T(8,128)(2,1)S(1)}, u32[]{:S(2)}, u32[]{:S(2)}) collective-permute-start(bf16[64,2560]{1,0:T(8,128)(2,1)S(1)} %get-tuple-element.94), channel_id=1, source_target_pairs={{0,24},{2,26},{4,28},{6,30},{8,0},{10,2},{12,4},{14,6},{16,8},{18,... | collective-permute-start | bytes 983048 | tf_op jit(solution)/shard_map/ppermute | solution.py:350
  62.4 22.1 %collective-permute-start.3 = (bf16[4,64,1536]{2,1,0:T(8,128)(2,1)S(1)}, bf16[4,64,1536]{2,1,0:T(8,128)(2,1)S(1)}, u32[]{:S(2)}, u32[]{:S(2)}) collective-permute-start(bf16[4,64,1536]{2,1,0:T(8,128)(2,1)S(1)} %pad_maximum_fusion.2.refs_0_), channel_id=1, source_target_pairs={{0,4},{2,6},{4,0},{6,2},{8,12},{10,14},{12,8},{14,10},{16,20},{18,... | collective-permute-start | bytes 2359304 | tf_op jit(solution)/shard_map/ppermute | solution.py:297
  77.5 55.9 %collective-permute-start.14 = (bf16[4,64,2560]{2,1,0:T(8,128)(2,1)S(1)}, bf16[4,64,2560]{2,1,0:T(8,128)(2,1)S(1)}, u32[]{:S(2)}, u32[]{:S(2)}) collective-permute-start(bf16[4,64,2560]{2,1,0:T(8,128)(2,1)S(1)} %pad_maximum_fusion.refs_0_), channel_id=1, source_target_pairs={{0,4},{2,6},{4,0},{6,2},{8,12},{10,14},{12,8},{14,10},{16,20},{18,... | collective-permute-start | bytes 3932168 | tf_op jit(solution)/shard_map/ppermute | solution.py:297
  79.0 25.4 %collective-permute-start.10 = (bf16[4,64,2560]{2,1,0:T(8,128)(2,1)S(1)}, bf16[4,64,2560]{2,1,0:T(8,128)(2,1)}, u32[]{:S(2)}, u32[]{:S(2)}) collective-permute-start(bf16[4,64,2560]{2,1,0:T(8,128)(2,1)S(1)} %pad_maximum_fusion.refs_0_), channel_id=1, source_target_pairs={{0,1},{1,0},{2,3},{3,2},{4,5},{5,4},{6,7},{7,6},{8,9},{9,8},{10,11... | collective-permute-start | bytes 3932168 | tf_op jit(solution)/shard_map/ppermute | solution.py:301
  80.6 117.2 %copy-start.9 = (s32[1,8]{1,0:T(1,128)}, s32[1,8]{1,0:T(1,128)S(1)}, u32[]{:S(2)}) copy-start(s32[1,8]{1,0:T(1,128)S(1)} %and_select_fusion.lo_ref) | copy-start | bytes 100
  80.6 110.5 %copy-start.29 = (f32[2048]{0:T(1024)}, f32[2048]{0:T(1024)S(1)}, u32[]{:S(2)}) copy-start(f32[2048]{0:T(1024)S(1)} %add_rsqrt_fusion) | copy-start | bytes 24580
  80.6 24.4 %collective-permute-start.4 = (bf16[4,64,1536]{2,1,0:T(8,128)(2,1)S(1)}, bf16[4,64,1536]{2,1,0:T(8,128)(2,1)S(1)}, u32[]{:S(2)}, u32[]{:S(2)}) collective-permute-start(bf16[4,64,1536]{2,1,0:T(8,128)(2,1)S(1)} %pad_maximum_fusion.2.refs_0_), channel_id=1, source_target_pairs={{0,2},{2,0},{4,6},{6,4},{8,10},{10,8},{12,14},{14,12},{16,18},{18,... | collective-permute-start | bytes 2359304 | tf_op jit(solution)/shard_map/ppermute | solution.py:293
  84.5 48.9 %collective-permute-start.5 = (bf16[4,64,1536]{2,1,0:T(8,128)(2,1)S(1)}, bf16[4,64,1536]{2,1,0:T(8,128)(2,1)S(1)}, u32[]{:S(2)}, u32[]{:S(2)}) collective-permute-start(bf16[4,64,1536]{2,1,0:T(8,128)(2,1)S(1)} %collective-permute-done.3.refs_1_), channel_id=1, source_target_pairs={{0,2},{2,0},{4,6},{6,4},{8,10},{10,8},{12,14},{14,12},{16,18},{18,... | collective-permute-start | bytes 2359304 | tf_op jit(solution)/shard_map/ppermute | solution.py:293
  84.6 59.7 %copy-start.34 = (f32[1,1024]{1,0:T(1,128)}, f32[1,1024]{1,0:T(1,128)S(1)}, u32[]{:S(2)}) copy-start(f32[1,1024]{1,0:T(1,128)S(1)} %get-tuple-element.104) | copy-start | bytes 12292
  84.7 59.7 %copy-start.41 = (f32[1,1024]{1,0:T(1,128)}, f32[1,1024]{1,0:T(1,128)S(1)}, u32[]{:S(2)}) copy-start(f32[1,1024]{1,0:T(1,128)S(1)} %get-tuple-element.108) | copy-start | bytes 12292
  84.7 133.0 %collective-permute-start.15 = (bf16[4,64,2560]{2,1,0:T(8,128)(2,1)S(1)}, bf16[4,64,2560]{2,1,0:T(8,128)(2,1)}, u32[]{:S(2)}, u32[]{:S(2)}) collective-permute-start(bf16[4,64,2560]{2,1,0:T(8,128)(2,1)S(1)} %pad_maximum_fusion.refs_0_), channel_id=1, source_target_pairs={{0,2},{2,0},{4,6},{6,4},{8,10},{10,8},{12,14},{14,12},{16,18},{18,... | collective-permute-start | bytes 3932168 | tf_op jit(solution)/shard_map/ppermute | solution.py:293
  104.5 56.1 %collective-permute-start.11 = (bf16[4,64,2560]{2,1,0:T(8,128)(2,1)}, bf16[4,64,2560]{2,1,0:T(8,128)(2,1)}, u32[]{:S(2)}, u32[]{:S(2)}) collective-permute-start(bf16[4,64,2560]{2,1,0:T(8,128)(2,1)} %collective-permute-done.10.refs_0_), channel_id=1, source_target_pairs={{0,4},{2,6},{4,0},{6,2},{8,12},{10,14},{12,8},{14,10},{16,20},{18,... | collective-permute-start | bytes 3932168 | tf_op jit(solution)/shard_map/ppermute | solution.py:297
  105.0 117.9 %collective-permute-start.12 = (bf16[4,64,2560]{2,1,0:T(8,128)(2,1)}, bf16[4,64,2560]{2,1,0:T(8,128)(2,1)}, u32[]{:S(2)}, u32[]{:S(2)}) collective-permute-start(bf16[4,64,2560]{2,1,0:T(8,128)(2,1)} %collective-permute-done.10.refs_0_), channel_id=1, source_target_pairs={{0,2},{2,0},{4,6},{6,4},{8,10},{10,8},{12,14},{14,12},{16,18},{18,... | collective-permute-start | bytes 3932168 | tf_op jit(solution)/shard_map/ppermute | solution.py:293
  133.4 84.3 %collective-permute-start.16 = (bf16[4,64,2560]{2,1,0:T(8,128)(2,1)S(1)}, bf16[4,64,2560]{2,1,0:T(8,128)(2,1)}, u32[]{:S(2)}, u32[]{:S(2)}) collective-permute-start(bf16[4,64,2560]{2,1,0:T(8,128)(2,1)S(1)} %collective-permute-done.14.refs_1_), channel_id=1, source_target_pairs={{0,2},{2,0},{4,6},{6,4},{8,10},{10,8},{12,14},{14,12},{16,18},{18,... | collective-permute-start | bytes 3932168 | tf_op jit(solution)/shard_map/ppermute | solution.py:293
  160.6 62.4 %collective-permute-start.13 = (bf16[4,64,2560]{2,1,0:T(8,128)(2,1)}, bf16[4,64,2560]{2,1,0:T(8,128)(2,1)}, u32[]{:S(2)}, u32[]{:S(2)}) collective-permute-start(bf16[4,64,2560]{2,1,0:T(8,128)(2,1)} %collective-permute-done.11.refs_1_), channel_id=1, source_target_pairs={{0,2},{2,0},{4,6},{6,4},{8,10},{10,8},{12,14},{14,12},{16,18},{18,... | collective-permute-start | bytes 3932168 | tf_op jit(solution)/shard_map/ppermute | solution.py:293
  187.0 28.8 %collective-permute-start.6 = (bf16[1024,512]{1,0:T(8,128)(2,1)}, bf16[1024,512]{1,0:T(8,128)(2,1)}, u32[]{:S(2)}, u32[]{:S(2)}) collective-permute-start(bf16[1024,512]{1,0:T(8,128)(2,1)} %get-tuple-element.16.refs_1_), channel_id=1, source_target_pairs={{0,1},{1,0},{2,3},{3,2},{4,5},{5,4},{6,7},{7,6},{8,9},{9,8},{10,11... | collective-permute-start | bytes 3145736 | tf_op jit(solution)/shard_map/ppermute | solution.py:301
  381.0 30.0 %collective-permute-start.18 = (bf16[1024,512]{1,0:T(8,128)(2,1)}, bf16[1024,512]{1,0:T(8,128)(2,1)S(1)}, u32[]{:S(2)}, u32[]{:S(2)}) collective-permute-start(bf16[1024,512]{1,0:T(8,128)(2,1)} %convolution_convert_fusion.4), channel_id=1, source_target_pairs={{0,1},{1,0},{2,3},{3,2},{4,5},{5,4},{6,7},{7,6},{8,9},{9,8},{10,11... | collective-permute-start | bytes 3145736 | tf_op jit(solution)/shard_map/ppermute | solution.py:301
  394.9 103.8 %collective-permute-start.25 = (bf16[4,2,64,1024]{3,2,0,1:T(8,128)(2,1)}, bf16[4,2,64,1024]{3,2,0,1:T(8,128)(2,1)}, u32[]{:S(2)}, u32[]{:S(2)}) collective-permute-start(bf16[4,2,64,1024]{3,2,0,1:T(8,128)(2,1)} %bitcast.161), channel_id=1, source_target_pairs={{0,2},{2,0},{4,6},{6,4},{8,10},{10,8},{12,14},{14,12},{16,18},{18,... | collective-permute-start | bytes 3145736 | tf_op jit(solution)/shard_map/ppermute | solution.py:293
  403.4 113.6 %collective-permute-start.27 = (bf16[4,2,64,4096]{3,2,0,1:T(8,128)(2,1)}, bf16[4,2,64,4096]{3,2,0,1:T(8,128)(2,1)}, u32[]{:S(2)}, u32[]{:S(2)}) collective-permute-start(bf16[4,2,64,4096]{3,2,0,1:T(8,128)(2,1)} %bitcast.159), channel_id=1, source_target_pairs={{0,2},{2,0},{4,6},{6,4},{8,10},{10,8},{12,14},{14,12},{16,18},{18,... | collective-permute-start | bytes 12582920 | tf_op jit(solution)/shard_map/ppermute | solution.py:293
  447.2 36.2 %copy-start.13 = (bf16[2048,1024]{0,1:T(8,128)(2,1)S(1)}, bf16[2048,1024]{0,1:T(8,128)(2,1)}, u32[]{:S(2)}) copy-start(bf16[2048,1024]{0,1:T(8,128)(2,1)} %copy.41) | copy-start | bytes 12582916
  447.2 36.2 %copy-start.28 = (f32[2048]{0:T(1024)S(1)}, f32[2048]{0:T(1024)}, u32[]{:S(2)}) copy-start(f32[2048]{0:T(1024)} %copy-done.27) | copy-start | bytes 24580
  447.2 36.2 %copy-start.30 = (f32[2048]{0:T(1024)S(1)}, f32[2048]{0:T(1024)}, u32[]{:S(2)}) copy-start(f32[2048]{0:T(1024)} %copy-done.29) | copy-start | bytes 24580
  447.2 36.2 %copy-start.35 = (f32[1,1024]{1,0:T(1,128)S(1)}, f32[1,1024]{1,0:T(1,128)}, u32[]{:S(2)}) copy-start(f32[1,1024]{1,0:T(1,128)} %copy-done.34) | copy-start | bytes 12292
  447.2 36.2 %copy-start.42 = (f32[1,1024]{1,0:T(1,128)S(1)}, f32[1,1024]{1,0:T(1,128)}, u32[]{:S(2)}) copy-start(f32[1,1024]{1,0:T(1,128)} %copy-done.41) | copy-start | bytes 12292
  498.3 47.9 %collective-permute-start.19 = (bf16[1024,1024]{0,1:T(8,128)(2,1)}, bf16[1024,1024]{0,1:T(8,128)(2,1)}, u32[]{:S(2)}, u32[]{:S(2)}) collective-permute-start(bf16[1024,1024]{0,1:T(8,128)(2,1)} %fusion.33), channel_id=1, source_target_pairs={{0,1},{1,0},{2,3},{3,2},{4,5},{5,4},{6,7},{7,6},{8,9},{9,8},{10,11... | collective-permute-start | bytes 6291464 | tf_op jit(solution)/shard_map/ppermute | solution.py:301
  498.6 16.8 %collective-permute-start.20 = (bf16[4,2,64,1536]{3,2,0,1:T(8,128)(2,1)S(1)}, bf16[4,2,64,1536]{3,2,0,1:T(8,128)(2,1)S(1)}, u32[]{:S(2)}, u32[]{:S(2)}) collective-permute-start(bf16[4,2,64,1536]{3,2,0,1:T(8,128)(2,1)S(1)} %bitcast.181), channel_id=1, source_target_pairs={{0,2},{2,0},{4,6},{6,4},{8,10},{10,8},{12,14},{14,12},{16,18},{18,... | collective-permute-start | bytes 4718600 | tf_op jit(solution)/shard_map/ppermute | solution.py:293
  501.2 13.9 %collective-permute-start.26 = (bf16[4,64,1024]{2,1,0:T(8,128)(2,1)S(1)}, bf16[4,64,1024]{2,1,0:T(8,128)(2,1)S(1)}, u32[]{:S(2)}, u32[]{:S(2)}) collective-permute-start(bf16[4,64,1024]{2,1,0:T(8,128)(2,1)S(1)} %dynamic-slice_bitcast_fusion.2), channel_id=1, source_target_pairs={{0,4},{2,6},{4,0},{6,2},{8,12},{10,14},{12,8},{14,10},{16,20},{18,... | collective-permute-start | bytes 1572872 | tf_op jit(solution)/shard_map/ppermute | solution.py:297
  515.4 30.8 %slice-start = ((s8[8388608]{0:T(1024)(128)(4,1)}), s8[4194304]{0:T(1024)(128)(4,1)S(1)}, s32[]{:S(2)}) async-start(s8[8388608]{0:T(1024)(128)(4,1)} %bitcast.176), calls=%async_computation.3 | async-start | bytes 8388608
  517.0 29.2 %slice-start.1 = ((s8[8388608]{0:T(1024)(128)(4,1)}), s8[4194304]{0:T(1024)(128)(4,1)S(1)}, s32[]{:S(2)}) async-start(s8[8388608]{0:T(1024)(128)(4,1)} %bitcast.176), calls=%async_computation.4 | async-start | bytes 8388608
  522.2 32.4 %copy-start.20 = (bf16[4,2,64,4096]{3,2,0,1:T(8,128)(2,1)}, bf16[4,2,64,4096]{3,2,0,1:T(8,128)(2,1)S(1)}, u32[]{:S(2)}) copy-start(bf16[4,2,64,4096]{3,2,0,1:T(8,128)(2,1)S(1)} %fusion.10) | copy-start | bytes 12582916
  522.2 24.0 %copy-start.36 = (f32[1,1024]{1,0:T(1,128)S(1)}, f32[1,1024]{1,0:T(1,128)}, u32[]{:S(2)}) copy-start(f32[1,1024]{1,0:T(1,128)} %copy-done.34) | copy-start | bytes 12292
  523.9 30.7 %copy-start.31 = (f32[1024]{0:T(1024)S(1)}, f32[1024]{0:T(1024)}, u32[]{:S(2)}) copy-start(f32[1024]{0:T(1024)} %get-tuple-element.48) | copy-start | bytes 12292
  523.9 30.7 %copy-start.32 = (f32[1024]{0:T(1024)S(1)}, f32[1024]{0:T(1024)}, u32[]{:S(2)}) copy-start(f32[1024]{0:T(1024)} %get-tuple-element.56) | copy-start | bytes 12292
  523.9 30.7 %copy-start.33 = (f32[1024]{0:T(1024)S(1)}, f32[1024]{0:T(1024)}, u32[]{:S(2)}) copy-start(f32[1024]{0:T(1024)} %get-tuple-element.59) | copy-start | bytes 12292
  523.9 86.9 %dynamic-slice-start = ((f32[2048]{0:T(1024)}, s32[]{:T(128)}), f32[1024]{0:T(1024)S(1)}, s32[]{:S(2)}) async-start(f32[2048]{0:T(1024)} %copy-done.29, s32[]{:T(128)} %select_n.134), calls=%async_computation.5 | async-start | bytes 8704 | tf_op jit(solution)/shard_map/dynamic-slice
  523.9 98.9 %collective-permute-start.28 = (bf16[4,64,4096]{2,1,0:T(8,128)(2,1)}, bf16[4,64,4096]{2,1,0:T(8,128)(2,1)}, u32[]{:S(2)}, u32[]{:S(2)}) collective-permute-start(bf16[4,64,4096]{2,1,0:T(8,128)(2,1)} %dynamic-slice_bitcast_fusion), channel_id=1, source_target_pairs={{0,4},{2,6},{4,0},{6,2},{8,12},{10,14},{12,8},{14,10},{16,20},{18,... | collective-permute-start | bytes 6291464 | tf_op jit(solution)/shard_map/ppermute | solution.py:297
  556.1 2.2 collective-permute-start.34
  558.3 63.2 %collective-permute-start.21 = (bf16[4,64,1536]{2,1,0:T(8,128)(2,1)}, bf16[4,64,1536]{2,1,0:T(8,128)(2,1)S(1)}, u32[]{:S(2)}, u32[]{:S(2)}) collective-permute-start(bf16[4,64,1536]{2,1,0:T(8,128)(2,1)} %dynamic-slice_bitcast_fusion.1), channel_id=1, source_target_pairs={{0,4},{2,6},{4,0},{6,2},{8,12},{10,14},{12,8},{14,10},{16,20},{18,... | collective-permute-start | bytes 2359304 | tf_op jit(solution)/shard_map/ppermute | solution.py:297
  558.3 31.0 %collective-permute-start.35 = (f32[16,1024]{1,0:T(8,128)S(1)}, f32[16,1024]{1,0:T(8,128)S(1)}, u32[]{:S(2)}, u32[]{:S(2)}) collective-permute-start(f32[16,1024]{1,0:T(8,128)S(1)} %add.432), channel_id=1, source_target_pairs={{0,4},{2,6},{4,0},{6,2},{8,12},{10,14},{12,8},{14,10},{16,20},{18,... | collective-permute-start | bytes 196616 | tf_op jit(solution)/shard_map/ppermute | solution.py:297
  589.3 4.3 collective-permute-start.36
  593.6 23.2 %copy-start.26 = (f32[16,1024]{1,0:T(8,128)}, f32[16,1024]{1,0:T(8,128)S(1)}, u32[]{:S(2)}) copy-start(f32[16,1024]{1,0:T(8,128)S(1)} %add.434) | copy-start | bytes 196612
  593.6 25.8 %collective-permute-start.37 = (f32[16,1024]{1,0:T(8,128)S(1)}, f32[16,1024]{1,0:T(8,128)}, u32[]{:S(2)}, u32[]{:S(2)}) collective-permute-start(f32[16,1024]{1,0:T(8,128)S(1)} %add.434), channel_id=1, source_target_pairs={{0,8},{2,10},{4,12},{6,14},{8,0},{10,2},{12,4},{14,6},{16,24},{18,... | collective-permute-start | bytes 196616 | tf_op jit(solution)/shard_map/ppermute | solution.py:386
  620.3 11.0 %collective-permute-start.38 = (f32[16,1024]{1,0:T(8,128)S(1)}, f32[16,1024]{1,0:T(8,128)S(1)}, u32[]{:S(2)}, u32[]{:S(2)}) collective-permute-start(f32[16,1024]{1,0:T(8,128)S(1)} %add.435), channel_id=1, source_target_pairs={{0,16},{2,18},{4,20},{6,22},{8,24},{10,26},{12,28},{14,30},{16,0},... | collective-permute-start | bytes 196616 | tf_op jit(solution)/shard_map/ppermute | solution.py:387
  626.0 27.3 %collective-permute-start.29 = (bf16[4,64,2560]{2,1,0:T(8,128)(2,1)S(1)}, bf16[4,64,2560]{2,1,0:T(8,128)(2,1)S(1)}, u32[]{:S(2)}, u32[]{:S(2)}) collective-permute-start(bf16[4,64,2560]{2,1,0:T(8,128)(2,1)S(1)} %pad_maximum_fusion.1), channel_id=1, source_target_pairs={{0,1},{1,0},{2,3},{3,2},{4,5},{5,4},{6,7},{7,6},{8,9},{9,8},{10,11... | collective-permute-start | bytes 3932168 | tf_op jit(solution)/shard_map/ppermute | solution.py:301
  626.4 9.4 %collective-permute-start.22 = (bf16[64,1536]{1,0:T(8,128)(2,1)S(1)}, bf16[64,1536]{1,0:T(8,128)(2,1)S(1)}, u32[]{:S(2)}, u32[]{:S(2)}) collective-permute-start(bf16[64,1536]{1,0:T(8,128)(2,1)S(1)} %get-tuple-element.79), channel_id=1, source_target_pairs={{0,8},{2,10},{4,12},{6,14},{8,16},{10,18},{12,20},{14,22},{16,24},... | collective-permute-start | bytes 589832 | tf_op jit(solution)/shard_map/ppermute | solution.py:375
  626.5 13.6 %collective-permute-start.23 = (bf16[64,1536]{1,0:T(8,128)(2,1)S(1)}, bf16[64,1536]{1,0:T(8,128)(2,1)S(1)}, u32[]{:S(2)}, u32[]{:S(2)}) collective-permute-start(bf16[64,1536]{1,0:T(8,128)(2,1)S(1)} %get-tuple-element.81), channel_id=1, source_target_pairs={{0,16},{2,18},{4,20},{6,22},{8,24},{10,26},{12,28},{14,30},{16,0},... | collective-permute-start | bytes 589832 | tf_op jit(solution)/shard_map/ppermute | solution.py:375
  628.4 11.6 %collective-permute-start.24 = (bf16[64,1536]{1,0:T(8,128)(2,1)S(1)}, bf16[64,1536]{1,0:T(8,128)(2,1)S(1)}, u32[]{:S(2)}, u32[]{:S(2)}) collective-permute-start(bf16[64,1536]{1,0:T(8,128)(2,1)S(1)} %get-tuple-element.80), channel_id=1, source_target_pairs={{0,24},{2,26},{4,28},{6,30},{8,0},{10,2},{12,4},{14,6},{16,8},{18,... | collective-permute-start | bytes 589832 | tf_op jit(solution)/shard_map/ppermute | solution.py:375
  653.8 12.6 %collective-permute-start.30 = (bf16[64,2560]{1,0:T(8,128)(2,1)S(1)}, bf16[64,2560]{1,0:T(8,128)(2,1)S(1)}, u32[]{:S(2)}, u32[]{:S(2)}) collective-permute-start(bf16[64,2560]{1,0:T(8,128)(2,1)S(1)} %get-tuple-element.76), channel_id=1, source_target_pairs={{0,8},{2,10},{4,12},{6,14},{8,16},{10,18},{12,20},{14,22},{16,24},... | collective-permute-start | bytes 983048 | tf_op jit(solution)/shard_map/ppermute | solution.py:375
  654.1 21.0 %collective-permute-start.31 = (bf16[64,2560]{1,0:T(8,128)(2,1)S(1)}, bf16[64,2560]{1,0:T(8,128)(2,1)S(1)}, u32[]{:S(2)}, u32[]{:S(2)}) collective-permute-start(bf16[64,2560]{1,0:T(8,128)(2,1)S(1)} %get-tuple-element.78), channel_id=1, source_target_pairs={{0,16},{2,18},{4,20},{6,22},{8,24},{10,26},{12,28},{14,30},{16,0},... | collective-permute-start | bytes 983048 | tf_op jit(solution)/shard_map/ppermute | solution.py:375
  655.7 19.5 %collective-permute-start.32 = (bf16[64,2560]{1,0:T(8,128)(2,1)S(1)}, bf16[64,2560]{1,0:T(8,128)(2,1)S(1)}, u32[]{:S(2)}, u32[]{:S(2)}) collective-permute-start(bf16[64,2560]{1,0:T(8,128)(2,1)S(1)} %get-tuple-element.77), channel_id=1, source_target_pairs={{0,24},{2,26},{4,28},{6,30},{8,0},{10,2},{12,4},{14,6},{16,8},{18,... | collective-permute-start | bytes 983048 | tf_op jit(solution)/shard_map/ppermute | solution.py:375
  660.1 16.8 %collective-permute-start.33 = (bf16[64,2048]{1,0:T(8,128)(2,1)S(1)}, bf16[64,2048]{1,0:T(8,128)(2,1)S(1)}, u32[]{:S(2)}, u32[]{:S(2)}) collective-permute-start(bf16[64,2048]{1,0:T(8,128)(2,1)S(1)} %slice.129), channel_id=1, source_target_pairs={{0,1},{1,0},{2,3},{3,2},{4,5},{5,4},{6,7},{7,6},{8,9},{9,8},{10,11... | collective-permute-start | bytes 786440 | tf_op jit(solution)/shard_map/ppermute | solution.py:301
  (29 other events, 167.2 us)
Sparse Core Ops, SparseCore 0:
  24.5 118.8 all-gather.1
  391.3 121.7 reduce-scatter.1

commit v3 on v2

v3 whole, which is shorter than its diff:
```python
import functools
import math

import jax
import jax.numpy as jnp
from jax import lax
from jax.experimental import pallas as pl
from jax.experimental.pallas import tpu as pltpu
from jax.sharding import PartitionSpec as P

HD = 64
QB = 256
KB = 256
MAX_SEGMENT = 1024
max_chunks = MAX_SEGMENT // KB + 1
SCORE_SCALE = 0.125 * math.log2(math.e)
NEG = -1e30
EPS = 1e-05
BF16 = jnp.bfloat16
F32 = jnp.float32
NT = (((1,), (1,)), ((), ()))
NN = (((1,), (0,)), ((), ()))
TN = (((0,), (0,)), ((), ()))

SMALL = pl.CostEstimate(flops=1, bytes_accessed=1, transcendentals=0)
VMEM = 60 << 20
PAIR = 2 * HD


def dot(a, b, dims):
    return lax.dot_general(a, b, dims, preferred_element_type=jnp.float32)


def split_pair(block):
    lane = lax.broadcasted_iota(jnp.int32, block.shape, 1)
    zero = jnp.zeros_like(block)
    return (jnp.where(lane < HD, block, zero), jnp.where(lane >= HD, block, zero))


def fwd_kernel(pairs, lo_ref, off_ref, *refs):
    q_refs, k_refs, v_refs = refs[:pairs], refs[pairs : 2 * pairs], refs[2 * pairs : 3 * pairs]
    start_ref, o_ref, l_ref, vt_ref = refs[3 * pairs :]
    step = pl.program_id(1)
    block = off_ref[0] + step

    @pl.when(step == 0)
    def _():
        for pair in range(pairs):
            vt_ref[pair] = v_refs[pair][...].T

    pair_step = math.gcd(pairs, 4)
    row_start = start_ref[...]
    query_pos = block * QB + lax.broadcasted_iota(jnp.int32, (1, QB), 1)
    first = lo_ref[pl.program_id(0), block]
    count = block + 1 - first
    base = pl.multiple_of(first * KB, KB)

    for chunks in range(1, max_chunks + 1):

        @pl.when(count == chunks)
        def _(size=chunks * KB):
            window = pl.ds(base, size)
            key_pos = lax.broadcasted_iota(jnp.int32, (size, QB), 0) + base
            ok = (key_pos >= row_start) & (key_pos <= query_pos)
            for pair in range(pairs):
                q_heads = split_pair(q_refs[pair][...])
                keys = k_refs[pair][window, :]
                outs = []
                for h in range(2):
                    s = jnp.where(ok, dot(keys, q_heads[h], NT) * SCORE_SCALE, NEG)
                    peak = jnp.max(s, axis=0, keepdims=True)
                    p = jnp.exp2(s - peak)
                    total = jnp.sum(p, axis=0, keepdims=True)
                    vt = vt_ref[pair, h * HD : (h + 1) * HD, window]
                    outs.append(dot(vt, p.astype(BF16), NN) / total)
                    l_ref[pair, h : h + 1, :] = peak + jnp.log2(total)
                cols = slice(pair * PAIR, (pair + 1) * PAIR)
                o_ref[:, cols] = jnp.concatenate(outs, axis=0).T.astype(BF16)


def attention_forward(first, pairs, qkv, starts, lo, offset, blocks):
    seqs, length = starts.shape
    nq = length // QB
    every = range(first, first + pairs)

    def rows_at(p):
        return pl.BlockSpec((QB, PAIR), lambda s, b, lo, off: (s * nq + off[0] + b, 3 * p))

    def all_at(p, kind):
        return pl.BlockSpec((length, PAIR), lambda s, b, lo, off: (s, 3 * p + kind))

    grid_spec = pltpu.PrefetchScalarGridSpec(
        num_scalar_prefetch=2,
        grid=(seqs, blocks),
        in_specs=[rows_at(p) for p in every]
        + [all_at(p, kind) for kind in (1, 2) for p in every]
        + [pl.BlockSpec((None, 1, QB), lambda s, b, lo, off: (s, 0, off[0] + b))],
        out_specs=[
            pl.BlockSpec((QB, pairs * PAIR), lambda s, b, lo, off: (s * blocks + b, 0)),
            pl.BlockSpec((None, pairs, 2, QB), lambda s, b, lo, off: (s, 0, 0, b)),
        ],
        scratch_shapes=[pltpu.VMEM((pairs, PAIR, length), BF16)],
    )
    return pl.pallas_call(
        functools.partial(fwd_kernel, pairs),
        grid_spec=grid_spec,
        out_shape=(
            jax.ShapeDtypeStruct((seqs * blocks * QB, pairs * PAIR), BF16),
            jax.ShapeDtypeStruct((seqs, pairs, 2, blocks * QB), F32),
        ),
        compiler_params=pltpu.CompilerParams(
            dimension_semantics=("arbitrary",) * 2, vmem_limit_bytes=VMEM
        ),
        cost_estimate=SMALL,
        name="attention_forward",
    )(lo, offset, *[qkv] * (3 * pairs), starts[:, None, :])


def bwd_kernel(halves, lo_ref, place_ref, q_ref, k_ref, v_ref, start_ref, *refs):
    o_refs, do_refs, l_refs = refs[:halves], refs[halves : 2 * halves], refs[2 * halves : 3 * halves]
    out_ref, kt_ref, dk_ref, dv_ref = refs[-4:]
    block = pl.program_id(1)
    blocks = pl.num_programs(1)
    @pl.when(block == 0)
    def _():
        kt_ref[...] = k_ref[...].T
        dk_ref[...] = jnp.zeros_like(dk_ref)
        dv_ref[...] = jnp.zeros_like(dv_ref)

    mine = block // (blocks // halves) == place_ref[0]

    def pick(two, index=slice(None)):
        if halves == 1:
            return two[0][index]
        return jnp.where(mine, two[0][index], two[1][index])

    row_start = start_ref[...]
    query_pos = block * QB + lax.broadcasted_iota(jnp.int32, (1, QB), 1)
    key_iota = lax.broadcasted_iota(jnp.int32, (KB, QB), 0)
    first = lo_ref[pl.program_id(0), block]
    last = (block + 1) * (QB // KB)
    rows = pl.ds(pl.multiple_of(block * QB, QB), QB)
    q_heads = split_pair(q_ref[...])
    g_pair = pick(do_refs)
    g_heads = split_pair(g_pair)
    prod = (g_pair.astype(F32) * pick(o_refs).astype(F32)).T
    deltas = [jnp.sum(prod[h * HD : (h + 1) * HD], axis=0, keepdims=True) for h in range(2)]
    lses = [pick(l_refs, slice(h, h + 1)) for h in range(2)]

    def chunk(j, carry):
        base = pl.multiple_of(j * KB, KB)
        window = pl.ds(base, KB)
        keys = k_ref[window, :]
        vals = v_ref[window, :]
        key_pos = key_iota + base
        ok = (key_pos >= row_start) & (key_pos <= query_pos)
        new = []
        dv = dv_ref[window, :]
        dk = dk_ref[window, :]
        for h in range(2):
            s = jnp.where(ok, dot(keys, q_heads[h], NT) * SCORE_SCALE, NEG)
            p = jnp.exp2(s - lses[h])
            dp = dot(vals, g_heads[h], NT)
            ds = (p * (dp - deltas[h])).astype(BF16)
            dv = dv + dot(p.astype(BF16), g_heads[h], NN)
            dk = dk + dot(ds, q_heads[h], NN)
            kt = kt_ref[h * HD : (h + 1) * HD, window]
            new.append(carry[h] + dot(kt, ds, NN))
        dv_ref[window, :] = dv
        dk_ref[window, :] = dk
        return tuple(new)

    dq = lax.fori_loop(first, last, chunk, tuple(jnp.zeros((HD, QB), F32) for _ in range(2)))
    out_ref[rows, :PAIR] = (jnp.concatenate(dq, axis=0) * 0.125).T.astype(BF16)

    @pl.when(block == blocks - 1)
    def _():
        out_ref[:, PAIR : 2 * PAIR] = (dk_ref[...] * 0.125).astype(BF16)
        out_ref[:, 2 * PAIR :] = dv_ref[...].astype(BF16)


def attention_backward(pair, qkv, o_rows, d_o_rows, lse_rows, column, starts, lo, place, before):
    seqs, length = starts.shape
    nq = length // QB
    halves = len(o_rows)
    half = nq // halves

    def row(g, s, b, place):
        if halves == 1:
            return s, b, s * nq + b
        at = jnp.clip(b - jnp.bitwise_xor(place[0], g) * half, 0, half - 1)
        return s, at, at

    def rows_of(g, col):
        return pl.BlockSpec((QB, PAIR), lambda s, b, lo, place: (row(g, s, b, place)[2], col))

    def lse_of(g):
        return pl.BlockSpec(
            (None, None, 2, QB), lambda s, b, lo, place: (s, column, 0, row(g, s, b, place)[1])
        )

    in_specs = [
        pl.BlockSpec((QB, PAIR), lambda s, b, lo, place: (s * nq + b, 3 * pair)),
        pl.BlockSpec((length, PAIR), lambda s, b, lo, place: (s, 3 * pair + 1)),
        pl.BlockSpec((length, PAIR), lambda s, b, lo, place: (s, 3 * pair + 2)),
        pl.BlockSpec((None, 1, QB), lambda s, b, lo, place: (s, 0, b)),
        *[rows_of(g, column) for g in range(halves)],
        *[rows_of(g, pair) for g in range(halves)],
        *[lse_of(g) for g in range(halves)],
    ]
    operands = [qkv, qkv, qkv, starts[:, None, :], *o_rows, *d_o_rows, *lse_rows]
    alias = {}
    if before is not None:
        alias = {2 + len(operands): 0}
        in_specs.append(pl.BlockSpec(memory_space=pl.ANY))
        operands.append(before)
    return pl.pallas_call(
        functools.partial(bwd_kernel, halves),
        grid_spec=pltpu.PrefetchScalarGridSpec(
            num_scalar_prefetch=2,
            grid=(seqs, nq),
            in_specs=in_specs,
            out_specs=pl.BlockSpec((length, 3 * PAIR), lambda s, b, lo, place: (s, pair)),
            scratch_shapes=[
                pltpu.VMEM((PAIR, length), BF16),
                pltpu.VMEM((length, PAIR), F32),
                pltpu.VMEM((length, PAIR), F32),
            ],
        ),
        out_shape=jax.ShapeDtypeStruct(qkv.shape, BF16),
        input_output_aliases=alias,
        compiler_params=pltpu.CompilerParams(
            dimension_semantics=("arbitrary", "arbitrary"), vmem_limit_bytes=VMEM
        ),
        cost_estimate=SMALL,
        name="attention_backward",
    )(lo, place, *operands)


def segment_bounds(segment_ids):
    starts = jnp.sum((segment_ids[:, None, :] < segment_ids[:, :, None]).astype(jnp.int32), axis=2)
    return starts, starts[:, ::QB] // KB


ROWS = 256
HIDDEN_BLOCK = 1024
NZ, NX, NC = 4, 2, 2


def unit_rows(v):
    centered = v - jnp.mean(v, axis=-1, keepdims=True)
    scale = lax.rsqrt(jnp.mean(centered * centered, axis=-1, keepdims=True) + EPS)
    return centered * scale, scale


def norm_back(normed, scale, inner):
    return scale * (
        inner
        - jnp.mean(inner, axis=-1, keepdims=True)
        - normed * jnp.mean(inner * normed, axis=-1, keepdims=True)
    )


def rows_sum(v):
    return jnp.sum(v, axis=0, keepdims=True)


def store_turned(ref, block, by_device):
    turned = block.T
    if not by_device:
        ref[...] = turned
        return
    size = turned.shape[0] // (NZ * NX * NC)
    for z in range(NZ):
        for x in range(NX):
            for c in range(NC):
                old = ((z * NX + x) * NC + c) * size
                new = ((c * NX + x) * NZ + z) * size
                ref[new : new + size, :] = turned[old : old + size]


def turned_spec(features):
    return pl.BlockSpec((features, ROWS), lambda i, *_: (0, i))


def fixed(shape):
    return pl.BlockSpec(shape, lambda *_: (0,) * len(shape), pipeline_mode=pl.Buffered(1))


def call(body, name, grid, ins, outs, shapes, operands, prefetch=(), scratch=(), vmem=VMEM):
    return pl.pallas_call(
        body,
        grid_spec=pltpu.PrefetchScalarGridSpec(
            num_scalar_prefetch=len(prefetch),
            grid=grid,
            in_specs=ins,
            out_specs=outs,
            scratch_shapes=scratch,
        ),
        out_shape=shapes,
        compiler_params=pltpu.CompilerParams(
            dimension_semantics=("arbitrary",) * len(grid), vmem_limit_bytes=vmem
        ),
        cost_estimate=SMALL,
        name=name,
    )(*prefetch, *operands)


def shaped(rows, cols, dtype):
    return jax.ShapeDtypeStruct((rows, cols), dtype)


def row_spec(cols):
    return pl.BlockSpec((ROWS, cols), lambda i, *_: (i, 0))


def shifted_spec(cols):
    return pl.BlockSpec((ROWS, cols), lambda i, at, *_: (at[0] + i, 0))


def first_norm_kernel(turn, x_ref, gain_ref, bias_ref, u_ref, turned_ref):
    normed, _ = unit_rows(x_ref[...].astype(F32))
    u = (normed * gain_ref[0:1, :] + bias_ref[0:1, :]).astype(BF16)
    u_ref[...] = u
    store_turned(turned_ref, u, turn)


def first_norm(turn, inputs, gain, bias):
    tokens, features = inputs.shape
    return call(
        functools.partial(first_norm_kernel, turn),
        "first_norm",
        (tokens // ROWS,),
        [row_spec(features), fixed(gain.shape), fixed(bias.shape)],
        [row_spec(features), turned_spec(features)],
        [shaped(tokens, features, BF16), shaped(features, tokens, BF16)],
        [inputs, gain, bias],
        vmem=24 << 20,
    )


class Blocks:
    def __init__(self, operands, specs, load):
        self.operands, self.specs, self.load = operands, specs, load


def whole_blocks(weight):
    steps = weight.shape[1] // HIDDEN_BLOCK
    spec = pl.BlockSpec(
        (weight.shape[0], HIDDEN_BLOCK), lambda j, *_: (0, jnp.minimum(j, steps - 1))
    )

    def load(at_ref, step, refs, hold_ref):
        hold_ref[...] = refs[0][...]

    return Blocks([weight], [spec], load)


def piece_blocks(groups, columns):
    rows = groups[0][0].shape[1]
    steps = columns // HIDDEN_BLOCK
    operands, specs = [], []
    for g, pieces in enumerate(groups):
        for piece in pieces:
            operands.append(piece)
            specs.append(
                pl.BlockSpec(
                    (NZ, rows, HIDDEN_BLOCK),
                    lambda j, *_, g=g: (0, 0, jnp.clip(j - g * steps, 0, steps - 1)),
                )
            )

    def load(at_ref, step, refs, hold_ref):
        for g in range(len(groups)):

            @pl.when(step // steps == g)
            def _(g=g):
                place_pieces(at_ref, refs[4 * g : 4 * g + 4], hold_ref, rows)

    return Blocks(operands, specs, load)


def place_pieces(at_ref, refs, hold_ref, rows):
    z, x, c = at_ref[1], at_ref[2], at_ref[3]
    for n, ref in enumerate(refs):
        dx, dc = n % 2, n // 2
        for k in range(NZ):
            index = lax.rem(z - k + NZ, NZ) * NX + lax.bitwise_xor(x, dx)
            row = pl.multiple_of((index * NC + lax.bitwise_xor(c, dc)) * rows, rows)
            hold_ref[pl.ds(row, rows), :] = ref[k]


def middle_kernel(turn, groups, pieces, at_ref, *refs):
    o_refs, w_refs = refs[:groups], refs[groups : groups + pieces]
    x_ref, gain_ref, bias_ref, ob_ref = refs[groups + pieces : groups + pieces + 4]
    attn_ref, resid_ref, u_ref, o_ref, turned_ref, w_ref = refs[groups + pieces + 4 :]
    width = w_refs[0].shape[2] if pieces > 1 else 0

    @pl.when(pl.program_id(0) == 0)
    def _():
        if pieces == 1:
            w_ref[...] = w_refs[0][...]
        else:
            for g in range(pieces // 4):
                place_pieces(
                    at_ref,
                    w_refs[4 * g : 4 * g + 4],
                    w_ref.at[:, g * width : (g + 1) * width],
                    w_refs[0].shape[1],
                )

    attn = ob_ref[0:1, :]
    width = o_refs[0].shape[1]
    for g in range(groups):
        cols = slice(g * width, (g + 1) * width)
        o_ref[:, cols] = o_refs[g][...]
        attn = attn + dot(o_refs[g][...], w_ref[:, cols], NT)
    attn_ref[...] = attn
    normed, _ = unit_rows(attn)
    resid = x_ref[...].astype(F32) + normed * gain_ref[1:2, :] + bias_ref[1:2, :]
    resid_ref[...] = resid
    normed, _ = unit_rows(resid)
    u = (normed * gain_ref[2:3, :] + bias_ref[2:3, :]).astype(BF16)
    u_ref[...] = u
    store_turned(turned_ref, u, turn)


def middle(turn, at, o_groups, weight_out, inputs, gain, bias, out_bias):
    rows, width = o_groups[0].shape
    features = inputs.shape[1]
    if len(weight_out) == 1:
        weight_specs = [fixed(weight_out[0].shape)]
    else:
        part = features * 4 // len(weight_out)
        last = weight_out[0].shape[2] // part - 1
        shape = (NZ, weight_out[0].shape[1], part)
        spec = pl.BlockSpec(shape, lambda *_: (0, 0, last), pipeline_mode=pl.Buffered(1))
        weight_specs = [spec] * len(weight_out)
    return call(
        functools.partial(middle_kernel, turn, len(o_groups), len(weight_out)),
        "middle",
        (rows // ROWS,),
        [row_spec(width)] * len(o_groups)
        + weight_specs
        + [shifted_spec(features)]
        + [fixed(a.shape) for a in (gain, bias, out_bias)],
        [row_spec(features)] * 4 + [turned_spec(features), fixed((features, features))],
        [shaped(rows, features, d) for d in (F32, F32, BF16, BF16)]
        + [shaped(features, rows, BF16), shaped(features, features, BF16)],
        [*o_groups, *weight_out, inputs, gain, bias, out_bias],
        prefetch=[at],
    )


GELU_C = math.sqrt(2.0 / math.pi)


def gelu_tanh_of(z):
    square = z * z
    return square, jnp.tanh(z * (GELU_C + (GELU_C * 0.044715) * square))


def later_spec(cols, steps, shift=False):
    if shift:
        return pl.BlockSpec((ROWS, cols), lambda j, at, *_: (at[0] + jnp.maximum(j - steps, 0), 0))
    return pl.BlockSpec((ROWS, cols), lambda j, *_: (jnp.maximum(j - steps, 0), 0))


def later_turned(features, steps):
    return pl.BlockSpec((features, ROWS), lambda j, *_: (0, jnp.maximum(j - steps, 0)))


def column_spec(rows, steps):
    return pl.BlockSpec((rows, HIDDEN_BLOCK), lambda j, *_: (0, jnp.minimum(j, steps - 1)))


def feed_kernel(up, down, steps, at_ref, u_ref, b_ref, *refs):
    n, m = len(up.operands), len(down.operands)
    up_refs, down_refs = refs[:n], refs[n : n + m]
    resid_ref, dy_ref, gain_ref, bias_ref, ob_ref = refs[n + m : n + m + 5]
    pre_ref, out_ref, d_ref, turned_ref, sum_ref, up_hold, down_hold, total_ref = refs[n + m + 5 :]
    step = pl.program_id(0)
    rows = u_ref.shape[0]

    @pl.when(step == 0)
    def _():
        total_ref[...] = jnp.zeros_like(total_ref)
        sum_ref[...] = jnp.zeros_like(sum_ref)

    @pl.when(step < steps)
    def _():
        up.load(at_ref, step, up_refs, up_hold)
        down.load(at_ref, step, down_refs, down_hold)
        for r in range(0, rows, ROWS):
            part = slice(r, r + ROWS)
            z = dot(u_ref[part, :], up_hold[...], NN) + b_ref[...]
            pre_ref[part, :] = z.astype(BF16)
            _, t = gelu_tanh_of(z)
            act = (z * (0.5 + 0.5 * t)).astype(BF16)
            total_ref[part, :] += dot(act, down_hold[...], NT)

    @pl.when(step >= steps)
    def _():
        mlp = total_ref[pl.ds(pl.multiple_of((step - steps) * ROWS, ROWS), ROWS), :] + ob_ref[1:2, :]
        normed, scale = unit_rows(mlp)
        out_ref[...] = (resid_ref[...] + normed * gain_ref[3:4, :] + bias_ref[3:4, :]).astype(BF16)
        dy = dy_ref[...].astype(F32)
        d_mlp = norm_back(normed, scale, dy * gain_ref[3:4, :]).astype(BF16)
        d_ref[...] = d_mlp
        store_turned(turned_ref, d_mlp, False)
        sum_ref[0:1, :] += rows_sum(normed * dy)
        sum_ref[1:2, :] += rows_sum(dy)
        sum_ref[2:3, :] += rows_sum(d_mlp.astype(F32))


def feed(at, u, up, down, hidden_bias, resid, cotangent, gain, bias, out_bias):
    rows, features = u.shape
    hidden = hidden_bias.shape[1]
    steps = hidden // HIDDEN_BLOCK
    return call(
        functools.partial(feed_kernel, up, down, steps),
        "feed",
        (steps + rows // ROWS,),
        [fixed(u.shape), column_spec(1, steps), *up.specs, *down.specs]
        + [later_spec(features, steps), later_spec(features, steps, True)]
        + [fixed(a.shape) for a in (gain, bias, out_bias)],
        [column_spec(rows, steps), later_spec(features, steps), later_spec(features, steps)]
        + [later_turned(features, steps), fixed((8, features))],
        [shaped(rows, hidden, BF16), shaped(rows, features, BF16), shaped(rows, features, BF16)]
        + [shaped(features, rows, BF16), shaped(8, features, F32)],
        [u, hidden_bias, *up.operands, *down.operands, resid, cotangent, gain, bias, out_bias],
        prefetch=[at],
        scratch=[
            pltpu.VMEM((features, HIDDEN_BLOCK), BF16),
            pltpu.VMEM((features, HIDDEN_BLOCK), BF16),
            pltpu.VMEM((rows, features), F32),
        ],
    )


def feed_back_kernel(turn, groups, up, down, steps, at_ref, d_ref, ut_ref, pre_ref, *refs):
    n, m = len(up.operands), len(down.operands)
    up_refs, down_refs = refs[:n], refs[n : n + m]
    resid_ref, attn_ref, dy_ref, wo_ref, gain_ref = refs[n + m : n + m + 5]
    refs = refs[n + m + 5 :]
    send_ref, keep_ref, hid_ref, d_resid_ref, sum_ref, turned_ref = refs[:6]
    d_o_refs = refs[6 : 6 + groups]
    up_hold, down_hold, total_ref = refs[6 + groups :]
    step = pl.program_id(0)
    rows, features = d_ref.shape
    half = features // NC

    @pl.when(step == 0)
    def _():
        total_ref[...] = jnp.zeros_like(total_ref)
        sum_ref[...] = jnp.zeros_like(sum_ref)

    @pl.when(step < steps)
    def _():
        up.load(at_ref, step, up_refs, up_hold)
        down.load(at_ref, step, down_refs, down_hold)
        column_sum = 0.0
        d_pres = []
        for r in range(0, rows, ROWS):
            part = slice(r, r + ROWS)
            d_act = dot(d_ref[part, :], down_hold[...], NN)
            z = pre_ref[part, :].astype(F32)
            square, t = gelu_tanh_of(z)
            gate = 0.5 + 0.5 * t
            slope = gate + (1.0 - t * t) * (
                z * (0.5 * GELU_C + (1.5 * GELU_C * 0.044715) * square)
            )
            d_pre = (slope * d_act).astype(BF16)
            d_pres.append(d_pre)
            column_sum = column_sum + rows_sum(d_pre.astype(F32))
            total_ref[part, :] += dot(d_pre, up_hold[...], NT)
        hid_ref[...] = column_sum
        d_pre = jnp.concatenate(d_pres, axis=0)
        c = at_ref[3]
        there = pl.ds(pl.multiple_of((1 - c) * half, half), half)
        here = pl.ds(pl.multiple_of(c * half, half), half)
        send_ref[...] = dot(ut_ref[there, :], d_pre, NN).astype(BF16)
        keep_ref[...] = dot(ut_ref[here, :], d_pre, NN).astype(BF16)

    @pl.when(step >= steps)
    def _():
        d_u = total_ref[pl.ds(pl.multiple_of((step - steps) * ROWS, ROWS), ROWS), :]
        normed, scale = unit_rows(resid_ref[...])
        sum_ref[0:1, :] += rows_sum(normed * d_u)
        sum_ref[1:2, :] += rows_sum(d_u)
        d_resid = dy_ref[...].astype(F32) + norm_back(normed, scale, d_u * gain_ref[2:3, :])
        d_resid_ref[...] = d_resid
        normed, scale = unit_rows(attn_ref[...])
        sum_ref[2:3, :] += rows_sum(normed * d_resid)
        sum_ref[3:4, :] += rows_sum(d_resid)
        d_attn = norm_back(normed, scale, d_resid * gain_ref[1:2, :]).astype(BF16)
        sum_ref[4:5, :] += rows_sum(d_attn.astype(F32))
        store_turned(turned_ref, d_attn, turn)
        width = d_o_refs[0].shape[1]
        for g in range(groups):
            d_o_refs[g][...] = dot(d_attn, wo_ref[:, g * width : (g + 1) * width], NN).astype(BF16)


def feed_back(turn, groups, at, d_mlp, u_turned, pre, up, down, resid, attn, cotangent, weight_out, gain):
    rows, features = d_mlp.shape
    hidden = pre.shape[1]
    steps = hidden // HIDDEN_BLOCK
    width = features // groups
    half = features // NC
    return call(
        functools.partial(feed_back_kernel, turn, groups, up, down, steps),
        "feed_back",
        (steps + rows // ROWS,),
        [fixed(d_mlp.shape), fixed(u_turned.shape)]
        + [column_spec(rows, steps), *up.specs, *down.specs]
        + [later_spec(features, steps), later_spec(features, steps), later_spec(features, steps, True)]
        + [fixed(weight_out.shape), fixed(gain.shape)],
        [column_spec(half, steps), column_spec(half, steps)]
        + [column_spec(1, steps), later_spec(features, steps), fixed((8, features))]
        + [later_turned(features, steps)]
        + [later_spec(width, steps)] * groups,
        [shaped(half, hidden, BF16), shaped(half, hidden, BF16)]
        + [shaped(1, hidden, F32), shaped(rows, features, F32), shaped(8, features, F32)]
        + [shaped(features, rows, BF16)]
        + [shaped(rows, width, BF16)] * groups,
        [d_mlp, u_turned, pre, *up.operands, *down.operands]
        + [resid, attn, cotangent, weight_out, gain],
        prefetch=[at],
        scratch=[
            pltpu.VMEM((features, HIDDEN_BLOCK), BF16),
            pltpu.VMEM((features, HIDDEN_BLOCK), BF16),
            pltpu.VMEM((rows, features), F32),
        ],
    )


def d_in_kernel(at_ref, dq_ref, w_ref, x_ref, part_ref, sum_ref, head_ref):
    @pl.when(pl.program_id(0) == 0)
    def _():
        sum_ref[...] = jnp.zeros_like(sum_ref)
        head_ref[...] = jnp.zeros_like(head_ref)

    d_qkv = dq_ref[...]
    part = dot(d_qkv, w_ref[...], NT).astype(BF16)
    part_ref[...] = part
    part = part.astype(F32)
    normed, _ = unit_rows(x_ref[...].astype(F32))
    sum_ref[0:1, :] += rows_sum(normed * part)
    sum_ref[1:2, :] += rows_sum(part)
    head_ref[0:1, :] += rows_sum(d_qkv.astype(F32))


def d_in(row_at, rows, d_qkv, weight_qkv, inputs):
    features, width = weight_qkv.shape
    return call(
        d_in_kernel,
        "d_in",
        (rows // ROWS,),
        [shifted_spec(width), fixed(weight_qkv.shape), shifted_spec(features)],
        [row_spec(features), fixed((8, features)), fixed((8, width))],
        [shaped(rows, features, BF16), shaped(8, features, F32), shaped(8, width, F32)],
        [d_qkv, weight_qkv, inputs],
        prefetch=[row_at],
    )


def last_kernel(terms, at_ref, *refs):
    x_ref, d_resid_ref, gain_ref, out_ref = refs[terms:]
    d_u = sum(r[...].astype(F32) for r in refs[:terms])
    normed, scale = unit_rows(x_ref[...].astype(F32))
    out_ref[...] = (d_resid_ref[...] + norm_back(normed, scale, d_u * gain_ref[0:1, :])).astype(BF16)


def last(row_at, parts, inputs, d_resid, gain):
    rows, features = d_resid.shape
    return call(
        functools.partial(last_kernel, len(parts)),
        "last",
        (rows // ROWS,),
        [row_spec(features)] * len(parts) + [shifted_spec(features), row_spec(features), fixed(gain.shape)],
        row_spec(features),
        shaped(rows, features, BF16),
        [*parts, inputs, d_resid, gain],
        prefetch=[row_at],
    )


def grad_rows_kernel(terms, at_ref, left_ref, right_ref, *refs):
    total = dot(left_ref[...], right_ref[...], NN)
    for r in refs[:terms]:
        total = total + r[...].astype(F32)
    refs[terms][...] = total.astype(BF16)


def grad_rows(left, at, right, terms=()):
    _, rows, tokens = left.shape
    columns = right.shape[1]
    block = math.gcd(columns, 512)
    return call(
        functools.partial(grad_rows_kernel, len(terms)),
        "grad_rows",
        (columns // block,),
        [
            pl.BlockSpec((None, rows, tokens), lambda j, at: (at[0], 0, 0)),
            pl.BlockSpec((tokens, block), lambda j, at: (0, j)),
        ]
        + [pl.BlockSpec((None, rows, block), lambda j, at: (at[1], 0, j))] * len(terms),
        pl.BlockSpec((rows, block), lambda j, at: (0, j)),
        shaped(rows, columns, BF16),
        [left, right, *terms],
        prefetch=[at],
    )


def grad_down_kernel(left_ref, pre_ref, out_ref):
    z = pre_ref[...].astype(F32)
    _, t = gelu_tanh_of(z)
    out_ref[...] = dot(left_ref[...], (z * (0.5 + 0.5 * t)).astype(BF16), NN).astype(BF16)


def grad_down_of(d_mlp_turned, pre):
    features, rows = d_mlp_turned.shape
    hidden = pre.shape[1]
    column = lambda size: pl.BlockSpec((size, 512), lambda j: (0, j))
    return call(
        grad_down_kernel,
        "grad_down",
        (hidden // 512,),
        [fixed(d_mlp_turned.shape), column(rows)],
        column(features),
        shaped(features, hidden, BF16),
        [d_mlp_turned, pre],
    )


def merge_kernel(outs, ups, at_ref, *refs):
    out_refs, up_refs, both_refs, to_ref = refs[:outs], refs[outs : outs + ups], refs[outs + ups : -1], refs[-1]

    def fill(parts):
        to_ref[...] = sum(r[...].astype(F32) for r in (*parts, *both_refs)).astype(BF16)

    @pl.when(pl.program_id(0) == 0)
    def _():
        fill(out_refs)

    @pl.when(pl.program_id(0) > 0)
    def _():
        fill(up_refs)


def merge(at, rows, outs, ups, group, both=()):
    width = outs[0].shape[1] // 2
    hidden = ups[0].shape[1] // 2
    steps = hidden // width
    pick_row = lambda a, at: at[0] if a.shape[0] > rows else 0
    specs = [pl.BlockSpec((rows, width), lambda j, at, a=a: (pick_row(a, at), group)) for a in outs]
    specs += [
        pl.BlockSpec(
            (rows, width),
            lambda j, at, a=a: (pick_row(a, at), group * steps + jnp.maximum(j - 1, 0)),
        )
        for a in ups
    ]
    specs += [pl.BlockSpec((rows, width), lambda j, at, a=a: (pick_row(a, at), j)) for a in both]
    return call(
        functools.partial(merge_kernel, len(outs), len(ups)),
        "merge",
        (1 + steps,),
        specs,
        pl.BlockSpec((rows, width), lambda j, at: (0, j)),
        shaped(rows, width + hidden, BF16),
        [*outs, *ups, *both],
        prefetch=[at],
    )


def tie(*values):
    return lax.optimization_barrier(values)


def pick(array, index, axis=0):
    return lax.dynamic_index_in_dim(array, index, axis, keepdims=False)


def add(a, b):
    return (a.astype(F32) + b.astype(F32)).astype(BF16)


def flips(bit):
    return [(i, i ^ bit) for i in range(NZ * NX * NC)]


def z_pairs(shift):
    return [(i, (i + shift * NX * NC) % (NZ * NX * NC)) for i in range(NZ * NX * NC)]


def swap_core(a):
    return lax.ppermute(a, "dp", flips(1))


def swap_x(a):
    return lax.ppermute(a, "dp", flips(NC))


def swap_y(a):
    return lax.ppermute(a, "tensor", [(0, 1), (1, 0)])


def spread_z(shard):
    return [shard] + [lax.ppermute(shard, "dp", z_pairs(k)) for k in range(1, NZ)]


def assemble_qkv_kernel(pos_ref, *refs):
    out_ref = refs[-1]
    z, x, c = pos_ref[0], pos_ref[1], pos_ref[2]
    kinds, _, width = refs[0].shape[1:]
    for n, ref in enumerate(refs[:-1]):
        for k in range(NZ):
            to = out_ref.at[
                lax.rem(z - k + NZ, NZ), lax.bitwise_xor(x, n % 2), lax.bitwise_xor(c, n // 2)
            ]
            for p in range(width // PAIR):
                for kind in range(kinds):
                    at = (p * kinds + kind) * PAIR
                    to[:, at : at + PAIR] = ref[k, kind, :, p * PAIR : (p + 1) * PAIR]


def assemble_qkv(position, pieces):
    _, kinds, rows, width = pieces[0].shape
    step = 16
    out = pl.pallas_call(
        assemble_qkv_kernel,
        grid_spec=pltpu.PrefetchScalarGridSpec(
            num_scalar_prefetch=1,
            grid=(rows // step,),
            in_specs=[pl.BlockSpec((NZ, kinds, step, width), lambda i, pos: (0, 0, i, 0))] * 4,
            out_specs=pl.BlockSpec(
                (NZ, NX, NC, step, kinds * width), lambda i, pos: (0, 0, 0, i, 0)
            ),
        ),
        out_shape=jax.ShapeDtypeStruct((NZ, NX, NC, rows, kinds * width), BF16),
        compiler_params=pltpu.CompilerParams(
            dimension_semantics=("arbitrary",), vmem_limit_bytes=24 << 20
        ),
        cost_estimate=SMALL,
        name="assemble_qkv",
    )(position, *pieces)
    return out.reshape(-1, kinds * width)


class Staged:
    turn = True

    def __init__(self):
        index = lax.axis_index("dp")
        self.z, self.x, self.c = index // (NX * NC), (index // NC) % NX, index % NC
        self.position = jnp.stack([self.z, self.x, self.c]).astype(jnp.int32)

    def gather_first(self, u1, shard_qkv, shard_out, shard_up, shard_down):
        self.hidden = shard_up.shape[1]
        first = spread_z(shard_qkv)
        u1, *first, shard = tie(u1, *first, jnp.concatenate([shard_up, shard_out], axis=1))
        column = jnp.stack(first)
        own = spread_z(shard)
        both_down = jnp.concatenate([shard_down, swap_y(shard_down)], axis=1)
        from_x, both_down, *own = tie(swap_x(column), both_down, *own)
        self.own = jnp.stack(own)
        self.own_x, self.other = swap_x(self.own), swap_y(self.own)
        self.down = lax.all_gather(both_down, "dp", axis=0, tiled=True)
        pieces = [column, from_x]
        pieces += [swap_core(a) for a in pieces]
        return u1, assemble_qkv(self.position, pieces)

    def beside_forward(self, index, values):
        if index == 0:
            *values, self.own, self.own_x, self.other = tie(*values, self.own, self.own_x, self.other)
            self.other_x = swap_x(self.other)
            self.cores = [swap_core(a) for a in (self.own, self.own_x, self.other)]
        if index == 1:
            n = len(values)
            values = tie(*values, *self.cores)
            values, self.cores = values[:n], list(values[n:])
        if index == 2:
            *values, self.other_x = tie(*values, self.other_x)
            self.cores.append(swap_core(self.other_x))
        return values

    def gather_last(self, *attended):
        groups = [
            [self.own, self.own_x, *self.cores[:2]],
            [self.other, self.other_x, *self.cores[2:]],
        ]
        up = piece_blocks(groups, self.hidden)
        return attended, [p for g in groups for p in g], up, whole_blocks(self.down)

    def reduce_down(self, grad):
        self.down = lax.psum_scatter(grad, "dp", scatter_dimension=0, tiled=True)

    def rows_times(self, left, index, right, terms=()):
        parts = NC if not terms else NC * NX
        left = left.reshape(parts, -1, left.shape[-1])
        return grad_rows(left, jnp.stack(index), right, terms)

    def reduce_first(self, send, keep, turned, o_own, d_o_rows):
        up_there = swap_core(send)
        out_there = swap_core(self.rows_times(turned, [1 - self.c, self.c], o_own))
        out_keep = self.rows_times(turned, [self.c, self.c], o_own)
        out_there, up_there, out_keep, *d_o_rows = tie(out_there, up_there, out_keep, *d_o_rows)
        self.outs, self.ups = [out_keep, out_there], [keep, up_there]
        zero = jnp.zeros((1,), jnp.int32)
        send, *d_o_rows = tie(merge(zero, keep.shape[0], self.outs, self.ups, 1), *d_o_rows)
        self.from_y = swap_y(send)
        return d_o_rows

    def beside_backward(self, index, d_qkv):
        if index == 2:
            d_qkv, self.from_y = tie(d_qkv, self.from_y)
            rows = self.from_y.shape[0] // NX

            def part(x):
                return merge(jnp.reshape(x, (1,)), rows, self.outs, self.ups, 0, [self.from_y])

            send, d_qkv = tie(part(1 - self.x), d_qkv)
            self.from_x, self.here = swap_x(send), part
        if index == 3:
            d_qkv, self.from_x = tie(d_qkv, self.from_x)
        return d_qkv

    def reduce_z(self, total):
        total = total.reshape(NZ, -1, total.shape[1])
        out = pick(total, self.z).astype(F32)
        for k in range(1, NZ):
            piece = pick(total, lax.rem(self.z + k, NZ))
            out = out + lax.ppermute(piece, "dp", z_pairs(k)).astype(F32)
        return out

    def tail(self, turned, d_qkv, d_in_own, terms):
        send = self.rows_times(turned, [1 - self.c, self.c], d_qkv)
        there = swap_core(send)
        d_qkv, send, *parts = tie(d_qkv, send, *self.outs, *self.ups)
        self.outs, self.ups = parts[:2], parts[2:]
        there, total = tie(there, add(self.here(self.x), self.from_x))
        from_core = there.reshape(NX, -1, there.shape[-1])
        parts = lambda x, d_qkv: self.rows_times(turned, [self.c * NX + x, x], d_qkv, [from_core])
        send, d_qkv = tie(parts(1 - self.x, d_qkv), d_qkv)
        own = d_in_own(d_qkv)
        keep = parts(self.x, d_qkv)
        there, received, keep, first, *rest = tie(swap_x(send), terms[1], keep, *own)
        own = [first, *rest]
        total = self.reduce_z(total)
        qkv = self.reduce_z(add(keep, there))
        width = self.outs[0].shape[1] // 2
        return own, total[:, width:], total[:, :width], qkv, [None, received]

    def reduce_down_last(self, terms):
        *terms, down = tie(*terms, self.down)
        half = down.shape[1] // 2
        return terms, down[:, :half].astype(F32) + swap_y(down[:, half:]).astype(F32)

    def exchange(self, parts):
        return [parts[0], swap_y(parts[1])]

    def total(self, vector):
        for bit in (1, NC, NX * NC, 2 * NX * NC):
            vector = vector + lax.ppermute(vector, "dp", flips(bit))
        return vector + swap_y(vector)


class Plain:
    turn = False

    def __init__(self):
        self.n = lax.axis_size("tensor")
        self.position = jnp.zeros((3,), jnp.int32)
        self.rank = lax.axis_index("tensor")

    def gather_groups(self, shard):
        own = lax.all_gather(shard, "dp", axis=0, tiled=True)
        every = lax.all_gather(own, "tensor", axis=0)
        return jnp.concatenate([pick(every, (self.rank + g) % self.n) for g in range(self.n)], axis=1)

    def gather_first(self, u1, shard_qkv, *shards):
        weights = [self.gather_groups(w) for w in shards]
        self.weights = [weights[:1], *(whole_blocks(w) for w in weights[1:])]
        every = lax.all_gather(shard_qkv, "dp", axis=1, tiled=True)
        pairs = jnp.split(every, every.shape[2] // PAIR, axis=2)
        return u1, jnp.concatenate([p[j] for p in pairs for j in range(3)], axis=1)

    def beside_forward(self, index, values):
        return values

    def gather_last(self, *attended):
        return attended, *self.weights

    def reduce_rows(self, grad):
        grads = self.absolute(jnp.split(grad, self.n, axis=1))
        own = lax.psum_scatter(grads, "tensor", scatter_dimension=0, tiled=True)
        return lax.psum_scatter(own[0], "dp", scatter_dimension=0, tiled=True).astype(F32)

    def reduce_down(self, grad):
        self.down = self.reduce_rows(grad)

    def reduce_first(self, send, keep, turned, o_own, d_o_rows):
        self.up = self.reduce_rows(jnp.concatenate([keep, send], axis=0))
        self.out = self.reduce_rows(dot(turned, o_own, NN).astype(BF16))
        return d_o_rows

    def beside_backward(self, index, d_qkv):
        return d_qkv

    def tail(self, turned, d_qkv, d_in_own, terms):
        grad = dot(turned, d_qkv, NN).astype(BF16)
        qkv = lax.psum_scatter(grad, "dp", scatter_dimension=0, tiled=True).astype(F32)
        return d_in_own(d_qkv), self.up, self.out, qkv, terms

    def reduce_down_last(self, terms):
        return terms, self.down

    def absolute(self, parts):
        order = (jnp.arange(self.n) - self.rank) % self.n
        return jnp.take(jnp.stack(parts), order, axis=0)

    def exchange(self, parts):
        got = lax.all_to_all(self.absolute(parts), "tensor", 0, 0, tiled=True)
        return [pick(got, (self.rank + g) % self.n) for g in range(self.n)]

    def total(self, vector):
        return lax.psum(vector, ("dp", "tensor"))


def per_device(
    staged,
    inputs,
    cotangent,
    segment_ids,
    w_qkv,
    w_out,
    w_fc1,
    w_fc2,
    norm_gain,
    norm_bias,
    head_bias,
    out_bias,
    fc1_bias,
):
    n = lax.axis_size("tensor")
    rank = lax.axis_index("tensor")
    comm = Staged() if staged else Plain()
    tokens, features = inputs.shape
    seqs, length = segment_ids.shape
    own_rows = tokens // n
    width = w_qkv.shape[2]
    hidden = w_fc1.shape[1]

    def group_slice(array, g, size, axis=0):
        return lax.dynamic_slice_in_dim(array, ((rank + g) % n) * size, size, axis)

    def scalar(value):
        return jnp.reshape(value, (1,)).astype(jnp.int32)

    row_at = [scalar(((rank + g) % n) * (own_rows // ROWS)) for g in range(n)]

    u1, turned1 = first_norm(comm.turn, inputs, norm_gain, norm_bias)
    u1, weight_qkv = comm.gather_first(
        u1,
        w_qkv.astype(BF16),
        w_out.T.astype(BF16),
        w_fc1.astype(BF16),
        w_fc2.T.astype(BF16),
    )
    pairs = width // PAIR
    heads_bias = group_slice(head_bias, 0, width, 1)
    qkv_bias = jnp.stack([heads_bias[0], jnp.zeros((width,), F32), heads_bias[1]])
    qkv_bias = qkv_bias.reshape(3, pairs, PAIR).transpose(1, 0, 2).reshape(-1)
    qkv = (dot(u1, weight_qkv, NN) + qkv_bias).astype(BF16)

    starts, lo = segment_bounds(segment_ids)
    blocks = length // QB
    halves = 2 if n == 2 and seqs == 1 else 1
    half = blocks // halves
    places = [(rank + g) % halves for g in range(halves)]
    per_call = math.gcd(pairs, 2)
    calls = pairs // per_call
    o_rows, lse_rows = ([[None] * calls for _ in range(halves)] for _ in range(2))
    received = [None] * calls
    index = 0
    for g in reversed(range(halves)):
        for i in range(calls):
            o, lse = attention_forward(
                i * per_call, per_call, qkv, starts, lo, scalar(places[g] * half), half
            )
            qkv, o, lse = comm.beside_forward(index, [qkv, o, lse])
            o_rows[g][i], lse_rows[g][i] = o, lse
            if g > 0:
                received[i] = comm.exchange([None, o])[1]
            index += 1
    if halves < n:
        whole = jnp.concatenate(o_rows[0], axis=1)
        o_groups = comm.exchange([group_slice(whole, g, own_rows) for g in range(n)])
        _, weight_out, up, down = comm.gather_last()
    else:
        o_groups, weight_out, up, down = comm.gather_last(*o_rows[0], *received)
        o_rows[0] = list(o_groups[:calls])

    at = jnp.concatenate([row_at[0], comm.position])
    attn, resid, u2, o_own, turned2, weight_out = middle(
        comm.turn, at, o_groups, weight_out, inputs, norm_gain, norm_bias, out_bias
    )
    hidden_bias = jnp.concatenate([group_slice(fc1_bias, g, hidden) for g in range(n)])
    pre, output, d_mlp, d_mlp_turned, sums3 = feed(
        at, u2, up, down, hidden_bias[None], resid, cotangent, norm_gain, norm_bias, out_bias
    )
    send, keep, bias_hidden, d_resid, sums12, turned_attn, *d_o = feed_back(
        comm.turn,
        n,
        at,
        d_mlp,
        turned2,
        pre,
        up,
        down,
        resid,
        attn,
        cotangent,
        weight_out,
        norm_gain,
    )
    d_mlp_turned, *d_o = tie(d_mlp_turned, *d_o)
    d_o_rows = comm.exchange(d_o)
    grad_down, *d_o_rows = tie(grad_down_of(d_mlp_turned, pre), *d_o_rows)
    comm.reduce_down(grad_down)
    if halves < n:
        order = (jnp.arange(n) - rank) % n
        d_o_rows = [jnp.take(jnp.stack(d_o_rows), order, axis=0).reshape(tokens, width)]
    d_o_rows = comm.reduce_first(send, keep, turned_attn, o_own, d_o_rows)

    d_qkv = None
    for pair in range(pairs):
        i, column = divmod(pair, per_call)
        d_qkv = attention_backward(
            pair,
            qkv,
            [o[i] for o in o_rows],
            d_o_rows,
            [l[i] for l in lse_rows],
            column,
            starts,
            lo,
            scalar(places[0]),
            d_qkv,
        )
        d_qkv = comm.beside_backward(pair, d_qkv)

    d_u1_parts, sums0, head_sums = [None] * n, 0.0, 0.0
    for g in reversed(range(1, n)):
        d_u1_parts[g], sums, head_row = d_in(row_at[g], own_rows, d_qkv, weight_qkv, inputs)
        d_u1_parts[g], d_qkv = tie(d_u1_parts[g], d_qkv)
        sums0, head_sums = sums0 + sums, head_sums + head_row[0]
    d_u1_terms = comm.exchange(d_u1_parts) if staged else None
    (d_u1_parts[0], sums, head_row), grad_up, grad_out, grad_qkv, d_u1_terms = comm.tail(
        turned1,
        d_qkv,
        lambda d_qkv: d_in(row_at[0], own_rows, d_qkv, weight_qkv, inputs),
        d_u1_terms,
    )
    sums0, head_sums = sums0 + sums, head_sums + head_row[0]
    if staged:
        d_u1_terms = [d_u1_parts[0], *d_u1_terms[1:]]
    else:
        d_u1_terms = comm.exchange(d_u1_parts)

    hidden_full = jnp.roll(bias_hidden[0], rank * hidden)
    head_terms = head_sums.reshape(pairs, 3, PAIR).transpose(1, 0, 2).reshape(3, width)[0::2]
    head_full = lax.dynamic_update_slice_in_dim(
        jnp.zeros(head_bias.shape, F32), head_terms, rank * width, 1
    )
    gains = [sums0[0], sums12[2], sums12[0], sums3[0]]
    shifts = [sums0[1], sums12[3], sums12[1], sums3[1]]
    rows = jnp.stack(gains + shifts + [sums12[4], sums3[2]])
    small = jnp.concatenate([rows, head_full, hidden_full.reshape(-1, features)])
    small, *d_u1_terms = tie(small, *d_u1_terms)
    small = comm.total(small)
    d_u1_terms, grad_down = comm.reduce_down_last(d_u1_terms)
    d_inputs = last(row_at[0], d_u1_terms, inputs, d_resid, norm_gain)

    grad_qkv = grad_qkv.reshape(-1, pairs, 3, PAIR).transpose(2, 0, 1, 3).reshape(3, -1, width)
    return (
        output,
        d_inputs,
        grad_qkv,
        grad_out.T,
        grad_up,
        grad_down.T,
        small[0:4],
        small[4:8],
        small[10:12],
        small[8:10],
        small[12:].reshape(-1),
    )


def solution(mesh):
    staged = mesh.shape["dp"] == NZ * NX * NC and mesh.shape["tensor"] == 2
    return jax.shard_map(
        functools.partial(per_device, staged),
        mesh=mesh,
        in_specs=(
            P("dp", None),
            P("dp", None),
            P("dp", None),
            P(None, "dp", "tensor"),
            P("tensor", "dp"),
            P("dp", "tensor"),
            P("tensor", "dp"),
            P(),
            P(),
            P(),
            P(),
            P(),
        ),
        out_specs=(
            P(("dp", "tensor"), None),
            P(("dp", "tensor"), None),
            P(None, "dp", "tensor"),
            P("tensor", "dp"),
            P("dp", "tensor"),
            P("tensor", "dp"),
            P(),
            P(),
            P(),
            P(),
            P(),
        ),
        check_vma=False,
    )
```

time: 699 us -> 570 us (0.82)
  Pallas kernels: 129 us -> 307 us
  matrix products: 146 us -> 8.5 us
  waiting for transfers between devices: 205 us -> 123 us
  other arithmetic: 68.9 us -> 20.2 us
  local copies, waits for them, and re-layouts: 59.8 us -> 36.8 us
  starting transfers between devices: 61.2 us -> 52 us
    pallas_call x9 -> x25, Pallas kernels: 129 us -> 307 us  [the longest x16 187 us: call(): pl.pallas_call(body, grid_spec=pltpu.PrefetchScalarGridSpec(num_scalar_pr...]
    dot_general x14 -> x1, matrix products: 146 us -> 8.5 us  [dot(): return lax.dot_general(a, b, dims, preferred_element_type=jnp.float32)]
    ppermute x33, waiting for transfers between devices: 183 us -> 117 us  [the longest x5 49.5 us: swap_x(): return lax.ppermute(a, 'dp', flips(NC))]
    reduce_sum x12 -> x0, other arithmetic: 31.4 us -> none  [the longest x1 6 us: per_device(): jnp.sum(normed1 * d_resid, axis=0)]
    ppermute x6, waiting for transfers between devices: 21.7 us -> 6.04 us  [reduce_z(): out = out + lax.ppermute(piece, 'dp', z_pairs(k)).astype(F32)]
    dynamic_slice x6 -> x0, local copies, waits for them, and re-layouts: 12.6 us -> none  [half_rows(): return lax.dynamic_index_in_dim(h, index, axis, keepdims=False)]
    convert_element_type x7 -> x2, other arithmetic: 13.3 us -> 2.21 us  [add(): return (a.astype(F32) + b.astype(F32)).astype(BF16)]
    ppermute x33, starting transfers between devices: 51.7 us -> 41.2 us  [the longest x6 11.5 us: spread_z(): lax.ppermute(shard, 'dp', z_pairs(k))]
  transfers between devices with their start and end apart: 41 -> 41, of which waited for: 16 -> 14; matrix products, arithmetic and copies ran while one was open for 21% -> 7% of each run, Pallas kernels for 19% -> 39%
where the time goes in v3:
time: 570 us; the launch traced here: 562 us
  Pallas kernels  307 us (54%)
  waiting for transfers between devices  123 us (22%)
  starting transfers between devices  52 us (9%)
  local copies, waits for them, and re-layouts  36.8 us (6%)
  other arithmetic  20.2 us (4%)
  between operations  14.8 us (3%)
  matrix products  8.5 us (1%)
    pallas_call x16, Pallas kernels, call(): pl.pallas_call(body, grid_spec=pltpu.PrefetchScalarGridSpec(num_scalar_pr...  187 us
    pallas_call x4, Pallas kernels, attention_backward(): pl.pallas_call(functools.partial(bwd_kernel, halves), grid_spec=pltpu.Pre...  70.3 us
    ppermute x5, waiting for transfers between devices, swap_x(): return lax.ppermute(a, 'dp', flips(NC))  49.5 us
    pallas_call x4, Pallas kernels, attention_forward(): pl.pallas_call(functools.partial(fwd_kernel, pairs), grid_spec=grid_spec,...  47.6 us
    ppermute x9, waiting for transfers between devices, swap_y(): return lax.ppermute(a, 'tensor', [(0, 1), (1, 0)])  32.4 us
    unnamed x84, local copies, waits for them, and re-layouts  22.5 us
    ppermute x6, waiting for transfers between devices, spread_z(): lax.ppermute(shard, 'dp', z_pairs(k))  17.8 us
    ppermute x4, waiting for transfers between devices, total(): vector = vector + lax.ppermute(vector, 'dp', flips(bit))  17.1 us
  transfers between devices with their start and end apart: 41, of which 14 were waited for; matrix products, arithmetic and copies ran while one was open for 7% of the time, Pallas kernels for 39%

profile of v3, /device:TPU:0, one launch (start us, length us, event | category | flops | bytes accessed | tf_op | source)
XLA Modules:
  0.0 562.1 jit_solution(12427505324313142515)
XLA Ops:
  8.2 3.1 collective-permute-start
  11.3 2.6 collective-permute-start.1
  17.3 2.2 copy-done
  20.9 4.2 first_norm.1
  25.1 2.0 copy-done.1
  27.1 2.1 copy-done.13
  29.4 1.6 collective-permute-start.3
  31.0 1.6 collective-permute-start.4
  32.6 2.1 collective-permute-start.5
  34.7 1.6 collective-permute-start.6
  38.9 6.3 %collective-permute-done.5 = bf16[64,2560]{1,0:T(8,128)(2,1)S(1)} collective-permute-done((bf16[64,2560]{1,0:T(8,128)(2,1)S(1)}, bf16[64,2560]{1,0:T(8,128)(2,1)S(1)}, u32[]{:S(2)}, u32[]{:S(2)}) %collective-permute-start.5) | collective-permute-done | bytes 327712 | tf_op jit(solution)/shard_map/ppermute | solution.py:810
  45.2 11.4 %collective-permute-done.6 = bf16[64,2560]{1,0:T(8,128)(2,1)S(1)} collective-permute-done((bf16[64,2560]{1,0:T(8,128)(2,1)S(1)}, bf16[64,2560]{1,0:T(8,128)(2,1)S(1)}, u32[]{:S(2)}, u32[]{:S(2)}) %collective-permute-start.6) | collective-permute-done | bytes 327712 | tf_op jit(solution)/shard_map/ppermute | solution.py:810
  57.5 1.8 convert_reduce_fusion
  60.7 2.4 pad_maximum_fusion.refs_4_.refs_0_
  71.2 1.7 assemble_qkv.1
  73.4 8.5 %add_convert_fusion.refs_0_.refs_1_.refs_2_.refs_3_.refs_4_.refs_5_.q_ref.k_ref.v_ref = bf16[2048,1536]{1,0:T(8,128)(2,1)} fusion(bf16[2048,1024]{1,0:T(8,128)(2,1)S(1)} %copy-done.14, bf16[1024,1536]{1,0:T(8,128)(2,1)S(1)} %bitcast.75, f32[1536]{0:T(1024)S(1)} %add.152), kind=kOutput, calls=%fused_computation.1 | convolution fusion | flops 6448742400 | bytes 13637632 | tf_op jit(solution)/shard_map/dot_general | solution.py:31
  81.9 11.2 %attention_forward.4 = (bf16[1024,256]{1,0:T(8,128)(2,1)}, f32[1,2,2,1024]{3,2,1,0:T(2,128)}) custom-call(s32[1,8]{1,0:T(1,128)} %and_select_fusion.lo_ref, s32[1]{0:T(128)} %bitcast.15.off_ref.at_ref, bf16[2048,1536]{1,0:T(8,128)(2,1)} %add_convert_fusion.refs_0_.refs_1_.refs_2_.refs_3_.refs_4_.refs_5_.q_ref.k_ref.v_ref, ...), custom_call_target="tpu_custom_call" | custom-call | flops 1 | bytes 1 | tf_op jit(solution)/shard_map/attention_forward/pallas_call | solution.py:104
  93.1 6.7 %collective-permute-done.10.refs_5_.refs_1_ = bf16[4,64,2560]{2,1,0:T(8,128)(2,1)} collective-permute-done((bf16[4,64,2560]{2,1,0:T(8,128)(2,1)}, bf16[4,64,2560]{2,1,0:T(8,128)(2,1)}, u32[]{:S(2)}, u32[]{:S(2)}) %collective-permute-start.10) | collective-permute-done | bytes 1310752 | tf_op jit(solution)/shard_map/ppermute | solution.py:802
  101.4 10.9 %attention_forward.5 = (bf16[1024,256]{1,0:T(8,128)(2,1)}, f32[1,2,2,1024]{3,2,1,0:T(2,128)}) custom-call(s32[1,8]{1,0:T(1,128)} %and_select_fusion.lo_ref, s32[1]{0:T(128)} %bitcast.15.off_ref.at_ref, bf16[2048,1536]{1,0:T(8,128)(2,1)} %add_convert_fusion.refs_0_.refs_1_.refs_2_.refs_3_.refs_4_.refs_5_.q_ref.k_ref.v_ref, ...), custom_call_target="tpu_custom_call" | custom-call | flops 1 | bytes 1 | tf_op jit(solution)/shard_map/attention_forward/pallas_call | solution.py:104
  112.4 13.0 %attention_forward.6 = (bf16[1024,256]{1,0:T(8,128)(2,1)}, f32[1,2,2,1024]{3,2,1,0:T(2,128)}) custom-call(s32[1,8]{1,0:T(1,128)} %and_select_fusion.lo_ref, s32[1]{0:T(128)} %bitcast.off_ref.at_ref, bf16[2048,1536]{1,0:T(8,128)(2,1)} %add_convert_fusion.refs_0_.refs_1_.refs_2_.refs_3_.refs_4_.refs_5_.q_ref.k_ref.v_ref, ...), custom_call_target="tpu_custom_call" | custom-call | flops 1 | bytes 1 | tf_op jit(solution)/shard_map/attention_forward/pallas_call | solution.py:104
  125.3 25.6 %collective-permute-done.15.refs_9_.refs_5_ = bf16[4,64,2560]{2,1,0:T(8,128)(2,1)} collective-permute-done((bf16[4,64,2560]{2,1,0:T(8,128)(2,1)}, bf16[4,64,2560]{2,1,0:T(8,128)(2,1)}, u32[]{:S(2)}, u32[]{:S(2)}) %collective-permute-start.15) | collective-permute-done | bytes 1310752 | tf_op jit(solution)/shard_map/ppermute | solution.py:802
  150.9 1.5 collective-permute-start.16
  154.1 12.6 %attention_forward.7 = (bf16[1024,256]{1,0:T(8,128)(2,1)}, f32[1,2,2,1024]{3,2,1,0:T(2,128)}) custom-call(s32[1,8]{1,0:T(1,128)} %and_select_fusion.lo_ref, s32[1]{0:T(128)} %bitcast.off_ref.at_ref, bf16[2048,1536]{1,0:T(8,128)(2,1)} %add_convert_fusion.refs_0_.refs_1_.refs_2_.refs_3_.refs_4_.refs_5_.q_ref.k_ref.v_ref, ...), custom_call_target="tpu_custom_call" | custom-call | flops 1 | bytes 1 | tf_op jit(solution)/shard_map/attention_forward/pallas_call | solution.py:104
  166.8 9.9 %collective-permute-done.17.refs_3_ = bf16[1024,256]{1,0:T(8,128)(2,1)S(1)} collective-permute-done((bf16[1024,256]{1,0:T(8,128)(2,1)S(1)}, bf16[1024,256]{1,0:T(8,128)(2,1)S(1)}, u32[]{:S(2)}, u32[]{:S(2)}) %collective-permute-start.17) | collective-permute-done | bytes 524320 | tf_op jit(solution)/shard_map/ppermute | solution.py:806
  178.0 11.9 %middle.1 = (f32[1024,1024]{1,0:T(8,128)}, f32[1024,1024]{1,0:T(8,128)}, bf16[1024,1024]{1,0:T(8,128)(2,1)}, bf16[1024,1024]{1,0:T(8,128)(2,1)}, bf16[1024,1024]{1,0:T(8,128)(2,1)}, /*index=5*/bf16[1024,1024]{1,0:T(8,128)(2,1)}) custom-call(s32[4]{0:T(128)} %pad_add_fusion.at_ref, bf16[1024,256]{1,0:T(8,128)(2,1)} %get-tuple-element.140.refs_0_, ...), custom_call_target="tpu_custom_call" | custom-call | flops 1 | bytes 1 | tf_op jit(solution)/shard_map/middle/pallas_call | solution.py:291
  190.0 33.7 %feed.1 = (bf16[1024,4096]{1,0:T(8,128)(2,1)}, bf16[1024,1024]{1,0:T(8,128)(2,1)}, bf16[1024,1024]{1,0:T(8,128)(2,1)}, bf16[1024,1024]{1,0:T(8,128)(2,1)}, f32[8,1024]{1,0:T(8,128)}) custom-call(s32[4]{0:T(128)} %pad_add_fusion.at_ref, bf16[1024,1024]{1,0:T(8,128)(2,1)} %get-tuple-element.149.u_ref, f32[1,4096]{1,0:T(1,128)} %bitcast.104, ...), custom_call_target="tpu_custom_call" | custom-call | flops 1 | bytes 1 | tf_op jit(solution)/shard_map/feed/pallas_call | solution.py:291
  223.7 51.9 %feed_back.1 = (bf16[512,4096]{1,0:T(8,128)(2,1)}, bf16[512,4096]{1,0:T(8,128)(2,1)}, f32[1,4096]{1,0:T(1,128)}, f32[1024,1024]{1,0:T(8,128)}, f32[8,1024]{1,0:T...) custom-call(s32[4]{0:T(128)} %pad_add_fusion.at_ref, ...), custom_call_target="tpu_custom_call" | custom-call | flops 1 | bytes 1 | tf_op jit(solution)/shard_map/feed_back/pallas_call | solution.py:291
  275.5 1.5 collective-permute-start.21
  277.1 14.9 %grad_down.1 = bf16[1024,4096]{1,0:T(8,128)(2,1)} custom-call(bf16[1024,1024]{1,0:T(8,128)(2,1)} %get-tuple-element.164.left_ref, bf16[1024,4096]{1,0:T(8,128)(2,1)} %get-tuple-element.155.pre_ref), custom_call_target="tpu_custom_call" | custom-call | flops 1 | bytes 1 | tf_op jit(solution)/shard_map/grad_down/pallas_call | solution.py:291
  292.0 8.6 %collective-permute-done.21.refs_3_ = bf16[1024,512]{1,0:T(8,128)(2,1)S(1)} collective-permute-done((bf16[1024,512]{1,0:T(8,128)(2,1)}, bf16[1024,512]{1,0:T(8,128)(2,1)S(1)}, u32[]{:S(2)}, u32[]{:S(2)}) %collective-permute-start.21) | collective-permute-done | bytes 1048608 | tf_op jit(solution)/shard_map/ppermute | solution.py:806
  302.2 4.6 grad_rows.5
  307.4 4.7 grad_rows.6.refs_0_
  313.1 6.4 %merge.3 = bf16[512,2560]{1,0:T(8,128)(2,1)} custom-call(s32[1]{0:T(128)} %constant.137.clone.1.at_ref, bf16[512,1024]{1,0:T(8,128)(2,1)} %grad_rows.6.refs_0_, bf16[512,1024]{1,0:T(8,128)(2,1)} %copy-done.20, bf16[512,4096]{1,0:T(8,128)(2,1)} %get-tuple-element.194.refs_2_, bf16[512,4096]{1,0:T(8,128)(2,1)} %collective-permute-done.20.refs_3_), custom_call_target="tpu_custom_call" | custom-call | flops 1 | bytes 1 | tf_op jit(solution)/shard_map/merge/pallas_call | solution.py:291
  320.8 17.7 %attention_backward.4.refs_6_ = bf16[2048,1536]{1,0:T(8,128)(2,1)} custom-call(s32[1,8]{1,0:T(1,128)} %and_select_fusion.lo_ref, s32[1]{0:T(128)} %bitcast.22.place_ref, bf16[2048,1536]{1,0:T(8,128)(2,1)} %add_convert_fusion.refs_0_.refs_1_.refs_2_.refs_3_.refs_4_.refs_5_.q_ref.k_ref.v_ref, ...), custom_call_target="tpu_custom_call" | custom-call | flops 1 | bytes 1 | tf_op jit(solution)/shard_map/attention_backward/pallas_call | solution.py:217
  338.5 17.6 %attention_backward.5.refs_6_ = bf16[2048,1536]{1,0:T(8,128)(2,1)} custom-call(s32[1,8]{1,0:T(1,128)} %and_select_fusion.lo_ref, s32[1]{0:T(128)} %bitcast.22.place_ref, bf16[2048,1536]{1,0:T(8,128)(2,1)} %add_convert_fusion.refs_0_.refs_1_.refs_2_.refs_3_.refs_4_.refs_5_.q_ref.k_ref.v_ref, ...), custom_call_target="tpu_custom_call", output_to_operand_aliasing={{}: (12, {})} | custom-call | flops 1 | bytes 1 | tf_op jit(solution)/shard_map/attention_backward/pallas_call | solution.py:217
  356.1 17.5 %attention_backward.6.refs_6_ = bf16[2048,1536]{1,0:T(8,128)(2,1)} custom-call(s32[1,8]{1,0:T(1,128)} %and_select_fusion.lo_ref, s32[1]{0:T(128)} %bitcast.22.place_ref, bf16[2048,1536]{1,0:T(8,128)(2,1)} %add_convert_fusion.refs_0_.refs_1_.refs_2_.refs_3_.refs_4_.refs_5_.q_ref.k_ref.v_ref, ...), custom_call_target="tpu_custom_call", output_to_operand_aliasing={{}: (12, {})} | custom-call | flops 1 | bytes 1 | tf_op jit(solution)/shard_map/attention_backward/pallas_call | solution.py:217
  373.6 5.3 collective-permute-done.22.refs_4_
  378.8 1.5 copy-done.19
  380.4 4.9 merge.4
  385.3 3.1 collective-permute-start.23
  388.4 17.6 %attention_backward.7.dq_ref.right_ref = bf16[2048,1536]{1,0:T(8,128)(2,1)} custom-call(s32[1,8]{1,0:T(1,128)} %and_select_fusion.lo_ref, s32[1]{0:T(128)} %bitcast.22.place_ref, bf16[2048,1536]{1,0:T(8,128)(2,1)} %add_convert_fusion.refs_0_.refs_1_.refs_2_.refs_3_.refs_4_.refs_5_.q_ref.k_ref.v_ref, ...), custom_call_target="tpu_custom_call", output_to_operand_aliasing={{}: (12, {})} | custom-call | flops 1 | bytes 1 | tf_op jit(solution)/shard_map/attention_backward/pallas_call | solution.py:217
  406.0 17.2 %collective-permute-done.23 = bf16[256,2560]{1,0:T(8,128)(2,1)S(1)} collective-permute-done((bf16[256,2560]{1,0:T(8,128)(2,1)}, bf16[256,2560]{1,0:T(8,128)(2,1)S(1)}, u32[]{:S(2)}, u32[]{:S(2)}) %collective-permute-start.23) | collective-permute-done | bytes 1310752 | tf_op jit(solution)/shard_map/ppermute | solution.py:802
  423.2 8.5 %d_in.2 = (bf16[1024,1024]{1,0:T(8,128)(2,1)}, f32[8,1024]{1,0:T(8,128)}, f32[8,1536]{1,0:T(8,128)}) custom-call(s32[1]{0:T(128)} %bitcast.15.off_ref.at_ref, bf16[2048,1536]{1,0:T(8,128)(2,1)} %attention_backward.7.dq_ref.right_ref, bf16[1024,1536]{1,0:T(8,128)(2,1)} %bitcast.76, bf16[2048,1024]{1,0:T(8,128)(2,1)} %refs_2_.1), custom_call_target="tpu_custom_call" | custom-call | flops 1 | bytes 1 | tf_op jit(solution)/shard_map/d_in/pallas_call | solution.py:291
  431.7 8.2 %grad_rows.7 = bf16[512,1536]{1,0:T(8,128)(2,1)} custom-call(s32[2]{0:T(128)} %pad_add_fusion.2.at_ref, bf16[2,512,2048]{2,1,0:T(8,128)(2,1)} %bitcast.72, bf16[2048,1536]{1,0:T(8,128)(2,1)} %attention_backward.7.dq_ref.right_ref), custom_call_target="tpu_custom_call" | custom-call | flops 1 | bytes 1 | tf_op jit(solution)/shard_map/grad_rows/pallas_call | solution.py:291
  442.2 4.9 merge.5
  447.1 2.0 add_convert_fusion.1
  450.3 6.7 %grad_rows.8 = bf16[256,1536]{1,0:T(8,128)(2,1)} custom-call(s32[2]{0:T(128)} %pad_add_fusion.4.at_ref, bf16[4,256,2048]{2,1,0:T(8,128)(2,1)} %bitcast.73, bf16[2048,1536]{1,0:T(8,128)(2,1)} %attention_backward.7.dq_ref.right_ref, bf16[2,256,1536]{2,1,0:T(8,128)(2,1)} %bitcast.80), custom_call_target="tpu_custom_call" | custom-call | flops 1 | bytes 1 | tf_op jit(solution)/shard_map/grad_rows/pallas_call | solution.py:291
  457.0 1.5 collective-permute-start.25
  460.6 8.1 %d_in.3 = (bf16[1024,1024]{1,0:T(8,128)(2,1)}, f32[8,1024]{1,0:T(8,128)}, f32[8,1536]{1,0:T(8,128)}) custom-call(s32[1]{0:T(128)} %bitcast.off_ref.at_ref, bf16[2048,1536]{1,0:T(8,128)(2,1)} %attention_backward.7.dq_ref.right_ref, bf16[1024,1536]{1,0:T(8,128)(2,1)} %bitcast.77, bf16[2048,1024]{1,0:T(8,128)(2,1)} %refs_2_.1), custom_call_target="tpu_custom_call" | custom-call | flops 1 | bytes 1 | tf_op jit(solution)/shard_map/d_in/pallas_call | solution.py:291
  468.7 6.6 %grad_rows.9 = bf16[256,1536]{1,0:T(8,128)(2,1)} custom-call(s32[2]{0:T(128)} %pad_add_fusion.5.at_ref, bf16[4,256,2048]{2,1,0:T(8,128)(2,1)} %bitcast.74, bf16[2048,1536]{1,0:T(8,128)(2,1)} %attention_backward.7.dq_ref.right_ref, bf16[2,256,1536]{2,1,0:T(8,128)(2,1)} %bitcast.81), custom_call_target="tpu_custom_call" | custom-call | flops 1 | bytes 1 | tf_op jit(solution)/shard_map/grad_rows/pallas_call | solution.py:291
  476.2 2.8 collective-permute-start.30
  479.0 2.5 collective-permute-start.31
  483.0 5.3 collective-permute-done.26.refs_1_
  488.3 1.5 add_reduce_fusion
  494.5 2.8 concatenate.25
  497.3 6.0 %collective-permute-done.31 = bf16[64,2560]{1,0:T(8,128)(2,1)} collective-permute-done((bf16[64,2560]{1,0:T(8,128)(2,1)}, bf16[64,2560]{1,0:T(8,128)(2,1)}, u32[]{:S(2)}, u32[]{:S(2)}) %collective-permute-start.31) | collective-permute-done | bytes 327712 | tf_op jit(solution)/shard_map/ppermute | solution.py:934
  505.5 1.5 collective-permute-start.35
  507.2 2.6 collective-permute-done.35
  509.8 7.5 %collective-permute-start.36 = (f32[16,1024]{1,0:T(8,128)S(1)}, f32[16,1024]{1,0:T(8,128)S(1)}, u32[]{:S(2)}, u32[]{:S(2)}) collective-permute-start(f32[16,1024]{1,0:T(8,128)S(1)} %add.184), channel_id=1, source_target_pairs={{0,8},{2,10},{4,12},{6,14},{8,0},{10,2},{12,4},{14,6},{16,24},{18,... | collective-permute-start | bytes 196616 | tf_op jit(solution)/shard_map/ppermute | solution.py:965
  518.5 2.8 collective-permute-start.29
  521.4 2.0 collective-permute-start.37
  524.9 14.4 %collective-permute-done.37 = f32[16,1024]{1,0:T(8,128)S(1)} collective-permute-done((f32[16,1024]{1,0:T(8,128)S(1)}, f32[16,1024]{1,0:T(8,128)S(1)}, u32[]{:S(2)}, u32[]{:S(2)}) %collective-permute-start.37) | collective-permute-done | bytes 65568 | tf_op jit(solution)/shard_map/ppermute | solution.py:965
  541.3 2.3 collective-permute-done.38
  547.1 7.1 %last.1 = bf16[1024,1024]{1,0:T(8,128)(2,1)} custom-call(s32[1]{0:T(128)} %bitcast.off_ref.at_ref, bf16[1024,1024]{1,0:T(8,128)(2,1)} %get-tuple-element.215.refs_0_, bf16[1024,1024]{1,0:T(8,128)(2,1)} %collective-permute-done.26.refs_1_, bf16[2048,1024]{1,0:T(8,128)(2,1)} %refs_2_.1, f32[1024,1024]{1,0:T(8,128)} %get-tuple-element.217.refs_3_, ...), custom_call_target="tpu_custom_call" | custom-call | flops 1 | bytes 1 | tf_op jit(solution)/shard_map/last/pallas_call | solution.py:291
  (184 shorter events, 52.2 us)
Async XLA Ops:
  7.2 182.8 %all-gather.2.cloned.1.call-start = ((), (), s32[]{:S(2)}) async-start(), calls=%async_computation.1 | async-start | bytes 8912896 | tf_op jit(solution)/shard_map/all_gather | solution.py:869
  8.2 21.0 %collective-permute-start = (bf16[3,64,512]{2,1,0:T(8,128)(2,1)S(1)}, bf16[3,64,512]{2,1,0:T(8,128)(2,1)S(1)}, u32[]{:S(2)}, u32[]{:S(2)}) collective-permute-start(bf16[3,64,512]{2,1,0:T(8,128)(2,1)S(1)} %convert_element_type.86), channel_id=1, source_target_pairs={{0,8},{2,10},{4,12},{6,14},{8,16},{10,18},{12,20},{14,22},{16,24},... | collective-permute-start | bytes 589832 | tf_op jit(solution)/shard_map/ppermute | solution.py:810
  11.3 18.0 %collective-permute-start.1 = (bf16[3,64,512]{2,1,0:T(8,128)(2,1)S(1)}, bf16[3,64,512]{2,1,0:T(8,128)(2,1)S(1)}, u32[]{:S(2)}, u32[]{:S(2)}) collective-permute-start(bf16[3,64,512]{2,1,0:T(8,128)(2,1)S(1)} %convert_element_type.86), channel_id=1, source_target_pairs={{0,16},{2,18},{4,20},{6,22},{8,24},{10,26},{12,28},{14,30},{16,0},... | collective-permute-start | bytes 589832 | tf_op jit(solution)/shard_map/ppermute | solution.py:810
  13.9 15.4 %collective-permute-start.2 = (bf16[3,64,512]{2,1,0:T(8,128)(2,1)S(1)}, bf16[3,64,512]{2,1,0:T(8,128)(2,1)S(1)}, u32[]{:S(2)}, u32[]{:S(2)}) collective-permute-start(bf16[3,64,512]{2,1,0:T(8,128)(2,1)S(1)} %convert_element_type.86), channel_id=1, source_target_pairs={{0,24},{2,26},{4,28},{6,30},{8,0},{10,2},{12,4},{14,6},{16,8},{18,... | collective-permute-start | bytes 589832 | tf_op jit(solution)/shard_map/ppermute | solution.py:810
  17.3 2.2 copy-start
  25.1 2.0 copy-start.1
  27.1 2.1 copy-start.13
  29.2 27.6 %copy-start.39 = (f32[2,1024]{1,0:T(2,128)S(1)}, f32[2,1024]{1,0:T(2,128)}, u32[]{:S(2)}) copy-start(f32[2,1024]{1,0:T(2,128)} %param.21) | copy-start | bytes 24580
  29.3 28.2 %copy-start.40 = (s32[1,2048]{1,0:T(1,128)S(1)}, s32[1,2048]{1,0:T(1,128)}, u32[]{:S(2)}) copy-start(s32[1,2048]{1,0:T(1,128)} %param.14) | copy-start | bytes 24580
  29.4 33.7 %copy-start.3 = (bf16[4,3,64,512]{3,2,1,0:T(8,128)(2,1)}, bf16[4,3,64,512]{3,2,1,0:T(8,128)(2,1)S(1)}, u32[]{:S(2)}) copy-start(bf16[4,3,64,512]{3,2,1,0:T(8,128)(2,1)S(1)} %pad_maximum_fusion.1.refs_0_) | copy-start | bytes 2359300
  29.4 27.2 %collective-permute-start.3 = (bf16[4,3,64,512]{3,2,1,0:T(8,128)(2,1)S(1)}, bf16[4,3,64,512]{3,2,1,0:T(8,128)(2,1)S(1)}, u32[]{:S(2)}, u32[]{:S(2)}) collective-permute-start(bf16[4,3,64,512]{3,2,1,0:T(8,128)(2,1)S(1)} %pad_maximum_fusion.1.refs_0_), channel_id=1, source_target_pairs={{0,4},{2,6},{4,0},{6,2},{8,12},{10,14},{12,8},{14,10},{16,20},{18,... | collective-permute-start | bytes 2359304 | tf_op jit(solution)/shard_map/ppermute | solution.py:802
  31.0 7.0 %collective-permute-start.4 = (bf16[64,2048]{1,0:T(8,128)(2,1)S(1)}, bf16[64,2048]{1,0:T(8,128)(2,1)S(1)}, u32[]{:S(2)}, u32[]{:S(2)}) collective-permute-start(bf16[64,2048]{1,0:T(8,128)(2,1)S(1)} %convert_bitcast_fusion), channel_id=1, source_target_pairs={{0,1},{1,0},{2,3},{3,2},{4,5},{5,4},{6,7},{7,6},{8,9},{9,8},{10,11... | collective-permute-start | bytes 786440 | tf_op jit(solution)/shard_map/ppermute | solution.py:806
  32.6 12.6 %collective-permute-start.5 = (bf16[64,2560]{1,0:T(8,128)(2,1)S(1)}, bf16[64,2560]{1,0:T(8,128)(2,1)S(1)}, u32[]{:S(2)}, u32[]{:S(2)}) collective-permute-start(bf16[64,2560]{1,0:T(8,128)(2,1)S(1)} %pad_maximum_fusion.3), channel_id=1, source_target_pairs={{0,8},{2,10},{4,12},{6,14},{8,16},{10,18},{12,20},{14,22},{16,24},... | collective-permute-start | bytes 983048 | tf_op jit(solution)/shard_map/ppermute | solution.py:810
  34.7 21.9 %collective-permute-start.6 = (bf16[64,2560]{1,0:T(8,128)(2,1)S(1)}, bf16[64,2560]{1,0:T(8,128)(2,1)S(1)}, u32[]{:S(2)}, u32[]{:S(2)}) collective-permute-start(bf16[64,2560]{1,0:T(8,128)(2,1)S(1)} %pad_maximum_fusion.3), channel_id=1, source_target_pairs={{0,16},{2,18},{4,20},{6,22},{8,24},{10,26},{12,28},{14,30},{16,0},... | collective-permute-start | bytes 983048 | tf_op jit(solution)/shard_map/ppermute | solution.py:810
  36.4 20.3 %collective-permute-start.7 = (bf16[64,2560]{1,0:T(8,128)(2,1)S(1)}, bf16[64,2560]{1,0:T(8,128)(2,1)S(1)}, u32[]{:S(2)}, u32[]{:S(2)}) collective-permute-start(bf16[64,2560]{1,0:T(8,128)(2,1)S(1)} %pad_maximum_fusion.3), channel_id=1, source_target_pairs={{0,24},{2,26},{4,28},{6,30},{8,0},{10,2},{12,4},{14,6},{16,8},{18,... | collective-permute-start | bytes 983048 | tf_op jit(solution)/shard_map/ppermute | solution.py:810
  45.2 11.7 %copy-start.32 = (bf16[64,2560]{1,0:T(8,128)(2,1)}, bf16[64,2560]{1,0:T(8,128)(2,1)S(1)}, u32[]{:S(2)}) copy-start(bf16[64,2560]{1,0:T(8,128)(2,1)S(1)} %collective-permute-done.5) | copy-start | bytes 983044
  56.6 8.0 %copy-start.5 = (bf16[4,3,64,512]{3,2,1,0:T(8,128)(2,1)}, bf16[4,3,64,512]{3,2,1,0:T(8,128)(2,1)S(1)}, u32[]{:S(2)}) copy-start(bf16[4,3,64,512]{3,2,1,0:T(8,128)(2,1)S(1)} %collective-permute-done.3.refs_1_) | copy-start | bytes 2359300
  56.7 487.0 %reduce-scatter.2.cloned.1.call-start = ((), (), s32[]{:S(2)}) async-start(), calls=%async_computation.2 | async-start | bytes 8912896 | tf_op jit(solution)/shard_map/reduce_scatter | solution.py:897
  59.3 13.6 %copy-start.31 = (s32[2048]{0:T(1024)}, s32[2048]{0:T(1024)S(1)}, u32[]{:S(2)}) copy-start(s32[2048]{0:T(1024)S(1)} %convert_reduce_fusion) | copy-start | bytes 24580
  59.3 5.4 collective-permute-start.8
  59.4 6.2 %collective-permute-start.9 = (bf16[4,3,64,512]{3,2,1,0:T(8,128)(2,1)S(1)}, bf16[4,3,64,512]{3,2,1,0:T(8,128)(2,1)S(1)}, u32[]{:S(2)}, u32[]{:S(2)}) collective-permute-start(bf16[4,3,64,512]{3,2,1,0:T(8,128)(2,1)S(1)} %collective-permute-done.3.refs_1_), channel_id=1, source_target_pairs={{0,2},{2,0},{4,6},{6,4},{8,10},{10,8},{12,14},{14,12},{16,18},{18,... | collective-permute-start | bytes 2359304 | tf_op jit(solution)/shard_map/ppermute | solution.py:798
  63.1 36.7 %collective-permute-start.10 = (bf16[4,64,2560]{2,1,0:T(8,128)(2,1)}, bf16[4,64,2560]{2,1,0:T(8,128)(2,1)}, u32[]{:S(2)}, u32[]{:S(2)}) collective-permute-start(bf16[4,64,2560]{2,1,0:T(8,128)(2,1)} %pad_maximum_fusion.refs_4_.refs_0_), channel_id=1, source_target_pairs={{0,4},{2,6},{4,0},{6,2},{8,12},{10,14},{12,8},{14,10},{16,20},{18,... | collective-permute-start | bytes 3932168 | tf_op jit(solution)/shard_map/ppermute | solution.py:802
  64.1 35.6 %collective-permute-start.11 = (bf16[4,64,2560]{2,1,0:T(8,128)(2,1)}, bf16[4,64,2560]{2,1,0:T(8,128)(2,1)}, u32[]{:S(2)}, u32[]{:S(2)}) collective-permute-start(bf16[4,64,2560]{2,1,0:T(8,128)(2,1)} %pad_maximum_fusion.refs_4_.refs_0_), channel_id=1, source_target_pairs={{0,1},{1,0},{2,3},{3,2},{4,5},{5,4},{6,7},{7,6},{8,9},{9,8},{10,11... | collective-permute-start | bytes 3932168 | tf_op jit(solution)/shard_map/ppermute | solution.py:806
  71.2 2.2 copy-start.14
  72.9 9.0 %copy-start.2 = (bf16[4,2,2,64,1536]{4,3,2,1,0:T(8,128)(2,1)}, bf16[4,2,2,64,1536]{4,3,2,1,0:T(8,128)(2,1)S(1)}, u32[]{:S(2)}) copy-start(bf16[4,2,2,64,1536]{4,3,2,1,0:T(8,128)(2,1)S(1)} %assemble_qkv.1) | copy-start | bytes 9437188
  99.8 12.5 %collective-permute-start.12 = (bf16[4,64,2560]{2,1,0:T(8,128)(2,1)}, bf16[4,64,2560]{2,1,0:T(8,128)(2,1)S(1)}, u32[]{:S(2)}, u32[]{:S(2)}) collective-permute-start(bf16[4,64,2560]{2,1,0:T(8,128)(2,1)} %pad_maximum_fusion.refs_4_.refs_0_), channel_id=1, source_target_pairs={{0,2},{2,0},{4,6},{6,4},{8,10},{10,8},{12,14},{14,12},{16,18},{18,... | collective-permute-start | bytes 3932168 | tf_op jit(solution)/shard_map/ppermute | solution.py:798
  99.8 12.5 %collective-permute-start.13 = (bf16[4,64,2560]{2,1,0:T(8,128)(2,1)}, bf16[4,64,2560]{2,1,0:T(8,128)(2,1)S(1)}, u32[]{:S(2)}, u32[]{:S(2)}) collective-permute-start(bf16[4,64,2560]{2,1,0:T(8,128)(2,1)} %collective-permute-done.10.refs_5_.refs_1_), channel_id=1, source_target_pairs={{0,2},{2,0},{4,6},{6,4},{8,10},{10,8},{12,14},{14,12},{16,18},{18,... | collective-permute-start | bytes 3932168 | tf_op jit(solution)/shard_map/ppermute | solution.py:798
  100.3 12.0 %collective-permute-start.14 = (bf16[4,64,2560]{2,1,0:T(8,128)(2,1)}, bf16[4,64,2560]{2,1,0:T(8,128)(2,1)}, u32[]{:S(2)}, u32[]{:S(2)}) collective-permute-start(bf16[4,64,2560]{2,1,0:T(8,128)(2,1)} %collective-permute-done.11.refs_8_.refs_4_), channel_id=1, source_target_pairs={{0,2},{2,0},{4,6},{6,4},{8,10},{10,8},{12,14},{14,12},{16,18},{18,... | collective-permute-start | bytes 3932168 | tf_op jit(solution)/shard_map/ppermute | solution.py:798
  100.3 50.6 %collective-permute-start.15 = (bf16[4,64,2560]{2,1,0:T(8,128)(2,1)}, bf16[4,64,2560]{2,1,0:T(8,128)(2,1)}, u32[]{:S(2)}, u32[]{:S(2)}) collective-permute-start(bf16[4,64,2560]{2,1,0:T(8,128)(2,1)} %collective-permute-done.11.refs_8_.refs_4_), channel_id=1, source_target_pairs={{0,4},{2,6},{4,0},{6,2},{8,12},{10,14},{12,8},{14,10},{16,20},{18,... | collective-permute-start | bytes 3932168 | tf_op jit(solution)/shard_map/ppermute | solution.py:802
  112.3 13.0 %copy-start.16 = (bf16[4,64,2560]{2,1,0:T(8,128)(2,1)}, bf16[4,64,2560]{2,1,0:T(8,128)(2,1)S(1)}, u32[]{:S(2)}) copy-start(bf16[4,64,2560]{2,1,0:T(8,128)(2,1)S(1)} %collective-permute-done.12.refs_6_.refs_2_) | copy-start | bytes 3932164
  112.3 13.0 %copy-start.17 = (bf16[4,64,2560]{2,1,0:T(8,128)(2,1)}, bf16[4,64,2560]{2,1,0:T(8,128)(2,1)S(1)}, u32[]{:S(2)}) copy-start(bf16[4,64,2560]{2,1,0:T(8,128)(2,1)S(1)} %collective-permute-done.13.refs_7_.refs_3_) | copy-start | bytes 3932164
  112.3 40.1 %copy-start.23 = (bf16[1024,256]{1,0:T(8,128)(2,1)S(1)}, bf16[1024,256]{1,0:T(8,128)(2,1)}, u32[]{:S(2)}) copy-start(bf16[1024,256]{1,0:T(8,128)(2,1)} %get-tuple-element.144.refs_1_) | copy-start | bytes 1572868
  112.3 41.2 %copy-start.36 = (f32[4096]{0:T(1024)S(1)}, f32[4096]{0:T(1024)}, u32[]{:S(2)}) copy-start(f32[4096]{0:T(1024)} %param.23) | copy-start | bytes 49156
  150.9 25.8 %collective-permute-start.18 = (bf16[4,64,2560]{2,1,0:T(8,128)(2,1)}, bf16[4,64,2560]{2,1,0:T(8,128)(2,1)S(1)}, u32[]{:S(2)}, u32[]{:S(2)}) collective-permute-start(bf16[4,64,2560]{2,1,0:T(8,128)(2,1)} %collective-permute-done.15.refs_9_.refs_5_), channel_id=1, source_target_pairs={{0,2},{2,0},{4,6},{6,4},{8,10},{10,8},{12,14},{14,12},{16,18},{18,... | collective-permute-start | bytes 3932168 | tf_op jit(solution)/shard_map/ppermute | solution.py:798
  150.9 15.8 %collective-permute-start.16 = (bf16[1024,256]{1,0:T(8,128)(2,1)}, bf16[1024,256]{1,0:T(8,128)(2,1)S(1)}, u32[]{:S(2)}, u32[]{:S(2)}) collective-permute-start(bf16[1024,256]{1,0:T(8,128)(2,1)} %get-tuple-element.143.refs_1_), channel_id=1, source_target_pairs={{0,1},{1,0},{2,3},{3,2},{4,5},{5,4},{6,7},{7,6},{8,9},{9,8},{10,11... | collective-permute-start | bytes 1572872 | tf_op jit(solution)/shard_map/ppermute | solution.py:806
  152.4 24.3 %collective-permute-start.17 = (bf16[1024,256]{1,0:T(8,128)(2,1)S(1)}, bf16[1024,256]{1,0:T(8,128)(2,1)S(1)}, u32[]{:S(2)}, u32[]{:S(2)}) collective-permute-start(bf16[1024,256]{1,0:T(8,128)(2,1)S(1)} %copy-done.23), channel_id=1, source_target_pairs={{0,1},{1,0},{2,3},{3,2},{4,5},{5,4},{6,7},{7,6},{8,9},{9,8},{10,11... | collective-permute-start | bytes 1572872 | tf_op jit(solution)/shard_map/ppermute | solution.py:806
  166.8 10.0 %copy-start.27 = (bf16[1024,256]{1,0:T(8,128)(2,1)}, bf16[1024,256]{1,0:T(8,128)(2,1)S(1)}, u32[]{:S(2)}) copy-start(bf16[1024,256]{1,0:T(8,128)(2,1)S(1)} %collective-permute-done.16.refs_2_) | copy-start | bytes 1572868
  275.5 25.1 %collective-permute-start.21 = (bf16[1024,512]{1,0:T(8,128)(2,1)}, bf16[1024,512]{1,0:T(8,128)(2,1)S(1)}, u32[]{:S(2)}, u32[]{:S(2)}) collective-permute-start(bf16[1024,512]{1,0:T(8,128)(2,1)} %get-tuple-element.166), channel_id=1, source_target_pairs={{0,1},{1,0},{2,3},{3,2},{4,5},{5,4},{6,7},{7,6},{8,9},{9,8},{10,11... | collective-permute-start | bytes 3145736 | tf_op jit(solution)/shard_map/ppermute | solution.py:806
  277.1 35.0 %collective-permute-start.20 = (bf16[512,4096]{1,0:T(8,128)(2,1)}, bf16[512,4096]{1,0:T(8,128)(2,1)}, u32[]{:S(2)}, u32[]{:S(2)}) collective-permute-start(bf16[512,4096]{1,0:T(8,128)(2,1)} %get-tuple-element.160), channel_id=1, source_target_pairs={{0,2},{2,0},{4,6},{6,4},{8,10},{10,8},{12,14},{14,12},{16,18},{18,... | collective-permute-start | bytes 12582920 | tf_op jit(solution)/shard_map/ppermute | solution.py:798
  306.8 5.3 collective-permute-start.19
  319.5 59.3 %collective-permute-start.22 = (bf16[512,2560]{1,0:T(8,128)(2,1)}, bf16[512,2560]{1,0:T(8,128)(2,1)S(1)}, u32[]{:S(2)}, u32[]{:S(2)}) collective-permute-start(bf16[512,2560]{1,0:T(8,128)(2,1)} %merge.3), channel_id=1, source_target_pairs={{0,1},{1,0},{2,3},{3,2},{4,5},{5,4},{6,7},{7,6},{8,9},{9,8},{10,11... | collective-permute-start | bytes 7864328 | tf_op jit(solution)/shard_map/ppermute | solution.py:806
  385.3 37.9 %collective-permute-start.23 = (bf16[256,2560]{1,0:T(8,128)(2,1)}, bf16[256,2560]{1,0:T(8,128)(2,1)S(1)}, u32[]{:S(2)}, u32[]{:S(2)}) collective-permute-start(bf16[256,2560]{1,0:T(8,128)(2,1)} %merge.4), channel_id=1, source_target_pairs={{0,4},{2,6},{4,0},{6,2},{8,12},{10,14},{12,8},{14,10},{16,20},{18,... | collective-permute-start | bytes 3932168 | tf_op jit(solution)/shard_map/ppermute | solution.py:802
  423.2 8.5 %copy-start.24 = (bf16[256,2560]{1,0:T(8,128)(2,1)}, bf16[256,2560]{1,0:T(8,128)(2,1)S(1)}, u32[]{:S(2)}) copy-start(bf16[256,2560]{1,0:T(8,128)(2,1)S(1)} %collective-permute-done.23) | copy-start | bytes 3932164
  431.7 10.5 %copy-start.37 = (f32[1,4096]{1,0:T(1,128)S(1)}, f32[1,4096]{1,0:T(1,128)}, u32[]{:S(2)}) copy-start(f32[1,4096]{1,0:T(1,128)} %get-tuple-element.209) | copy-start | bytes 49156
  439.9 9.2 %collective-permute-start.24 = (bf16[512,1536]{1,0:T(8,128)(2,1)}, bf16[512,1536]{1,0:T(8,128)(2,1)S(1)}, u32[]{:S(2)}, u32[]{:S(2)}) collective-permute-start(bf16[512,1536]{1,0:T(8,128)(2,1)} %grad_rows.7), channel_id=1, source_target_pairs={{0,2},{2,0},{4,6},{6,4},{8,10},{10,8},{12,14},{14,12},{16,18},{18,... | collective-permute-start | bytes 4718600 | tf_op jit(solution)/shard_map/ppermute | solution.py:798
  440.4 47.9 %collective-permute-start.26 = (bf16[1024,1024]{1,0:T(8,128)(2,1)}, bf16[1024,1024]{1,0:T(8,128)(2,1)}, u32[]{:S(2)}, u32[]{:S(2)}) collective-permute-start(bf16[1024,1024]{1,0:T(8,128)(2,1)} %get-tuple-element.199), channel_id=1, source_target_pairs={{0,1},{1,0},{2,3},{3,2},{4,5},{5,4},{6,7},{7,6},{8,9},{9,8},{10,11... | collective-permute-start | bytes 6291464 | tf_op jit(solution)/shard_map/ppermute | solution.py:806
  450.3 9.7 %copy-start.38 = (f32[8,1024]{1,0:T(8,128)S(1)}, f32[8,1024]{1,0:T(8,128)}, u32[]{:S(2)}) copy-start(f32[8,1024]{1,0:T(8,128)} %get-tuple-element.205) | copy-start | bytes 98308
  457.0 31.3 %collective-permute-start.25 = (bf16[256,1536]{1,0:T(8,128)(2,1)}, bf16[256,1536]{1,0:T(8,128)(2,1)S(1)}, u32[]{:S(2)}, u32[]{:S(2)}) collective-permute-start(bf16[256,1536]{1,0:T(8,128)(2,1)} %grad_rows.8), channel_id=1, source_target_pairs={{0,4},{2,6},{4,0},{6,2},{8,12},{10,14},{12,8},{14,10},{16,20},{18,... | collective-permute-start | bytes 2359304 | tf_op jit(solution)/shard_map/ppermute | solution.py:802
  475.3 31.7 %copy-start.22 = (bf16[256,1536]{1,0:T(8,128)(2,1)S(1)}, bf16[256,1536]{1,0:T(8,128)(2,1)}, u32[]{:S(2)}) copy-start(bf16[256,1536]{1,0:T(8,128)(2,1)} %grad_rows.9) | copy-start | bytes 2359300
  476.2 21.1 %collective-permute-start.30 = (bf16[64,2560]{1,0:T(8,128)(2,1)}, bf16[64,2560]{1,0:T(8,128)(2,1)S(1)}, u32[]{:S(2)}, u32[]{:S(2)}) collective-permute-start(bf16[64,2560]{1,0:T(8,128)(2,1)} %get-tuple-element.223), channel_id=1, source_target_pairs={{0,8},{2,10},{4,12},{6,14},{8,16},{10,18},{12,20},{14,22},{16,24},... | collective-permute-start | bytes 983048 | tf_op jit(solution)/shard_map/ppermute | solution.py:934
  479.0 24.3 %collective-permute-start.31 = (bf16[64,2560]{1,0:T(8,128)(2,1)}, bf16[64,2560]{1,0:T(8,128)(2,1)}, u32[]{:S(2)}, u32[]{:S(2)}) collective-permute-start(bf16[64,2560]{1,0:T(8,128)(2,1)} %get-tuple-element.225), channel_id=1, source_target_pairs={{0,16},{2,18},{4,20},{6,22},{8,24},{10,26},{12,28},{14,30},{16,0},... | collective-permute-start | bytes 983048 | tf_op jit(solution)/shard_map/ppermute | solution.py:934
  481.5 21.8 %collective-permute-start.32 = (bf16[64,2560]{1,0:T(8,128)(2,1)S(1)}, bf16[64,2560]{1,0:T(8,128)(2,1)}, u32[]{:S(2)}, u32[]{:S(2)}) collective-permute-start(bf16[64,2560]{1,0:T(8,128)(2,1)S(1)} %get-tuple-element.224), channel_id=1, source_target_pairs={{0,24},{2,26},{4,28},{6,30},{8,0},{10,2},{12,4},{14,6},{16,8},{18,... | collective-permute-start | bytes 983048 | tf_op jit(solution)/shard_map/ppermute | solution.py:934
  488.3 15.0 %copy-start.25 = (bf16[256,1536]{1,0:T(8,128)(2,1)}, bf16[256,1536]{1,0:T(8,128)(2,1)S(1)}, u32[]{:S(2)}) copy-start(bf16[256,1536]{1,0:T(8,128)(2,1)S(1)} %collective-permute-done.25) | copy-start | bytes 2359300
  497.3 7.3 %collective-permute-start.34 = (f32[16,1024]{1,0:T(8,128)}, f32[16,1024]{1,0:T(8,128)S(1)}, u32[]{:S(2)}, u32[]{:S(2)}) collective-permute-start(f32[16,1024]{1,0:T(8,128)} %concatenate.25), channel_id=1, source_target_pairs={{0,2},{2,0},{4,6},{6,4},{8,10},{10,8},{12,14},{14,12},{16,18},{18,... | collective-permute-start | bytes 196616 | tf_op jit(solution)/shard_map/ppermute | solution.py:965
  503.3 3.7 copy-start.26
  505.5 4.3 collective-permute-start.35
  509.8 11.6 %collective-permute-start.36 = (f32[16,1024]{1,0:T(8,128)S(1)}, f32[16,1024]{1,0:T(8,128)S(1)}, u32[]{:S(2)}, u32[]{:S(2)}) collective-permute-start(f32[16,1024]{1,0:T(8,128)S(1)} %add.184), channel_id=1, source_target_pairs={{0,8},{2,10},{4,12},{6,14},{8,0},{10,2},{12,4},{14,6},{16,24},{18,... | collective-permute-start | bytes 196616 | tf_op jit(solution)/shard_map/ppermute | solution.py:965
  517.4 22.5 %collective-permute-start.27 = (bf16[64,1536]{1,0:T(8,128)(2,1)S(1)}, bf16[64,1536]{1,0:T(8,128)(2,1)S(1)}, u32[]{:S(2)}, u32[]{:S(2)}) collective-permute-start(bf16[64,1536]{1,0:T(8,128)(2,1)S(1)} %get-tuple-element.226), channel_id=1, source_target_pairs={{0,8},{2,10},{4,12},{6,14},{8,16},{10,18},{12,20},{14,22},{16,24},... | collective-permute-start | bytes 589832 | tf_op jit(solution)/shard_map/ppermute | solution.py:934
  517.5 22.4 %collective-permute-start.28 = (bf16[64,1536]{1,0:T(8,128)(2,1)S(1)}, bf16[64,1536]{1,0:T(8,128)(2,1)S(1)}, u32[]{:S(2)}, u32[]{:S(2)}) collective-permute-start(bf16[64,1536]{1,0:T(8,128)(2,1)S(1)} %get-tuple-element.228), channel_id=1, source_target_pairs={{0,16},{2,18},{4,20},{6,22},{8,24},{10,26},{12,28},{14,30},{16,0},... | collective-permute-start | bytes 589832 | tf_op jit(solution)/shard_map/ppermute | solution.py:934
  518.5 21.4 %collective-permute-start.29 = (bf16[64,1536]{1,0:T(8,128)(2,1)S(1)}, bf16[64,1536]{1,0:T(8,128)(2,1)S(1)}, u32[]{:S(2)}, u32[]{:S(2)}) collective-permute-start(bf16[64,1536]{1,0:T(8,128)(2,1)S(1)} %get-tuple-element.227), channel_id=1, source_target_pairs={{0,24},{2,26},{4,28},{6,30},{8,0},{10,2},{12,4},{14,6},{16,8},{18,... | collective-permute-start | bytes 589832 | tf_op jit(solution)/shard_map/ppermute | solution.py:934
  521.4 17.9 %collective-permute-start.37 = (f32[16,1024]{1,0:T(8,128)S(1)}, f32[16,1024]{1,0:T(8,128)S(1)}, u32[]{:S(2)}, u32[]{:S(2)}) collective-permute-start(f32[16,1024]{1,0:T(8,128)S(1)} %add.185), channel_id=1, source_target_pairs={{0,16},{2,18},{4,20},{6,22},{8,24},{10,26},{12,28},{14,30},{16,0},... | collective-permute-start | bytes 196616 | tf_op jit(solution)/shard_map/ppermute | solution.py:965
  539.3 4.3 collective-permute-start.38
  544.7 9.5 %collective-permute-start.33 = (bf16[64,2048]{1,0:T(8,128)(2,1)S(1)}, bf16[64,2048]{1,0:T(8,128)(2,1)S(1)}, u32[]{:S(2)}, u32[]{:S(2)}) collective-permute-start(bf16[64,2048]{1,0:T(8,128)(2,1)S(1)} %slice.94), channel_id=1, source_target_pairs={{0,1},{1,0},{2,3},{3,2},{4,5},{5,4},{6,7},{7,6},{8,9},{9,8},{10,11... | collective-permute-start | bytes 786440 | tf_op jit(solution)/shard_map/ppermute | solution.py:806
  547.1 7.1 %copy-start.30 = (bf16[64,4096]{1,0:T(8,128)(2,1)S(1)}, bf16[64,4096]{1,0:T(8,128)(2,1)}, u32[]{:S(2)}) copy-start(bf16[64,4096]{1,0:T(8,128)(2,1)} %reduce-scatter.2.cloned.1.call-done) | copy-start | bytes 1572868
  (18 other events, 18.6 us)
Sparse Core Ops, SparseCore 0:
  56.8 100.5 all-gather.1
  300.8 111.0 reduce-scatter.1

commit v4 on v3

--- a/solution.py
+++ b/solution.py
@@ -287,7 +287,7 @@
     return pl.BlockSpec(shape, lambda *_: (0,) * len(shape), pipeline_mode=pl.Buffered(1))
 
 
-def call(body, name, grid, ins, outs, shapes, operands, prefetch=(), scratch=(), vmem=VMEM):
+def call(body, name, grid, ins, outs, shapes, operands, prefetch=(), scratch=(), vmem=VMEM, micros=0):
     return pl.pallas_call(
         body,
         grid_spec=pltpu.PrefetchScalarGridSpec(
@@ -301,7 +301,9 @@
         compiler_params=pltpu.CompilerParams(
             dimension_semantics=("arbitrary",) * len(grid), vmem_limit_bytes=vmem
         ),
-        cost_estimate=SMALL,
+        cost_estimate=pl.CostEstimate(
+            flops=1 + int(micros * 1.1e9), bytes_accessed=1, transcendentals=0
+        ),
         name=name,
     )(*prefetch, *operands)
 
@@ -660,6 +662,7 @@
         [row_spec(features), fixed((8, features)), fixed((8, width))],
         [shaped(rows, features, BF16), shaped(8, features, F32), shaped(8, width, F32)],
         [d_qkv, weight_qkv, inputs],
+        micros=2,
         prefetch=[row_at],
     )
 
@@ -695,7 +698,7 @@
 def grad_rows(left, at, right, terms=()):
     _, rows, tokens = left.shape
     columns = right.shape[1]
-    block = math.gcd(columns, 512)
+    block = math.gcd(columns, 256 if tokens > 1024 else 512)
     return call(
         functools.partial(grad_rows_kernel, len(terms)),
         "grad_rows",
@@ -774,6 +777,81 @@
     )
 
 
+def grad_both_kernel(at_ref, left_ref, right_ref, there_ref, send_ref, keep_ref):
+    x = at_ref[1]
+    for ref, index in ((send_ref, 1 - x), (keep_ref, x)):
+        total = dot(left_ref[index], right_ref[...], NN) + there_ref[index].astype(F32)
+        ref[...] = total.astype(BF16)
+
+
+def grad_both(left, at, right, there):
+    tokens = left.shape[1]
+    rows = left.shape[0] // (NC * NX)
+    columns = right.shape[1]
+    block = math.gcd(columns, 256)
+    out = pl.BlockSpec((rows, block), lambda j, at: (0, j))
+    return call(
+        grad_both_kernel,
+        "grad_both",
+        (columns // block,),
+        [
+            pl.BlockSpec((None, NX, rows, tokens), lambda j, at: (at[0], 0, 0, 0)),
+            pl.BlockSpec((tokens, block), lambda j, at: (0, j)),
+            pl.BlockSpec((NX, rows, block), lambda j, at: (0, 0, j)),
+        ],
+        [out, out],
+        [shaped(rows, columns, BF16)] * 2,
+        [left.reshape(NC, NX, rows, tokens), right, there.reshape(NX, rows, columns)],
+        prefetch=[at],
+    )
+
+
+def by_pair_kernel(in_ref, out_ref):
+    kinds, _, width = in_ref.shape
+    for p in range(width // PAIR):
+        for kind in range(kinds):
+            at = (p * kinds + kind) * PAIR
+            out_ref[:, at : at + PAIR] = in_ref[kind, :, p * PAIR : (p + 1) * PAIR].astype(BF16)
+
+
+def by_pair(weight):
+    kinds, rows, width = weight.shape
+    whole = lambda shape: pl.BlockSpec(shape, lambda i: (0,) * len(shape))
+    return call(
+        by_pair_kernel,
+        "by_pair",
+        (1,),
+        [whole(weight.shape)],
+        whole((rows, kinds * width)),
+        shaped(rows, kinds * width, BF16),
+        [weight],
+        vmem=16 << 20,
+    )
+
+
+def project_kernel(u_ref, w_ref, b_ref, out_ref):
+    rows = min(512, u_ref.shape[0])
+    for r in range(0, u_ref.shape[0], rows):
+        part = slice(r, r + rows)
+        out_ref[part, :] = (dot(u_ref[part, :], w_ref[...], NN) + b_ref[...]).astype(BF16)
+
+
+def project(u, weight, bias):
+    rows, features = u.shape
+    columns = weight.shape[1]
+    block = math.gcd(columns, 512)
+    column = lambda size: pl.BlockSpec((size, block), lambda j: (0, j))
+    return call(
+        project_kernel,
+        "project",
+        (columns // block,),
+        [fixed(u.shape), column(features), column(1)],
+        column(rows),
+        shaped(rows, columns, BF16),
+        [u, weight, bias],
+    )
+
+
 def tie(*values):
     return lax.optimization_barrier(values)
 
@@ -808,44 +886,6 @@
 
 def spread_z(shard):
     return [shard] + [lax.ppermute(shard, "dp", z_pairs(k)) for k in range(1, NZ)]
-
-
-def assemble_qkv_kernel(pos_ref, *refs):
-    out_ref = refs[-1]
-    z, x, c = pos_ref[0], pos_ref[1], pos_ref[2]
-    kinds, _, width = refs[0].shape[1:]
-    for n, ref in enumerate(refs[:-1]):
-        for k in range(NZ):
-            to = out_ref.at[
-                lax.rem(z - k + NZ, NZ), lax.bitwise_xor(x, n % 2), lax.bitwise_xor(c, n // 2)
-            ]
-            for p in range(width // PAIR):
-                for kind in range(kinds):
-                    at = (p * kinds + kind) * PAIR
-                    to[:, at : at + PAIR] = ref[k, kind, :, p * PAIR : (p + 1) * PAIR]
-
-
-def assemble_qkv(position, pieces):
-    _, kinds, rows, width = pieces[0].shape
-    step = 16
-    out = pl.pallas_call(
-        assemble_qkv_kernel,
-        grid_spec=pltpu.PrefetchScalarGridSpec(
-            num_scalar_prefetch=1,
-            grid=(rows // step,),
-            in_specs=[pl.BlockSpec((NZ, kinds, step, width), lambda i, pos: (0, 0, i, 0))] * 4,
-            out_specs=pl.BlockSpec(
-                (NZ, NX, NC, step, kinds * width), lambda i, pos: (0, 0, 0, i, 0)
-            ),
-        ),
-        out_shape=jax.ShapeDtypeStruct((NZ, NX, NC, rows, kinds * width), BF16),
-        compiler_params=pltpu.CompilerParams(
-            dimension_semantics=("arbitrary",), vmem_limit_bytes=24 << 20
-        ),
-        cost_estimate=SMALL,
-        name="assemble_qkv",
-    )(position, *pieces)
-    return out.reshape(-1, kinds * width)
 
 
 class Staged:
@@ -858,30 +898,27 @@
 
     def gather_first(self, u1, shard_qkv, shard_out, shard_up, shard_down):
         self.hidden = shard_up.shape[1]
-        first = spread_z(shard_qkv)
-        u1, *first, shard = tie(u1, *first, jnp.concatenate([shard_up, shard_out], axis=1))
-        column = jnp.stack(first)
-        own = spread_z(shard)
+        qkv = lax.all_gather(shard_qkv, "dp", axis=0, tiled=True)
+        own = spread_z(jnp.concatenate([shard_up, shard_out], axis=1))
         both_down = jnp.concatenate([shard_down, swap_y(shard_down)], axis=1)
-        from_x, both_down, *own = tie(swap_x(column), both_down, *own)
-        self.own = jnp.stack(own)
-        self.own_x, self.other = swap_x(self.own), swap_y(self.own)
+        u1, *own = tie(u1, *own)
+        own = jnp.stack(own)
+        self.own_x, self.other = swap_x(own), swap_y(own)
+        qkv, self.own, both_down = tie(qkv, own, both_down)
         self.down = lax.all_gather(both_down, "dp", axis=0, tiled=True)
-        pieces = [column, from_x]
-        pieces += [swap_core(a) for a in pieces]
-        return u1, assemble_qkv(self.position, pieces)
-
-    def beside_forward(self, index, values):
+        return u1, qkv
+
+    def beside_forward(self, index, values, received):
         if index == 0:
             *values, self.own, self.own_x, self.other = tie(*values, self.own, self.own_x, self.other)
-            self.other_x = swap_x(self.other)
+            self.other_x = swap_y(self.own_x)
             self.cores = [swap_core(a) for a in (self.own, self.own_x, self.other)]
         if index == 1:
             n = len(values)
             values = tie(*values, *self.cores)
             values, self.cores = values[:n], list(values[n:])
         if index == 2:
-            *values, self.other_x = tie(*values, self.other_x)
+            *values, self.other_x, received[0] = tie(*values, self.other_x, received[0])
             self.cores.append(swap_core(self.other_x))
         return values
 
@@ -901,69 +938,75 @@
         left = left.reshape(parts, -1, left.shape[-1])
         return grad_rows(left, jnp.stack(index), right, terms)
 
-    def reduce_first(self, send, keep, turned, o_own, d_o_rows):
+    def reduce_start(self, send, keep, turned, o_own, later):
         up_there = swap_core(send)
         out_there = swap_core(self.rows_times(turned, [1 - self.c, self.c], o_own))
         out_keep = self.rows_times(turned, [self.c, self.c], o_own)
-        out_there, up_there, out_keep, *d_o_rows = tie(out_there, up_there, out_keep, *d_o_rows)
+        later, out_keep = tie(later, out_keep)
         self.outs, self.ups = [out_keep, out_there], [keep, up_there]
+        return later
+
+    def reduce_first(self, d_o_rows):
+        outs_ups_rows = tie(*self.outs, *self.ups, *d_o_rows)
+        self.outs, self.ups, d_o_rows = outs_ups_rows[:2], outs_ups_rows[2:4], outs_ups_rows[4:]
         zero = jnp.zeros((1,), jnp.int32)
-        send, *d_o_rows = tie(merge(zero, keep.shape[0], self.outs, self.ups, 1), *d_o_rows)
+        rows = self.outs[0].shape[0]
+        send, *d_o_rows = tie(merge(zero, rows, self.outs, self.ups, 1), *d_o_rows)
         self.from_y = swap_y(send)
         return d_o_rows
+
+    def own_rows(self, x, both):
+        rows = self.from_y.shape[0] // NX
+        return merge(jnp.reshape(x, (1,)), rows, self.outs, self.ups, 0, both)
 
     def beside_backward(self, index, d_qkv):
         if index == 2:
             d_qkv, self.from_y = tie(d_qkv, self.from_y)
-            rows = self.from_y.shape[0] // NX
-
-            def part(x):
-                return merge(jnp.reshape(x, (1,)), rows, self.outs, self.ups, 0, [self.from_y])
-
-            send, d_qkv = tie(part(1 - self.x), d_qkv)
-            self.from_x, self.here = swap_x(send), part
-        if index == 3:
-            d_qkv, self.from_x = tie(d_qkv, self.from_x)
+            send, d_qkv = tie(self.own_rows(1 - self.x, [self.from_y]), d_qkv)
+            self.from_x = swap_x(send)
         return d_qkv
 
-    def reduce_z(self, total):
+    def z_pieces(self, total):
         total = total.reshape(NZ, -1, total.shape[1])
-        out = pick(total, self.z).astype(F32)
-        for k in range(1, NZ):
-            piece = pick(total, lax.rem(self.z + k, NZ))
-            out = out + lax.ppermute(piece, "dp", z_pairs(k)).astype(F32)
-        return out
-
-    def tail(self, turned, d_qkv, d_in_own, terms):
+        send = [pick(total, lax.rem(self.z + k, NZ)) for k in range(1, NZ)]
+        got = [lax.ppermute(a, "dp", z_pairs(k)) for k, a in zip(range(1, NZ), send)]
+        return pick(total, self.z), got
+
+    def z_sum(self, total, pieces):
+        return sum((a.astype(F32) for a in pieces), total.astype(F32))
+
+    def tail(self, turned, d_qkv, parts, d_in_own, small, finish):
+        terms = self.exchange([None, parts[1]])
         send = self.rows_times(turned, [1 - self.c, self.c], d_qkv)
+        send, self.from_x = tie(send, self.from_x)
         there = swap_core(send)
         d_qkv, send, *parts = tie(d_qkv, send, *self.outs, *self.ups)
         self.outs, self.ups = parts[:2], parts[2:]
-        there, total = tie(there, add(self.here(self.x), self.from_x))
-        from_core = there.reshape(NX, -1, there.shape[-1])
-        parts = lambda x, d_qkv: self.rows_times(turned, [self.c * NX + x, x], d_qkv, [from_core])
-        send, d_qkv = tie(parts(1 - self.x, d_qkv), d_qkv)
+        there, total = tie(there, self.own_rows(self.x, [self.from_y, self.from_x]))
+        send, keep = grad_both(turned, jnp.stack([self.c, self.x]), d_qkv, there)
+        send, d_qkv = tie(send, d_qkv)
         own = d_in_own(d_qkv)
-        keep = parts(self.x, d_qkv)
-        there, received, keep, first, *rest = tie(swap_x(send), terms[1], keep, *own)
-        own = [first, *rest]
-        total = self.reduce_z(total)
-        qkv = self.reduce_z(add(keep, there))
+        total, pieces = self.z_pieces(total)
+        there, received, keep, vector, down, part, *pieces = tie(
+            swap_x(send), terms[1], keep, small(own), self.down, own[0], *pieces
+        )
+        half = down.shape[1] // 2
+        from_y = swap_y(down[:, half:])
+        total = self.z_sum(total, pieces)
+        send, pieces = self.z_pieces(add(keep, there))
+        for bit in (1, NC):
+            vector = vector + lax.ppermute(vector, "dp", flips(bit))
+        vector = vector + swap_y(vector)
+        d_inputs, vector, from_y, *pieces = tie(finish([part, received]), vector, from_y, *pieces)
+        down = down[:, :half].astype(F32) + from_y.astype(F32)
+        qkv = self.z_sum(send, pieces)
+        for bit in (NX * NC, 2 * NX * NC):
+            vector = vector + lax.ppermute(vector, "dp", flips(bit))
         width = self.outs[0].shape[1] // 2
-        return own, total[:, width:], total[:, :width], qkv, [None, received]
-
-    def reduce_down_last(self, terms):
-        *terms, down = tie(*terms, self.down)
-        half = down.shape[1] // 2
-        return terms, down[:, :half].astype(F32) + swap_y(down[:, half:]).astype(F32)
+        return d_inputs, vector, total[:, width:], total[:, :width], qkv, down
 
     def exchange(self, parts):
         return [parts[0], swap_y(parts[1])]
-
-    def total(self, vector):
-        for bit in (1, NC, NX * NC, 2 * NX * NC):
-            vector = vector + lax.ppermute(vector, "dp", flips(bit))
-        return vector + swap_y(vector)
 
 
 class Plain:
@@ -980,13 +1023,12 @@
         return jnp.concatenate([pick(every, (self.rank + g) % self.n) for g in range(self.n)], axis=1)
 
     def gather_first(self, u1, shard_qkv, *shards):
+        qkv = lax.all_gather(shard_qkv, "dp", axis=0, tiled=True)
         weights = [self.gather_groups(w) for w in shards]
         self.weights = [weights[:1], *(whole_blocks(w) for w in weights[1:])]
-        every = lax.all_gather(shard_qkv, "dp", axis=1, tiled=True)
-        pairs = jnp.split(every, every.shape[2] // PAIR, axis=2)
-        return u1, jnp.concatenate([p[j] for p in pairs for j in range(3)], axis=1)
-
-    def beside_forward(self, index, values):
+        return u1, qkv
+
+    def beside_forward(self, index, values, received):
         return values
 
     def gather_last(self, *attended):
@@ -1000,21 +1042,24 @@
     def reduce_down(self, grad):
         self.down = self.reduce_rows(grad)
 
-    def reduce_first(self, send, keep, turned, o_own, d_o_rows):
+    def reduce_start(self, send, keep, turned, o_own, later):
         self.up = self.reduce_rows(jnp.concatenate([keep, send], axis=0))
         self.out = self.reduce_rows(dot(turned, o_own, NN).astype(BF16))
+        return later
+
+    def reduce_first(self, d_o_rows):
         return d_o_rows
 
     def beside_backward(self, index, d_qkv):
         return d_qkv
 
-    def tail(self, turned, d_qkv, d_in_own, terms):
+    def tail(self, turned, d_qkv, parts, d_in_own, small, finish):
         grad = dot(turned, d_qkv, NN).astype(BF16)
         qkv = lax.psum_scatter(grad, "dp", scatter_dimension=0, tiled=True).astype(F32)
-        return d_in_own(d_qkv), self.up, self.out, qkv, terms
-
-    def reduce_down_last(self, terms):
-        return terms, self.down
+        own = d_in_own(d_qkv)
+        vector = lax.psum(small(own), ("dp", "tensor"))
+        d_inputs = finish(self.exchange([own[0], *parts[1:]]))
+        return d_inputs, vector, self.up, self.out, qkv, self.down
 
     def absolute(self, parts):
         order = (jnp.arange(self.n) - self.rank) % self.n
@@ -1023,9 +1068,6 @@
     def exchange(self, parts):
         got = lax.all_to_all(self.absolute(parts), "tensor", 0, 0, tiled=True)
         return [pick(got, (self.rank + g) % self.n) for g in range(self.n)]
-
-    def total(self, vector):
-        return lax.psum(vector, ("dp", "tensor"))
 
 
 def per_device(
@@ -1063,7 +1105,7 @@
     u1, turned1 = first_norm(comm.turn, inputs, norm_gain, norm_bias)
     u1, weight_qkv = comm.gather_first(
         u1,
-        w_qkv.astype(BF16),
+        by_pair(w_qkv),
         w_out.T.astype(BF16),
         w_fc1.astype(BF16),
         w_fc2.T.astype(BF16),
@@ -1072,7 +1114,7 @@
     heads_bias = group_slice(head_bias, 0, width, 1)
     qkv_bias = jnp.stack([heads_bias[0], jnp.zeros((width,), F32), heads_bias[1]])
     qkv_bias = qkv_bias.reshape(3, pairs, PAIR).transpose(1, 0, 2).reshape(-1)
-    qkv = (dot(u1, weight_qkv, NN) + qkv_bias).astype(BF16)
+    qkv = project(u1, weight_qkv, qkv_bias[None])
 
     starts, lo = segment_bounds(segment_ids)
     blocks = length // QB
@@ -1089,7 +1131,7 @@
             o, lse = attention_forward(
                 i * per_call, per_call, qkv, starts, lo, scalar(places[g] * half), half
             )
-            qkv, o, lse = comm.beside_forward(index, [qkv, o, lse])
+            qkv, o, lse = comm.beside_forward(index, [qkv, o, lse], received)
             o_rows[g][i], lse_rows[g][i] = o, lse
             if g > 0:
                 received[i] = comm.exchange([None, o])[1]
@@ -1125,14 +1167,14 @@
         weight_out,
         norm_gain,
     )
-    d_mlp_turned, *d_o = tie(d_mlp_turned, *d_o)
     d_o_rows = comm.exchange(d_o)
+    d_mlp_turned = comm.reduce_start(send, keep, turned_attn, o_own, d_mlp_turned)
     grad_down, *d_o_rows = tie(grad_down_of(d_mlp_turned, pre), *d_o_rows)
     comm.reduce_down(grad_down)
     if halves < n:
         order = (jnp.arange(n) - rank) % n
         d_o_rows = [jnp.take(jnp.stack(d_o_rows), order, axis=0).reshape(tokens, width)]
-    d_o_rows = comm.reduce_first(send, keep, turned_attn, o_own, d_o_rows)
+    d_o_rows = comm.reduce_first(d_o_rows)
 
     d_qkv = None
     for pair in range(pairs):
@@ -1156,33 +1198,27 @@
         d_u1_parts[g], sums, head_row = d_in(row_at[g], own_rows, d_qkv, weight_qkv, inputs)
         d_u1_parts[g], d_qkv = tie(d_u1_parts[g], d_qkv)
         sums0, head_sums = sums0 + sums, head_sums + head_row[0]
-    d_u1_terms = comm.exchange(d_u1_parts) if staged else None
-    (d_u1_parts[0], sums, head_row), grad_up, grad_out, grad_qkv, d_u1_terms = comm.tail(
+
+    def small(own):
+        totals, head_totals = sums0 + own[1], head_sums + own[2][0]
+        hidden_full = jnp.roll(bias_hidden[0], rank * hidden)
+        head_terms = head_totals.reshape(pairs, 3, PAIR).transpose(1, 0, 2).reshape(3, width)[0::2]
+        head_full = lax.dynamic_update_slice_in_dim(
+            jnp.zeros(head_bias.shape, F32), head_terms, rank * width, 1
+        )
+        gains = [totals[0], sums12[2], sums12[0], sums3[0]]
+        shifts = [totals[1], sums12[3], sums12[1], sums3[1]]
+        rows = jnp.stack(gains + shifts + [sums12[4], sums3[2]])
+        return jnp.concatenate([rows, head_full, hidden_full.reshape(-1, features)])
+
+    d_inputs, small_sums, grad_up, grad_out, grad_qkv, grad_down = comm.tail(
         turned1,
         d_qkv,
+        d_u1_parts,
         lambda d_qkv: d_in(row_at[0], own_rows, d_qkv, weight_qkv, inputs),
-        d_u1_terms,
-    )
-    sums0, head_sums = sums0 + sums, head_sums + head_row[0]
-    if staged:
-        d_u1_terms = [d_u1_parts[0], *d_u1_terms[1:]]
-    else:
-        d_u1_terms = comm.exchange(d_u1_parts)
-
-    hidden_full = jnp.roll(bias_hidden[0], rank * hidden)
-    head_terms = head_sums.reshape(pairs, 3, PAIR).transpose(1, 0, 2).reshape(3, width)[0::2]
-    head_full = lax.dynamic_update_slice_in_dim(
-        jnp.zeros(head_bias.shape, F32), head_terms, rank * width, 1
-    )
-    gains = [sums0[0], sums12[2], sums12[0], sums3[0]]
-    shifts = [sums0[1], sums12[3], sums12[1], sums3[1]]
-    rows = jnp.stack(gains + shifts + [sums12[4], sums3[2]])
-    small = jnp.concatenate([rows, head_full, hidden_full.reshape(-1, features)])
-    small, *d_u1_terms = tie(small, *d_u1_terms)
-    small = comm.total(small)
-    d_u1_terms, grad_down = comm.reduce_down_last(d_u1_terms)
-    d_inputs = last(row_at[0], d_u1_terms, inputs, d_resid, norm_gain)
-
+        small,
+        lambda terms: last(row_at[0], terms, inputs, d_resid, norm_gain),
+    )
     grad_qkv = grad_qkv.reshape(-1, pairs, 3, PAIR).transpose(2, 0, 1, 3).reshape(3, -1, width)
     return (
         output,
@@ -1191,11 +1227,11 @@
         grad_out.T,
         grad_up,
         grad_down.T,
-        small[0:4],
-        small[4:8],
-        small[10:12],
-        small[8:10],
-        small[12:].reshape(-1),
+        small_sums[0:4],
+        small_sums[4:8],
+        small_sums[10:12],
+        small_sums[8:10],
+        small_sums[12:].reshape(-1),
     )
 
 

time: 570 us -> 523 us (0.918)
  waiting for transfers between devices: 123 us -> 93.8 us
  Pallas kernels: 307 us -> 332 us
  local copies, waits for them, and re-layouts: 36.8 us -> 20.6 us
  starting transfers between devices: 52 us -> 41.1 us
  matrix products: 8.5 us -> 0 us
    ppermute x5 -> x3, waiting for transfers between devices: 49.5 us -> 6.19 us  [swap_x(): return lax.ppermute(a, 'dp', flips(NC))]
    all_gather x0 -> x1, waiting for transfers between devices: none -> 26.5 us  [gather_first(): qkv = lax.all_gather(shard_qkv, 'dp', axis=0, tiled=True)]
    ppermute x10, waiting for transfers between devices: 23.1 us -> 9.95 us  [the longest x6 5.34 us: z_pieces(): lax.ppermute(a, 'dp', z_pairs(k))]
    pallas_call x4, Pallas kernels: 70.3 us -> 83 us  [attention_backward(): pl.pallas_call(functools.partial(bwd_kernel, halves), grid_spec=pltpu.Pre...]
    unnamed x84 -> x54, local copies, waits for them, and re-layouts: 22.5 us -> 13.4 us
    pallas_call x16 -> x17, Pallas kernels: 187 us -> 196 us  [call(): pl.pallas_call(body, grid_spec=pltpu.PrefetchScalarGridSpec(num_scalar_pr...]
    dot_general x1 -> x0, matrix products: 8.5 us -> none  [dot(): return lax.dot_general(a, b, dims, preferred_element_type=jnp.float32)]
    ppermute x5 -> x3, starting transfers between devices: 8.36 us -> 1.93 us  [swap_x(): return lax.ppermute(a, 'dp', flips(NC))]
  transfers between devices with their start and end apart: 41 -> 36, of which waited for: 14 -> 12; matrix products, arithmetic and copies ran while one was open for 7% -> 4% of each run, Pallas kernels for 39% -> 48%
where the time goes in v4:
time: 523 us; the launch traced here: 517 us
  Pallas kernels  332 us (63%)
  waiting for transfers between devices  93.8 us (18%)
  starting transfers between devices  41.1 us (8%)
  local copies, waits for them, and re-layouts  20.6 us (4%)
  other arithmetic  15.2 us (3%)
  between operations  14.4 us (3%)
    pallas_call x17, Pallas kernels, call(): pl.pallas_call(body, grid_spec=pltpu.PrefetchScalarGridSpec(num_scalar_pr...  196 us
    pallas_call x4, Pallas kernels, attention_backward(): pl.pallas_call(functools.partial(bwd_kernel, halves), grid_spec=pltpu.Pre...  83 us
    pallas_call x4, Pallas kernels, attention_forward(): pl.pallas_call(functools.partial(fwd_kernel, pairs), grid_spec=grid_spec,...  52.8 us
    ppermute x10, waiting for transfers between devices, swap_y(): return lax.ppermute(a, 'tensor', [(0, 1), (1, 0)])  32.8 us
    all_gather x1, waiting for transfers between devices, gather_first(): qkv = lax.all_gather(shard_qkv, 'dp', axis=0, tiled=True)  26.5 us
    ppermute x3, waiting for transfers between devices, spread_z(): lax.ppermute(shard, 'dp', z_pairs(k))  14.4 us
    unnamed x54, local copies, waits for them, and re-layouts  13.4 us
    ppermute x10, starting transfers between devices, swap_y(): return lax.ppermute(a, 'tensor', [(0, 1), (1, 0)])  13.4 us
  transfers between devices with their start and end apart: 36, of which 12 were waited for; matrix products, arithmetic and copies ran while one was open for 4% of the time, Pallas kernels for 48%

profile of v4, /device:TPU:0, one launch (start us, length us, event | category | flops | bytes accessed | tf_op | source)
XLA Modules:
  0.0 517.1 jit_solution(5089821073883457972)
XLA Ops:
  7.2 1.0 copy-done.4
  9.0 1.1 convert_bitcast_fusion
  10.1 3.0 collective-permute-start.3
  13.1 1.1 convert_element_type.71
  14.3 1.6 collective-permute-start
  15.9 2.6 collective-permute-start.1
  18.5 1.3 collective-permute-start.2
  19.8 2.3 copy-done
  22.1 4.2 first_norm.1
  26.4 2.1 copy-done.1
  28.4 2.1 copy-done.2
  31.4 14.3 %collective-permute-done.1 = bf16[64,2560]{1,0:T(8,128)(2,1)S(1)} collective-permute-done((bf16[64,2560]{1,0:T(8,128)(2,1)S(1)}, bf16[64,2560]{1,0:T(8,128)(2,1)S(1)}, u32[]{:S(2)}, u32[]{:S(2)}) %collective-permute-start.1) | collective-permute-done | bytes 327712 | tf_op jit(solution)/shard_map/ppermute | solution.py:888
  45.9 26.5 %all-gather.3.cloned.1.call-done.w_ref = bf16[1024,1536]{1,0:T(8,128)(2,1)} async-done(((bf16[64,1536]{1,0:T(8,128)(2,1)}), bf16[1024,1536]{1,0:T(8,128)(2,1)}) %all-gather.3.cloned.1.call-update) | async-done | bytes 3145744 | tf_op jit(solution)/shard_map/all_gather | solution.py:901
  73.0 1.5 collective-permute-start.5
  75.4 1.8 convert_reduce_fusion
  77.8 11.5 %project.1.refs_0_.refs_1_.refs_2_.refs_3_.refs_4_.refs_5_.q_ref.k_ref.v_ref = bf16[2048,1536]{1,0:T(8,128)(2,1)} custom-call(bf16[2048,1024]{1,0:T(8,128)(2,1)} %copy-done.2, bf16[1024,1536]{1,0:T(8,128)(2,1)} %all-gather.3.cloned.1.call-done.w_ref, f32[1,1536]{1,0:T(1,128)} %broadcast_in_dim_reshape.3.b_ref), custom_call_target="tpu_custom_call" | custom-call | flops 1 | bytes 1 | tf_op jit(solution)/shard_map/project/pallas_call | solution.py:291
  89.3 13.5 %attention_forward.4 = (bf16[1024,256]{1,0:T(8,128)(2,1)}, f32[1,2,2,1024]{3,2,1,0:T(2,128)}) custom-call(s32[1,8]{1,0:T(1,128)} %and_select_fusion.lo_ref, s32[1]{0:T(128)} %bitcast.14.off_ref.at_ref, bf16[2048,1536]{1,0:T(8,128)(2,1)} %project.1.refs_0_.refs_1_.refs_2_.refs_3_.refs_4_.refs_5_.q_ref.k_ref.v_ref, ...), custom_call_target="tpu_custom_call" | custom-call | flops 1 | bytes 1 | tf_op jit(solution)/shard_map/attention_forward/pallas_call | solution.py:104
  102.9 6.2 %collective-permute-done.4.refs_5_.refs_1_ = bf16[4,64,2560]{2,1,0:T(8,128)(2,1)S(1)} collective-permute-done((bf16[4,64,2560]{2,1,0:T(8,128)(2,1)S(1)}, bf16[4,64,2560]{2,1,0:T(8,128)(2,1)S(1)}, u32[]{:S(2)}, u32[]{:S(2)}) %collective-permute-start.4) | collective-permute-done | bytes 1310752 | tf_op jit(solution)/shard_map/ppermute | solution.py:880
  109.7 1.5 collective-permute-start.9
  111.7 13.7 %attention_forward.5 = (bf16[1024,256]{1,0:T(8,128)(2,1)}, f32[1,2,2,1024]{3,2,1,0:T(2,128)}) custom-call(s32[1,8]{1,0:T(1,128)} %and_select_fusion.lo_ref, s32[1]{0:T(128)} %bitcast.14.off_ref.at_ref, bf16[2048,1536]{1,0:T(8,128)(2,1)} %project.1.refs_0_.refs_1_.refs_2_.refs_3_.refs_4_.refs_5_.q_ref.k_ref.v_ref, ...), custom_call_target="tpu_custom_call" | custom-call | flops 1 | bytes 1 | tf_op jit(solution)/shard_map/attention_forward/pallas_call | solution.py:104
  125.5 13.0 %attention_forward.6 = (bf16[1024,256]{1,0:T(8,128)(2,1)}, f32[1,2,2,1024]{3,2,1,0:T(2,128)}) custom-call(s32[1,8]{1,0:T(1,128)} %and_select_fusion.lo_ref, s32[1]{0:T(128)} %bitcast.off_ref.at_ref, bf16[2048,1536]{1,0:T(8,128)(2,1)} %project.1.refs_0_.refs_1_.refs_2_.refs_3_.refs_4_.refs_5_.q_ref.k_ref.v_ref, ...), custom_call_target="tpu_custom_call" | custom-call | flops 1 | bytes 1 | tf_op jit(solution)/shard_map/attention_forward/pallas_call | solution.py:104
  138.4 13.7 %collective-permute-done.10.refs_2_ = bf16[1024,256]{1,0:T(8,128)(2,1)} collective-permute-done((bf16[1024,256]{1,0:T(8,128)(2,1)}, bf16[1024,256]{1,0:T(8,128)(2,1)}, u32[]{:S(2)}, u32[]{:S(2)}) %collective-permute-start.10) | collective-permute-done | bytes 524320 | tf_op jit(solution)/shard_map/ppermute | solution.py:884
  152.2 1.5 collective-permute-start.11
  155.0 12.6 %attention_forward.7 = (bf16[1024,256]{1,0:T(8,128)(2,1)}, f32[1,2,2,1024]{3,2,1,0:T(2,128)}) custom-call(s32[1,8]{1,0:T(1,128)} %and_select_fusion.lo_ref, s32[1]{0:T(128)} %bitcast.off_ref.at_ref, bf16[2048,1536]{1,0:T(8,128)(2,1)} %project.1.refs_0_.refs_1_.refs_2_.refs_3_.refs_4_.refs_5_.q_ref.k_ref.v_ref, ...), custom_call_target="tpu_custom_call" | custom-call | flops 1 | bytes 1 | tf_op jit(solution)/shard_map/attention_forward/pallas_call | solution.py:104
  168.8 11.9 %middle.1 = (f32[1024,1024]{1,0:T(8,128)}, f32[1024,1024]{1,0:T(8,128)}, bf16[1024,1024]{1,0:T(8,128)(2,1)}, bf16[1024,1024]{1,0:T(8,128)(2,1)}, bf16[1024,1024]{1,0:T(8,128)(2,1)}, /*index=5*/bf16[1024,1024]{1,0:T(8,128)(2,1)}) custom-call(s32[4]{0:T(128)} %pad_add_fusion.at_ref, bf16[1024,256]{1,0:T(8,128)(2,1)} %get-tuple-element.139.refs_0_, ...), custom_call_target="tpu_custom_call" | custom-call | flops 1 | bytes 1 | tf_op jit(solution)/shard_map/middle/pallas_call | solution.py:291
  180.8 33.6 %feed.1 = (bf16[1024,4096]{1,0:T(8,128)(2,1)}, bf16[1024,1024]{1,0:T(8,128)(2,1)}, bf16[1024,1024]{1,0:T(8,128)(2,1)}, bf16[1024,1024]{1,0:T(8,128)(2,1)}, f32[8,1024]{1,0:T(8,128)}) custom-call(s32[4]{0:T(128)} %pad_add_fusion.at_ref, bf16[1024,1024]{1,0:T(8,128)(2,1)} %get-tuple-element.148.u_ref, f32[1,4096]{1,0:T(1,128)} %bitcast.85, ...), custom_call_target="tpu_custom_call" | custom-call | flops 1 | bytes 1 | tf_op jit(solution)/shard_map/feed/pallas_call | solution.py:291
  214.5 51.9 %feed_back.1 = (bf16[512,4096]{1,0:T(8,128)(2,1)}, bf16[512,4096]{1,0:T(8,128)(2,1)}, f32[1,4096]{1,0:T(1,128)}, f32[1024,1024]{1,0:T(8,128)}, f32[8,1024]{1,0:T...) custom-call(s32[4]{0:T(128)} %pad_add_fusion.at_ref, ...), custom_call_target="tpu_custom_call" | custom-call | flops 1 | bytes 1 | tf_op jit(solution)/shard_map/feed_back/pallas_call | solution.py:291
  266.3 1.7 collective-permute-start.15
  268.7 4.5 grad_rows.3.refs_0_
  273.1 14.9 %grad_down.1 = bf16[1024,4096]{1,0:T(8,128)(2,1)} custom-call(bf16[1024,1024]{1,0:T(8,128)(2,1)} %get-tuple-element.164.left_ref, bf16[1024,4096]{1,0:T(8,128)(2,1)} %get-tuple-element.156.pre_ref), custom_call_target="tpu_custom_call" | custom-call | flops 1 | bytes 1 | tf_op jit(solution)/shard_map/grad_down/pallas_call | solution.py:291
  288.1 3.8 collective-permute-done.15.refs_3_
  293.4 4.7 grad_rows.4
  298.5 3.9 collective-permute-done.13.refs_1_
  303.4 6.4 %merge.3 = bf16[512,2560]{1,0:T(8,128)(2,1)} custom-call(s32[1]{0:T(128)} %constant.137.clone.1.at_ref, bf16[512,1024]{1,0:T(8,128)(2,1)} %grad_rows.3.refs_0_, bf16[512,1024]{1,0:T(8,128)(2,1)} %copy-done.11, bf16[512,4096]{1,0:T(8,128)(2,1)} %get-tuple-element.192.refs_2_, bf16[512,4096]{1,0:T(8,128)(2,1)} %collective-permute-done.14.refs_3_), custom_call_target="tpu_custom_call" | custom-call | flops 1 | bytes 1 | tf_op jit(solution)/shard_map/merge/pallas_call | solution.py:291
  309.8 1.1 collective-permute-start.16
  310.9 20.8 %attention_backward.4.refs_6_ = bf16[2048,1536]{1,0:T(8,128)(2,1)} custom-call(s32[1,8]{1,0:T(1,128)} %and_select_fusion.lo_ref, s32[1]{0:T(128)} %bitcast.18.place_ref, bf16[2048,1536]{1,0:T(8,128)(2,1)} %project.1.refs_0_.refs_1_.refs_2_.refs_3_.refs_4_.refs_5_.q_ref.k_ref.v_ref, ...), custom_call_target="tpu_custom_call" | custom-call | flops 1 | bytes 1 | tf_op jit(solution)/shard_map/attention_backward/pallas_call | solution.py:217
  331.7 20.8 %attention_backward.5.refs_6_ = bf16[2048,1536]{1,0:T(8,128)(2,1)} custom-call(s32[1,8]{1,0:T(1,128)} %and_select_fusion.lo_ref, s32[1]{0:T(128)} %bitcast.18.place_ref, bf16[2048,1536]{1,0:T(8,128)(2,1)} %project.1.refs_0_.refs_1_.refs_2_.refs_3_.refs_4_.refs_5_.q_ref.k_ref.v_ref, ...), custom_call_target="tpu_custom_call", output_to_operand_aliasing={{}: (12, {})} | custom-call | flops 1 | bytes 1 | tf_op jit(solution)/shard_map/attention_backward/pallas_call | solution.py:217
  352.5 20.7 %attention_backward.6.refs_6_ = bf16[2048,1536]{1,0:T(8,128)(2,1)} custom-call(s32[1,8]{1,0:T(1,128)} %and_select_fusion.lo_ref, s32[1]{0:T(128)} %bitcast.18.place_ref, bf16[2048,1536]{1,0:T(8,128)(2,1)} %project.1.refs_0_.refs_1_.refs_2_.refs_3_.refs_4_.refs_5_.q_ref.k_ref.v_ref, ...), custom_call_target="tpu_custom_call", output_to_operand_aliasing={{}: (12, {})} | custom-call | flops 1 | bytes 1 | tf_op jit(solution)/shard_map/attention_backward/pallas_call | solution.py:217
  373.2 1.5 copy-done.10
  374.7 5.0 merge.4
  380.1 20.7 %attention_backward.7.dq_ref.right_ref = bf16[2048,1536]{1,0:T(8,128)(2,1)} custom-call(s32[1,8]{1,0:T(1,128)} %and_select_fusion.lo_ref, s32[1]{0:T(128)} %bitcast.18.place_ref, bf16[2048,1536]{1,0:T(8,128)(2,1)} %project.1.refs_0_.refs_1_.refs_2_.refs_3_.refs_4_.refs_5_.q_ref.k_ref.v_ref, ...), custom_call_target="tpu_custom_call", output_to_operand_aliasing={{}: (12, {})} | custom-call | flops 1 | bytes 1 | tf_op jit(solution)/shard_map/attention_backward/pallas_call | solution.py:217
  400.7 8.1 %d_in.2 = (bf16[1024,1024]{1,0:T(8,128)(2,1)}, f32[8,1024]{1,0:T(8,128)}, f32[8,1536]{1,0:T(8,128)}) custom-call(s32[1]{0:T(128)} %bitcast.14.off_ref.at_ref, bf16[2048,1536]{1,0:T(8,128)(2,1)} %attention_backward.7.dq_ref.right_ref, bf16[1024,1536]{1,0:T(8,128)(2,1)} %all-gather.3.cloned.1.call-done.w_ref, bf16[2048,1024]{1,0:T(8,128)(2,1)} %refs_2_.1), custom_call_target="tpu_custom_call" | custom-call | flops 2200000000 | bytes 1 | tf_op jit(solution)/shard_map/d_in/pallas_call | solution.py:291
  408.8 9.2 %grad_rows.5 = bf16[512,1536]{1,0:T(8,128)(2,1)} custom-call(s32[2]{0:T(128)} %pad_add_fusion.2.at_ref, bf16[2,512,2048]{2,1,0:T(8,128)(2,1)} %bitcast.63, bf16[2048,1536]{1,0:T(8,128)(2,1)} %attention_backward.7.dq_ref.right_ref), custom_call_target="tpu_custom_call" | custom-call | flops 1 | bytes 1 | tf_op jit(solution)/shard_map/grad_rows/pallas_call | solution.py:291
  420.8 5.3 %merge.5 = bf16[256,2560]{1,0:T(8,128)(2,1)} custom-call(s32[1]{0:T(128)} %bitcast.2.at_ref, bf16[512,1024]{1,0:T(8,128)(2,1)} %grad_rows.3.refs_0_, bf16[512,1024]{1,0:T(8,128)(2,1)} %copy-done.11, bf16[512,4096]{1,0:T(8,128)(2,1)} %get-tuple-element.192.refs_2_, bf16[512,4096]{1,0:T(8,128)(2,1)} %collective-permute-done.14.refs_3_, ...), custom_call_target="tpu_custom_call" | custom-call | flops 1 | bytes 1 | tf_op jit(solution)/shard_map/merge/pallas_call | solution.py:291
  426.1 9.3 %grad_both.1 = (bf16[256,1536]{1,0:T(8,128)(2,1)}, bf16[256,1536]{1,0:T(8,128)(2,1)}) custom-call(s32[2]{0:T(128)} %pad_add_fusion.1.at_ref, bf16[2,2,256,2048]{3,2,1,0:T(8,128)(2,1)} %bitcast.64, bf16[2048,1536]{1,0:T(8,128)(2,1)} %attention_backward.7.dq_ref.right_ref, bf16[2,256,1536]{2,1,0:T(8,128)(2,1)} %bitcast.23.there_ref), custom_call_target="tpu_custom_call" | custom-call | flops 1 | bytes 1 | tf_op jit(solution)/shard_map/grad_both/pallas_call | solution.py:291
  435.4 1.0 collective-permute-start.19
  436.4 8.0 %d_in.3 = (bf16[1024,1024]{1,0:T(8,128)(2,1)}, f32[8,1024]{1,0:T(8,128)}, f32[8,1536]{1,0:T(8,128)}) custom-call(s32[1]{0:T(128)} %bitcast.off_ref.at_ref, bf16[2048,1536]{1,0:T(8,128)(2,1)} %attention_backward.7.dq_ref.right_ref, bf16[1024,1536]{1,0:T(8,128)(2,1)} %all-gather.3.cloned.1.call-done.w_ref, bf16[2048,1024]{1,0:T(8,128)(2,1)} %refs_2_.1), custom_call_target="tpu_custom_call" | custom-call | flops 2200000000 | bytes 1 | tf_op jit(solution)/shard_map/d_in/pallas_call | solution.py:291
  446.3 3.1 collective-permute-start.22
  449.4 1.0 collective-permute-start.23
  451.3 15.4 %collective-permute-done.20.refs_1_ = bf16[1024,1024]{1,0:T(8,128)(2,1)S(1)} collective-permute-done((bf16[1024,1024]{1,0:T(8,128)(2,1)}, bf16[1024,1024]{1,0:T(8,128)(2,1)S(1)}, u32[]{:S(2)}, u32[]{:S(2)}) %collective-permute-start.20) | collective-permute-done | bytes 2097184 | tf_op jit(solution)/shard_map/ppermute | solution.py:884
  466.7 5.3 %collective-permute-done.22 = bf16[64,2560]{1,0:T(8,128)(2,1)} collective-permute-done((bf16[64,2560]{1,0:T(8,128)(2,1)}, bf16[64,2560]{1,0:T(8,128)(2,1)}, u32[]{:S(2)}, u32[]{:S(2)}) %collective-permute-start.22) | collective-permute-done | bytes 327712 | tf_op jit(solution)/shard_map/ppermute | solution.py:972
  472.1 1.6 add_convert_fusion
  474.6 6.8 %collective-permute-start.28 = (bf16[64,1536]{1,0:T(8,128)(2,1)}, bf16[64,1536]{1,0:T(8,128)(2,1)}, u32[]{:S(2)}, u32[]{:S(2)}) collective-permute-start(bf16[64,1536]{1,0:T(8,128)(2,1)} %get-tuple-element.232), channel_id=1, source_target_pairs={{0,8},{2,10},{4,12},{6,14},{8,16},{10,18},{12,20},{14,22},{16,24},... | collective-permute-start | bytes 589832 | tf_op jit(solution)/shard_map/ppermute | solution.py:972
  481.4 1.0 collective-permute-start.29
  482.4 1.4 collective-permute-start.30
  483.8 1.6 collective-permute-start.27
  486.1 1.3 fusion.1
  487.5 2.3 collective-permute-done.25
  491.0 7.0 %last.1 = bf16[1024,1024]{1,0:T(8,128)(2,1)} custom-call(s32[1]{0:T(128)} %bitcast.off_ref.at_ref, bf16[1024,1024]{1,0:T(8,128)(2,1)} %get-tuple-element.211.refs_0_, bf16[1024,1024]{1,0:T(8,128)(2,1)} %copy-done.14, bf16[2048,1024]{1,0:T(8,128)(2,1)} %refs_2_.1, f32[1024,1024]{1,0:T(8,128)} %get-tuple-element.213.refs_3_, f32[4,1024]{1,0:T(4,128)} %refs_4_.1), custom_call_target="tpu_custom_call" | custom-call | flops 1 | bytes 1 | tf_op jit(solution)/shard_map/last/pallas_call | solution.py:291
  498.9 2.0 collective-permute-start.31
  500.9 1.2 fusion.3
  502.1 1.1 collective-permute-done.31
  503.2 1.9 collective-permute-start.32
  507.3 1.2 collective-permute-done.32
  (139 shorter events, 25.0 us)
Async XLA Ops:
  7.2 12.6 %copy-start.3 = (f32[4,1024]{1,0:T(4,128)S(1)}, f32[4,1024]{1,0:T(4,128)}, u32[]{:S(2)}) copy-start(f32[4,1024]{1,0:T(4,128)} %refs_4_.1) | copy-start | bytes 49156
  7.2 65.2 %all-gather.3.cloned.1.call-start = ((), (), s32[]{:S(2)}) async-start(), calls=%async_computation.1 | async-start | bytes 3342336 | tf_op jit(solution)/shard_map/all_gather | solution.py:901
  7.2 1.0 copy-start.4
  8.2 6.0 %copy-start.19 = (f32[512,64]{0,1:T(8,128)S(1)}, f32[512,64]{0,1:T(8,128)}, u32[]{:S(2)}) copy-start(f32[512,64]{0,1:T(8,128)} %param.16) | copy-start | bytes 393220
  8.2 11.6 %copy-start.5 = (f32[4,1024]{1,0:T(4,128)S(1)}, f32[4,1024]{1,0:T(4,128)}, u32[]{:S(2)}) copy-start(f32[4,1024]{1,0:T(4,128)} %refs_12_.3) | copy-start | bytes 49156
  9.0 171.8 %all-gather.5.cloned.1.call-start = ((), (), s32[]{:S(2)}) async-start(), calls=%async_computation.2 | async-start | bytes 8912896 | tf_op jit(solution)/shard_map/all_gather | solution.py:908
  10.1 20.4 %collective-permute-start.3 = (bf16[64,2048]{1,0:T(8,128)(2,1)S(1)}, bf16[64,2048]{1,0:T(8,128)(2,1)S(1)}, u32[]{:S(2)}, u32[]{:S(2)}) collective-permute-start(bf16[64,2048]{1,0:T(8,128)(2,1)S(1)} %convert_bitcast_fusion), channel_id=1, source_target_pairs={{0,1},{1,0},{2,3},{3,2},{4,5},{5,4},{6,7},{7,6},{8,9},{9,8},{10,11... | collective-permute-start | bytes 786440 | tf_op jit(solution)/shard_map/ppermute | solution.py:884
  14.3 17.1 %collective-permute-start = (bf16[64,2560]{1,0:T(8,128)(2,1)S(1)}, bf16[64,2560]{1,0:T(8,128)(2,1)S(1)}, u32[]{:S(2)}, u32[]{:S(2)}) collective-permute-start(bf16[64,2560]{1,0:T(8,128)(2,1)S(1)} %pad_maximum_fusion.2), channel_id=1, source_target_pairs={{0,8},{2,10},{4,12},{6,14},{8,16},{10,18},{12,20},{14,22},{16,24},... | collective-permute-start | bytes 983048 | tf_op jit(solution)/shard_map/ppermute | solution.py:888
  15.9 29.7 %collective-permute-start.1 = (bf16[64,2560]{1,0:T(8,128)(2,1)S(1)}, bf16[64,2560]{1,0:T(8,128)(2,1)S(1)}, u32[]{:S(2)}, u32[]{:S(2)}) collective-permute-start(bf16[64,2560]{1,0:T(8,128)(2,1)S(1)} %pad_maximum_fusion.2), channel_id=1, source_target_pairs={{0,16},{2,18},{4,20},{6,22},{8,24},{10,26},{12,28},{14,30},{16,0},... | collective-permute-start | bytes 983048 | tf_op jit(solution)/shard_map/ppermute | solution.py:888
  18.5 27.2 %collective-permute-start.2 = (bf16[64,2560]{1,0:T(8,128)(2,1)S(1)}, bf16[64,2560]{1,0:T(8,128)(2,1)S(1)}, u32[]{:S(2)}, u32[]{:S(2)}) collective-permute-start(bf16[64,2560]{1,0:T(8,128)(2,1)S(1)} %pad_maximum_fusion.2), channel_id=1, source_target_pairs={{0,24},{2,26},{4,28},{6,30},{8,0},{10,2},{12,4},{14,6},{16,8},{18,... | collective-permute-start | bytes 983048 | tf_op jit(solution)/shard_map/ppermute | solution.py:888
  19.8 2.3 copy-start
  26.4 2.1 copy-start.1
  28.4 2.1 copy-start.2
  30.5 44.1 %copy-start.24 = (f32[2,1024]{1,0:T(2,128)S(1)}, f32[2,1024]{1,0:T(2,128)}, u32[]{:S(2)}) copy-start(f32[2,1024]{1,0:T(2,128)} %param.21) | copy-start | bytes 24580
  30.5 44.8 %copy-start.25 = (s32[1,2048]{1,0:T(1,128)S(1)}, s32[1,2048]{1,0:T(1,128)}, u32[]{:S(2)}) copy-start(s32[1,2048]{1,0:T(1,128)} %param.14) | copy-start | bytes 24580
  45.9 63.2 %copy-start.6 = (bf16[4,64,2560]{2,1,0:T(8,128)(2,1)}, bf16[4,64,2560]{2,1,0:T(8,128)(2,1)S(1)}, u32[]{:S(2)}) copy-start(bf16[4,64,2560]{2,1,0:T(8,128)(2,1)S(1)} %pad_maximum_fusion.refs_4_.refs_0_) | copy-start | bytes 3932164
  72.4 399.7 %reduce-scatter.2.cloned.1.call-start = ((), (), s32[]{:S(2)}) async-start(), calls=%async_computation.3 | async-start | bytes 8912896 | tf_op jit(solution)/shard_map/reduce_scatter | solution.py:934
  72.4 36.6 %collective-permute-start.4 = (bf16[4,64,2560]{2,1,0:T(8,128)(2,1)S(1)}, bf16[4,64,2560]{2,1,0:T(8,128)(2,1)S(1)}, u32[]{:S(2)}, u32[]{:S(2)}) collective-permute-start(bf16[4,64,2560]{2,1,0:T(8,128)(2,1)S(1)} %pad_maximum_fusion.refs_4_.refs_0_), channel_id=1, source_target_pairs={{0,4},{2,6},{4,0},{6,2},{8,12},{10,14},{12,8},{14,10},{16,20},{18,... | collective-permute-start | bytes 3932168 | tf_op jit(solution)/shard_map/ppermute | solution.py:880
  73.0 36.0 %collective-permute-start.5 = (bf16[4,64,2560]{2,1,0:T(8,128)(2,1)S(1)}, bf16[4,64,2560]{2,1,0:T(8,128)(2,1)}, u32[]{:S(2)}, u32[]{:S(2)}) collective-permute-start(bf16[4,64,2560]{2,1,0:T(8,128)(2,1)S(1)} %pad_maximum_fusion.refs_4_.refs_0_), channel_id=1, source_target_pairs={{0,1},{1,0},{2,3},{3,2},{4,5},{5,4},{6,7},{7,6},{8,9},{9,8},{10,11... | collective-permute-start | bytes 3932168 | tf_op jit(solution)/shard_map/ppermute | solution.py:884
  77.2 12.1 %copy-start.18 = (s32[2048]{0:T(1024)}, s32[2048]{0:T(1024)S(1)}, u32[]{:S(2)}) copy-start(s32[2048]{0:T(1024)S(1)} %convert_reduce_fusion) | copy-start | bytes 24580
  109.0 16.4 %copy-start.8 = (bf16[4,64,2560]{2,1,0:T(8,128)(2,1)}, bf16[4,64,2560]{2,1,0:T(8,128)(2,1)S(1)}, u32[]{:S(2)}) copy-start(bf16[4,64,2560]{2,1,0:T(8,128)(2,1)S(1)} %collective-permute-done.4.refs_5_.refs_1_) | copy-start | bytes 3932164
  109.0 16.4 %collective-permute-start.6 = (bf16[4,64,2560]{2,1,0:T(8,128)(2,1)S(1)}, bf16[4,64,2560]{2,1,0:T(8,128)(2,1)}, u32[]{:S(2)}, u32[]{:S(2)}) collective-permute-start(bf16[4,64,2560]{2,1,0:T(8,128)(2,1)S(1)} %pad_maximum_fusion.refs_4_.refs_0_), channel_id=1, source_target_pairs={{0,2},{2,0},{4,6},{6,4},{8,10},{10,8},{12,14},{14,12},{16,18},{18,... | collective-permute-start | bytes 3932168 | tf_op jit(solution)/shard_map/ppermute | solution.py:876
  109.1 16.3 %collective-permute-start.7 = (bf16[4,64,2560]{2,1,0:T(8,128)(2,1)S(1)}, bf16[4,64,2560]{2,1,0:T(8,128)(2,1)}, u32[]{:S(2)}, u32[]{:S(2)}) collective-permute-start(bf16[4,64,2560]{2,1,0:T(8,128)(2,1)S(1)} %collective-permute-done.4.refs_5_.refs_1_), channel_id=1, source_target_pairs={{0,2},{2,0},{4,6},{6,4},{8,10},{10,8},{12,14},{14,12},{16,18},{18,... | collective-permute-start | bytes 3932168 | tf_op jit(solution)/shard_map/ppermute | solution.py:876
  109.6 15.8 %collective-permute-start.8 = (bf16[4,64,2560]{2,1,0:T(8,128)(2,1)}, bf16[4,64,2560]{2,1,0:T(8,128)(2,1)}, u32[]{:S(2)}, u32[]{:S(2)}) collective-permute-start(bf16[4,64,2560]{2,1,0:T(8,128)(2,1)} %collective-permute-done.5.refs_8_.refs_4_), channel_id=1, source_target_pairs={{0,2},{2,0},{4,6},{6,4},{8,10},{10,8},{12,14},{14,12},{16,18},{18,... | collective-permute-start | bytes 3932168 | tf_op jit(solution)/shard_map/ppermute | solution.py:876
  109.7 42.5 %collective-permute-start.9 = (bf16[4,64,2560]{2,1,0:T(8,128)(2,1)S(1)}, bf16[4,64,2560]{2,1,0:T(8,128)(2,1)}, u32[]{:S(2)}, u32[]{:S(2)}) collective-permute-start(bf16[4,64,2560]{2,1,0:T(8,128)(2,1)S(1)} %collective-permute-done.4.refs_5_.refs_1_), channel_id=1, source_target_pairs={{0,1},{1,0},{2,3},{3,2},{4,5},{5,4},{6,7},{7,6},{8,9},{9,8},{10,11... | collective-permute-start | bytes 3932168 | tf_op jit(solution)/shard_map/ppermute | solution.py:884
  111.2 41.0 %collective-permute-start.10 = (bf16[1024,256]{1,0:T(8,128)(2,1)}, bf16[1024,256]{1,0:T(8,128)(2,1)}, u32[]{:S(2)}, u32[]{:S(2)}) collective-permute-start(bf16[1024,256]{1,0:T(8,128)(2,1)} %get-tuple-element.138.refs_1_), channel_id=1, source_target_pairs={{0,1},{1,0},{2,3},{3,2},{4,5},{5,4},{6,7},{7,6},{8,9},{9,8},{10,11... | collective-permute-start | bytes 1572872 | tf_op jit(solution)/shard_map/ppermute | solution.py:884
  125.5 26.7 %copy-start.13 = (bf16[1024,256]{1,0:T(8,128)(2,1)S(1)}, bf16[1024,256]{1,0:T(8,128)(2,1)}, u32[]{:S(2)}) copy-start(bf16[1024,256]{1,0:T(8,128)(2,1)} %get-tuple-element.143.refs_1_) | copy-start | bytes 1572868
  125.5 28.9 %copy-start.21 = (f32[4096]{0:T(1024)S(1)}, f32[4096]{0:T(1024)}, u32[]{:S(2)}) copy-start(f32[4096]{0:T(1024)} %param.23) | copy-start | bytes 49156
  152.2 15.4 %collective-permute-start.12 = (bf16[4,64,2560]{2,1,0:T(8,128)(2,1)}, bf16[4,64,2560]{2,1,0:T(8,128)(2,1)S(1)}, u32[]{:S(2)}, u32[]{:S(2)}) collective-permute-start(bf16[4,64,2560]{2,1,0:T(8,128)(2,1)} %collective-permute-done.9.refs_9_.refs_5_), channel_id=1, source_target_pairs={{0,2},{2,0},{4,6},{6,4},{8,10},{10,8},{12,14},{14,12},{16,18},{18,... | collective-permute-start | bytes 3932168 | tf_op jit(solution)/shard_map/ppermute | solution.py:876
  152.2 15.4 %collective-permute-start.11 = (bf16[1024,256]{1,0:T(8,128)(2,1)S(1)}, bf16[1024,256]{1,0:T(8,128)(2,1)S(1)}, u32[]{:S(2)}, u32[]{:S(2)}) collective-permute-start(bf16[1024,256]{1,0:T(8,128)(2,1)S(1)} %copy-done.13), channel_id=1, source_target_pairs={{0,1},{1,0},{2,3},{3,2},{4,5},{5,4},{6,7},{7,6},{8,9},{9,8},{10,11... | collective-permute-start | bytes 1572872 | tf_op jit(solution)/shard_map/ppermute | solution.py:884
  167.6 0.8 copy-start.16
  167.6 1.2 copy-start.9
  266.3 25.5 %collective-permute-start.15 = (bf16[1024,512]{1,0:T(8,128)(2,1)}, bf16[1024,512]{1,0:T(8,128)(2,1)S(1)}, u32[]{:S(2)}, u32[]{:S(2)}) collective-permute-start(bf16[1024,512]{1,0:T(8,128)(2,1)} %get-tuple-element.166), channel_id=1, source_target_pairs={{0,1},{1,0},{2,3},{3,2},{4,5},{5,4},{6,7},{7,6},{8,9},{9,8},{10,11... | collective-permute-start | bytes 3145736 | tf_op jit(solution)/shard_map/ppermute | solution.py:884
  291.8 1.0 copy-start.7
  292.8 9.6 %collective-permute-start.14 = (bf16[512,4096]{1,0:T(8,128)(2,1)}, bf16[512,4096]{1,0:T(8,128)(2,1)}, u32[]{:S(2)}, u32[]{:S(2)}) collective-permute-start(bf16[512,4096]{1,0:T(8,128)(2,1)} %get-tuple-element.163), channel_id=1, source_target_pairs={{0,2},{2,0},{4,6},{6,4},{8,10},{10,8},{12,14},{14,12},{16,18},{18,... | collective-permute-start | bytes 12582920 | tf_op jit(solution)/shard_map/ppermute | solution.py:876
  298.1 4.4 collective-permute-start.13
  302.4 1.0 copy-start.11
  309.8 63.4 %collective-permute-start.16 = (bf16[512,2560]{1,0:T(8,128)(2,1)}, bf16[512,2560]{1,0:T(8,128)(2,1)S(1)}, u32[]{:S(2)}, u32[]{:S(2)}) collective-permute-start(bf16[512,2560]{1,0:T(8,128)(2,1)} %merge.3), channel_id=1, source_target_pairs={{0,1},{1,0},{2,3},{3,2},{4,5},{5,4},{6,7},{7,6},{8,9},{9,8},{10,11... | collective-permute-start | bytes 7864328 | tf_op jit(solution)/shard_map/ppermute | solution.py:884
  373.2 1.5 copy-start.10
  379.8 38.2 %collective-permute-start.17 = (bf16[256,2560]{1,0:T(8,128)(2,1)}, bf16[256,2560]{1,0:T(8,128)(2,1)S(1)}, u32[]{:S(2)}, u32[]{:S(2)}) collective-permute-start(bf16[256,2560]{1,0:T(8,128)(2,1)} %merge.4), channel_id=1, source_target_pairs={{0,4},{2,6},{4,0},{6,2},{8,12},{10,14},{12,8},{14,10},{16,20},{18,... | collective-permute-start | bytes 3932168 | tf_op jit(solution)/shard_map/ppermute | solution.py:880
  408.8 11.1 %copy-start.22 = (f32[1,4096]{1,0:T(1,128)S(1)}, f32[1,4096]{1,0:T(1,128)}, u32[]{:S(2)}) copy-start(f32[1,4096]{1,0:T(1,128)} %get-tuple-element.207) | copy-start | bytes 49156
  408.8 12.0 %copy-start.23 = (f32[8,1024]{1,0:T(8,128)S(1)}, f32[8,1024]{1,0:T(8,128)}, u32[]{:S(2)}) copy-start(f32[8,1024]{1,0:T(8,128)} %get-tuple-element.203) | copy-start | bytes 98308
  418.0 2.8 copy-start.15
  418.0 8.1 %collective-permute-start.18 = (bf16[512,1536]{1,0:T(8,128)(2,1)}, bf16[512,1536]{1,0:T(8,128)(2,1)}, u32[]{:S(2)}, u32[]{:S(2)}) collective-permute-start(bf16[512,1536]{1,0:T(8,128)(2,1)} %grad_rows.5), channel_id=1, source_target_pairs={{0,2},{2,0},{4,6},{6,4},{8,10},{10,8},{12,14},{14,12},{16,18},{18,... | collective-permute-start | bytes 4718600 | tf_op jit(solution)/shard_map/ppermute | solution.py:876
  418.9 47.8 %collective-permute-start.20 = (bf16[1024,1024]{1,0:T(8,128)(2,1)}, bf16[1024,1024]{1,0:T(8,128)(2,1)S(1)}, u32[]{:S(2)}, u32[]{:S(2)}) collective-permute-start(bf16[1024,1024]{1,0:T(8,128)(2,1)} %get-tuple-element.198), channel_id=1, source_target_pairs={{0,1},{1,0},{2,3},{3,2},{4,5},{5,4},{6,7},{7,6},{8,9},{9,8},{10,11... | collective-permute-start | bytes 6291464 | tf_op jit(solution)/shard_map/ppermute | solution.py:884
  435.4 9.9 %copy-start.12 = (bf16[256,2560]{1,0:T(8,128)(2,1)S(1)}, bf16[256,2560]{1,0:T(8,128)(2,1)}, u32[]{:S(2)}) copy-start(bf16[256,2560]{1,0:T(8,128)(2,1)} %merge.5) | copy-start | bytes 3932164
  435.4 15.0 %copy-start.20 = (f32[8,1024]{1,0:T(8,128)S(1)}, f32[8,1024]{1,0:T(8,128)}, u32[]{:S(2)}) copy-start(f32[8,1024]{1,0:T(8,128)} %get-tuple-element.200) | copy-start | bytes 98308
  435.4 36.6 %collective-permute-start.19 = (bf16[256,1536]{1,0:T(8,128)(2,1)}, bf16[256,1536]{1,0:T(8,128)(2,1)}, u32[]{:S(2)}, u32[]{:S(2)}) collective-permute-start(bf16[256,1536]{1,0:T(8,128)(2,1)} %get-tuple-element.197), channel_id=1, source_target_pairs={{0,4},{2,6},{4,0},{6,2},{8,12},{10,14},{12,8},{14,10},{16,20},{18,... | collective-permute-start | bytes 2359304 | tf_op jit(solution)/shard_map/ppermute | solution.py:880
  446.3 20.4 %collective-permute-start.21 = (bf16[64,2560]{1,0:T(8,128)(2,1)}, bf16[64,2560]{1,0:T(8,128)(2,1)}, u32[]{:S(2)}, u32[]{:S(2)}) collective-permute-start(bf16[64,2560]{1,0:T(8,128)(2,1)} %get-tuple-element.229), channel_id=1, source_target_pairs={{0,8},{2,10},{4,12},{6,14},{8,16},{10,18},{12,20},{14,22},{16,24},... | collective-permute-start | bytes 983048 | tf_op jit(solution)/shard_map/ppermute | solution.py:972
  446.3 25.7 %collective-permute-start.22 = (bf16[64,2560]{1,0:T(8,128)(2,1)}, bf16[64,2560]{1,0:T(8,128)(2,1)}, u32[]{:S(2)}, u32[]{:S(2)}) collective-permute-start(bf16[64,2560]{1,0:T(8,128)(2,1)} %get-tuple-element.228), channel_id=1, source_target_pairs={{0,16},{2,18},{4,20},{6,22},{8,24},{10,26},{12,28},{14,30},{16,0},... | collective-permute-start | bytes 983048 | tf_op jit(solution)/shard_map/ppermute | solution.py:972
  449.4 22.6 %collective-permute-start.23 = (bf16[64,2560]{1,0:T(8,128)(2,1)}, bf16[64,2560]{1,0:T(8,128)(2,1)}, u32[]{:S(2)}, u32[]{:S(2)}) collective-permute-start(bf16[64,2560]{1,0:T(8,128)(2,1)} %get-tuple-element.227), channel_id=1, source_target_pairs={{0,24},{2,26},{4,28},{6,30},{8,0},{10,2},{12,4},{14,6},{16,8},{18,... | collective-permute-start | bytes 983048 | tf_op jit(solution)/shard_map/ppermute | solution.py:972
  466.7 5.4 %copy-start.14 = (bf16[1024,1024]{1,0:T(8,128)(2,1)}, bf16[1024,1024]{1,0:T(8,128)(2,1)S(1)}, u32[]{:S(2)}) copy-start(bf16[1024,1024]{1,0:T(8,128)(2,1)S(1)} %collective-permute-done.20.refs_1_) | copy-start | bytes 6291460
  472.0 11.7 %copy-start.17 = (bf16[64,4096]{1,0:T(8,128)(2,1)S(1)}, bf16[64,4096]{1,0:T(8,128)(2,1)}, u32[]{:S(2)}) copy-start(bf16[64,4096]{1,0:T(8,128)(2,1)} %reduce-scatter.2.cloned.1.call-done) | copy-start | bytes 1572868
  472.1 13.4 %collective-permute-start.24 = (f32[16,1024]{1,0:T(8,128)S(1)}, f32[16,1024]{1,0:T(8,128)S(1)}, u32[]{:S(2)}, u32[]{:S(2)}) collective-permute-start(f32[16,1024]{1,0:T(8,128)S(1)} %concatenate.24), channel_id=1, source_target_pairs={{0,2},{2,0},{4,6},{6,4},{8,10},{10,8},{12,14},{14,12},{16,18},{18,... | collective-permute-start | bytes 196616 | tf_op jit(solution)/shard_map/ppermute | solution.py:998
  474.6 24.3 %collective-permute-start.28 = (bf16[64,1536]{1,0:T(8,128)(2,1)}, bf16[64,1536]{1,0:T(8,128)(2,1)}, u32[]{:S(2)}, u32[]{:S(2)}) collective-permute-start(bf16[64,1536]{1,0:T(8,128)(2,1)} %get-tuple-element.232), channel_id=1, source_target_pairs={{0,8},{2,10},{4,12},{6,14},{8,16},{10,18},{12,20},{14,22},{16,24},... | collective-permute-start | bytes 589832 | tf_op jit(solution)/shard_map/ppermute | solution.py:972
  481.4 17.4 %collective-permute-start.29 = (bf16[64,1536]{1,0:T(8,128)(2,1)}, bf16[64,1536]{1,0:T(8,128)(2,1)}, u32[]{:S(2)}, u32[]{:S(2)}) collective-permute-start(bf16[64,1536]{1,0:T(8,128)(2,1)} %get-tuple-element.231), channel_id=1, source_target_pairs={{0,16},{2,18},{4,20},{6,22},{8,24},{10,26},{12,28},{14,30},{16,0},... | collective-permute-start | bytes 589832 | tf_op jit(solution)/shard_map/ppermute | solution.py:972
  482.4 16.4 %collective-permute-start.30 = (bf16[64,1536]{1,0:T(8,128)(2,1)}, bf16[64,1536]{1,0:T(8,128)(2,1)}, u32[]{:S(2)}, u32[]{:S(2)}) collective-permute-start(bf16[64,1536]{1,0:T(8,128)(2,1)} %get-tuple-element.230), channel_id=1, source_target_pairs={{0,24},{2,26},{4,28},{6,30},{8,0},{10,2},{12,4},{14,6},{16,8},{18,... | collective-permute-start | bytes 589832 | tf_op jit(solution)/shard_map/ppermute | solution.py:972
  483.8 15.1 %collective-permute-start.27 = (bf16[64,2048]{1,0:T(8,128)(2,1)S(1)}, bf16[64,2048]{1,0:T(8,128)(2,1)S(1)}, u32[]{:S(2)}, u32[]{:S(2)}) collective-permute-start(bf16[64,2048]{1,0:T(8,128)(2,1)S(1)} %slice.91), channel_id=1, source_target_pairs={{0,1},{1,0},{2,3},{3,2},{4,5},{5,4},{6,7},{7,6},{8,9},{9,8},{10,11... | collective-permute-start | bytes 786440 | tf_op jit(solution)/shard_map/ppermute | solution.py:884
  485.5 4.3 collective-permute-start.25
  489.8 9.0 %collective-permute-start.26 = (f32[16,1024]{1,0:T(8,128)S(1)}, f32[16,1024]{1,0:T(8,128)S(1)}, u32[]{:S(2)}, u32[]{:S(2)}) collective-permute-start(f32[16,1024]{1,0:T(8,128)S(1)} %add.150), channel_id=1, source_target_pairs={{0,1},{1,0},{2,3},{3,2},{4,5},{5,4},{6,7},{7,6},{8,9},{9,8},{10,11... | collective-permute-start | bytes 196616 | tf_op jit(solution)/shard_map/ppermute | solution.py:884
  498.9 4.3 collective-permute-start.31
  503.2 5.3 %collective-permute-start.32 = (f32[16,1024]{1,0:T(8,128)S(1)}, f32[16,1024]{1,0:T(8,128)S(1)}, u32[]{:S(2)}, u32[]{:S(2)}) collective-permute-start(f32[16,1024]{1,0:T(8,128)S(1)} %add.161), channel_id=1, source_target_pairs={{0,16},{2,18},{4,20},{6,22},{8,24},{10,26},{12,28},{14,30},{16,0},... | collective-permute-start | bytes 196616 | tf_op jit(solution)/shard_map/ppermute | solution.py:1004
Sparse Core Ops, SparseCore 0:
  10.9 61.4 all-gather.2
  74.5 77.0 all-gather.4
  292.0 109.0 reduce-scatter.1

commit v5 on v4

--- a/solution.py
+++ b/solution.py
@@ -136,7 +136,6 @@
 
     row_start = start_ref[...]
     query_pos = block * QB + lax.broadcasted_iota(jnp.int32, (1, QB), 1)
-    key_iota = lax.broadcasted_iota(jnp.int32, (KB, QB), 0)
     first = lo_ref[pl.program_id(0), block]
     last = (block + 1) * (QB // KB)
     rows = pl.ds(pl.multiple_of(block * QB, QB), QB)
@@ -147,31 +146,31 @@
     deltas = [jnp.sum(prod[h * HD : (h + 1) * HD], axis=0, keepdims=True) for h in range(2)]
     lses = [pick(l_refs, slice(h, h + 1)) for h in range(2)]
 
-    def chunk(j, carry):
-        base = pl.multiple_of(j * KB, KB)
-        window = pl.ds(base, KB)
-        keys = k_ref[window, :]
-        vals = v_ref[window, :]
-        key_pos = key_iota + base
-        ok = (key_pos >= row_start) & (key_pos <= query_pos)
-        new = []
-        dv = dv_ref[window, :]
-        dk = dk_ref[window, :]
-        for h in range(2):
-            s = jnp.where(ok, dot(keys, q_heads[h], NT) * SCORE_SCALE, NEG)
-            p = jnp.exp2(s - lses[h])
-            dp = dot(vals, g_heads[h], NT)
-            ds = (p * (dp - deltas[h])).astype(BF16)
-            dv = dv + dot(p.astype(BF16), g_heads[h], NN)
-            dk = dk + dot(ds, q_heads[h], NN)
-            kt = kt_ref[h * HD : (h + 1) * HD, window]
-            new.append(carry[h] + dot(kt, ds, NN))
-        dv_ref[window, :] = dv
-        dk_ref[window, :] = dk
-        return tuple(new)
-
-    dq = lax.fori_loop(first, last, chunk, tuple(jnp.zeros((HD, QB), F32) for _ in range(2)))
-    out_ref[rows, :PAIR] = (jnp.concatenate(dq, axis=0) * 0.125).T.astype(BF16)
+    count = last - first
+    base = pl.multiple_of(first * KB, KB)
+
+    for chunks in range(1, max_chunks + 1):
+
+        @pl.when(count == chunks)
+        def _(size=chunks * KB):
+            window = pl.ds(base, size)
+            keys = k_ref[window, :]
+            vals = v_ref[window, :]
+            key_pos = lax.broadcasted_iota(jnp.int32, (size, QB), 0) + base
+            ok = (key_pos >= row_start) & (key_pos <= query_pos)
+            dv = dk = 0.0
+            dq = []
+            for h in range(2):
+                s = jnp.where(ok, dot(keys, q_heads[h], NT) * SCORE_SCALE, NEG)
+                p = jnp.exp2(s - lses[h])
+                dp = dot(vals, g_heads[h], NT)
+                ds = (p * (dp - deltas[h])).astype(BF16)
+                dv = dv + dot(p.astype(BF16), g_heads[h], NN)
+                dk = dk + dot(ds, q_heads[h], NN)
+                dq.append(dot(kt_ref[h * HD : (h + 1) * HD, window], ds, NN))
+            dv_ref[window, :] += dv
+            dk_ref[window, :] += dk
+            out_ref[rows, :PAIR] = (jnp.concatenate(dq, axis=0) * 0.125).T.astype(BF16)
 
     @pl.when(block == blocks - 1)
     def _():
@@ -547,10 +546,11 @@
     refs = refs[n + m + 5 :]
     send_ref, keep_ref, hid_ref, d_resid_ref, sum_ref, turned_ref = refs[:6]
     d_o_refs = refs[6 : 6 + groups]
-    up_hold, down_hold, total_ref = refs[6 + groups :]
+    up_hold, down_hold, total_ref, held_ref = refs[6 + groups :]
     step = pl.program_id(0)
     rows, features = d_ref.shape
     half = features // NC
+    width = send_ref.shape[1]
 
     @pl.when(step == 0)
     def _():
@@ -562,7 +562,7 @@
         up.load(at_ref, step, up_refs, up_hold)
         down.load(at_ref, step, down_refs, down_hold)
         column_sum = 0.0
-        d_pres = []
+        block = pl.ds(pl.multiple_of(step * HIDDEN_BLOCK, HIDDEN_BLOCK), HIDDEN_BLOCK)
         for r in range(0, rows, ROWS):
             part = slice(r, r + ROWS)
             d_act = dot(d_ref[part, :], down_hold[...], NN)
@@ -573,19 +573,19 @@
                 z * (0.5 * GELU_C + (1.5 * GELU_C * 0.044715) * square)
             )
             d_pre = (slope * d_act).astype(BF16)
-            d_pres.append(d_pre)
+            held_ref[part, block] = d_pre
             column_sum = column_sum + rows_sum(d_pre.astype(F32))
             total_ref[part, :] += dot(d_pre, up_hold[...], NT)
         hid_ref[...] = column_sum
-        d_pre = jnp.concatenate(d_pres, axis=0)
+
+    @pl.when(step >= steps)
+    def _():
+        d_pre = held_ref[:, pl.ds(pl.multiple_of((step - steps) * width, width), width)]
         c = at_ref[3]
         there = pl.ds(pl.multiple_of((1 - c) * half, half), half)
         here = pl.ds(pl.multiple_of(c * half, half), half)
         send_ref[...] = dot(ut_ref[there, :], d_pre, NN).astype(BF16)
         keep_ref[...] = dot(ut_ref[here, :], d_pre, NN).astype(BF16)
-
-    @pl.when(step >= steps)
-    def _():
         d_u = total_ref[pl.ds(pl.multiple_of((step - steps) * ROWS, ROWS), ROWS), :]
         normed, scale = unit_rows(resid_ref[...])
         sum_ref[0:1, :] += rows_sum(normed * d_u)
@@ -598,9 +598,9 @@
         d_attn = norm_back(normed, scale, d_resid * gain_ref[1:2, :]).astype(BF16)
         sum_ref[4:5, :] += rows_sum(d_attn.astype(F32))
         store_turned(turned_ref, d_attn, turn)
-        width = d_o_refs[0].shape[1]
+        size = d_o_refs[0].shape[1]
         for g in range(groups):
-            d_o_refs[g][...] = dot(d_attn, wo_ref[:, g * width : (g + 1) * width], NN).astype(BF16)
+            d_o_refs[g][...] = dot(d_attn, wo_ref[:, g * size : (g + 1) * size], NN).astype(BF16)
 
 
 def feed_back(turn, groups, at, d_mlp, u_turned, pre, up, down, resid, attn, cotangent, weight_out, gain):
@@ -609,6 +609,9 @@
     steps = hidden // HIDDEN_BLOCK
     width = features // groups
     half = features // NC
+    later_columns = pl.BlockSpec(
+        (half, hidden * ROWS // rows), lambda j, *_: (0, jnp.maximum(j - steps, 0))
+    )
     return call(
         functools.partial(feed_back_kernel, turn, groups, up, down, steps),
         "feed_back",
@@ -617,7 +620,7 @@
         + [column_spec(rows, steps), *up.specs, *down.specs]
         + [later_spec(features, steps), later_spec(features, steps), later_spec(features, steps, True)]
         + [fixed(weight_out.shape), fixed(gain.shape)],
-        [column_spec(half, steps), column_spec(half, steps)]
+        [later_columns, later_columns]
         + [column_spec(1, steps), later_spec(features, steps), fixed((8, features))]
         + [later_turned(features, steps)]
         + [later_spec(width, steps)] * groups,
@@ -632,6 +635,7 @@
             pltpu.VMEM((features, HIDDEN_BLOCK), BF16),
             pltpu.VMEM((features, HIDDEN_BLOCK), BF16),
             pltpu.VMEM((rows, features), F32),
+            pltpu.VMEM((rows, hidden), BF16),
         ],
     )
 
@@ -942,7 +946,7 @@
         up_there = swap_core(send)
         out_there = swap_core(self.rows_times(turned, [1 - self.c, self.c], o_own))
         out_keep = self.rows_times(turned, [self.c, self.c], o_own)
-        later, out_keep = tie(later, out_keep)
+        later, out_keep, out_there, up_there = tie(later, out_keep, out_there, up_there)
         self.outs, self.ups = [out_keep, out_there], [keep, up_there]
         return later
 

time: 523 us -> 510 us (0.975)
  Pallas kernels: 332 us -> 308 us
  waiting for transfers between devices: 93.8 us -> 102 us
    pallas_call x4, Pallas kernels: 83 us -> 61.2 us  [attention_backward(): pl.pallas_call(functools.partial(bwd_kernel, halves), grid_spec=pltpu.Pre...]
    ppermute x10, waiting for transfers between devices: 32.8 us -> 43.9 us  [swap_y(): return lax.ppermute(a, 'tensor', [(0, 1), (1, 0)])]
    unnamed x54 -> x56, local copies, waits for them, and re-layouts: 13.4 us -> 12.5 us
  transfers between devices with their start and end apart: 36 -> 36, of which waited for: 12 -> 14; matrix products, arithmetic and copies ran while one was open for 4% -> 4% of each run, Pallas kernels for 48% -> 44%
where the time goes in v5:
time: 510 us; the launch traced here: 505 us
  Pallas kernels  308 us (60%)
  waiting for transfers between devices  102 us (20%)
  starting transfers between devices  45.7 us (9%)
  local copies, waits for them, and re-layouts  19.6 us (4%)
  other arithmetic  15.2 us (3%)
  between operations  14.7 us (3%)
    pallas_call x17, Pallas kernels, call(): pl.pallas_call(body, grid_spec=pltpu.PrefetchScalarGridSpec(num_scalar_pr...  194 us
    pallas_call x4, Pallas kernels, attention_backward(): pl.pallas_call(functools.partial(bwd_kernel, halves), grid_spec=pltpu.Pre...  61.2 us
    pallas_call x4, Pallas kernels, attention_forward(): pl.pallas_call(functools.partial(fwd_kernel, pairs), grid_spec=grid_spec,...  51.9 us
    ppermute x10, waiting for transfers between devices, swap_y(): return lax.ppermute(a, 'tensor', [(0, 1), (1, 0)])  43.9 us
    all_gather x1, waiting for transfers between devices, gather_first(): qkv = lax.all_gather(shard_qkv, 'dp', axis=0, tiled=True)  26.5 us
    ppermute x10, starting transfers between devices, swap_y(): return lax.ppermute(a, 'tensor', [(0, 1), (1, 0)])  17 us
    ppermute x6, starting transfers between devices, z_pieces(): lax.ppermute(a, 'dp', z_pairs(k))  15.1 us
    ppermute x3, waiting for transfers between devices, spread_z(): lax.ppermute(shard, 'dp', z_pairs(k))  14.3 us
  transfers between devices with their start and end apart: 36, of which 14 were waited for; matrix products, arithmetic and copies ran while one was open for 4% of the time, Pallas kernels for 44%

profile of v5, /device:TPU:0, one launch (start us, length us, event | category | flops | bytes accessed | tf_op | source)
XLA Modules:
  0.0 504.9 jit_solution(5853029154992305999)
XLA Ops:
  9.0 1.1 convert_bitcast_fusion
  10.1 3.0 collective-permute-start.3
  14.3 1.6 collective-permute-start
  15.9 2.6 collective-permute-start.1
  18.5 1.3 collective-permute-start.2
  19.8 2.3 copy-done
  22.1 4.2 first_norm.1
  26.4 2.1 copy-done.1
  28.4 2.1 copy-done.2
  31.4 14.2 %collective-permute-done.1 = bf16[64,2560]{1,0:T(8,128)(2,1)S(1)} collective-permute-done((bf16[64,2560]{1,0:T(8,128)(2,1)S(1)}, bf16[64,2560]{1,0:T(8,128)(2,1)S(1)}, u32[]{:S(2)}, u32[]{:S(2)}) %collective-permute-start.1) | collective-permute-done | bytes 327712 | tf_op jit(solution)/shard_map/ppermute | solution.py:892
  45.9 26.5 %all-gather.3.cloned.1.call-done.w_ref = bf16[1024,1536]{1,0:T(8,128)(2,1)} async-done(((bf16[64,1536]{1,0:T(8,128)(2,1)}), bf16[1024,1536]{1,0:T(8,128)(2,1)}) %all-gather.3.cloned.1.call-update) | async-done | bytes 3145744 | tf_op jit(solution)/shard_map/all_gather | solution.py:905
  73.0 1.5 collective-permute-start.5
  75.4 1.8 convert_reduce_fusion
  77.8 11.3 %project.1.refs_0_.refs_1_.refs_2_.refs_3_.refs_4_.refs_5_.q_ref.k_ref.v_ref = bf16[2048,1536]{1,0:T(8,128)(2,1)} custom-call(bf16[2048,1024]{1,0:T(8,128)(2,1)} %copy-done.2, bf16[1024,1536]{1,0:T(8,128)(2,1)} %all-gather.3.cloned.1.call-done.w_ref, f32[1,1536]{1,0:T(1,128)} %broadcast_in_dim_reshape.3.b_ref), custom_call_target="tpu_custom_call" | custom-call | flops 1 | bytes 1 | tf_op jit(solution)/shard_map/project/pallas_call | solution.py:290
  89.1 14.8 %attention_forward.4 = (bf16[1024,256]{1,0:T(8,128)(2,1)}, f32[1,2,2,1024]{3,2,1,0:T(2,128)}) custom-call(s32[1,8]{1,0:T(1,128)} %and_select_fusion.lo_ref, s32[1]{0:T(128)} %bitcast.14.off_ref.at_ref, bf16[2048,1536]{1,0:T(8,128)(2,1)} %project.1.refs_0_.refs_1_.refs_2_.refs_3_.refs_4_.refs_5_.q_ref.k_ref.v_ref, ...), custom_call_target="tpu_custom_call" | custom-call | flops 1 | bytes 1 | tf_op jit(solution)/shard_map/attention_forward/pallas_call | solution.py:104
  103.8 5.2 %collective-permute-done.4.refs_5_.refs_1_ = bf16[4,64,2560]{2,1,0:T(8,128)(2,1)S(1)} collective-permute-done((bf16[4,64,2560]{2,1,0:T(8,128)(2,1)S(1)}, bf16[4,64,2560]{2,1,0:T(8,128)(2,1)S(1)}, u32[]{:S(2)}, u32[]{:S(2)}) %collective-permute-start.4) | collective-permute-done | bytes 1310752 | tf_op jit(solution)/shard_map/ppermute | solution.py:884
  109.7 1.5 collective-permute-start.9
  111.7 15.0 %attention_forward.5 = (bf16[1024,256]{1,0:T(8,128)(2,1)}, f32[1,2,2,1024]{3,2,1,0:T(2,128)}) custom-call(s32[1,8]{1,0:T(1,128)} %and_select_fusion.lo_ref, s32[1]{0:T(128)} %bitcast.14.off_ref.at_ref, bf16[2048,1536]{1,0:T(8,128)(2,1)} %project.1.refs_0_.refs_1_.refs_2_.refs_3_.refs_4_.refs_5_.q_ref.k_ref.v_ref, ...), custom_call_target="tpu_custom_call" | custom-call | flops 1 | bytes 1 | tf_op jit(solution)/shard_map/attention_forward/pallas_call | solution.py:104
  126.8 11.3 %attention_forward.6 = (bf16[1024,256]{1,0:T(8,128)(2,1)}, f32[1,2,2,1024]{3,2,1,0:T(2,128)}) custom-call(s32[1,8]{1,0:T(1,128)} %and_select_fusion.lo_ref, s32[1]{0:T(128)} %bitcast.off_ref.at_ref, bf16[2048,1536]{1,0:T(8,128)(2,1)} %project.1.refs_0_.refs_1_.refs_2_.refs_3_.refs_4_.refs_5_.q_ref.k_ref.v_ref, ...), custom_call_target="tpu_custom_call" | custom-call | flops 1 | bytes 1 | tf_op jit(solution)/shard_map/attention_forward/pallas_call | solution.py:104
  138.1 14.1 %collective-permute-done.10.refs_2_ = bf16[1024,256]{1,0:T(8,128)(2,1)} collective-permute-done((bf16[1024,256]{1,0:T(8,128)(2,1)}, bf16[1024,256]{1,0:T(8,128)(2,1)}, u32[]{:S(2)}, u32[]{:S(2)}) %collective-permute-start.10) | collective-permute-done | bytes 524320 | tf_op jit(solution)/shard_map/ppermute | solution.py:888
  152.2 1.5 collective-permute-start.11
  154.9 10.8 %attention_forward.7 = (bf16[1024,256]{1,0:T(8,128)(2,1)}, f32[1,2,2,1024]{3,2,1,0:T(2,128)}) custom-call(s32[1,8]{1,0:T(1,128)} %and_select_fusion.lo_ref, s32[1]{0:T(128)} %bitcast.off_ref.at_ref, bf16[2048,1536]{1,0:T(8,128)(2,1)} %project.1.refs_0_.refs_1_.refs_2_.refs_3_.refs_4_.refs_5_.q_ref.k_ref.v_ref, ...), custom_call_target="tpu_custom_call" | custom-call | flops 1 | bytes 1 | tf_op jit(solution)/shard_map/attention_forward/pallas_call | solution.py:104
  167.8 11.9 %middle.1 = (f32[1024,1024]{1,0:T(8,128)}, f32[1024,1024]{1,0:T(8,128)}, bf16[1024,1024]{1,0:T(8,128)(2,1)}, bf16[1024,1024]{1,0:T(8,128)(2,1)}, bf16[1024,1024]{1,0:T(8,128)(2,1)}, /*index=5*/bf16[1024,1024]{1,0:T(8,128)(2,1)}) custom-call(s32[4]{0:T(128)} %pad_add_fusion.at_ref, bf16[1024,256]{1,0:T(8,128)(2,1)} %get-tuple-element.141.refs_0_, ...), custom_call_target="tpu_custom_call" | custom-call | flops 1 | bytes 1 | tf_op jit(solution)/shard_map/middle/pallas_call | solution.py:290
  179.7 33.7 %feed.1 = (bf16[1024,4096]{1,0:T(8,128)(2,1)}, bf16[1024,1024]{1,0:T(8,128)(2,1)}, bf16[1024,1024]{1,0:T(8,128)(2,1)}, bf16[1024,1024]{1,0:T(8,128)(2,1)}, f32[8,1024]{1,0:T(8,128)}) custom-call(s32[4]{0:T(128)} %pad_add_fusion.at_ref, bf16[1024,1024]{1,0:T(8,128)(2,1)} %get-tuple-element.150.u_ref, f32[1,4096]{1,0:T(1,128)} %bitcast.85, ...), custom_call_target="tpu_custom_call" | custom-call | flops 1 | bytes 1 | tf_op jit(solution)/shard_map/feed/pallas_call | solution.py:290
  213.4 50.3 %feed_back.1 = (bf16[512,4096]{1,0:T(8,128)(2,1)}, bf16[512,4096]{1,0:T(8,128)(2,1)}, f32[1,4096]{1,0:T(1,128)}, f32[1024,1024]{1,0:T(8,128)}, f32[8,1024]{1,0:T...) custom-call(s32[4]{0:T(128)} %pad_add_fusion.at_ref, ...), custom_call_target="tpu_custom_call" | custom-call | flops 1 | bytes 1 | tf_op jit(solution)/shard_map/feed_back/pallas_call | solution.py:290
  264.4 4.6 grad_rows.4
  269.5 3.8 collective-permute-start.15
  274.0 4.5 grad_rows.3.refs_0_
  278.5 15.3 %grad_down.1 = bf16[1024,4096]{1,0:T(8,128)(2,1)} custom-call(bf16[1024,1024]{1,0:T(8,128)(2,1)} %get-tuple-element.168.left_ref, bf16[1024,4096]{1,0:T(8,128)(2,1)} %get-tuple-element.158.pre_ref), custom_call_target="tpu_custom_call" | custom-call | flops 1 | bytes 1 | tf_op jit(solution)/shard_map/grad_down/pallas_call | solution.py:290
  293.8 3.0 collective-permute-done.15.refs_3_
  297.8 6.0 %merge.3 = bf16[512,2560]{1,0:T(8,128)(2,1)} custom-call(s32[1]{0:T(128)} %constant.137.clone.1.at_ref, bf16[512,1024]{1,0:T(8,128)(2,1)} %grad_rows.3.refs_0_, bf16[512,1024]{1,0:T(8,128)(2,1)} %copy-done.11, bf16[512,4096]{1,0:T(8,128)(2,1)} %get-tuple-element.196.refs_2_, bf16[512,4096]{1,0:T(8,128)(2,1)} %collective-permute-done.14.refs_3_), custom_call_target="tpu_custom_call" | custom-call | flops 1 | bytes 1 | tf_op jit(solution)/shard_map/merge/pallas_call | solution.py:290
  303.8 1.7 collective-permute-start.16
  305.6 15.2 %attention_backward.4.refs_6_ = bf16[2048,1536]{1,0:T(8,128)(2,1)} custom-call(s32[1,8]{1,0:T(1,128)} %and_select_fusion.lo_ref, s32[1]{0:T(128)} %bitcast.18.place_ref, bf16[2048,1536]{1,0:T(8,128)(2,1)} %project.1.refs_0_.refs_1_.refs_2_.refs_3_.refs_4_.refs_5_.q_ref.k_ref.v_ref, ...), custom_call_target="tpu_custom_call" | custom-call | flops 1 | bytes 1 | tf_op jit(solution)/shard_map/attention_backward/pallas_call | solution.py:216
  320.8 15.3 %attention_backward.5.refs_6_ = bf16[2048,1536]{1,0:T(8,128)(2,1)} custom-call(s32[1,8]{1,0:T(1,128)} %and_select_fusion.lo_ref, s32[1]{0:T(128)} %bitcast.18.place_ref, bf16[2048,1536]{1,0:T(8,128)(2,1)} %project.1.refs_0_.refs_1_.refs_2_.refs_3_.refs_4_.refs_5_.q_ref.k_ref.v_ref, ...), custom_call_target="tpu_custom_call", output_to_operand_aliasing={{}: (12, {})} | custom-call | flops 1 | bytes 1 | tf_op jit(solution)/shard_map/attention_backward/pallas_call | solution.py:216
  336.0 15.3 %attention_backward.6.refs_6_ = bf16[2048,1536]{1,0:T(8,128)(2,1)} custom-call(s32[1,8]{1,0:T(1,128)} %and_select_fusion.lo_ref, s32[1]{0:T(128)} %bitcast.18.place_ref, bf16[2048,1536]{1,0:T(8,128)(2,1)} %project.1.refs_0_.refs_1_.refs_2_.refs_3_.refs_4_.refs_5_.q_ref.k_ref.v_ref, ...), custom_call_target="tpu_custom_call", output_to_operand_aliasing={{}: (12, {})} | custom-call | flops 1 | bytes 1 | tf_op jit(solution)/shard_map/attention_backward/pallas_call | solution.py:216
  351.4 11.4 %collective-permute-done.16.refs_4_ = bf16[512,2560]{1,0:T(8,128)(2,1)S(1)} collective-permute-done((bf16[512,2560]{1,0:T(8,128)(2,1)}, bf16[512,2560]{1,0:T(8,128)(2,1)S(1)}, u32[]{:S(2)}, u32[]{:S(2)}) %collective-permute-start.16) | collective-permute-done | bytes 2621472 | tf_op jit(solution)/shard_map/ppermute | solution.py:888
  362.7 1.5 copy-done.10
  364.2 4.9 merge.4
  369.5 15.3 %attention_backward.7.dq_ref.right_ref = bf16[2048,1536]{1,0:T(8,128)(2,1)} custom-call(s32[1,8]{1,0:T(1,128)} %and_select_fusion.lo_ref, s32[1]{0:T(128)} %bitcast.18.place_ref, bf16[2048,1536]{1,0:T(8,128)(2,1)} %project.1.refs_0_.refs_1_.refs_2_.refs_3_.refs_4_.refs_5_.q_ref.k_ref.v_ref, ...), custom_call_target="tpu_custom_call", output_to_operand_aliasing={{}: (12, {})} | custom-call | flops 1 | bytes 1 | tf_op jit(solution)/shard_map/attention_backward/pallas_call | solution.py:216
  384.8 8.1 %d_in.2 = (bf16[1024,1024]{1,0:T(8,128)(2,1)}, f32[8,1024]{1,0:T(8,128)}, f32[8,1536]{1,0:T(8,128)}) custom-call(s32[1]{0:T(128)} %bitcast.14.off_ref.at_ref, bf16[2048,1536]{1,0:T(8,128)(2,1)} %attention_backward.7.dq_ref.right_ref, bf16[1024,1536]{1,0:T(8,128)(2,1)} %all-gather.3.cloned.1.call-done.w_ref, bf16[2048,1024]{1,0:T(8,128)(2,1)} %refs_2_.1), custom_call_target="tpu_custom_call" | custom-call | flops 2200000000 | bytes 1 | tf_op jit(solution)/shard_map/d_in/pallas_call | solution.py:290
  392.9 9.2 %grad_rows.5 = bf16[512,1536]{1,0:T(8,128)(2,1)} custom-call(s32[2]{0:T(128)} %pad_add_fusion.2.at_ref, bf16[2,512,2048]{2,1,0:T(8,128)(2,1)} %bitcast.63, bf16[2048,1536]{1,0:T(8,128)(2,1)} %attention_backward.7.dq_ref.right_ref), custom_call_target="tpu_custom_call" | custom-call | flops 1 | bytes 1 | tf_op jit(solution)/shard_map/grad_rows/pallas_call | solution.py:290
  402.1 2.8 collective-permute-done.17.refs_5_
  404.8 1.1 collective-permute-start.20
  407.5 5.3 %merge.5 = bf16[256,2560]{1,0:T(8,128)(2,1)} custom-call(s32[1]{0:T(128)} %bitcast.2.at_ref, bf16[512,1024]{1,0:T(8,128)(2,1)} %grad_rows.3.refs_0_, bf16[512,1024]{1,0:T(8,128)(2,1)} %copy-done.11, bf16[512,4096]{1,0:T(8,128)(2,1)} %get-tuple-element.196.refs_2_, bf16[512,4096]{1,0:T(8,128)(2,1)} %collective-permute-done.14.refs_3_, ...), custom_call_target="tpu_custom_call" | custom-call | flops 1 | bytes 1 | tf_op jit(solution)/shard_map/merge/pallas_call | solution.py:290
  412.9 9.3 %grad_both.1 = (bf16[256,1536]{1,0:T(8,128)(2,1)}, bf16[256,1536]{1,0:T(8,128)(2,1)}) custom-call(s32[2]{0:T(128)} %pad_add_fusion.1.at_ref, bf16[2,2,256,2048]{3,2,1,0:T(8,128)(2,1)} %bitcast.64, bf16[2048,1536]{1,0:T(8,128)(2,1)} %attention_backward.7.dq_ref.right_ref, bf16[2,256,1536]{2,1,0:T(8,128)(2,1)} %bitcast.23.there_ref), custom_call_target="tpu_custom_call" | custom-call | flops 1 | bytes 1 | tf_op jit(solution)/shard_map/grad_both/pallas_call | solution.py:290
  422.6 8.1 %d_in.3 = (bf16[1024,1024]{1,0:T(8,128)(2,1)}, f32[8,1024]{1,0:T(8,128)}, f32[8,1536]{1,0:T(8,128)}) custom-call(s32[1]{0:T(128)} %bitcast.off_ref.at_ref, bf16[2048,1536]{1,0:T(8,128)(2,1)} %attention_backward.7.dq_ref.right_ref, bf16[1024,1536]{1,0:T(8,128)(2,1)} %all-gather.3.cloned.1.call-done.w_ref, bf16[2048,1024]{1,0:T(8,128)(2,1)} %refs_2_.1), custom_call_target="tpu_custom_call" | custom-call | flops 2200000000 | bytes 1 | tf_op jit(solution)/shard_map/d_in/pallas_call | solution.py:290
  432.5 2.6 collective-permute-start.21
  435.9 1.6 collective-permute-start.23
  438.4 14.7 %collective-permute-done.20.refs_1_ = bf16[1024,1024]{1,0:T(8,128)(2,1)S(1)} collective-permute-done((bf16[1024,1024]{1,0:T(8,128)(2,1)}, bf16[1024,1024]{1,0:T(8,128)(2,1)S(1)}, u32[]{:S(2)}, u32[]{:S(2)}) %collective-permute-start.20) | collective-permute-done | bytes 2097184 | tf_op jit(solution)/shard_map/ppermute | solution.py:888
  453.1 5.3 %collective-permute-done.22 = bf16[64,2560]{1,0:T(8,128)(2,1)} collective-permute-done((bf16[64,2560]{1,0:T(8,128)(2,1)}, bf16[64,2560]{1,0:T(8,128)(2,1)}, u32[]{:S(2)}, u32[]{:S(2)}) %collective-permute-start.22) | collective-permute-done | bytes 327712 | tf_op jit(solution)/shard_map/ppermute | solution.py:976
  458.6 1.6 add_convert_fusion
  461.0 7.5 %collective-permute-start.28 = (bf16[64,1536]{1,0:T(8,128)(2,1)}, bf16[64,1536]{1,0:T(8,128)(2,1)}, u32[]{:S(2)}, u32[]{:S(2)}) collective-permute-start(bf16[64,1536]{1,0:T(8,128)(2,1)} %get-tuple-element.236), channel_id=1, source_target_pairs={{0,8},{2,10},{4,12},{6,14},{8,16},{10,18},{12,20},{14,22},{16,24},... | collective-permute-start | bytes 589832 | tf_op jit(solution)/shard_map/ppermute | solution.py:976
  468.5 1.4 collective-permute-start.29
  469.9 1.3 collective-permute-start.30
  472.1 1.7 collective-permute-start.25
  473.8 1.3 fusion.1
  475.2 1.3 collective-permute-done.25
  476.5 1.2 collective-permute-start.26
  478.3 7.0 %last.1 = bf16[1024,1024]{1,0:T(8,128)(2,1)} custom-call(s32[1]{0:T(128)} %bitcast.off_ref.at_ref, bf16[1024,1024]{1,0:T(8,128)(2,1)} %get-tuple-element.215.refs_0_, bf16[1024,1024]{1,0:T(8,128)(2,1)} %copy-done.14, bf16[2048,1024]{1,0:T(8,128)(2,1)} %refs_2_.1, f32[1024,1024]{1,0:T(8,128)} %get-tuple-element.217.refs_3_, f32[4,1024]{1,0:T(4,128)} %refs_4_.1), custom_call_target="tpu_custom_call" | custom-call | flops 1 | bytes 1 | tf_op jit(solution)/shard_map/last/pallas_call | solution.py:290
  486.2 2.1 collective-permute-start.31
  488.4 1.2 fusion.3
  489.6 1.1 collective-permute-done.31
  490.7 1.5 collective-permute-start.32
  494.3 1.6 collective-permute-done.32
  (141 shorter events, 26.4 us)
Async XLA Ops:
  7.2 12.6 %copy-start.3 = (f32[4,1024]{1,0:T(4,128)S(1)}, f32[4,1024]{1,0:T(4,128)}, u32[]{:S(2)}) copy-start(f32[4,1024]{1,0:T(4,128)} %refs_4_.1) | copy-start | bytes 49156
  7.2 65.2 %all-gather.3.cloned.1.call-start = ((), (), s32[]{:S(2)}) async-start(), calls=%async_computation.1 | async-start | bytes 3342336 | tf_op jit(solution)/shard_map/all_gather | solution.py:905
  7.2 1.0 copy-start.4
  8.2 6.0 %copy-start.19 = (f32[512,64]{0,1:T(8,128)S(1)}, f32[512,64]{0,1:T(8,128)}, u32[]{:S(2)}) copy-start(f32[512,64]{0,1:T(8,128)} %param.16) | copy-start | bytes 393220
  8.2 11.6 %copy-start.5 = (f32[4,1024]{1,0:T(4,128)S(1)}, f32[4,1024]{1,0:T(4,128)}, u32[]{:S(2)}) copy-start(f32[4,1024]{1,0:T(4,128)} %refs_12_.3) | copy-start | bytes 49156
  9.0 170.8 %all-gather.5.cloned.1.call-start = ((), (), s32[]{:S(2)}) async-start(), calls=%async_computation.2 | async-start | bytes 8912896 | tf_op jit(solution)/shard_map/all_gather | solution.py:912
  10.1 20.4 %collective-permute-start.3 = (bf16[64,2048]{1,0:T(8,128)(2,1)S(1)}, bf16[64,2048]{1,0:T(8,128)(2,1)S(1)}, u32[]{:S(2)}, u32[]{:S(2)}) collective-permute-start(bf16[64,2048]{1,0:T(8,128)(2,1)S(1)} %convert_bitcast_fusion), channel_id=1, source_target_pairs={{0,1},{1,0},{2,3},{3,2},{4,5},{5,4},{6,7},{7,6},{8,9},{9,8},{10,11... | collective-permute-start | bytes 786440 | tf_op jit(solution)/shard_map/ppermute | solution.py:888
  14.3 17.1 %collective-permute-start = (bf16[64,2560]{1,0:T(8,128)(2,1)S(1)}, bf16[64,2560]{1,0:T(8,128)(2,1)S(1)}, u32[]{:S(2)}, u32[]{:S(2)}) collective-permute-start(bf16[64,2560]{1,0:T(8,128)(2,1)S(1)} %pad_maximum_fusion.2), channel_id=1, source_target_pairs={{0,8},{2,10},{4,12},{6,14},{8,16},{10,18},{12,20},{14,22},{16,24},... | collective-permute-start | bytes 983048 | tf_op jit(solution)/shard_map/ppermute | solution.py:892
  15.9 29.7 %collective-permute-start.1 = (bf16[64,2560]{1,0:T(8,128)(2,1)S(1)}, bf16[64,2560]{1,0:T(8,128)(2,1)S(1)}, u32[]{:S(2)}, u32[]{:S(2)}) collective-permute-start(bf16[64,2560]{1,0:T(8,128)(2,1)S(1)} %pad_maximum_fusion.2), channel_id=1, source_target_pairs={{0,16},{2,18},{4,20},{6,22},{8,24},{10,26},{12,28},{14,30},{16,0},... | collective-permute-start | bytes 983048 | tf_op jit(solution)/shard_map/ppermute | solution.py:892
  18.5 27.2 %collective-permute-start.2 = (bf16[64,2560]{1,0:T(8,128)(2,1)S(1)}, bf16[64,2560]{1,0:T(8,128)(2,1)S(1)}, u32[]{:S(2)}, u32[]{:S(2)}) collective-permute-start(bf16[64,2560]{1,0:T(8,128)(2,1)S(1)} %pad_maximum_fusion.2), channel_id=1, source_target_pairs={{0,24},{2,26},{4,28},{6,30},{8,0},{10,2},{12,4},{14,6},{16,8},{18,... | collective-permute-start | bytes 983048 | tf_op jit(solution)/shard_map/ppermute | solution.py:892
  19.8 2.3 copy-start
  26.4 2.1 copy-start.1
  28.4 2.1 copy-start.2
  30.5 44.1 %copy-start.24 = (f32[2,1024]{1,0:T(2,128)S(1)}, f32[2,1024]{1,0:T(2,128)}, u32[]{:S(2)}) copy-start(f32[2,1024]{1,0:T(2,128)} %param.21) | copy-start | bytes 24580
  30.5 44.8 %copy-start.26 = (s32[1,2048]{1,0:T(1,128)S(1)}, s32[1,2048]{1,0:T(1,128)}, u32[]{:S(2)}) copy-start(s32[1,2048]{1,0:T(1,128)} %param.14) | copy-start | bytes 24580
  45.9 63.2 %copy-start.6 = (bf16[4,64,2560]{2,1,0:T(8,128)(2,1)}, bf16[4,64,2560]{2,1,0:T(8,128)(2,1)S(1)}, u32[]{:S(2)}) copy-start(bf16[4,64,2560]{2,1,0:T(8,128)(2,1)S(1)} %pad_maximum_fusion.refs_4_.refs_0_) | copy-start | bytes 3932164
  72.4 386.1 %reduce-scatter.2.cloned.1.call-start = ((), (), s32[]{:S(2)}) async-start(), calls=%async_computation.3 | async-start | bytes 8912896 | tf_op jit(solution)/shard_map/reduce_scatter | solution.py:938
  72.4 36.6 %collective-permute-start.4 = (bf16[4,64,2560]{2,1,0:T(8,128)(2,1)S(1)}, bf16[4,64,2560]{2,1,0:T(8,128)(2,1)S(1)}, u32[]{:S(2)}, u32[]{:S(2)}) collective-permute-start(bf16[4,64,2560]{2,1,0:T(8,128)(2,1)S(1)} %pad_maximum_fusion.refs_4_.refs_0_), channel_id=1, source_target_pairs={{0,4},{2,6},{4,0},{6,2},{8,12},{10,14},{12,8},{14,10},{16,20},{18,... | collective-permute-start | bytes 3932168 | tf_op jit(solution)/shard_map/ppermute | solution.py:884
  73.0 36.0 %collective-permute-start.5 = (bf16[4,64,2560]{2,1,0:T(8,128)(2,1)S(1)}, bf16[4,64,2560]{2,1,0:T(8,128)(2,1)}, u32[]{:S(2)}, u32[]{:S(2)}) collective-permute-start(bf16[4,64,2560]{2,1,0:T(8,128)(2,1)S(1)} %pad_maximum_fusion.refs_4_.refs_0_), channel_id=1, source_target_pairs={{0,1},{1,0},{2,3},{3,2},{4,5},{5,4},{6,7},{7,6},{8,9},{9,8},{10,11... | collective-permute-start | bytes 3932168 | tf_op jit(solution)/shard_map/ppermute | solution.py:888
  77.2 11.9 %copy-start.18 = (s32[2048]{0:T(1024)}, s32[2048]{0:T(1024)S(1)}, u32[]{:S(2)}) copy-start(s32[2048]{0:T(1024)S(1)} %convert_reduce_fusion) | copy-start | bytes 24580
  109.0 17.7 %copy-start.8 = (bf16[4,64,2560]{2,1,0:T(8,128)(2,1)}, bf16[4,64,2560]{2,1,0:T(8,128)(2,1)S(1)}, u32[]{:S(2)}) copy-start(bf16[4,64,2560]{2,1,0:T(8,128)(2,1)S(1)} %collective-permute-done.4.refs_5_.refs_1_) | copy-start | bytes 3932164
  109.0 17.7 %collective-permute-start.6 = (bf16[4,64,2560]{2,1,0:T(8,128)(2,1)S(1)}, bf16[4,64,2560]{2,1,0:T(8,128)(2,1)}, u32[]{:S(2)}, u32[]{:S(2)}) collective-permute-start(bf16[4,64,2560]{2,1,0:T(8,128)(2,1)S(1)} %pad_maximum_fusion.refs_4_.refs_0_), channel_id=1, source_target_pairs={{0,2},{2,0},{4,6},{6,4},{8,10},{10,8},{12,14},{14,12},{16,18},{18,... | collective-permute-start | bytes 3932168 | tf_op jit(solution)/shard_map/ppermute | solution.py:880
  109.1 17.6 %collective-permute-start.7 = (bf16[4,64,2560]{2,1,0:T(8,128)(2,1)S(1)}, bf16[4,64,2560]{2,1,0:T(8,128)(2,1)}, u32[]{:S(2)}, u32[]{:S(2)}) collective-permute-start(bf16[4,64,2560]{2,1,0:T(8,128)(2,1)S(1)} %collective-permute-done.4.refs_5_.refs_1_), channel_id=1, source_target_pairs={{0,2},{2,0},{4,6},{6,4},{8,10},{10,8},{12,14},{14,12},{16,18},{18,... | collective-permute-start | bytes 3932168 | tf_op jit(solution)/shard_map/ppermute | solution.py:880
  109.6 17.1 %collective-permute-start.8 = (bf16[4,64,2560]{2,1,0:T(8,128)(2,1)}, bf16[4,64,2560]{2,1,0:T(8,128)(2,1)}, u32[]{:S(2)}, u32[]{:S(2)}) collective-permute-start(bf16[4,64,2560]{2,1,0:T(8,128)(2,1)} %collective-permute-done.5.refs_8_.refs_4_), channel_id=1, source_target_pairs={{0,2},{2,0},{4,6},{6,4},{8,10},{10,8},{12,14},{14,12},{16,18},{18,... | collective-permute-start | bytes 3932168 | tf_op jit(solution)/shard_map/ppermute | solution.py:880
  109.7 42.5 %collective-permute-start.9 = (bf16[4,64,2560]{2,1,0:T(8,128)(2,1)S(1)}, bf16[4,64,2560]{2,1,0:T(8,128)(2,1)}, u32[]{:S(2)}, u32[]{:S(2)}) collective-permute-start(bf16[4,64,2560]{2,1,0:T(8,128)(2,1)S(1)} %collective-permute-done.4.refs_5_.refs_1_), channel_id=1, source_target_pairs={{0,1},{1,0},{2,3},{3,2},{4,5},{5,4},{6,7},{7,6},{8,9},{9,8},{10,11... | collective-permute-start | bytes 3932168 | tf_op jit(solution)/shard_map/ppermute | solution.py:888
  111.2 41.0 %collective-permute-start.10 = (bf16[1024,256]{1,0:T(8,128)(2,1)}, bf16[1024,256]{1,0:T(8,128)(2,1)}, u32[]{:S(2)}, u32[]{:S(2)}) collective-permute-start(bf16[1024,256]{1,0:T(8,128)(2,1)} %get-tuple-element.140.refs_1_), channel_id=1, source_target_pairs={{0,1},{1,0},{2,3},{3,2},{4,5},{5,4},{6,7},{7,6},{8,9},{9,8},{10,11... | collective-permute-start | bytes 1572872 | tf_op jit(solution)/shard_map/ppermute | solution.py:888
  126.8 25.4 %copy-start.13 = (bf16[1024,256]{1,0:T(8,128)(2,1)S(1)}, bf16[1024,256]{1,0:T(8,128)(2,1)}, u32[]{:S(2)}) copy-start(bf16[1024,256]{1,0:T(8,128)(2,1)} %get-tuple-element.145.refs_1_) | copy-start | bytes 1572868
  126.8 27.5 %copy-start.21 = (f32[4096]{0:T(1024)S(1)}, f32[4096]{0:T(1024)}, u32[]{:S(2)}) copy-start(f32[4096]{0:T(1024)} %param.23) | copy-start | bytes 49156
  152.2 14.3 %collective-permute-start.12 = (bf16[4,64,2560]{2,1,0:T(8,128)(2,1)}, bf16[4,64,2560]{2,1,0:T(8,128)(2,1)S(1)}, u32[]{:S(2)}, u32[]{:S(2)}) collective-permute-start(bf16[4,64,2560]{2,1,0:T(8,128)(2,1)} %collective-permute-done.9.refs_9_.refs_5_), channel_id=1, source_target_pairs={{0,2},{2,0},{4,6},{6,4},{8,10},{10,8},{12,14},{14,12},{16,18},{18,... | collective-permute-start | bytes 3932168 | tf_op jit(solution)/shard_map/ppermute | solution.py:880
  152.2 14.3 %collective-permute-start.11 = (bf16[1024,256]{1,0:T(8,128)(2,1)S(1)}, bf16[1024,256]{1,0:T(8,128)(2,1)S(1)}, u32[]{:S(2)}, u32[]{:S(2)}) collective-permute-start(bf16[1024,256]{1,0:T(8,128)(2,1)S(1)} %copy-done.13), channel_id=1, source_target_pairs={{0,1},{1,0},{2,3},{3,2},{4,5},{5,4},{6,7},{7,6},{8,9},{9,8},{10,11... | collective-permute-start | bytes 1572872 | tf_op jit(solution)/shard_map/ppermute | solution.py:888
  166.5 0.8 copy-start.16
  166.5 1.3 copy-start.9
  263.8 14.7 %collective-permute-start.14 = (bf16[512,4096]{1,0:T(8,128)(2,1)}, bf16[512,4096]{1,0:T(8,128)(2,1)}, u32[]{:S(2)}, u32[]{:S(2)}) collective-permute-start(bf16[512,4096]{1,0:T(8,128)(2,1)} %get-tuple-element.163), channel_id=1, source_target_pairs={{0,2},{2,0},{4,6},{6,4},{8,10},{10,8},{12,14},{14,12},{16,18},{18,... | collective-permute-start | bytes 12582920 | tf_op jit(solution)/shard_map/ppermute | solution.py:880
  264.4 5.1 %copy-start.25 = (bf16[1024,512]{1,0:T(8,128)(2,1)S(1)}, bf16[1024,512]{1,0:T(8,128)(2,1)}, u32[]{:S(2)}) copy-start(bf16[1024,512]{1,0:T(8,128)(2,1)} %get-tuple-element.170) | copy-start | bytes 3145732
  269.0 9.4 %collective-permute-start.13 = (bf16[512,1024]{1,0:T(8,128)(2,1)}, bf16[512,1024]{1,0:T(8,128)(2,1)S(1)}, u32[]{:S(2)}, u32[]{:S(2)}) collective-permute-start(bf16[512,1024]{1,0:T(8,128)(2,1)} %grad_rows.4), channel_id=1, source_target_pairs={{0,2},{2,0},{4,6},{6,4},{8,10},{10,8},{12,14},{14,12},{16,18},{18,... | collective-permute-start | bytes 3145736 | tf_op jit(solution)/shard_map/ppermute | solution.py:880
  269.5 27.3 %collective-permute-start.15 = (bf16[1024,512]{1,0:T(8,128)(2,1)S(1)}, bf16[1024,512]{1,0:T(8,128)(2,1)S(1)}, u32[]{:S(2)}, u32[]{:S(2)}) collective-permute-start(bf16[1024,512]{1,0:T(8,128)(2,1)S(1)} %copy-done.25), channel_id=1, source_target_pairs={{0,1},{1,0},{2,3},{3,2},{4,5},{5,4},{6,7},{7,6},{8,9},{9,8},{10,11... | collective-permute-start | bytes 3145736 | tf_op jit(solution)/shard_map/ppermute | solution.py:888
  278.5 15.3 %copy-start.11 = (bf16[512,1024]{1,0:T(8,128)(2,1)}, bf16[512,1024]{1,0:T(8,128)(2,1)S(1)}, u32[]{:S(2)}) copy-start(bf16[512,1024]{1,0:T(8,128)(2,1)S(1)} %collective-permute-done.13.refs_1_) | copy-start | bytes 3145732
  296.8 1.0 copy-start.7
  303.8 58.9 %collective-permute-start.16 = (bf16[512,2560]{1,0:T(8,128)(2,1)}, bf16[512,2560]{1,0:T(8,128)(2,1)S(1)}, u32[]{:S(2)}, u32[]{:S(2)}) collective-permute-start(bf16[512,2560]{1,0:T(8,128)(2,1)} %merge.3), channel_id=1, source_target_pairs={{0,1},{1,0},{2,3},{3,2},{4,5},{5,4},{6,7},{7,6},{8,9},{9,8},{10,11... | collective-permute-start | bytes 7864328 | tf_op jit(solution)/shard_map/ppermute | solution.py:888
  362.7 1.5 copy-start.10
  369.2 35.7 %collective-permute-start.17 = (bf16[256,2560]{1,0:T(8,128)(2,1)}, bf16[256,2560]{1,0:T(8,128)(2,1)S(1)}, u32[]{:S(2)}, u32[]{:S(2)}) collective-permute-start(bf16[256,2560]{1,0:T(8,128)(2,1)} %merge.4), channel_id=1, source_target_pairs={{0,4},{2,6},{4,0},{6,2},{8,12},{10,14},{12,8},{14,10},{16,20},{18,... | collective-permute-start | bytes 3932168 | tf_op jit(solution)/shard_map/ppermute | solution.py:884
  392.9 13.7 %copy-start.22 = (f32[1,4096]{1,0:T(1,128)S(1)}, f32[1,4096]{1,0:T(1,128)}, u32[]{:S(2)}) copy-start(f32[1,4096]{1,0:T(1,128)} %get-tuple-element.211) | copy-start | bytes 49156
  392.9 14.6 %copy-start.23 = (f32[8,1024]{1,0:T(8,128)S(1)}, f32[8,1024]{1,0:T(8,128)}, u32[]{:S(2)}) copy-start(f32[8,1024]{1,0:T(8,128)} %get-tuple-element.207) | copy-start | bytes 98308
  404.8 2.7 copy-start.15
  404.8 8.0 %collective-permute-start.18 = (bf16[512,1536]{1,0:T(8,128)(2,1)}, bf16[512,1536]{1,0:T(8,128)(2,1)}, u32[]{:S(2)}, u32[]{:S(2)}) collective-permute-start(bf16[512,1536]{1,0:T(8,128)(2,1)} %grad_rows.5), channel_id=1, source_target_pairs={{0,2},{2,0},{4,6},{6,4},{8,10},{10,8},{12,14},{14,12},{16,18},{18,... | collective-permute-start | bytes 4718600 | tf_op jit(solution)/shard_map/ppermute | solution.py:880
  404.8 48.3 %collective-permute-start.20 = (bf16[1024,1024]{1,0:T(8,128)(2,1)}, bf16[1024,1024]{1,0:T(8,128)(2,1)S(1)}, u32[]{:S(2)}, u32[]{:S(2)}) collective-permute-start(bf16[1024,1024]{1,0:T(8,128)(2,1)} %get-tuple-element.202), channel_id=1, source_target_pairs={{0,1},{1,0},{2,3},{3,2},{4,5},{5,4},{6,7},{7,6},{8,9},{9,8},{10,11... | collective-permute-start | bytes 6291464 | tf_op jit(solution)/shard_map/ppermute | solution.py:888
  422.2 9.3 %copy-start.12 = (bf16[256,2560]{1,0:T(8,128)(2,1)S(1)}, bf16[256,2560]{1,0:T(8,128)(2,1)}, u32[]{:S(2)}) copy-start(bf16[256,2560]{1,0:T(8,128)(2,1)} %merge.5) | copy-start | bytes 3932164
  422.2 15.3 %copy-start.20 = (f32[8,1024]{1,0:T(8,128)S(1)}, f32[8,1024]{1,0:T(8,128)}, u32[]{:S(2)}) copy-start(f32[8,1024]{1,0:T(8,128)} %get-tuple-element.204) | copy-start | bytes 98308
  422.2 36.2 %collective-permute-start.19 = (bf16[256,1536]{1,0:T(8,128)(2,1)}, bf16[256,1536]{1,0:T(8,128)(2,1)}, u32[]{:S(2)}, u32[]{:S(2)}) collective-permute-start(bf16[256,1536]{1,0:T(8,128)(2,1)} %get-tuple-element.201), channel_id=1, source_target_pairs={{0,4},{2,6},{4,0},{6,2},{8,12},{10,14},{12,8},{14,10},{16,20},{18,... | collective-permute-start | bytes 2359304 | tf_op jit(solution)/shard_map/ppermute | solution.py:884
  432.5 20.6 %collective-permute-start.21 = (bf16[64,2560]{1,0:T(8,128)(2,1)}, bf16[64,2560]{1,0:T(8,128)(2,1)}, u32[]{:S(2)}, u32[]{:S(2)}) collective-permute-start(bf16[64,2560]{1,0:T(8,128)(2,1)} %get-tuple-element.233), channel_id=1, source_target_pairs={{0,8},{2,10},{4,12},{6,14},{8,16},{10,18},{12,20},{14,22},{16,24},... | collective-permute-start | bytes 983048 | tf_op jit(solution)/shard_map/ppermute | solution.py:976
  435.1 23.3 %collective-permute-start.22 = (bf16[64,2560]{1,0:T(8,128)(2,1)}, bf16[64,2560]{1,0:T(8,128)(2,1)}, u32[]{:S(2)}, u32[]{:S(2)}) collective-permute-start(bf16[64,2560]{1,0:T(8,128)(2,1)} %get-tuple-element.232), channel_id=1, source_target_pairs={{0,16},{2,18},{4,20},{6,22},{8,24},{10,26},{12,28},{14,30},{16,0},... | collective-permute-start | bytes 983048 | tf_op jit(solution)/shard_map/ppermute | solution.py:976
  435.9 22.5 %collective-permute-start.23 = (bf16[64,2560]{1,0:T(8,128)(2,1)}, bf16[64,2560]{1,0:T(8,128)(2,1)}, u32[]{:S(2)}, u32[]{:S(2)}) collective-permute-start(bf16[64,2560]{1,0:T(8,128)(2,1)} %get-tuple-element.231), channel_id=1, source_target_pairs={{0,24},{2,26},{4,28},{6,30},{8,0},{10,2},{12,4},{14,6},{16,8},{18,... | collective-permute-start | bytes 983048 | tf_op jit(solution)/shard_map/ppermute | solution.py:976
  453.1 5.4 %copy-start.14 = (bf16[1024,1024]{1,0:T(8,128)(2,1)}, bf16[1024,1024]{1,0:T(8,128)(2,1)S(1)}, u32[]{:S(2)}) copy-start(bf16[1024,1024]{1,0:T(8,128)(2,1)S(1)} %collective-permute-done.20.refs_1_) | copy-start | bytes 6291460
  458.5 12.7 %copy-start.17 = (bf16[64,4096]{1,0:T(8,128)(2,1)S(1)}, bf16[64,4096]{1,0:T(8,128)(2,1)}, u32[]{:S(2)}) copy-start(bf16[64,4096]{1,0:T(8,128)(2,1)} %reduce-scatter.2.cloned.1.call-done) | copy-start | bytes 1572868
  458.5 13.6 %collective-permute-start.24 = (f32[16,1024]{1,0:T(8,128)S(1)}, f32[16,1024]{1,0:T(8,128)S(1)}, u32[]{:S(2)}, u32[]{:S(2)}) collective-permute-start(f32[16,1024]{1,0:T(8,128)S(1)} %concatenate.24), channel_id=1, source_target_pairs={{0,2},{2,0},{4,6},{6,4},{8,10},{10,8},{12,14},{14,12},{16,18},{18,... | collective-permute-start | bytes 196616 | tf_op jit(solution)/shard_map/ppermute | solution.py:1002
  461.0 25.2 %collective-permute-start.28 = (bf16[64,1536]{1,0:T(8,128)(2,1)}, bf16[64,1536]{1,0:T(8,128)(2,1)}, u32[]{:S(2)}, u32[]{:S(2)}) collective-permute-start(bf16[64,1536]{1,0:T(8,128)(2,1)} %get-tuple-element.236), channel_id=1, source_target_pairs={{0,8},{2,10},{4,12},{6,14},{8,16},{10,18},{12,20},{14,22},{16,24},... | collective-permute-start | bytes 589832 | tf_op jit(solution)/shard_map/ppermute | solution.py:976
  468.5 17.7 %collective-permute-start.29 = (bf16[64,1536]{1,0:T(8,128)(2,1)}, bf16[64,1536]{1,0:T(8,128)(2,1)}, u32[]{:S(2)}, u32[]{:S(2)}) collective-permute-start(bf16[64,1536]{1,0:T(8,128)(2,1)} %get-tuple-element.235), channel_id=1, source_target_pairs={{0,16},{2,18},{4,20},{6,22},{8,24},{10,26},{12,28},{14,30},{16,0},... | collective-permute-start | bytes 589832 | tf_op jit(solution)/shard_map/ppermute | solution.py:976
  469.9 16.4 %collective-permute-start.30 = (bf16[64,1536]{1,0:T(8,128)(2,1)}, bf16[64,1536]{1,0:T(8,128)(2,1)}, u32[]{:S(2)}, u32[]{:S(2)}) collective-permute-start(bf16[64,1536]{1,0:T(8,128)(2,1)} %get-tuple-element.234), channel_id=1, source_target_pairs={{0,24},{2,26},{4,28},{6,30},{8,0},{10,2},{12,4},{14,6},{16,8},{18,... | collective-permute-start | bytes 589832 | tf_op jit(solution)/shard_map/ppermute | solution.py:976
  471.2 15.1 %collective-permute-start.27 = (bf16[64,2048]{1,0:T(8,128)(2,1)S(1)}, bf16[64,2048]{1,0:T(8,128)(2,1)S(1)}, u32[]{:S(2)}, u32[]{:S(2)}) collective-permute-start(bf16[64,2048]{1,0:T(8,128)(2,1)S(1)} %slice.91), channel_id=1, source_target_pairs={{0,1},{1,0},{2,3},{3,2},{4,5},{5,4},{6,7},{7,6},{8,9},{9,8},{10,11... | collective-permute-start | bytes 786440 | tf_op jit(solution)/shard_map/ppermute | solution.py:888
  472.1 4.3 collective-permute-start.25
  476.5 9.7 %collective-permute-start.26 = (f32[16,1024]{1,0:T(8,128)S(1)}, f32[16,1024]{1,0:T(8,128)S(1)}, u32[]{:S(2)}, u32[]{:S(2)}) collective-permute-start(f32[16,1024]{1,0:T(8,128)S(1)} %add.150), channel_id=1, source_target_pairs={{0,1},{1,0},{2,3},{3,2},{4,5},{5,4},{6,7},{7,6},{8,9},{9,8},{10,11... | collective-permute-start | bytes 196616 | tf_op jit(solution)/shard_map/ppermute | solution.py:888
  486.2 4.4 collective-permute-start.31
  490.7 5.3 %collective-permute-start.32 = (f32[16,1024]{1,0:T(8,128)S(1)}, f32[16,1024]{1,0:T(8,128)S(1)}, u32[]{:S(2)}, u32[]{:S(2)}) collective-permute-start(f32[16,1024]{1,0:T(8,128)S(1)} %add.161), channel_id=1, source_target_pairs={{0,16},{2,18},{4,20},{6,22},{8,24},{10,26},{12,28},{14,30},{16,0},... | collective-permute-start | bytes 196616 | tf_op jit(solution)/shard_map/ppermute | solution.py:1008
Sparse Core Ops, SparseCore 0:
  10.9 61.4 all-gather.2
  74.5 76.8 all-gather.4
  297.0 109.2 reduce-scatter.1

commit v6 on v5

--- a/solution.py
+++ b/solution.py
@@ -702,7 +702,7 @@
 def grad_rows(left, at, right, terms=()):
     _, rows, tokens = left.shape
     columns = right.shape[1]
-    block = math.gcd(columns, 256 if tokens > 1024 else 512)
+    block = math.gcd(columns, 512)
     return call(
         functools.partial(grad_rows_kernel, len(terms)),
         "grad_rows",
@@ -792,7 +792,7 @@
     tokens = left.shape[1]
     rows = left.shape[0] // (NC * NX)
     columns = right.shape[1]
-    block = math.gcd(columns, 256)
+    block = math.gcd(columns, 512)
     out = pl.BlockSpec((rows, block), lambda j, at: (0, j))
     return call(
         grad_both_kernel,

time: 510 us -> 510 us (level)
  Pallas kernels: 308 us -> 298 us
  waiting for transfers between devices: 102 us -> 111 us
    ppermute x10, waiting for transfers between devices: 43.9 us -> 49.7 us  [swap_y(): return lax.ppermute(a, 'tensor', [(0, 1), (1, 0)])]
  transfers between devices with their start and end apart: 36 -> 36, of which waited for: 14 -> 14; matrix products, arithmetic and copies ran while one was open for 4% -> 4% of each run, Pallas kernels for 44% -> 42%
where the time goes in v6:
time: 510 us; the launch traced here: 504 us
  Pallas kernels  298 us (58%)
  waiting for transfers between devices  111 us (22%)
  starting transfers between devices  45 us (9%)
  local copies, waits for them, and re-layouts  19.6 us (4%)
  other arithmetic  15.2 us (3%)
  between operations  14.7 us (3%)
    pallas_call x17, Pallas kernels, call(): pl.pallas_call(body, grid_spec=pltpu.PrefetchScalarGridSpec(num_scalar_pr...  192 us
    pallas_call x4, Pallas kernels, attention_backward(): pl.pallas_call(functools.partial(bwd_kernel, halves), grid_spec=pltpu.Pre...  57.6 us
    ppermute x10, waiting for transfers between devices, swap_y(): return lax.ppermute(a, 'tensor', [(0, 1), (1, 0)])  49.7 us
    pallas_call x4, Pallas kernels, attention_forward(): pl.pallas_call(functools.partial(fwd_kernel, pairs), grid_spec=grid_spec,...  48.4 us
    all_gather x1, waiting for transfers between devices, gather_first(): qkv = lax.all_gather(shard_qkv, 'dp', axis=0, tiled=True)  26.5 us
    ppermute x10, starting transfers between devices, swap_y(): return lax.ppermute(a, 'tensor', [(0, 1), (1, 0)])  17 us
    ppermute x6, starting transfers between devices, z_pieces(): lax.ppermute(a, 'dp', z_pairs(k))  14.5 us
    ppermute x3, waiting for transfers between devices, spread_z(): lax.ppermute(shard, 'dp', z_pairs(k))  14.3 us
  transfers between devices with their start and end apart: 36, of which 14 were waited for; matrix products, arithmetic and copies ran while one was open for 4% of the time, Pallas kernels for 42%

profile of v6, /device:TPU:0, one launch (start us, length us, event | category | flops | bytes accessed | tf_op | source)
XLA Modules:
  0.0 504.2 jit_solution(13228057422254239643)
XLA Ops:
  9.0 1.1 convert_bitcast_fusion
  10.1 3.0 collective-permute-start.3
  13.1 1.1 convert_element_type.71
  14.3 1.6 collective-permute-start
  15.9 2.6 collective-permute-start.1
  18.5 1.3 collective-permute-start.2
  19.8 2.3 copy-done
  22.1 4.2 first_norm.1
  26.4 2.1 copy-done.1
  28.4 2.1 copy-done.2
  31.4 14.2 %collective-permute-done.1 = bf16[64,2560]{1,0:T(8,128)(2,1)S(1)} collective-permute-done((bf16[64,2560]{1,0:T(8,128)(2,1)S(1)}, bf16[64,2560]{1,0:T(8,128)(2,1)S(1)}, u32[]{:S(2)}, u32[]{:S(2)}) %collective-permute-start.1) | collective-permute-done | bytes 327712 | tf_op jit(solution)/shard_map/ppermute | solution.py:892
  45.9 26.5 %all-gather.3.cloned.1.call-done.w_ref = bf16[1024,1536]{1,0:T(8,128)(2,1)} async-done(((bf16[64,1536]{1,0:T(8,128)(2,1)}), bf16[1024,1536]{1,0:T(8,128)(2,1)}) %all-gather.3.cloned.1.call-update) | async-done | bytes 3145744 | tf_op jit(solution)/shard_map/all_gather | solution.py:905
  73.0 1.5 collective-permute-start.5
  75.4 1.8 convert_reduce_fusion
  77.8 11.3 %project.1.refs_0_.refs_1_.refs_2_.refs_3_.refs_4_.refs_5_.q_ref.k_ref.v_ref = bf16[2048,1536]{1,0:T(8,128)(2,1)} custom-call(bf16[2048,1024]{1,0:T(8,128)(2,1)} %copy-done.2, bf16[1024,1536]{1,0:T(8,128)(2,1)} %all-gather.3.cloned.1.call-done.w_ref, f32[1,1536]{1,0:T(1,128)} %broadcast_in_dim_reshape.3.b_ref), custom_call_target="tpu_custom_call" | custom-call | flops 1 | bytes 1 | tf_op jit(solution)/shard_map/project/pallas_call | solution.py:290
  89.1 12.4 %attention_forward.4 = (bf16[1024,256]{1,0:T(8,128)(2,1)}, f32[1,2,2,1024]{3,2,1,0:T(2,128)}) custom-call(s32[1,8]{1,0:T(1,128)} %and_select_fusion.lo_ref, s32[1]{0:T(128)} %bitcast.14.off_ref.at_ref, bf16[2048,1536]{1,0:T(8,128)(2,1)} %project.1.refs_0_.refs_1_.refs_2_.refs_3_.refs_4_.refs_5_.q_ref.k_ref.v_ref, ...), custom_call_target="tpu_custom_call" | custom-call | flops 1 | bytes 1 | tf_op jit(solution)/shard_map/attention_forward/pallas_call | solution.py:104
  101.5 7.5 %collective-permute-done.4.refs_5_.refs_1_ = bf16[4,64,2560]{2,1,0:T(8,128)(2,1)S(1)} collective-permute-done((bf16[4,64,2560]{2,1,0:T(8,128)(2,1)S(1)}, bf16[4,64,2560]{2,1,0:T(8,128)(2,1)S(1)}, u32[]{:S(2)}, u32[]{:S(2)}) %collective-permute-start.4) | collective-permute-done | bytes 1310752 | tf_op jit(solution)/shard_map/ppermute | solution.py:884
  109.7 1.5 collective-permute-start.9
  111.7 12.7 %attention_forward.5 = (bf16[1024,256]{1,0:T(8,128)(2,1)}, f32[1,2,2,1024]{3,2,1,0:T(2,128)}) custom-call(s32[1,8]{1,0:T(1,128)} %and_select_fusion.lo_ref, s32[1]{0:T(128)} %bitcast.14.off_ref.at_ref, bf16[2048,1536]{1,0:T(8,128)(2,1)} %project.1.refs_0_.refs_1_.refs_2_.refs_3_.refs_4_.refs_5_.q_ref.k_ref.v_ref, ...), custom_call_target="tpu_custom_call" | custom-call | flops 1 | bytes 1 | tf_op jit(solution)/shard_map/attention_forward/pallas_call | solution.py:104
  124.5 11.9 %attention_forward.6 = (bf16[1024,256]{1,0:T(8,128)(2,1)}, f32[1,2,2,1024]{3,2,1,0:T(2,128)}) custom-call(s32[1,8]{1,0:T(1,128)} %and_select_fusion.lo_ref, s32[1]{0:T(128)} %bitcast.off_ref.at_ref, bf16[2048,1536]{1,0:T(8,128)(2,1)} %project.1.refs_0_.refs_1_.refs_2_.refs_3_.refs_4_.refs_5_.q_ref.k_ref.v_ref, ...), custom_call_target="tpu_custom_call" | custom-call | flops 1 | bytes 1 | tf_op jit(solution)/shard_map/attention_forward/pallas_call | solution.py:104
  136.4 15.8 %collective-permute-done.10.refs_2_ = bf16[1024,256]{1,0:T(8,128)(2,1)} collective-permute-done((bf16[1024,256]{1,0:T(8,128)(2,1)}, bf16[1024,256]{1,0:T(8,128)(2,1)}, u32[]{:S(2)}, u32[]{:S(2)}) %collective-permute-start.10) | collective-permute-done | bytes 524320 | tf_op jit(solution)/shard_map/ppermute | solution.py:888
  152.2 1.5 collective-permute-start.11
  154.9 11.4 %attention_forward.7 = (bf16[1024,256]{1,0:T(8,128)(2,1)}, f32[1,2,2,1024]{3,2,1,0:T(2,128)}) custom-call(s32[1,8]{1,0:T(1,128)} %and_select_fusion.lo_ref, s32[1]{0:T(128)} %bitcast.off_ref.at_ref, bf16[2048,1536]{1,0:T(8,128)(2,1)} %project.1.refs_0_.refs_1_.refs_2_.refs_3_.refs_4_.refs_5_.q_ref.k_ref.v_ref, ...), custom_call_target="tpu_custom_call" | custom-call | flops 1 | bytes 1 | tf_op jit(solution)/shard_map/attention_forward/pallas_call | solution.py:104
  167.8 11.9 %middle.1 = (f32[1024,1024]{1,0:T(8,128)}, f32[1024,1024]{1,0:T(8,128)}, bf16[1024,1024]{1,0:T(8,128)(2,1)}, bf16[1024,1024]{1,0:T(8,128)(2,1)}, bf16[1024,1024]{1,0:T(8,128)(2,1)}, /*index=5*/bf16[1024,1024]{1,0:T(8,128)(2,1)}) custom-call(s32[4]{0:T(128)} %pad_add_fusion.at_ref, bf16[1024,256]{1,0:T(8,128)(2,1)} %get-tuple-element.141.refs_0_, ...), custom_call_target="tpu_custom_call" | custom-call | flops 1 | bytes 1 | tf_op jit(solution)/shard_map/middle/pallas_call | solution.py:290
  179.7 33.7 %feed.1 = (bf16[1024,4096]{1,0:T(8,128)(2,1)}, bf16[1024,1024]{1,0:T(8,128)(2,1)}, bf16[1024,1024]{1,0:T(8,128)(2,1)}, bf16[1024,1024]{1,0:T(8,128)(2,1)}, f32[8,1024]{1,0:T(8,128)}) custom-call(s32[4]{0:T(128)} %pad_add_fusion.at_ref, bf16[1024,1024]{1,0:T(8,128)(2,1)} %get-tuple-element.150.u_ref, f32[1,4096]{1,0:T(1,128)} %bitcast.85, ...), custom_call_target="tpu_custom_call" | custom-call | flops 1 | bytes 1 | tf_op jit(solution)/shard_map/feed/pallas_call | solution.py:290
  213.4 50.3 %feed_back.1 = (bf16[512,4096]{1,0:T(8,128)(2,1)}, bf16[512,4096]{1,0:T(8,128)(2,1)}, f32[1,4096]{1,0:T(1,128)}, f32[1024,1024]{1,0:T(8,128)}, f32[8,1024]{1,0:T...) custom-call(s32[4]{0:T(128)} %pad_add_fusion.at_ref, ...), custom_call_target="tpu_custom_call" | custom-call | flops 1 | bytes 1 | tf_op jit(solution)/shard_map/feed_back/pallas_call | solution.py:290
  264.4 4.6 grad_rows.4
  269.5 3.6 collective-permute-start.15
  273.7 4.5 grad_rows.3.refs_0_
  278.2 15.3 %grad_down.1 = bf16[1024,4096]{1,0:T(8,128)(2,1)} custom-call(bf16[1024,1024]{1,0:T(8,128)(2,1)} %get-tuple-element.168.left_ref, bf16[1024,4096]{1,0:T(8,128)(2,1)} %get-tuple-element.158.pre_ref), custom_call_target="tpu_custom_call" | custom-call | flops 1 | bytes 1 | tf_op jit(solution)/shard_map/grad_down/pallas_call | solution.py:290
  293.5 3.4 collective-permute-done.15.refs_3_
  297.8 6.0 %merge.3 = bf16[512,2560]{1,0:T(8,128)(2,1)} custom-call(s32[1]{0:T(128)} %constant.137.clone.1.at_ref, bf16[512,1024]{1,0:T(8,128)(2,1)} %grad_rows.3.refs_0_, bf16[512,1024]{1,0:T(8,128)(2,1)} %copy-done.11, bf16[512,4096]{1,0:T(8,128)(2,1)} %get-tuple-element.196.refs_2_, bf16[512,4096]{1,0:T(8,128)(2,1)} %collective-permute-done.14.refs_3_), custom_call_target="tpu_custom_call" | custom-call | flops 1 | bytes 1 | tf_op jit(solution)/shard_map/merge/pallas_call | solution.py:290
  303.8 1.7 collective-permute-start.16
  305.6 14.3 %attention_backward.4.refs_6_ = bf16[2048,1536]{1,0:T(8,128)(2,1)} custom-call(s32[1,8]{1,0:T(1,128)} %and_select_fusion.lo_ref, s32[1]{0:T(128)} %bitcast.18.place_ref, bf16[2048,1536]{1,0:T(8,128)(2,1)} %project.1.refs_0_.refs_1_.refs_2_.refs_3_.refs_4_.refs_5_.q_ref.k_ref.v_ref, ...), custom_call_target="tpu_custom_call" | custom-call | flops 1 | bytes 1 | tf_op jit(solution)/shard_map/attention_backward/pallas_call | solution.py:216
  319.9 14.4 %attention_backward.5.refs_6_ = bf16[2048,1536]{1,0:T(8,128)(2,1)} custom-call(s32[1,8]{1,0:T(1,128)} %and_select_fusion.lo_ref, s32[1]{0:T(128)} %bitcast.18.place_ref, bf16[2048,1536]{1,0:T(8,128)(2,1)} %project.1.refs_0_.refs_1_.refs_2_.refs_3_.refs_4_.refs_5_.q_ref.k_ref.v_ref, ...), custom_call_target="tpu_custom_call", output_to_operand_aliasing={{}: (12, {})} | custom-call | flops 1 | bytes 1 | tf_op jit(solution)/shard_map/attention_backward/pallas_call | solution.py:216
  334.3 14.4 %attention_backward.6.refs_6_ = bf16[2048,1536]{1,0:T(8,128)(2,1)} custom-call(s32[1,8]{1,0:T(1,128)} %and_select_fusion.lo_ref, s32[1]{0:T(128)} %bitcast.18.place_ref, bf16[2048,1536]{1,0:T(8,128)(2,1)} %project.1.refs_0_.refs_1_.refs_2_.refs_3_.refs_4_.refs_5_.q_ref.k_ref.v_ref, ...), custom_call_target="tpu_custom_call", output_to_operand_aliasing={{}: (12, {})} | custom-call | flops 1 | bytes 1 | tf_op jit(solution)/shard_map/attention_backward/pallas_call | solution.py:216
  348.7 14.1 %collective-permute-done.16.refs_4_ = bf16[512,2560]{1,0:T(8,128)(2,1)S(1)} collective-permute-done((bf16[512,2560]{1,0:T(8,128)(2,1)}, bf16[512,2560]{1,0:T(8,128)(2,1)S(1)}, u32[]{:S(2)}, u32[]{:S(2)}) %collective-permute-start.16) | collective-permute-done | bytes 2621472 | tf_op jit(solution)/shard_map/ppermute | solution.py:888
  362.8 1.5 copy-done.10
  364.3 4.9 merge.4
  369.5 14.5 %attention_backward.7.dq_ref.right_ref = bf16[2048,1536]{1,0:T(8,128)(2,1)} custom-call(s32[1,8]{1,0:T(1,128)} %and_select_fusion.lo_ref, s32[1]{0:T(128)} %bitcast.18.place_ref, bf16[2048,1536]{1,0:T(8,128)(2,1)} %project.1.refs_0_.refs_1_.refs_2_.refs_3_.refs_4_.refs_5_.q_ref.k_ref.v_ref, ...), custom_call_target="tpu_custom_call", output_to_operand_aliasing={{}: (12, {})} | custom-call | flops 1 | bytes 1 | tf_op jit(solution)/shard_map/attention_backward/pallas_call | solution.py:216
  384.0 8.0 %d_in.2 = (bf16[1024,1024]{1,0:T(8,128)(2,1)}, f32[8,1024]{1,0:T(8,128)}, f32[8,1536]{1,0:T(8,128)}) custom-call(s32[1]{0:T(128)} %bitcast.14.off_ref.at_ref, bf16[2048,1536]{1,0:T(8,128)(2,1)} %attention_backward.7.dq_ref.right_ref, bf16[1024,1536]{1,0:T(8,128)(2,1)} %all-gather.3.cloned.1.call-done.w_ref, bf16[2048,1024]{1,0:T(8,128)(2,1)} %refs_2_.1), custom_call_target="tpu_custom_call" | custom-call | flops 2200000000 | bytes 1 | tf_op jit(solution)/shard_map/d_in/pallas_call | solution.py:290
  392.0 8.2 %grad_rows.5 = bf16[512,1536]{1,0:T(8,128)(2,1)} custom-call(s32[2]{0:T(128)} %pad_add_fusion.2.at_ref, bf16[2,512,2048]{2,1,0:T(8,128)(2,1)} %bitcast.63, bf16[2048,1536]{1,0:T(8,128)(2,1)} %attention_backward.7.dq_ref.right_ref), custom_call_target="tpu_custom_call" | custom-call | flops 1 | bytes 1 | tf_op jit(solution)/shard_map/grad_rows/pallas_call | solution.py:290
  400.3 4.8 collective-permute-done.17.refs_5_
  405.1 1.5 collective-permute-start.20
  408.1 5.3 %merge.5 = bf16[256,2560]{1,0:T(8,128)(2,1)} custom-call(s32[1]{0:T(128)} %bitcast.2.at_ref, bf16[512,1024]{1,0:T(8,128)(2,1)} %grad_rows.3.refs_0_, bf16[512,1024]{1,0:T(8,128)(2,1)} %copy-done.11, bf16[512,4096]{1,0:T(8,128)(2,1)} %get-tuple-element.196.refs_2_, bf16[512,4096]{1,0:T(8,128)(2,1)} %collective-permute-done.14.refs_3_, ...), custom_call_target="tpu_custom_call" | custom-call | flops 1 | bytes 1 | tf_op jit(solution)/shard_map/merge/pallas_call | solution.py:290
  413.5 8.1 %grad_both.1 = (bf16[256,1536]{1,0:T(8,128)(2,1)}, bf16[256,1536]{1,0:T(8,128)(2,1)}) custom-call(s32[2]{0:T(128)} %pad_add_fusion.1.at_ref, bf16[2,2,256,2048]{3,2,1,0:T(8,128)(2,1)} %bitcast.64, bf16[2048,1536]{1,0:T(8,128)(2,1)} %attention_backward.7.dq_ref.right_ref, bf16[2,256,1536]{2,1,0:T(8,128)(2,1)} %bitcast.23.there_ref), custom_call_target="tpu_custom_call" | custom-call | flops 1 | bytes 1 | tf_op jit(solution)/shard_map/grad_both/pallas_call | solution.py:290
  422.0 8.1 %d_in.3 = (bf16[1024,1024]{1,0:T(8,128)(2,1)}, f32[8,1024]{1,0:T(8,128)}, f32[8,1536]{1,0:T(8,128)}) custom-call(s32[1]{0:T(128)} %bitcast.off_ref.at_ref, bf16[2048,1536]{1,0:T(8,128)(2,1)} %attention_backward.7.dq_ref.right_ref, bf16[1024,1536]{1,0:T(8,128)(2,1)} %all-gather.3.cloned.1.call-done.w_ref, bf16[2048,1024]{1,0:T(8,128)(2,1)} %refs_2_.1), custom_call_target="tpu_custom_call" | custom-call | flops 2200000000 | bytes 1 | tf_op jit(solution)/shard_map/d_in/pallas_call | solution.py:290
  431.9 2.0 collective-permute-start.21
  434.8 1.4 collective-permute-start.23
  437.1 16.2 %collective-permute-done.20.refs_1_ = bf16[1024,1024]{1,0:T(8,128)(2,1)S(1)} collective-permute-done((bf16[1024,1024]{1,0:T(8,128)(2,1)}, bf16[1024,1024]{1,0:T(8,128)(2,1)S(1)}, u32[]{:S(2)}, u32[]{:S(2)}) %collective-permute-start.20) | collective-permute-done | bytes 2097184 | tf_op jit(solution)/shard_map/ppermute | solution.py:888
  453.4 4.5 collective-permute-done.22
  457.9 1.6 add_convert_fusion
  460.4 7.8 %collective-permute-start.28 = (bf16[64,1536]{1,0:T(8,128)(2,1)}, bf16[64,1536]{1,0:T(8,128)(2,1)}, u32[]{:S(2)}, u32[]{:S(2)}) collective-permute-start(bf16[64,1536]{1,0:T(8,128)(2,1)} %get-tuple-element.236), channel_id=1, source_target_pairs={{0,8},{2,10},{4,12},{6,14},{8,16},{10,18},{12,20},{14,22},{16,24},... | collective-permute-start | bytes 589832 | tf_op jit(solution)/shard_map/ppermute | solution.py:976
  468.9 1.7 collective-permute-start.30
  471.2 1.7 collective-permute-start.25
  472.9 1.3 fusion.1
  474.2 1.3 collective-permute-done.25
  475.6 1.6 collective-permute-start.26
  477.8 7.0 %last.1 = bf16[1024,1024]{1,0:T(8,128)(2,1)} custom-call(s32[1]{0:T(128)} %bitcast.off_ref.at_ref, bf16[1024,1024]{1,0:T(8,128)(2,1)} %get-tuple-element.215.refs_0_, bf16[1024,1024]{1,0:T(8,128)(2,1)} %copy-done.14, bf16[2048,1024]{1,0:T(8,128)(2,1)} %refs_2_.1, f32[1024,1024]{1,0:T(8,128)} %get-tuple-element.217.refs_3_, f32[4,1024]{1,0:T(4,128)} %refs_4_.1), custom_call_target="tpu_custom_call" | custom-call | flops 1 | bytes 1 | tf_op jit(solution)/shard_map/last/pallas_call | solution.py:290
  485.7 1.7 collective-permute-start.31
  487.4 1.2 fusion.3
  488.6 1.4 collective-permute-done.31
  490.0 1.8 collective-permute-start.32
  494.0 1.2 collective-permute-done.32
  (141 shorter events, 25.3 us)
Async XLA Ops:
  7.2 12.6 %copy-start.3 = (f32[4,1024]{1,0:T(4,128)S(1)}, f32[4,1024]{1,0:T(4,128)}, u32[]{:S(2)}) copy-start(f32[4,1024]{1,0:T(4,128)} %refs_4_.1) | copy-start | bytes 49156
  7.2 65.2 %all-gather.3.cloned.1.call-start = ((), (), s32[]{:S(2)}) async-start(), calls=%async_computation.1 | async-start | bytes 3342336 | tf_op jit(solution)/shard_map/all_gather | solution.py:905
  7.2 1.0 copy-start.4
  8.2 6.0 %copy-start.19 = (f32[512,64]{0,1:T(8,128)S(1)}, f32[512,64]{0,1:T(8,128)}, u32[]{:S(2)}) copy-start(f32[512,64]{0,1:T(8,128)} %param.16) | copy-start | bytes 393220
  8.2 11.6 %copy-start.5 = (f32[4,1024]{1,0:T(4,128)S(1)}, f32[4,1024]{1,0:T(4,128)}, u32[]{:S(2)}) copy-start(f32[4,1024]{1,0:T(4,128)} %refs_12_.3) | copy-start | bytes 49156
  9.0 170.8 %all-gather.5.cloned.1.call-start = ((), (), s32[]{:S(2)}) async-start(), calls=%async_computation.2 | async-start | bytes 8912896 | tf_op jit(solution)/shard_map/all_gather | solution.py:912
  10.1 20.4 %collective-permute-start.3 = (bf16[64,2048]{1,0:T(8,128)(2,1)S(1)}, bf16[64,2048]{1,0:T(8,128)(2,1)S(1)}, u32[]{:S(2)}, u32[]{:S(2)}) collective-permute-start(bf16[64,2048]{1,0:T(8,128)(2,1)S(1)} %convert_bitcast_fusion), channel_id=1, source_target_pairs={{0,1},{1,0},{2,3},{3,2},{4,5},{5,4},{6,7},{7,6},{8,9},{9,8},{10,11... | collective-permute-start | bytes 786440 | tf_op jit(solution)/shard_map/ppermute | solution.py:888
  14.3 17.1 %collective-permute-start = (bf16[64,2560]{1,0:T(8,128)(2,1)S(1)}, bf16[64,2560]{1,0:T(8,128)(2,1)S(1)}, u32[]{:S(2)}, u32[]{:S(2)}) collective-permute-start(bf16[64,2560]{1,0:T(8,128)(2,1)S(1)} %pad_maximum_fusion.2), channel_id=1, source_target_pairs={{0,8},{2,10},{4,12},{6,14},{8,16},{10,18},{12,20},{14,22},{16,24},... | collective-permute-start | bytes 983048 | tf_op jit(solution)/shard_map/ppermute | solution.py:892
  15.9 29.7 %collective-permute-start.1 = (bf16[64,2560]{1,0:T(8,128)(2,1)S(1)}, bf16[64,2560]{1,0:T(8,128)(2,1)S(1)}, u32[]{:S(2)}, u32[]{:S(2)}) collective-permute-start(bf16[64,2560]{1,0:T(8,128)(2,1)S(1)} %pad_maximum_fusion.2), channel_id=1, source_target_pairs={{0,16},{2,18},{4,20},{6,22},{8,24},{10,26},{12,28},{14,30},{16,0},... | collective-permute-start | bytes 983048 | tf_op jit(solution)/shard_map/ppermute | solution.py:892
  18.5 27.2 %collective-permute-start.2 = (bf16[64,2560]{1,0:T(8,128)(2,1)S(1)}, bf16[64,2560]{1,0:T(8,128)(2,1)S(1)}, u32[]{:S(2)}, u32[]{:S(2)}) collective-permute-start(bf16[64,2560]{1,0:T(8,128)(2,1)S(1)} %pad_maximum_fusion.2), channel_id=1, source_target_pairs={{0,24},{2,26},{4,28},{6,30},{8,0},{10,2},{12,4},{14,6},{16,8},{18,... | collective-permute-start | bytes 983048 | tf_op jit(solution)/shard_map/ppermute | solution.py:892
  19.8 2.3 copy-start
  26.4 2.1 copy-start.1
  28.4 2.1 copy-start.2
  30.5 44.1 %copy-start.24 = (f32[2,1024]{1,0:T(2,128)S(1)}, f32[2,1024]{1,0:T(2,128)}, u32[]{:S(2)}) copy-start(f32[2,1024]{1,0:T(2,128)} %param.21) | copy-start | bytes 24580
  30.5 44.8 %copy-start.26 = (s32[1,2048]{1,0:T(1,128)S(1)}, s32[1,2048]{1,0:T(1,128)}, u32[]{:S(2)}) copy-start(s32[1,2048]{1,0:T(1,128)} %param.14) | copy-start | bytes 24580
  45.9 63.2 %copy-start.6 = (bf16[4,64,2560]{2,1,0:T(8,128)(2,1)}, bf16[4,64,2560]{2,1,0:T(8,128)(2,1)S(1)}, u32[]{:S(2)}) copy-start(bf16[4,64,2560]{2,1,0:T(8,128)(2,1)S(1)} %pad_maximum_fusion.refs_4_.refs_0_) | copy-start | bytes 3932164
  72.4 385.5 %reduce-scatter.2.cloned.1.call-start = ((), (), s32[]{:S(2)}) async-start(), calls=%async_computation.3 | async-start | bytes 8912896 | tf_op jit(solution)/shard_map/reduce_scatter | solution.py:938
  72.4 36.6 %collective-permute-start.4 = (bf16[4,64,2560]{2,1,0:T(8,128)(2,1)S(1)}, bf16[4,64,2560]{2,1,0:T(8,128)(2,1)S(1)}, u32[]{:S(2)}, u32[]{:S(2)}) collective-permute-start(bf16[4,64,2560]{2,1,0:T(8,128)(2,1)S(1)} %pad_maximum_fusion.refs_4_.refs_0_), channel_id=1, source_target_pairs={{0,4},{2,6},{4,0},{6,2},{8,12},{10,14},{12,8},{14,10},{16,20},{18,... | collective-permute-start | bytes 3932168 | tf_op jit(solution)/shard_map/ppermute | solution.py:884
  73.0 36.0 %collective-permute-start.5 = (bf16[4,64,2560]{2,1,0:T(8,128)(2,1)S(1)}, bf16[4,64,2560]{2,1,0:T(8,128)(2,1)}, u32[]{:S(2)}, u32[]{:S(2)}) collective-permute-start(bf16[4,64,2560]{2,1,0:T(8,128)(2,1)S(1)} %pad_maximum_fusion.refs_4_.refs_0_), channel_id=1, source_target_pairs={{0,1},{1,0},{2,3},{3,2},{4,5},{5,4},{6,7},{7,6},{8,9},{9,8},{10,11... | collective-permute-start | bytes 3932168 | tf_op jit(solution)/shard_map/ppermute | solution.py:888
  77.2 11.9 %copy-start.18 = (s32[2048]{0:T(1024)}, s32[2048]{0:T(1024)S(1)}, u32[]{:S(2)}) copy-start(s32[2048]{0:T(1024)S(1)} %convert_reduce_fusion) | copy-start | bytes 24580
  109.0 15.4 %copy-start.8 = (bf16[4,64,2560]{2,1,0:T(8,128)(2,1)}, bf16[4,64,2560]{2,1,0:T(8,128)(2,1)S(1)}, u32[]{:S(2)}) copy-start(bf16[4,64,2560]{2,1,0:T(8,128)(2,1)S(1)} %collective-permute-done.4.refs_5_.refs_1_) | copy-start | bytes 3932164
  109.0 15.4 %collective-permute-start.6 = (bf16[4,64,2560]{2,1,0:T(8,128)(2,1)S(1)}, bf16[4,64,2560]{2,1,0:T(8,128)(2,1)}, u32[]{:S(2)}, u32[]{:S(2)}) collective-permute-start(bf16[4,64,2560]{2,1,0:T(8,128)(2,1)S(1)} %pad_maximum_fusion.refs_4_.refs_0_), channel_id=1, source_target_pairs={{0,2},{2,0},{4,6},{6,4},{8,10},{10,8},{12,14},{14,12},{16,18},{18,... | collective-permute-start | bytes 3932168 | tf_op jit(solution)/shard_map/ppermute | solution.py:880
  109.1 15.3 %collective-permute-start.7 = (bf16[4,64,2560]{2,1,0:T(8,128)(2,1)S(1)}, bf16[4,64,2560]{2,1,0:T(8,128)(2,1)}, u32[]{:S(2)}, u32[]{:S(2)}) collective-permute-start(bf16[4,64,2560]{2,1,0:T(8,128)(2,1)S(1)} %collective-permute-done.4.refs_5_.refs_1_), channel_id=1, source_target_pairs={{0,2},{2,0},{4,6},{6,4},{8,10},{10,8},{12,14},{14,12},{16,18},{18,... | collective-permute-start | bytes 3932168 | tf_op jit(solution)/shard_map/ppermute | solution.py:880
  109.6 14.8 %collective-permute-start.8 = (bf16[4,64,2560]{2,1,0:T(8,128)(2,1)}, bf16[4,64,2560]{2,1,0:T(8,128)(2,1)}, u32[]{:S(2)}, u32[]{:S(2)}) collective-permute-start(bf16[4,64,2560]{2,1,0:T(8,128)(2,1)} %collective-permute-done.5.refs_8_.refs_4_), channel_id=1, source_target_pairs={{0,2},{2,0},{4,6},{6,4},{8,10},{10,8},{12,14},{14,12},{16,18},{18,... | collective-permute-start | bytes 3932168 | tf_op jit(solution)/shard_map/ppermute | solution.py:880
  109.7 42.5 %collective-permute-start.9 = (bf16[4,64,2560]{2,1,0:T(8,128)(2,1)S(1)}, bf16[4,64,2560]{2,1,0:T(8,128)(2,1)}, u32[]{:S(2)}, u32[]{:S(2)}) collective-permute-start(bf16[4,64,2560]{2,1,0:T(8,128)(2,1)S(1)} %collective-permute-done.4.refs_5_.refs_1_), channel_id=1, source_target_pairs={{0,1},{1,0},{2,3},{3,2},{4,5},{5,4},{6,7},{7,6},{8,9},{9,8},{10,11... | collective-permute-start | bytes 3932168 | tf_op jit(solution)/shard_map/ppermute | solution.py:888
  111.2 41.0 %collective-permute-start.10 = (bf16[1024,256]{1,0:T(8,128)(2,1)}, bf16[1024,256]{1,0:T(8,128)(2,1)}, u32[]{:S(2)}, u32[]{:S(2)}) collective-permute-start(bf16[1024,256]{1,0:T(8,128)(2,1)} %get-tuple-element.140.refs_1_), channel_id=1, source_target_pairs={{0,1},{1,0},{2,3},{3,2},{4,5},{5,4},{6,7},{7,6},{8,9},{9,8},{10,11... | collective-permute-start | bytes 1572872 | tf_op jit(solution)/shard_map/ppermute | solution.py:888
  124.4 27.7 %copy-start.13 = (bf16[1024,256]{1,0:T(8,128)(2,1)S(1)}, bf16[1024,256]{1,0:T(8,128)(2,1)}, u32[]{:S(2)}) copy-start(bf16[1024,256]{1,0:T(8,128)(2,1)} %get-tuple-element.145.refs_1_) | copy-start | bytes 1572868
  124.5 29.8 %copy-start.21 = (f32[4096]{0:T(1024)S(1)}, f32[4096]{0:T(1024)}, u32[]{:S(2)}) copy-start(f32[4096]{0:T(1024)} %param.23) | copy-start | bytes 49156
  152.2 14.3 %collective-permute-start.12 = (bf16[4,64,2560]{2,1,0:T(8,128)(2,1)}, bf16[4,64,2560]{2,1,0:T(8,128)(2,1)S(1)}, u32[]{:S(2)}, u32[]{:S(2)}) collective-permute-start(bf16[4,64,2560]{2,1,0:T(8,128)(2,1)} %collective-permute-done.9.refs_9_.refs_5_), channel_id=1, source_target_pairs={{0,2},{2,0},{4,6},{6,4},{8,10},{10,8},{12,14},{14,12},{16,18},{18,... | collective-permute-start | bytes 3932168 | tf_op jit(solution)/shard_map/ppermute | solution.py:880
  152.2 14.3 %collective-permute-start.11 = (bf16[1024,256]{1,0:T(8,128)(2,1)S(1)}, bf16[1024,256]{1,0:T(8,128)(2,1)S(1)}, u32[]{:S(2)}, u32[]{:S(2)}) collective-permute-start(bf16[1024,256]{1,0:T(8,128)(2,1)S(1)} %copy-done.13), channel_id=1, source_target_pairs={{0,1},{1,0},{2,3},{3,2},{4,5},{5,4},{6,7},{7,6},{8,9},{9,8},{10,11... | collective-permute-start | bytes 1572872 | tf_op jit(solution)/shard_map/ppermute | solution.py:888
  166.5 0.8 copy-start.16
  166.5 1.3 copy-start.9
  263.8 14.4 %collective-permute-start.14 = (bf16[512,4096]{1,0:T(8,128)(2,1)}, bf16[512,4096]{1,0:T(8,128)(2,1)}, u32[]{:S(2)}, u32[]{:S(2)}) collective-permute-start(bf16[512,4096]{1,0:T(8,128)(2,1)} %get-tuple-element.163), channel_id=1, source_target_pairs={{0,2},{2,0},{4,6},{6,4},{8,10},{10,8},{12,14},{14,12},{16,18},{18,... | collective-permute-start | bytes 12582920 | tf_op jit(solution)/shard_map/ppermute | solution.py:880
  264.4 5.1 %copy-start.25 = (bf16[1024,512]{1,0:T(8,128)(2,1)S(1)}, bf16[1024,512]{1,0:T(8,128)(2,1)}, u32[]{:S(2)}) copy-start(bf16[1024,512]{1,0:T(8,128)(2,1)} %get-tuple-element.170) | copy-start | bytes 3145732
  269.0 9.1 %collective-permute-start.13 = (bf16[512,1024]{1,0:T(8,128)(2,1)}, bf16[512,1024]{1,0:T(8,128)(2,1)S(1)}, u32[]{:S(2)}, u32[]{:S(2)}) collective-permute-start(bf16[512,1024]{1,0:T(8,128)(2,1)} %grad_rows.4), channel_id=1, source_target_pairs={{0,2},{2,0},{4,6},{6,4},{8,10},{10,8},{12,14},{14,12},{16,18},{18,... | collective-permute-start | bytes 3145736 | tf_op jit(solution)/shard_map/ppermute | solution.py:880
  269.5 27.3 %collective-permute-start.15 = (bf16[1024,512]{1,0:T(8,128)(2,1)S(1)}, bf16[1024,512]{1,0:T(8,128)(2,1)S(1)}, u32[]{:S(2)}, u32[]{:S(2)}) collective-permute-start(bf16[1024,512]{1,0:T(8,128)(2,1)S(1)} %copy-done.25), channel_id=1, source_target_pairs={{0,1},{1,0},{2,3},{3,2},{4,5},{5,4},{6,7},{7,6},{8,9},{9,8},{10,11... | collective-permute-start | bytes 3145736 | tf_op jit(solution)/shard_map/ppermute | solution.py:888
  278.2 15.3 %copy-start.11 = (bf16[512,1024]{1,0:T(8,128)(2,1)}, bf16[512,1024]{1,0:T(8,128)(2,1)S(1)}, u32[]{:S(2)}) copy-start(bf16[512,1024]{1,0:T(8,128)(2,1)S(1)} %collective-permute-done.13.refs_1_) | copy-start | bytes 3145732
  296.9 1.0 copy-start.7
  303.8 59.0 %collective-permute-start.16 = (bf16[512,2560]{1,0:T(8,128)(2,1)}, bf16[512,2560]{1,0:T(8,128)(2,1)S(1)}, u32[]{:S(2)}, u32[]{:S(2)}) collective-permute-start(bf16[512,2560]{1,0:T(8,128)(2,1)} %merge.3), channel_id=1, source_target_pairs={{0,1},{1,0},{2,3},{3,2},{4,5},{5,4},{6,7},{7,6},{8,9},{9,8},{10,11... | collective-permute-start | bytes 7864328 | tf_op jit(solution)/shard_map/ppermute | solution.py:888
  362.8 1.5 copy-start.10
  369.3 35.8 %collective-permute-start.17 = (bf16[256,2560]{1,0:T(8,128)(2,1)}, bf16[256,2560]{1,0:T(8,128)(2,1)S(1)}, u32[]{:S(2)}, u32[]{:S(2)}) collective-permute-start(bf16[256,2560]{1,0:T(8,128)(2,1)} %merge.4), channel_id=1, source_target_pairs={{0,4},{2,6},{4,0},{6,2},{8,12},{10,14},{12,8},{14,10},{16,20},{18,... | collective-permute-start | bytes 3932168 | tf_op jit(solution)/shard_map/ppermute | solution.py:884
  392.0 15.2 %copy-start.22 = (f32[1,4096]{1,0:T(1,128)S(1)}, f32[1,4096]{1,0:T(1,128)}, u32[]{:S(2)}) copy-start(f32[1,4096]{1,0:T(1,128)} %get-tuple-element.211) | copy-start | bytes 49156
  392.0 16.1 %copy-start.23 = (f32[8,1024]{1,0:T(8,128)S(1)}, f32[8,1024]{1,0:T(8,128)}, u32[]{:S(2)}) copy-start(f32[8,1024]{1,0:T(8,128)} %get-tuple-element.207) | copy-start | bytes 98308
  405.1 3.0 copy-start.15
  405.1 8.4 %collective-permute-start.18 = (bf16[512,1536]{1,0:T(8,128)(2,1)}, bf16[512,1536]{1,0:T(8,128)(2,1)}, u32[]{:S(2)}, u32[]{:S(2)}) collective-permute-start(bf16[512,1536]{1,0:T(8,128)(2,1)} %grad_rows.5), channel_id=1, source_target_pairs={{0,2},{2,0},{4,6},{6,4},{8,10},{10,8},{12,14},{14,12},{16,18},{18,... | collective-permute-start | bytes 4718600 | tf_op jit(solution)/shard_map/ppermute | solution.py:880
  405.1 48.3 %collective-permute-start.20 = (bf16[1024,1024]{1,0:T(8,128)(2,1)}, bf16[1024,1024]{1,0:T(8,128)(2,1)S(1)}, u32[]{:S(2)}, u32[]{:S(2)}) collective-permute-start(bf16[1024,1024]{1,0:T(8,128)(2,1)} %get-tuple-element.202), channel_id=1, source_target_pairs={{0,1},{1,0},{2,3},{3,2},{4,5},{5,4},{6,7},{7,6},{8,9},{9,8},{10,11... | collective-permute-start | bytes 6291464 | tf_op jit(solution)/shard_map/ppermute | solution.py:888
  421.6 9.3 %copy-start.12 = (bf16[256,2560]{1,0:T(8,128)(2,1)S(1)}, bf16[256,2560]{1,0:T(8,128)(2,1)}, u32[]{:S(2)}) copy-start(bf16[256,2560]{1,0:T(8,128)(2,1)} %merge.5) | copy-start | bytes 3932164
  421.6 14.6 %copy-start.20 = (f32[8,1024]{1,0:T(8,128)S(1)}, f32[8,1024]{1,0:T(8,128)}, u32[]{:S(2)}) copy-start(f32[8,1024]{1,0:T(8,128)} %get-tuple-element.204) | copy-start | bytes 98308
  421.6 36.2 %collective-permute-start.19 = (bf16[256,1536]{1,0:T(8,128)(2,1)}, bf16[256,1536]{1,0:T(8,128)(2,1)}, u32[]{:S(2)}, u32[]{:S(2)}) collective-permute-start(bf16[256,1536]{1,0:T(8,128)(2,1)} %get-tuple-element.201), channel_id=1, source_target_pairs={{0,4},{2,6},{4,0},{6,2},{8,12},{10,14},{12,8},{14,10},{16,20},{18,... | collective-permute-start | bytes 2359304 | tf_op jit(solution)/shard_map/ppermute | solution.py:884
  431.9 21.5 %collective-permute-start.21 = (bf16[64,2560]{1,0:T(8,128)(2,1)}, bf16[64,2560]{1,0:T(8,128)(2,1)}, u32[]{:S(2)}, u32[]{:S(2)}) collective-permute-start(bf16[64,2560]{1,0:T(8,128)(2,1)} %get-tuple-element.233), channel_id=1, source_target_pairs={{0,8},{2,10},{4,12},{6,14},{8,16},{10,18},{12,20},{14,22},{16,24},... | collective-permute-start | bytes 983048 | tf_op jit(solution)/shard_map/ppermute | solution.py:976
  433.9 23.9 %collective-permute-start.22 = (bf16[64,2560]{1,0:T(8,128)(2,1)}, bf16[64,2560]{1,0:T(8,128)(2,1)}, u32[]{:S(2)}, u32[]{:S(2)}) collective-permute-start(bf16[64,2560]{1,0:T(8,128)(2,1)} %get-tuple-element.232), channel_id=1, source_target_pairs={{0,16},{2,18},{4,20},{6,22},{8,24},{10,26},{12,28},{14,30},{16,0},... | collective-permute-start | bytes 983048 | tf_op jit(solution)/shard_map/ppermute | solution.py:976
  434.8 23.0 %collective-permute-start.23 = (bf16[64,2560]{1,0:T(8,128)(2,1)}, bf16[64,2560]{1,0:T(8,128)(2,1)}, u32[]{:S(2)}, u32[]{:S(2)}) collective-permute-start(bf16[64,2560]{1,0:T(8,128)(2,1)} %get-tuple-element.231), channel_id=1, source_target_pairs={{0,24},{2,26},{4,28},{6,30},{8,0},{10,2},{12,4},{14,6},{16,8},{18,... | collective-permute-start | bytes 983048 | tf_op jit(solution)/shard_map/ppermute | solution.py:976
  453.4 4.5 copy-start.14
  457.8 12.8 %copy-start.17 = (bf16[64,4096]{1,0:T(8,128)(2,1)S(1)}, bf16[64,4096]{1,0:T(8,128)(2,1)}, u32[]{:S(2)}) copy-start(bf16[64,4096]{1,0:T(8,128)(2,1)} %reduce-scatter.2.cloned.1.call-done) | copy-start | bytes 1572868
  457.9 13.3 %collective-permute-start.24 = (f32[16,1024]{1,0:T(8,128)S(1)}, f32[16,1024]{1,0:T(8,128)S(1)}, u32[]{:S(2)}, u32[]{:S(2)}) collective-permute-start(f32[16,1024]{1,0:T(8,128)S(1)} %concatenate.24), channel_id=1, source_target_pairs={{0,2},{2,0},{4,6},{6,4},{8,10},{10,8},{12,14},{14,12},{16,18},{18,... | collective-permute-start | bytes 196616 | tf_op jit(solution)/shard_map/ppermute | solution.py:1002
  460.4 25.3 %collective-permute-start.28 = (bf16[64,1536]{1,0:T(8,128)(2,1)}, bf16[64,1536]{1,0:T(8,128)(2,1)}, u32[]{:S(2)}, u32[]{:S(2)}) collective-permute-start(bf16[64,1536]{1,0:T(8,128)(2,1)} %get-tuple-element.236), channel_id=1, source_target_pairs={{0,8},{2,10},{4,12},{6,14},{8,16},{10,18},{12,20},{14,22},{16,24},... | collective-permute-start | bytes 589832 | tf_op jit(solution)/shard_map/ppermute | solution.py:976
  468.2 17.5 %collective-permute-start.29 = (bf16[64,1536]{1,0:T(8,128)(2,1)}, bf16[64,1536]{1,0:T(8,128)(2,1)}, u32[]{:S(2)}, u32[]{:S(2)}) collective-permute-start(bf16[64,1536]{1,0:T(8,128)(2,1)} %get-tuple-element.235), channel_id=1, source_target_pairs={{0,16},{2,18},{4,20},{6,22},{8,24},{10,26},{12,28},{14,30},{16,0},... | collective-permute-start | bytes 589832 | tf_op jit(solution)/shard_map/ppermute | solution.py:976
  468.9 16.8 %collective-permute-start.30 = (bf16[64,1536]{1,0:T(8,128)(2,1)}, bf16[64,1536]{1,0:T(8,128)(2,1)}, u32[]{:S(2)}, u32[]{:S(2)}) collective-permute-start(bf16[64,1536]{1,0:T(8,128)(2,1)} %get-tuple-element.234), channel_id=1, source_target_pairs={{0,24},{2,26},{4,28},{6,30},{8,0},{10,2},{12,4},{14,6},{16,8},{18,... | collective-permute-start | bytes 589832 | tf_op jit(solution)/shard_map/ppermute | solution.py:976
  470.6 15.1 %collective-permute-start.27 = (bf16[64,2048]{1,0:T(8,128)(2,1)S(1)}, bf16[64,2048]{1,0:T(8,128)(2,1)S(1)}, u32[]{:S(2)}, u32[]{:S(2)}) collective-permute-start(bf16[64,2048]{1,0:T(8,128)(2,1)S(1)} %slice.91), channel_id=1, source_target_pairs={{0,1},{1,0},{2,3},{3,2},{4,5},{5,4},{6,7},{7,6},{8,9},{9,8},{10,11... | collective-permute-start | bytes 786440 | tf_op jit(solution)/shard_map/ppermute | solution.py:888
  471.2 4.3 collective-permute-start.25
  475.6 10.1 %collective-permute-start.26 = (f32[16,1024]{1,0:T(8,128)S(1)}, f32[16,1024]{1,0:T(8,128)S(1)}, u32[]{:S(2)}, u32[]{:S(2)}) collective-permute-start(f32[16,1024]{1,0:T(8,128)S(1)} %add.150), channel_id=1, source_target_pairs={{0,1},{1,0},{2,3},{3,2},{4,5},{5,4},{6,7},{7,6},{8,9},{9,8},{10,11... | collective-permute-start | bytes 196616 | tf_op jit(solution)/shard_map/ppermute | solution.py:888
  485.7 4.3 collective-permute-start.31
  490.0 5.2 %collective-permute-start.32 = (f32[16,1024]{1,0:T(8,128)S(1)}, f32[16,1024]{1,0:T(8,128)S(1)}, u32[]{:S(2)}, u32[]{:S(2)}) collective-permute-start(f32[16,1024]{1,0:T(8,128)S(1)} %add.161), channel_id=1, source_target_pairs={{0,16},{2,18},{4,20},{6,22},{8,24},{10,26},{12,28},{14,30},{16,0},... | collective-permute-start | bytes 196616 | tf_op jit(solution)/shard_map/ppermute | solution.py:1008
Sparse Core Ops, SparseCore 0:
  10.9 61.4 all-gather.2
  74.5 76.8 all-gather.4
  297.0 109.3 reduce-scatter.1
